TPU v7x, 32 devices: a whole 2x2x4 slice. The times are simulated.
32 devices in a mesh: shard: 2 (over x), context: 4 (over y, core), tensor: 4 (over z).
Axes of the slice: x: 2, y: 2, z: 4, core: 2. Of those that a mesh axis runs over, the one named last changes fastest.
Arguments:
- tokens: bfloat16 [2, 2048, 2048], P('shard', 'context'), may hold values from -6 to 6
- block_order: int32 [2, 8], P('shard'), may hold values from 0 to 7, each once within a row
- w_query: bfloat16 [2048, 2048], P(('shard', 'context'), 'tensor'), may hold values from -0.5 to 0.5
- w_key: bfloat16 [2048, 512], P(('shard', 'context'), 'tensor'), may hold values from -0.5 to 0.5
- w_value: bfloat16 [2048, 512], P(('shard', 'context'), 'tensor'), may hold values from -0.125 to 0.125
- w_output: bfloat16 [2048, 2048], P('tensor', ('shard', 'context')), may hold values from -1.5 to 1.5
- w_gate: bfloat16 [2048, 8192], P(('shard', 'context'), 'tensor'), may hold values from -0.125 to 0.125
- w_up: bfloat16 [2048, 8192], P(('shard', 'context'), 'tensor'), may hold values from -0.125 to 0.125
- w_down: bfloat16 [8192, 2048], P('tensor', ('shard', 'context')), may hold values from -0.5 to 0.5
- norm_attn: bfloat16 [2048], P(('shard', 'context')), may hold values from 0.5 to 1.5
- norm_ffn: bfloat16 [2048], P(('shard', 'context')), may hold values from 0.5 to 1.5
- grad_out: bfloat16 [2, 2048, 2048], P('shard', 'context'), may hold values from -6 to 6
Outputs:
- layer_out: bfloat16 [2, 2048, 2048], P('shard', 'context')
- grad_tokens: float32 [2, 2048, 2048], P('shard', 'context')
- grad_w_query: float32 [2048, 2048], P(('shard', 'context'), 'tensor')
- grad_w_key: float32 [2048, 512], P(('shard', 'context'), 'tensor')
- grad_w_value: float32 [2048, 512], P(('shard', 'context'), 'tensor')
- grad_w_output: float32 [2048, 2048], P('tensor', ('shard', 'context'))
- grad_w_gate: float32 [2048, 8192], P(('shard', 'context'), 'tensor')
- grad_w_up: float32 [2048, 8192], P(('shard', 'context'), 'tensor')
- grad_w_down: float32 [8192, 2048], P('tensor', ('shard', 'context'))
- grad_norm_attn: float32 [2048], P(('shard', 'context'))
- grad_norm_ffn: float32 [2048], P(('shard', 'context'))
Inputs may be any that keep to these rules, and one draw needn't show every extreme that they name: Each row is a permutation of the 8 blocks of its sequence; stored block j of sequence s holds the tokens of block block_order[s, j].
All inputs are finite; a program needn't handle non-finite values.
Results may differ from a plain program's by a relative error of at most 0.015.
Values may be sent and summed in bfloat16 or wider, within the bound.
A program may use at most 192 MiB of HBM per device.

v0:
```python
import functools
import math

import jax
import jax.numpy as jnp
from jax import lax
from jax.experimental import pallas as pl
from jax.experimental.pallas import tpu as pltpu
from jax.sharding import PartitionSpec as P


HD = 64
BLK = 256
LANES = 128
EPSILON = 1e-05
SCORE_SCALE = 0.015625
RESIDUAL_SCALE = 0.22
ROPE_BASE = 10000000.0
MASKED_SCORE = -1e30
PLANE = ("shard", "context")
VMEM_BYTES = 64000 * 1024


F32 = jnp.float32
BF16 = jnp.bfloat16


def plane_size():
    return lax.axis_size("shard") * lax.axis_size("context")


def plane_index():
    return lax.axis_index("shard") * lax.axis_size("context") + lax.axis_index("context")


def swap(value, axes, size, bit):
    return lax.ppermute(value, axes, [(i, i ^ bit) for i in range(size)])


def gather_pair(first, second, far_after=(), near_after=(), cross_after=(), core_after=()):
    size = plane_size()
    bits = [1 << b for b in range(1, size.bit_length() - 1)]
    sides = [{0: first}, {0: second}]
    if len(bits) == 2:
        near, far = bits
        for side in sides:
            side[far] = swap(after(side[0], *far_after), PLANE, size, far)
        for side in reversed(sides):
            side[near] = swap(after(side[0], *near_after), PLANE, size, near)
        sides[0][near | far] = swap(after(sides[0][far], *cross_after), PLANE, size, near)
        sides[1][near | far] = swap(after(sides[1][near], *cross_after), PLANE, size, far)
    else:
        for side in sides:
            for bit in bits:
                for r in list(side):
                    side[r | bit] = swap(side[r], PLANE, size, bit)
    for side in sides:
        for r in list(side):
            side[r | 1] = swap(after(side[r], *core_after), PLANE, size, 1)
    return [[side[r] for r in range(size)] for side in sides]


def widened(pieces):
    level = 1
    while pieces[0].shape[1] < LANES:
        upper = (plane_index() // level) % 2 == 1
        pairs = zip(pieces[0::2], pieces[1::2])
        pieces = [jnp.where(upper, jnp.concatenate([b, a], 1), jnp.concatenate([a, b], 1)) for a, b in pairs]
        level *= 2
    return pieces


def take_sum(side, bit, kept):
    sent = side[kept | bit].astype(BF16)
    total = side[kept].astype(F32) + swap(sent, PLANE, plane_size(), bit).astype(F32)
    return total if kept == 0 else total.astype(BF16)


def reduce_pair(first, second):
    size = plane_size()
    bits = [1 << b for b in range(1, size.bit_length() - 1)]
    sides = [dict(first), dict(second)]
    if len(bits) == 2:
        near, far = bits
        sides[0][near] = take_sum(sides[0], far, near)
        sides[1][far] = take_sum(sides[1], near, far)
        done = []
        for side in sides:
            a = swap(side[near].astype(BF16), PLANE, size, near).astype(F32)
            b = swap(side[far].astype(BF16), PLANE, size, far).astype(F32)
            done.append(side[0] + a + b)
        return done
    done = []
    for side in sides:
        for bit in reversed(bits):
            side = {r: take_sum(side, bit, r) for r in side if not r & bit}
        done.append(side[0])
    return done


def gather_small(values):
    size = plane_size()
    stacked = values[None]
    bit = 1
    while bit < size:
        stacked = jnp.concatenate([stacked, swap(stacked, PLANE, size, bit)], axis=0)
        bit *= 2
    picks = jnp.arange(size, dtype=jnp.int32)[:, None] ^ plane_index()
    chosen = (picks == jnp.arange(size, dtype=jnp.int32)[None, :]).astype(F32)
    return jnp.einsum("ij,jkw->kiw", chosen, stacked.astype(F32), precision=lax.Precision.HIGHEST)


def chunk_of(rows, index, count):
    return lax.dynamic_slice_in_dim(rows, index * count, count, 0)


def rows_sum(partial):
    size = lax.axis_size("tensor")
    me = lax.axis_index("tensor")
    count = partial.shape[0] // size
    total = chunk_of(partial, me, count).astype(F32)
    for shift in range(1, size):
        sent = chunk_of(partial, lax.rem(me + shift, size), count)
        pairs = [(i, (i + shift) % size) for i in range(size)]
        total = total + lax.ppermute(sent, "tensor", pairs).astype(F32)
    return total


def rows_gather(chunk):
    size = lax.axis_size("tensor")
    me = lax.axis_index("tensor")
    count = chunk.shape[0]
    parts = [chunk]
    for shift in range(1, size):
        pairs = [(i, (i + shift) % size) for i in range(size)]
        parts.append(lax.ppermute(chunk, "tensor", pairs))
    whole = jnp.zeros((size * count,) + chunk.shape[1:], chunk.dtype)
    for shift in range(size):
        place = lax.rem(me - shift + size, size) * count
        whole = lax.dynamic_update_slice_in_dim(whole, parts[shift], place, 0)
    return whole


def params(steps):
    return pltpu.CompilerParams(
        dimension_semantics=("arbitrary",) * steps, vmem_limit_bytes=VMEM_BYTES
    )


def place_pieces(pieces, whole, sem, axis):
    size = len(pieces)
    me = plane_index() // (plane_size() // size)
    extent = whole.shape[axis] // size
    for r, piece in enumerate(pieces):
        start = pl.multiple_of((me ^ r) * extent, extent)
        target = whole.at[pl.ds(start, extent)] if axis == 0 else whole.at[:, pl.ds(start, extent)]
        pltpu.make_async_copy(piece, target, sem).start()


def await_whole(whole, sem):
    pltpu.make_async_copy(whole, whole, sem).wait()


ANYWHERE = pl.BlockSpec(memory_space=pl.ANY)


def turned(values, lane, sign):
    half = HD // 2
    upper = pltpu.roll(values, LANES - half, 1)
    lower = pltpu.roll(values, half, 1)
    return jnp.where(lane % HD < half, -sign * upper, sign * lower)


def qkv_body(count, tokens, gain, cosine, sine, *rest):
    pieces, (normed, queries, keys_values, weight, sem) = rest[:count], rest[count:]

    @pl.when(pl.program_id(0) == 0)
    def _():
        place_pieces(pieces, weight, sem, 0)

    values = tokens[...].astype(F32)
    inverse = lax.rsqrt(jnp.mean(values * values, axis=1, keepdims=True) + EPSILON)
    low = (values * inverse * gain[...]).astype(BF16)
    normed[...] = low

    @pl.when(pl.program_id(0) == 0)
    def _():
        await_whole(weight, sem)

    cos, sin = cosine[...], sine[...]
    lane = lax.broadcasted_iota(jnp.int32, cos.shape, 1)
    q_width = queries.shape[1]
    k_width = keys_values.shape[1] // 2
    for start in range(0, weight.shape[1], LANES):
        part = jnp.dot(low, weight[:, start : start + LANES * 1], preferred_element_type=F32)
        if start < q_width + k_width:
            part = part * cos + turned(part, lane, 1.0) * sin
        if start < q_width:
            queries[:, start : start + LANES] = (part.astype(BF16) * SCORE_SCALE).astype(BF16)
        else:
            keys_values[:, start - q_width : start - q_width + LANES] = part.astype(BF16)


def project_qkv(tokens, gain, cosine, sine, pieces, q_width):
    rows, width = tokens.shape
    total = pieces[0].shape[1]
    tile = min(rows, 256)
    row_spec = lambda w: pl.BlockSpec((tile, w), lambda i: (i, 0))
    return pl.pallas_call(
        functools.partial(qkv_body, len(pieces)),
        grid=(rows // tile,),
        in_specs=[row_spec(width), pl.BlockSpec((1, width), lambda i: (0, 0)), row_spec(LANES), row_spec(LANES)]
        + [ANYWHERE] * len(pieces),
        out_specs=[row_spec(width), row_spec(q_width), row_spec(total - q_width)],
        out_shape=[
            jax.ShapeDtypeStruct((rows, width), BF16),
            jax.ShapeDtypeStruct((rows, q_width), BF16),
            jax.ShapeDtypeStruct((rows, total - q_width), BF16),
        ],
        scratch_shapes=[pltpu.VMEM((width, total), BF16), pltpu.SemaphoreType.DMA],
        compiler_params=params(1),
        cost_estimate=pl.CostEstimate(
            flops=2 * rows * width * total, bytes_accessed=2 * (2 * rows * width + width * total), transcendentals=0
        ),
        name="project_qkv",
    )(tokens, gain, cosine, sine, *pieces)


def qkv_back_body(count, d_queries, d_keys_values, cosine, sine, *rest):
    pieces, (d_all, d_normed, weight, sem) = rest[:count], rest[count:]

    @pl.when(pl.program_id(0) == 0)
    def _():
        place_pieces(pieces, weight, sem, 0)

    cos, sin = cosine[...], sine[...]
    lane = lax.broadcasted_iota(jnp.int32, cos.shape, 1)
    q_width = d_queries.shape[1]
    k_width = d_keys_values.shape[1] // 2
    for start in range(0, d_all.shape[1], LANES):
        if start < q_width:
            part = d_queries[:, start : start + LANES]
        else:
            part = d_keys_values[:, start - q_width : start - q_width + LANES]
        if start < q_width + k_width:
            part = part * cos + turned(part * sin, lane, -1.0)
        d_all[:, start : start + LANES] = part.astype(BF16)

    @pl.when(pl.program_id(0) == 0)
    def _():
        await_whole(weight, sem)

    step = 512
    for start in range(0, weight.shape[0], step):
        d_normed[:, start : start + step] = lax.dot_general(
            d_all[...], weight[start : start + step, :], (((1,), (1,)), ((), ())), preferred_element_type=F32
        ).astype(BF16)


def project_qkv_back(d_queries, d_keys_values, cosine, sine, pieces):
    rows, q_width = d_queries.shape
    total = pieces[0].shape[1]
    width = pieces[0].shape[0] * len(pieces)
    tile = min(rows, 256)
    row_spec = lambda w: pl.BlockSpec((tile, w), lambda i: (i, 0))
    return pl.pallas_call(
        functools.partial(qkv_back_body, len(pieces)),
        grid=(rows // tile,),
        in_specs=[row_spec(q_width), row_spec(total - q_width), row_spec(LANES), row_spec(LANES)]
        + [ANYWHERE] * len(pieces),
        out_specs=[row_spec(total), row_spec(width)],
        out_shape=[jax.ShapeDtypeStruct((rows, total), BF16), jax.ShapeDtypeStruct((rows, width), BF16)],
        scratch_shapes=[pltpu.VMEM((width, total), BF16), pltpu.SemaphoreType.DMA],
        compiler_params=params(1),
        cost_estimate=pl.CostEstimate(
            flops=2 * rows * width * total, bytes_accessed=2 * (2 * rows * width + width * total), transcendentals=0
        ),
        name="project_qkv_back",
    )(d_queries, d_keys_values, cosine, sine, *pieces)


def gathered_body(count, axis, transposed, left, *rest):
    pieces, (out, weight, sem) = rest[:count], rest[count:]

    @pl.when(pl.program_id(0) == 0)
    def _():
        place_pieces(pieces, weight, sem, axis)
        await_whole(weight, sem)

    step = min(out.shape[1], 512)
    for start in range(0, out.shape[1], step):
        if transposed:
            part = lax.dot_general(
                left[...], weight[start : start + step, :], (((1,), (1,)), ((), ())), preferred_element_type=F32
            )
        else:
            part = jnp.dot(left[...], weight[:, start : start + step], preferred_element_type=F32)
        out[:, start : start + step] = part.astype(out.dtype)


def gathered_matmul(left, pieces, axis, transposed):
    rows = left.shape[0]
    shape = list(pieces[0].shape)
    shape[axis] *= len(pieces)
    outer = shape[0] if transposed else shape[1]
    tile = min(rows, 256)
    return pl.pallas_call(
        functools.partial(gathered_body, len(pieces), axis, transposed),
        grid=(rows // tile,),
        in_specs=[pl.BlockSpec((tile, left.shape[1]), lambda i: (i, 0))] + [ANYWHERE] * len(pieces),
        out_specs=pl.BlockSpec((tile, outer), lambda i: (i, 0)),
        out_shape=jax.ShapeDtypeStruct((rows, outer), BF16),
        scratch_shapes=[pltpu.VMEM(tuple(shape), BF16), pltpu.SemaphoreType.DMA],
        compiler_params=params(1),
        cost_estimate=pl.CostEstimate(
            flops=2 * rows * shape[0] * shape[1],
            bytes_accessed=2 * (rows * sum(shape) + shape[0] * shape[1]),
            transcendentals=0,
        ),
    )(left, *pieces)


def ffn_body(count, narrow, tile, normed, d_ffn, *rest):
    gate_pieces, up_pieces, rest = rest[:count], rest[count : 2 * count], rest[2 * count :]
    low_pieces, high_pieces, rest = rest[:narrow], rest[narrow : 2 * narrow], rest[2 * narrow :]
    active, d_gate, d_up, out, d_normed, gate, up, down, out_sum, d_sum, sems = rest
    f_step = pl.program_id(1)
    half = down.shape[0] // 2

    @pl.when((pl.program_id(0) == 0) & (f_step == 0))
    def _():
        place_pieces(gate_pieces, gate, sems.at[0], 0)
        place_pieces(up_pieces, up, sems.at[1], 0)
        place_pieces(low_pieces, down.at[pl.ds(0, half)], sems.at[2], 1)
        place_pieces(high_pieces, down.at[pl.ds(half, half)], sems.at[3], 1)
        await_whole(gate, sems.at[0])
        await_whole(up, sems.at[1])
        await_whole(down.at[pl.ds(0, half)], sems.at[2])
        await_whole(down.at[pl.ds(half, half)], sems.at[3])

    units = pl.ds(pl.multiple_of(f_step * tile, tile), tile)
    gate_tile, up_tile, down_tile = gate[:, units], up[:, units], down[units, :]
    gate_in = jnp.dot(normed[...], gate_tile, preferred_element_type=F32)
    upward = jnp.dot(normed[...], up_tile, preferred_element_type=F32)
    d_active = lax.dot_general(d_ffn[...], down_tile, (((1,), (1,)), ((), ())), preferred_element_type=F32)
    sigma = 1.0 / (1.0 + jnp.exp(-gate_in))
    silu = gate_in * sigma
    active_low = (silu * upward).astype(BF16)
    gate_low = (d_active * upward * (sigma * (1.0 + gate_in * (1.0 - sigma)))).astype(BF16)
    up_low = (d_active * silu).astype(BF16)
    active[...] = active_low
    d_gate[...] = gate_low
    d_up[...] = up_low
    part = jnp.dot(active_low, down_tile, preferred_element_type=F32)
    d_part = lax.dot_general(gate_low, gate_tile, (((1,), (1,)), ((), ())), preferred_element_type=F32)
    d_part += lax.dot_general(up_low, up_tile, (((1,), (1,)), ((), ())), preferred_element_type=F32)

    @pl.when(f_step == 0)
    def _():
        out_sum[...] = part
        d_sum[...] = d_part

    @pl.when(f_step > 0)
    def _():
        out_sum[...] += part
        d_sum[...] += d_part

    @pl.when(f_step == pl.num_programs(1) - 1)
    def _():
        out[...] = out_sum[...].astype(BF16)
        d_normed[...] = d_sum[...].astype(BF16)


def ffn(normed, d_ffn, gate_pieces, up_pieces, low_pieces, high_pieces):
    rows, width = normed.shape
    units = gate_pieces[0].shape[1]
    count = len(gate_pieces)
    tile = 256
    row_tile = min(rows, 512)
    once = pl.Buffered(1)
    row_spec = pl.BlockSpec((row_tile, width), lambda i, f: (i, 0), pipeline_mode=once)
    unit_spec = pl.BlockSpec((row_tile, tile), lambda i, f: (i, f))
    unit_shape = jax.ShapeDtypeStruct((rows, units), BF16)
    row_shape = jax.ShapeDtypeStruct((rows, width), BF16)
    return pl.pallas_call(
        functools.partial(ffn_body, count, len(low_pieces), tile),
        grid=(rows // row_tile, units // tile),
        in_specs=[row_spec, row_spec] + [ANYWHERE] * (2 * count + 2 * len(low_pieces)),
        out_specs=[unit_spec, unit_spec, unit_spec, row_spec, row_spec],
        out_shape=[unit_shape, unit_shape, unit_shape, row_shape, row_shape],
        scratch_shapes=[
            pltpu.VMEM((width, units), BF16),
            pltpu.VMEM((width, units), BF16),
            pltpu.VMEM((units, width), BF16),
            pltpu.VMEM((row_tile, width), F32),
            pltpu.VMEM((row_tile, width), F32),
            pltpu.SemaphoreType.DMA((4,)),
        ],
        compiler_params=params(2),
        cost_estimate=pl.CostEstimate(
            flops=12 * rows * width * units, bytes_accessed=6 * width * units + 14 * rows * width, transcendentals=rows * units
        ),
        name="feed_forward",
    )(normed, d_ffn, *gate_pieces, *up_pieces, *low_pieces, *high_pieces)


def doubled(values, lane, head):
    rolled = pltpu.roll(values.astype(F32), HD, 1).astype(BF16)
    return jnp.where((lane < HD) == (head == 0), values, rolled)


def block_bias(order, seq, r, block):
    per = order.shape[1] // lax.axis_size("context")
    own = order[seq, lax.axis_index("context") * per + pl.program_id(3)]
    other = order[seq, (lax.axis_index("context") ^ r) * per + block]
    return jnp.where(other <= own, 0.0, MASKED_SCORE).astype(F32)


def masked_scores(order, pieces_k, query):
    seq = pl.program_id(0)
    scores = []
    for r, key_rows in enumerate(pieces_k):
        part = lax.dot_general(key_rows, query, (((1,), (1,)), ((), ())), preferred_element_type=F32)
        for block in range(key_rows.shape[0] // BLK):
            bias = block_bias(order, seq, r, block)
            scores.append(part[block * BLK : (block + 1) * BLK] + bias)
    return scores


def attend_body(count, order, query_ref, *rest):
    pieces, (mixture, logs) = rest[:count], rest[count:]
    head = pl.program_id(1)
    lane = lax.broadcasted_iota(jnp.int32, (1, LANES), 1)
    keys = [doubled(piece[:, :LANES], lane, head) for piece in pieces]
    values = [doubled(piece[:, LANES:], lane, head) for piece in pieces]
    query = query_ref[...]
    parts = []
    for side in range(2):
        chosen = (lane < HD) if side == 0 else (lane >= HD)
        scores = masked_scores(order, keys, jnp.where(chosen, query, jnp.zeros_like(query)))
        top = functools.reduce(jnp.maximum, [jnp.max(s, axis=0, keepdims=True) for s in scores])
        powers = [jnp.exp(s - top) for s in scores]
        total = sum(jnp.sum(p, axis=0, keepdims=True) for p in powers)
        low = jnp.concatenate([p.astype(BF16) for p in powers], axis=0)
        whole = jnp.concatenate(values, axis=0)
        mixed = lax.dot_general(whole, low, (((0,), (0,)), ((), ())), preferred_element_type=F32)
        parts.append(mixed / total)
        logs[side : side + 1, :] = top + jnp.log(total)
    row = lax.broadcasted_iota(jnp.int32, (LANES, 1), 0)
    mixture[...] = jnp.where(row < HD, parts[0], parts[1]).T.astype(BF16)


def attend_specs(order, queries, group_pairs):
    seqs = order.shape[0]
    rows = queries.shape[0] // seqs
    tiles = rows // BLK
    grid = (seqs, 2, group_pairs, tiles)
    q_spec = pl.BlockSpec((BLK, LANES), lambda s, h, g, t: (s * tiles + t, h * group_pairs + g))
    kv_spec = pl.BlockSpec((rows, 2 * LANES), lambda s, h, g, t: (s, 0))
    log_spec = pl.BlockSpec((None, 2, BLK), lambda s, h, g, t: (h * group_pairs + g, 0, s * tiles + t))
    return grid, q_spec, kv_spec, log_spec


def attend(order, queries, pieces):
    rows, q_width = queries.shape
    pairs = q_width // LANES
    grid, q_spec, kv_spec, log_spec = attend_specs(order, queries, pairs // 2)
    keys = rows * len(pieces) // order.shape[0]
    return pl.pallas_call(
        functools.partial(attend_body, len(pieces)),
        grid=grid,
        in_specs=[pl.BlockSpec(memory_space=pltpu.SMEM), q_spec] + [kv_spec] * len(pieces),
        out_specs=[q_spec, log_spec],
        out_shape=[jax.ShapeDtypeStruct((rows, q_width), BF16), jax.ShapeDtypeStruct((pairs, 2, rows), F32)],
        compiler_params=params(4),
        cost_estimate=pl.CostEstimate(
            flops=8 * rows * keys * q_width * 2, bytes_accessed=8 * rows * q_width, transcendentals=rows * keys * q_width // HD
        ),
        name="attend",
    )(order, queries, *pieces)


def attend_back_body(count, order, query_ref, grad_ref, logs, *rest):
    pieces, rest = rest[:count], rest[count:]
    d_query, outs, (d_key_sum, d_value_sum) = rest[0], rest[1 : 1 + count], rest[1 + count :]
    head, pair, tile = pl.program_id(1), pl.program_id(2), pl.program_id(3)
    lane = lax.broadcasted_iota(jnp.int32, (1, LANES), 1)
    keys = [doubled(piece[:, :LANES], lane, head) for piece in pieces]
    values = jnp.concatenate([doubled(piece[:, LANES:], lane, head) for piece in pieces], axis=0)
    whole_keys = jnp.concatenate(keys, axis=0)
    parts, d_keys, d_values = [], 0.0, 0.0
    for side in range(2):
        chosen = (lane < HD) if side == 0 else (lane >= HD)
        query = jnp.where(chosen, query_ref[...], jnp.zeros_like(query_ref[...]))
        grad = jnp.where(chosen, grad_ref[...], jnp.zeros_like(grad_ref[...]))
        scores = jnp.concatenate(masked_scores(order, keys, query), axis=0)
        soft = jnp.exp(scores - logs[side : side + 1, :])
        d_soft = lax.dot_general(values, grad, (((1,), (1,)), ((), ())), preferred_element_type=F32)
        inner = jnp.sum(soft * d_soft, axis=0, keepdims=True)
        d_scores = (soft * (d_soft - inner)).astype(BF16)
        d_values += jnp.dot(soft.astype(BF16), grad, preferred_element_type=F32)
        d_keys += jnp.dot(d_scores, query, preferred_element_type=F32)
        parts.append(lax.dot_general(whole_keys, d_scores, (((0,), (0,)), ((), ())), preferred_element_type=F32))
    row = lax.broadcasted_iota(jnp.int32, (LANES, 1), 0)
    d_query[...] = jnp.where(row < HD, parts[0], parts[1]).T * SCORE_SCALE

    first = (pair == 0) & (tile == 0)
    last = (pair == pl.num_programs(2) - 1) & (tile == pl.num_programs(3) - 1)

    @pl.when(first)
    def _():
        d_key_sum[...] = d_keys
        d_value_sum[...] = d_values

    @pl.when(jnp.logical_not(first))
    def _():
        d_key_sum[...] += d_keys
        d_value_sum[...] += d_values

    @pl.when(last)
    def _():
        wanted = (lane < HD) == (head == 0)
        rows = outs[0].shape[0]
        for r, out in enumerate(outs):
            for base, total in ((0, d_key_sum), (LANES, d_value_sum)):
                part = total[r * rows : (r + 1) * rows, :]
                both = (part + pltpu.roll(part, HD, 1)).astype(out.dtype)
                spot = pl.ds(base, LANES)

                @pl.when(head == 0)
                def _():
                    out[:, spot] = both

                @pl.when(head == 1)
                def _():
                    out[:, spot] = jnp.where(wanted, both.astype(F32), out[:, spot].astype(F32)).astype(out.dtype)


def attend_back(order, queries, grads, logs, pieces):
    rows, q_width = queries.shape
    pairs = q_width // LANES
    grid, q_spec, kv_spec, log_spec = attend_specs(order, queries, pairs // 2)
    keys = rows * len(pieces) // order.shape[0]
    return pl.pallas_call(
        functools.partial(attend_back_body, len(pieces)),
        grid=grid,
        in_specs=[pl.BlockSpec(memory_space=pltpu.SMEM), q_spec, q_spec, log_spec] + [kv_spec] * len(pieces),
        out_specs=[q_spec] + [kv_spec] * len(pieces),
        out_shape=[jax.ShapeDtypeStruct((rows, q_width), F32)]
        + [jax.ShapeDtypeStruct((rows, 2 * LANES), F32 if r % 2 == 0 else BF16) for r in range(len(pieces))],
        scratch_shapes=[pltpu.VMEM((keys, LANES), F32), pltpu.VMEM((keys, LANES), F32)],
        compiler_params=params(4),
        cost_estimate=pl.CostEstimate(
            flops=20 * rows * keys * q_width * 2, bytes_accessed=12 * rows * q_width, transcendentals=rows * keys * q_width // HD
        ),
        name="attend_back",
    )(order, queries, grads, logs, *pieces)


def line_steps(rows):
    half = rows // 2
    sub = 16
    return half, sub, half // sub


def line_body(finish, keep_state, gain_sum, n_in, *refs):
    partial, ins, rest = refs[0], refs[1 : 1 + n_in], refs[1 + n_in :]
    result, rest = rest[0], rest[1:]
    state_out, rest = (rest[0], rest[1:]) if keep_state else (None, rest)
    gain_out, rest = (rest[0], rest[1:]) if gain_sum else (None, rest)
    from_outer, from_peer, staged, send, recv = rest
    half, sub, count = line_steps(partial.shape[0])
    me = lax.axis_index("tensor")
    side = me // 2
    inner = lax.rem(me, 3) != 0
    to_outer, to_inner, to_peer = side * 3, 1 + side, 3 - me
    near, far = side * half, (1 - side) * half

    def rows(base, k):
        return pl.ds(pl.multiple_of(base + k * sub, sub), sub)

    def remote(source, target, s, r, k, where):
        return pltpu.make_async_remote_copy(
            src_ref=source,
            dst_ref=target,
            send_sem=send.at[s, k],
            recv_sem=recv.at[r, k],
            device_id={"tensor": where},
            device_id_type=pl.DeviceIdType.MESH,
        )

    def up_far(k):
        return remote(partial.at[rows(far, k)], from_outer.at[0, rows(0, k)], 0, 0, k, to_inner)

    def up_near(k):
        return remote(partial.at[rows(near, k)], from_outer.at[1, rows(0, k)], 1, 1, k, to_inner)

    def across(k):
        return remote(staged.at[rows(0, k)], from_peer.at[rows(0, k)], 0, 2, k, to_peer)

    def over(k, base):
        return remote(result.at[rows(base, k)], result.at[rows(base, k)], 2, 4, k, to_peer)

    def down_near(k):
        return remote(result.at[rows(near, k)], result.at[rows(near, k)], 1, 3, k, to_outer)

    def down_far(k):
        return remote(result.at[rows(far, k)], result.at[rows(far, k)], 3, 4, k, to_outer)

    barrier = pltpu.get_barrier_semaphore()

    def greet(where):
        pl.semaphore_signal(barrier, inc=1, device_id={"tensor": where}, device_id_type=pl.DeviceIdType.MESH)

    if gain_sum:
        gain_out[...] = jnp.zeros_like(gain_out)

    @pl.when(inner)
    def _():
        greet(to_outer)
        greet(to_peer)
        pl.semaphore_wait(barrier, 2)

        def step(k, carry):
            @pl.when(k < count)
            def _():
                up_far(k).wait_recv()
                total = partial[rows(far, k), :].astype(F32) + from_outer[0, rows(0, k), :].astype(F32)
                staged[rows(0, k), :] = total.astype(BF16)
                across(k).start()

            @pl.when((k >= 1) & (k <= count))
            def _():
                j = k - 1
                up_near(j).wait_recv()
                across(j).wait_recv()
                total = partial[rows(near, j), :].astype(F32) + from_outer[1, rows(0, j), :].astype(F32)
                total = total + from_peer[rows(0, j), :].astype(F32)
                low, state, gains = finish(total, rows(near, j), rows(0, j), ins)
                result[rows(near, j), :] = low
                if keep_state:
                    state_out[rows(0, j), :] = state
                if gain_sum:
                    gain_out[...] += jnp.sum(gains.reshape(sub // 8, 8, gains.shape[1]), axis=0)
                down_near(j).start()
                over(j, near).start()

            @pl.when(k >= 3)
            def _():
                over(k - 3, far).wait_recv()
                down_far(k - 3).start()

            return carry

        lax.fori_loop(0, count + 3, step, 0)

        def drain(k, carry):
            across(k).wait_send()
            down_near(k).wait_send()
            over(k, near).wait_send()
            down_far(k).wait_send()
            return carry

        lax.fori_loop(0, count, drain, 0)

    @pl.when(jnp.logical_not(inner))
    def _():
        greet(to_inner)
        pl.semaphore_wait(barrier, 1)

        def step(k, carry):
            up_far(k).start()
            up_near(k).start()
            return carry

        lax.fori_loop(0, count, step, 0)

        def drain(k, carry):
            down_near(k).wait_recv()
            down_far(k).wait_recv()
            up_far(k).wait_send()
            up_near(k).wait_send()
            return carry

        lax.fori_loop(0, count, drain, 0)


def line_sum(partial, ins, finish, keep_state, gain_sum, identity):
    rows, width = partial.shape
    half, _, count = line_steps(rows)
    vmem = pl.BlockSpec(memory_space=pltpu.VMEM)
    shapes = [jax.ShapeDtypeStruct((rows, width), BF16)]
    if keep_state:
        shapes.append(jax.ShapeDtypeStruct((half, width), F32))
    if gain_sum:
        shapes.append(jax.ShapeDtypeStruct((8, width), F32))
    return pl.pallas_call(
        functools.partial(line_body, finish, keep_state, gain_sum, len(ins)),
        in_specs=[vmem] * (1 + len(ins)),
        out_specs=[vmem] * len(shapes),
        out_shape=shapes,
        scratch_shapes=[
            pltpu.VMEM((2, half, width), BF16),
            pltpu.VMEM((half, width), BF16),
            pltpu.VMEM((half, width), BF16),
            pltpu.SemaphoreType.DMA((4, count)),
            pltpu.SemaphoreType.DMA((5, count)),
        ],
        compiler_params=pltpu.CompilerParams(
            collective_id=identity, has_side_effects=True, vmem_limit_bytes=VMEM_BYTES
        ),
        cost_estimate=pl.CostEstimate(flops=0, bytes_accessed=100 * rows * width, transcendentals=0),
    )(partial, *ins)


def mean_square(values):
    return lax.rsqrt(jnp.mean(values * values, axis=1, keepdims=True) + EPSILON)


def finish_attention(total, whole, own, ins):
    tokens, gain = ins
    hidden = tokens[whole, :].astype(F32) + RESIDUAL_SCALE * total
    return (hidden * mean_square(hidden) * gain[...]).astype(BF16), hidden, None


def norm_pull(d_normed, values, gain):
    inverse = mean_square(values)
    scaled = gain * d_normed
    inner = jnp.mean(scaled * values, axis=1, keepdims=True)
    return inverse * scaled - values * inverse * inverse * inverse * inner, d_normed * values * inverse


def finish_ffn_back(total, whole, own, ins):
    hidden, grads, gain = ins
    pulled, gains = norm_pull(total, hidden[own, :], gain[...])
    d_hidden = grads[whole, :].astype(F32) + pulled
    return (RESIDUAL_SCALE * d_hidden).astype(BF16), d_hidden, gains


def finish_attention_back(total, whole, own, ins):
    tokens, d_hidden, gain = ins
    pulled, gains = norm_pull(total, tokens[whole, :].astype(F32), gain[...])
    return (d_hidden[own, :] + pulled).astype(BF16), None, gains


def grads_body(count, jobs, *refs):
    ins, rest = refs[: 2 * jobs], refs[2 * jobs :]
    halves = count // 2
    outs, rest = rest[: halves * jobs], rest[halves * jobs :]
    sent, got, own = rest[:jobs], rest[jobs : 2 * jobs], rest[2 * jobs : 3 * jobs]
    send, recv, done = rest[3 * jobs :]
    me = plane_index()
    mate = {"context": lax.axis_index("context") ^ 1}
    mesh_ids = pl.DeviceIdType.MESH

    def piece(j, r):
        left, right = ins[2 * j], ins[2 * j + 1]
        extent = left.shape[1] // count
        columns = pl.ds(pl.multiple_of((me ^ r) * extent, extent), extent)
        return lax.dot_general(left[:, columns], right[...], (((0,), (0,)), ((), ())), preferred_element_type=F32)

    def across(j, i):
        return pltpu.make_async_remote_copy(
            src_ref=sent[j].at[i],
            dst_ref=got[j].at[i],
            send_sem=send.at[j, i],
            recv_sem=recv.at[j, i],
            device_id=mate,
            device_id_type=mesh_ids,
        )

    barrier = pltpu.get_barrier_semaphore()
    pl.semaphore_signal(barrier, inc=1, device_id=mate, device_id_type=mesh_ids)
    pl.semaphore_wait(barrier, 1)

    def odd(step, carry):
        i = halves - 1 - step
        for j in range(jobs):
            sent[j][i] = piece(j, 2 * i + 1).astype(BF16)
            across(j, i).start()
        return carry

    lax.fori_loop(0, halves, odd, 0)

    def even(step, carry):
        i = halves - 1 - step
        for j in range(jobs):
            value = piece(j, 2 * i)
            across(j, i).wait_recv()
            value = value + got[j][i].astype(F32)

            @pl.when(i > 0)
            def _():
                got[j][i] = value.astype(BF16)

            @pl.when(i == 0)
            def _():
                own[j][...] = value

        for known in range(halves):

            @pl.when(i == known)
            def _():
                for j in range(jobs):
                    source = got[j].at[known] if known else own[j]
                    pltpu.make_async_copy(source, outs[known * jobs + j], done.at[known, j]).start()

        return carry

    lax.fori_loop(0, halves, even, 0)
    for known in range(halves):
        for j in range(jobs):
            source = got[j].at[known] if known else own[j]
            pltpu.make_async_copy(source, outs[known * jobs + j], done.at[known, j]).wait()
            across(j, known).wait_send()


def plane_grads(pairs, identity):
    count = plane_size()
    halves = count // 2
    jobs = len(pairs)
    extents = [left.shape[1] // count for left, _ in pairs]
    if any(extent % LANES for extent in extents):
        me = plane_index()
        sides = []
        for (left, right), e in zip(pairs, extents):
            columns = lambda r: lax.dynamic_slice_in_dim(left, (me ^ r) * e, e, 1)
            whole = {r: weight_grad(columns(r), right).astype(BF16) for r in range(count)}
            sides.append({r: take_sum(whole, 1, r) for r in range(0, count, 2)})
        return sides
    shapes = [(e, right.shape[1]) for e, (_, right) in zip(extents, pairs)]
    flat = pl.pallas_call(
        functools.partial(grads_body, count, jobs),
        in_specs=[pl.BlockSpec(memory_space=pltpu.VMEM)] * (2 * jobs),
        out_specs=[ANYWHERE] * (halves * jobs),
        out_shape=[jax.ShapeDtypeStruct(shape, BF16 if i else F32) for i in range(halves) for shape in shapes],
        scratch_shapes=[pltpu.VMEM((halves,) + shape, BF16) for shape in shapes] * 2
        + [pltpu.VMEM(shape, F32) for shape in shapes]
        + [
            pltpu.SemaphoreType.DMA((jobs, halves)),
            pltpu.SemaphoreType.DMA((jobs, halves)),
            pltpu.SemaphoreType.DMA((halves, jobs)),
        ],
        compiler_params=pltpu.CompilerParams(
            collective_id=identity, has_side_effects=True, vmem_limit_bytes=VMEM_BYTES
        ),
        cost_estimate=pl.CostEstimate(
            flops=sum(2 * left.shape[0] * left.shape[1] * right.shape[1] for left, right in pairs),
            bytes_accessed=sum(2 * left.shape[1] * right.shape[1] for left, right in pairs),
            transcendentals=0,
        ),
    )(*[value for pair in pairs for value in pair])
    return [{2 * i: flat[i * jobs + j] for i in range(halves)} for j in range(jobs)]


def after(value, *others):
    return lax.optimization_barrier((value,) + others)[0] if others else value


def gather_context(piece):
    size = lax.axis_size("context")
    held = {0: piece}
    bit = size // 2
    while bit:
        for r in list(held):
            held[r | bit] = swap(held[r], "context", size, bit)
        bit //= 2
    return [held[r] for r in range(size)]


def reduce_context(pieces):
    size = len(pieces)
    held = dict(enumerate(pieces))
    bit = 1
    while bit < size:
        held = {
            r: held[r].astype(F32) + swap(held[r | bit].astype(BF16), "context", size, bit).astype(F32)
            for r in held
            if not r & bit
        }
        bit *= 2
    return held[0]


def stored_places(order_row, first, count):
    stored = first + jnp.arange(count, dtype=jnp.int32)
    picks = (stored // BLK)[:, None] == jnp.arange(order_row.shape[0], dtype=jnp.int32)[None, :]
    return jnp.sum(jnp.where(picks, order_row[None, :], 0), axis=1) * BLK + stored % BLK


def rope_tables(order, local_len):
    first = lax.axis_index("context") * local_len
    places = jnp.concatenate([stored_places(order[s], first, local_len) for s in range(order.shape[0])])
    half = HD // 2
    inverse = jnp.exp(jnp.arange(half, dtype=F32) * (-2.0 * math.log(ROPE_BASE) / HD))
    angles = places.astype(F32)[:, None] * jnp.tile(inverse, LANES // half)[None, :]
    return jnp.cos(angles), jnp.sin(angles)


def weight_grad(left, right):
    return lax.dot_general(left, right, (((0,), (0,)), ((), ())), preferred_element_type=F32)


def local(
    tokens, block_order, w_query, w_key, w_value, w_output, w_gate, w_up, w_down, norm_attn, norm_ffn, grad_out
):
    seqs, local_len, width = tokens.shape
    rows = seqs * local_len
    size = plane_size()
    me = plane_index()
    z = lax.axis_index("tensor")
    token_rows = tokens.reshape(rows, width)
    grad_rows = grad_out.reshape(rows, width)
    q_width, kv_width = w_query.shape[1], w_key.shape[1]
    units = w_down.shape[0]
    half = units // 2

    gains = gather_small(jnp.stack([norm_attn, norm_ffn])).reshape(2, width)
    gain_attn, gain_ffn = gains[0:1], gains[1:2]
    w_qkv = jnp.concatenate([w_query, w_key, w_value], axis=1)
    qkv_pieces, output_pieces = gather_pair(w_qkv, w_output)
    cosine, sine = rope_tables(block_order, local_len)
    normed, queries, keys_values = project_qkv(token_rows, gain_attn, cosine, sine, qkv_pieces, q_width)
    kv_pieces = gather_context(keys_values)
    early, late = [qkv_pieces[-2], output_pieces[-2], output_pieces[size // 2]], [kv_pieces[-2]]
    mixture, logs = attend(block_order, queries, kv_pieces)
    output_pieces = widened(output_pieces)
    branch = gathered_matmul(mixture, output_pieces, 1, False)
    normed_ffn, hidden = line_sum(branch, [token_rows, gain_ffn], finish_attention, True, False, 0)
    gate_pieces, up_pieces = gather_pair(w_gate, w_up, early, late, [mixture], [normed_ffn])
    low_pieces, high_pieces = gather_pair(w_down[:half], w_down[half:], early, late, [normed_ffn], [normed_ffn])
    low_pieces, high_pieces = widened(low_pieces), widened(high_pieces)
    d_ffn = (RESIDUAL_SCALE * grad_rows.astype(F32)).astype(BF16)
    active, d_gate, d_up, ffn_out, d_normed_ffn = ffn(
        normed_ffn, d_ffn, gate_pieces, up_pieces, low_pieces, high_pieces
    )
    grad_gate, grad_up, grad_low, grad_high = plane_grads(
        [(normed_ffn, d_gate), (normed_ffn, d_up), (d_ffn, active[:, :half]), (d_ffn, active[:, half:])], 3
    )
    d_normed_ffn = after(d_normed_ffn, grad_gate[0])
    d_branch, d_hidden, ffn_gain = line_sum(d_normed_ffn, [hidden, grad_rows, gain_ffn], finish_ffn_back, True, True, 1)

    grad_gate, grad_up = reduce_pair(grad_gate, grad_up)
    grad_low, grad_high = reduce_pair(grad_low, grad_high)

    owner = lax.rem(z, 3) != 0
    padded = lax.dynamic_update_slice_in_dim(jnp.zeros((rows, width), F32), hidden, (z // 2) * (rows // 2), 0)
    out_part = RESIDUAL_SCALE * after(ffn_out, d_branch).astype(F32) + jnp.where(owner, padded, 0.0)
    layer_out = rows_gather(rows_sum(out_part.astype(BF16)).astype(BF16))

    d_mixture = gathered_matmul(d_branch, output_pieces, 1, True)
    d_queries, *d_pieces = attend_back(block_order, queries, d_mixture, logs, kv_pieces)
    d_keys_values = reduce_context(d_pieces)
    d_qkv, d_normed = project_qkv_back(d_queries, d_keys_values, cosine, sine, qkv_pieces)
    grad_qkv, grad_output = plane_grads([(normed, d_qkv), (d_branch, mixture)], 4)
    d_normed = after(d_normed, grad_qkv[0])
    grad_tokens, attn_gain = line_sum(
        d_normed, [token_rows, d_hidden, gain_attn], finish_attention_back, False, True, 2
    )
    grad_tokens = grad_tokens.astype(F32)
    grad_qkv, grad_output = reduce_pair(grad_qkv, grad_output)
    attn_gain, ffn_gain = jnp.sum(attn_gain, axis=0), jnp.sum(ffn_gain, axis=0)
    gain_grads = jnp.stack([attn_gain, ffn_gain])
    everyone = ("shard", "context", "tensor")
    world = size * lax.axis_size("tensor")
    bit = 1
    while bit < world:
        gain_grads = gain_grads + swap(gain_grads, everyone, world, bit)
        bit *= 2
    gain_grads = lax.dynamic_slice_in_dim(gain_grads, me * (width // size), width // size, 1)
    return (
        layer_out.reshape(seqs, local_len, width),
        grad_tokens.reshape(seqs, local_len, width),
        grad_qkv[:, :q_width],
        grad_qkv[:, q_width : q_width + kv_width],
        grad_qkv[:, q_width + kv_width :],
        grad_output.T,
        grad_gate,
        grad_up,
        jnp.concatenate([grad_low.T, grad_high.T], axis=0),
        gain_grads[0],
        gain_grads[1],
    )


def solution(mesh):
    split = P("shard", "context", None)
    inward, outward = P(PLANE, "tensor"), P("tensor", PLANE)
    gain = P(PLANE)
    return jax.shard_map(
        local,
        mesh=mesh,
        in_specs=(split, P("shard", None), inward, inward, inward, outward, inward, inward, outward, gain, gain, split),
        out_specs=(split, split, inward, inward, inward, outward, inward, inward, outward, gain, gain),
        check_vma=False,
    )
```

profile of v0, /device:TPU:0, one launch (start us, length us, event | category | flops | bytes accessed | tf_op | source)
XLA Modules:
  0.0 691.8 jit_solution(14420050880144318341)
XLA Ops:
  3.3 3.0 collective-permute-start.6
  11.2 1.6 collective-permute-start.1
  12.8 2.7 collective-permute-done.6.rest_4_
  15.5 1.8 collective-permute-start.8
  17.3 1.8 multiply_sine_fusion
  19.1 5.0 collective-permute-done.1
  24.2 3.6 collective-permute-done.2
  28.4 2.7 collective-permute-done.8.rest_6_
  31.9 2.5 collective-permute-done.16.rest_4_
  35.9 8.4 %project_qkv.1 = (bf16[512,2048]{1,0:T(8,128)(2,1)}, bf16[512,512]{1,0:T(8,128)(2,1)}, bf16[512,256]{1,0:T(8,128)(2,1)}) custom-call(bf16[512,2048]{1,0:T(8,128)(2,1)} %bitcast.39, f32[1,2048]{1,0:T(1,128)} %bitcast.50, f32[512,128]{1,0:T(8,128)} %get-tuple-element.212.cosine, f32[512,128]{1,0:T(8,128)} %get-tuple-element.211.sine, ...), custom_call_target="tpu_custom_call" | custom-call | flops 1610612736 | bytes 7340032 | tf_op jit(solution)/shard_map/project_qkv/pallas_call | solution.py:209
  44.3 2.0 collective-permute-start.11
  46.3 1.6 collective-permute-start.23
  48.4 4.7 collective-permute-done.11.rest_2_
  53.2 2.2 fusion.19
  56.8 1.7 collective-permute-start.37
  60.7 21.3 %attend.1 = (bf16[512,512]{1,0:T(8,128)(2,1)}, f32[4,2,512]{2,1,0:T(2,128)}) custom-call(s32[1,8]{1,0:T(1,128)} %order.3, bf16[512,512]{1,0:T(8,128)(2,1)} %get-tuple-element.88.query_ref, bf16[512,256]{1,0:T(8,128)(2,1)} %get-tuple-element.89.rest_0_, bf16[512,256]{1,0:T(8,128)(2,1)} %copy-done.49, bf16[512,256]{1,0:T(8,128)(2,1)} %copy-done.48, ...), custom_call_target="tpu_custom_call" | custom-call | flops 8589934592 | bytes 2097152 | tf_op jit(solution)/shard_map/attend/pallas_call | solution.py:469
  82.0 24.5 %collective-permute-done.37.rest_20_ = bf16[1024,256]{1,0:T(8,128)(2,1)} collective-permute-done((bf16[1024,256]{1,0:T(8,128)(2,1)}, bf16[1024,256]{1,0:T(8,128)(2,1)}, u32[]{:S(2)}, u32[]{:S(2)}) %collective-permute-start.37) | collective-permute-done | bytes 524320 | tf_op jit(solution)/shard_map/ppermute | solution.py:37
  106.6 4.9 shard_map.203.refs_0_
  111.6 63.4 %shard_map.204 = (bf16[512,2048]{1,0:T(8,128)(2,1)}, f32[256,2048]{1,0:T(8,128)}) custom-call(bf16[512,2048]{1,0:T(8,128)(2,1)} %shard_map.203.refs_0_, bf16[512,2048]{1,0:T(8,128)(2,1)} %bitcast.40, f32[1,2048]{1,0:T(1,128)} %bitcast.48), custom_call_target="tpu_custom_call" | custom-call | bytes 104857600 | tf_op jit(solution)/shard_map/pallas_call | solution.py:697
  174.9 1.6 collective-permute-start.35
  177.1 1.6 collective-permute-start.21
  178.6 11.4 %collective-permute-done.35.rest_18_ = bf16[1024,256]{1,0:T(8,128)(2,1)S(1)} collective-permute-done((bf16[1024,256]{1,0:T(8,128)(2,1)}, bf16[1024,256]{1,0:T(8,128)(2,1)S(1)}, u32[]{:S(2)}, u32[]{:S(2)}) %collective-permute-start.35) | collective-permute-done | bytes 524320 | tf_op jit(solution)/shard_map/ppermute | solution.py:37
  190.0 11.2 %collective-permute-done.39.rest_22_ = bf16[1024,256]{1,0:T(8,128)(2,1)S(1)} collective-permute-done((bf16[1024,256]{1,0:T(8,128)(2,1)}, bf16[1024,256]{1,0:T(8,128)(2,1)S(1)}, u32[]{:S(2)}, u32[]{:S(2)}) %collective-permute-start.39) | collective-permute-done | bytes 524320 | tf_op jit(solution)/shard_map/ppermute | solution.py:37
  205.4 18.3 %collective-permute-done.21.rest_2_ = bf16[256,2048]{1,0:T(8,128)(2,1)S(1)} collective-permute-done((bf16[256,2048]{1,0:T(8,128)(2,1)}, bf16[256,2048]{1,0:T(8,128)(2,1)S(1)}, u32[]{:S(2)}, u32[]{:S(2)}) %collective-permute-start.21) | collective-permute-done | bytes 1048608 | tf_op jit(solution)/shard_map/ppermute | solution.py:37
  223.7 15.9 %collective-permute-done.46.rest_30_ = bf16[1024,256]{1,0:T(8,128)(2,1)S(1)} collective-permute-done((bf16[1024,256]{1,0:T(8,128)(2,1)}, bf16[1024,256]{1,0:T(8,128)(2,1)S(1)}, u32[]{:S(2)}, u32[]{:S(2)}) %collective-permute-start.46) | collective-permute-done | bytes 524320 | tf_op jit(solution)/shard_map/ppermute | solution.py:37
  240.3 1.7 collective-permute-done.25.rest_6_
  242.5 5.3 collective-permute-done.40.rest_23_
  249.2 3.4 multiply_convert_fusion.d_ffn.refs_4_.refs_6_
  252.7 3.2 collective-permute-done.47.rest_31_
  256.7 48.5 %feed_forward.1 = (bf16[512,2048]{1,0:T(8,128)(2,1)}, bf16[512,2048]{1,0:T(8,128)(2,1)}, bf16[512,2048]{1,0:T(8,128)(2,1)}, bf16[512,2048]{1,0:T(8,128)(2,1)}, bf16[512,2048]{1,0:T(8,128)(2,1)}) custom-call(bf16[512,2048]{1,0:T(8,128)(2,1)} %get-tuple-element.91.normed.refs_0_.refs_2_, bf16[512,2048]{1,0:T(8,128)(2,1)} %multiply_convert_fusion.d_ffn.refs_4_.refs_6_, ...), custom_call_target="tpu_custom_call" | custom-call | flops 25769803776 | bytes 39845888 | tf_op jit(solution)/shard_map/feed_forward/pallas_call | solution.py:385
  305.2 3.0 fusion.18
  308.2 31.3 %shard_map.205 = (f32[256,2048]{1,0:T(8,128)}, f32[256,2048]{1,0:T(8,128)}, f32[256,1024]{1,0:T(8,128)}, f32[256,1024]{1,0:T(8,128)}, bf16[256,2048]{1,0:T(8,128...) custom-call(bf16[512,2048]{1,0:T(8,128)(2,1)} %get-tuple-element.91., ...), custom_call_target="tpu_custom_call" | custom-call | flops 12884901888 | bytes 25165824 | tf_op jit(solution)/shard_map/pallas_call | solution.py:832
  339.6 62.6 %shard_map.206 = (bf16[512,2048]{1,0:T(8,128)(2,1)}, f32[256,2048]{1,0:T(8,128)}, f32[8,2048]{1,0:T(8,128)}) custom-call(bf16[512,2048]{1,0:T(8,128)(2,1)} %get-tuple-element.124.refs_0_, f32[256,2048]{1,0:T(8,128)} %get-tuple-element.125.refs_1_, bf16[512,2048]{1,0:T(8,128)(2,1)} %bitcast.38, f32[1,2048]{1,0:T(1,128)} %bitcast.49), custom_call_target="tpu_custom_call" | custom-call | bytes 104857600 | tf_op jit(solution)/shard_map/pallas_call | solution.py:697
  402.1 5.2 shard_map.207.grad_ref
  407.4 35.5 %attend_back.1 = (f32[512,512]{1,0:T(8,128)}, f32[512,256]{1,0:T(8,128)}, bf16[512,256]{1,0:T(8,128)(2,1)}, f32[512,256]{1,0:T(8,128)}, bf16[512,256]{1,0:T(8,128)(2,1)}) custom-call(s32[1,8]{1,0:T(1,128)} %order.3, bf16[512,512]{1,0:T(8,128)(2,1)} %get-tuple-element.88.query_ref, bf16[512,512]{1,0:T(8,128)(2,1)} %shard_map.207.grad_ref, ...), custom_call_target="tpu_custom_call" | custom-call | flops 21474836480 | bytes 3145728 | tf_op jit(solution)/shard_map/attend_back/pallas_call | solution.py:544
  443.5 2.3 convert_multiply_fusion
  448.9 2.5 collective-permute-start.49
  452.8 3.0 collective-permute-done.56
  456.6 6.8 project_qkv_back.1
  463.5 10.7 %shard_map.208 = (f32[256,768]{1,0:T(8,128)}, f32[256,512]{1,0:T(8,128)}, bf16[256,768]{1,0:T(8,128)(2,1)}, bf16[256,512]{1,0:T(8,128)(2,1)}, bf16[256,768]{1,0:...) custom-call(bf16[512,2048]{1,0:T(8,128)(2,1)} %get-tuple-element.135.refs_0_, ...), custom_call_target="tpu_custom_call" | custom-call | flops 2684354560 | bytes 5242880 | tf_op jit(solution)/shard_map/pallas_call | solution.py:832
  474.2 75.3 %shard_map.209 = (bf16[512,2048]{1,0:T(8,128)(2,1)}, f32[8,2048]{1,0:T(8,128)}) custom-call(bf16[512,2048]{1,0:T(8,128)(2,1)} %get-tuple-element.138.refs_0_, bf16[512,2048]{1,0:T(8,128)(2,1)} %bitcast.41, f32[256,2048]{1,0:T(8,128)} %get-tuple-element.139.refs_2_, f32[1,2048]{1,0:T(1,128)} %bitcast.51), custom_call_target="tpu_custom_call" | custom-call | bytes 104857600 | tf_op jit(solution)/shard_map/pallas_call | solution.py:697
  550.5 1.6 collective-permute-start.69
  552.1 2.2 collective-permute-done.75
  555.7 1.6 collective-permute-start.73
  558.4 2.8 bitcast_dynamic-update-slice_fusion.3
  563.4 2.1 collective-permute-done.69
  566.8 1.6 collective-permute-start.78
  568.3 2.5 collective-permute-done.73
  571.0 1.6 collective-permute-start.61
  572.6 8.8 %collective-permute-done.78 = f32[2,2048]{1,0:T(2,128)S(1)} collective-permute-done((f32[2,2048]{1,0:T(2,128)S(1)}, f32[2,2048]{1,0:T(2,128)S(1)}, u32[]{:S(2)}, u32[]{:S(2)}) %collective-permute-start.78) | collective-permute-done | bytes 16416 | tf_op jit(solution)/shard_map/ppermute | solution.py:37
  582.1 2.5 bitcast_convert_fusion
  589.0 7.2 %collective-permute-done.57 = bf16[256,768]{1,0:T(8,128)(2,1)S(1)} collective-permute-done((bf16[256,768]{1,0:T(8,128)(2,1)S(1)}, bf16[256,768]{1,0:T(8,128)(2,1)S(1)}, u32[]{:S(2)}, u32[]{:S(2)}) %collective-permute-start.57) | collective-permute-done | bytes 393248 | tf_op jit(solution)/shard_map/ppermute | solution.py:37
  596.2 2.5 collective-permute-start.70
  600.1 17.8 %collective-permute-done.70 = bf16[256,1024]{1,0:T(8,128)(2,1)S(1)} collective-permute-done((bf16[256,1024]{1,0:T(8,128)(2,1)S(1)}, bf16[256,1024]{1,0:T(8,128)(2,1)S(1)}, u32[]{:S(2)}, u32[]{:S(2)}) %collective-permute-start.70) | collective-permute-done | bytes 524320 | tf_op jit(solution)/shard_map/ppermute | solution.py:37
  621.5 11.2 %collective-permute-done.74 = bf16[256,1024]{1,0:T(8,128)(2,1)S(1)} collective-permute-done((bf16[256,1024]{1,0:T(8,128)(2,1)S(1)}, bf16[256,1024]{1,0:T(8,128)(2,1)S(1)}, u32[]{:S(2)}, u32[]{:S(2)}) %collective-permute-start.74) | collective-permute-done | bytes 524320 | tf_op jit(solution)/shard_map/ppermute | solution.py:37
  634.7 1.8 copy.36
  637.0 1.9 bitcast_dynamic-update-slice_fusion
  640.4 1.6 add_convert_fusion.1
  644.2 1.6 add_convert_fusion
  645.8 17.4 %collective-permute-done.62 = bf16[256,512]{1,0:T(8,128)(2,1)S(1)} collective-permute-done((bf16[256,512]{1,0:T(8,128)(2,1)}, bf16[256,512]{1,0:T(8,128)(2,1)S(1)}, u32[]{:S(2)}, u32[]{:S(2)}) %collective-permute-start.62) | collective-permute-done | bytes 262176 | tf_op jit(solution)/shard_map/ppermute | solution.py:37
  663.3 2.4 collective-permute-start.66
  671.8 3.3 convert_add_fusion.1
  675.1 13.4 %collective-permute-done.66 = bf16[256,2048]{1,0:T(8,128)(2,1)} collective-permute-done((bf16[256,2048]{1,0:T(8,128)(2,1)}, bf16[256,2048]{1,0:T(8,128)(2,1)}, u32[]{:S(2)}, u32[]{:S(2)}) %collective-permute-start.66) | collective-permute-done | bytes 1048608 | tf_op jit(solution)/shard_map/ppermute | solution.py:37
  688.6 3.0 convert_add_fusion
  (274 shorter events, 58.1 us)
Async XLA Ops:
  3.3 12.1 %collective-permute-start.6 = (bf16[256,768]{1,0:T(8,128)(2,1)S(1)}, bf16[256,768]{1,0:T(8,128)(2,1)S(1)}, u32[]{:S(2)}, u32[]{:S(2)}) collective-permute-start(bf16[256,768]{1,0:T(8,128)(2,1)S(1)} %constant_dynamic-update-slice_fusion.rest_0_), channel_id=1, source_target_pairs={{0,16},{4,20},{8,24},{12,28},{16,0},{20,4},{24,8},{28,12},{1,17},{... | collective-permute-start | bytes 1179656 | tf_op jit(solution)/shard_map/ppermute | solution.py:37
  6.4 21.5 %collective-permute-start.4 = (bf16[256,768]{1,0:T(8,128)(2,1)S(1)}, bf16[256,768]{1,0:T(8,128)(2,1)S(1)}, u32[]{:S(2)}, u32[]{:S(2)}) collective-permute-start(bf16[256,768]{1,0:T(8,128)(2,1)S(1)} %constant_dynamic-update-slice_fusion.rest_0_), channel_id=1, source_target_pairs={{0,8},{4,12},{8,0},{12,4},{16,24},{20,28},{24,16},{28,20},{1,9},{5... | collective-permute-start | bytes 1179656 | tf_op jit(solution)/shard_map/ppermute | solution.py:37
  7.9 26.4 %collective-permute-start.3 = (bf16[256,768]{1,0:T(8,128)(2,1)S(1)}, bf16[256,768]{1,0:T(8,128)(2,1)}, u32[]{:S(2)}, u32[]{:S(2)}) collective-permute-start(bf16[256,768]{1,0:T(8,128)(2,1)S(1)} %constant_dynamic-update-slice_fusion.rest_0_), channel_id=1, source_target_pairs={{0,4},{4,0},{8,12},{12,8},{16,20},{20,16},{24,28},{28,24},{1,5},{5... | collective-permute-start | bytes 1179656 | tf_op jit(solution)/shard_map/ppermute | solution.py:37
  9.8 18.0 %collective-permute-start.14 = (bf16[512,256]{1,0:T(8,128)(2,1)}, bf16[512,256]{1,0:T(8,128)(2,1)S(1)}, u32[]{:S(2)}, u32[]{:S(2)}) collective-permute-start(bf16[512,256]{1,0:T(8,128)(2,1)} %rest_0_.5), channel_id=1, source_target_pairs={{0,8},{4,12},{8,0},{12,4},{16,24},{20,28},{24,16},{28,20},{1,9},{5... | collective-permute-start | bytes 786440 | tf_op jit(solution)/shard_map/ppermute | solution.py:37
  11.2 12.8 %collective-permute-start.1 = (bf16[2,2,256]{2,0,1:T(2,128)(2,1)S(1)}, bf16[2,2,256]{2,0,1:T(2,128)(2,1)S(1)}, u32[]{:S(2)}, u32[]{:S(2)}) collective-permute-start(bf16[2,2,256]{2,0,1:T(2,128)(2,1)S(1)} %pad_maximum_fusion.3), channel_id=1, source_target_pairs={{0,8},{4,12},{8,0},{12,4},{16,24},{20,28},{24,16},{28,20},{1,9},{5... | collective-permute-start | bytes 6152 | tf_op jit(solution)/shard_map/ppermute | solution.py:37
  15.5 15.5 %collective-permute-start.8 = (bf16[256,768]{1,0:T(8,128)(2,1)S(1)}, bf16[256,768]{1,0:T(8,128)(2,1)S(1)}, u32[]{:S(2)}, u32[]{:S(2)}) collective-permute-start(bf16[256,768]{1,0:T(8,128)(2,1)S(1)} %collective-permute-done.6.rest_4_), channel_id=1, source_target_pairs={{0,8},{4,12},{8,0},{12,4},{16,24},{20,28},{24,16},{28,20},{1,9},{5... | collective-permute-start | bytes 1179656 | tf_op jit(solution)/shard_map/ppermute | solution.py:37
  27.9 7.1 %collective-permute-start.5 = (bf16[256,768]{1,0:T(8,128)(2,1)S(1)}, bf16[256,768]{1,0:T(8,128)(2,1)S(1)}, u32[]{:S(2)}, u32[]{:S(2)}) collective-permute-start(bf16[256,768]{1,0:T(8,128)(2,1)S(1)} %collective-permute-done.4.rest_2_), channel_id=1, source_target_pairs={{0,4},{4,0},{8,12},{12,8},{16,20},{20,16},{24,28},{28,24},{1,5},{5... | collective-permute-start | bytes 1179656 | tf_op jit(solution)/shard_map/ppermute | solution.py:37
  34.3 12.0 %collective-permute-start.13 = (bf16[512,256]{1,0:T(8,128)(2,1)}, bf16[512,256]{1,0:T(8,128)(2,1)S(1)}, u32[]{:S(2)}, u32[]{:S(2)}) collective-permute-start(bf16[512,256]{1,0:T(8,128)(2,1)} %rest_0_.5), channel_id=1, source_target_pairs={{0,4},{4,0},{8,12},{12,8},{16,20},{20,16},{24,28},{28,24},{1,5},{5... | collective-permute-start | bytes 786440 | tf_op jit(solution)/shard_map/ppermute | solution.py:37
  34.4 12.0 %collective-permute-start.18 = (bf16[512,256]{1,0:T(8,128)(2,1)S(1)}, bf16[512,256]{1,0:T(8,128)(2,1)S(1)}, u32[]{:S(2)}, u32[]{:S(2)}) collective-permute-start(bf16[512,256]{1,0:T(8,128)(2,1)S(1)} %collective-permute-done.14.rest_2_), channel_id=1, source_target_pairs={{0,16},{4,20},{8,24},{12,28},{16,0},{20,4},{24,8},{28,12},{1,17},{... | collective-permute-start | bytes 786440 | tf_op jit(solution)/shard_map/ppermute | solution.py:37
  34.5 13.9 %collective-permute-start.15 = (bf16[512,256]{1,0:T(8,128)(2,1)S(1)}, bf16[512,256]{1,0:T(8,128)(2,1)S(1)}, u32[]{:S(2)}, u32[]{:S(2)}) collective-permute-start(bf16[512,256]{1,0:T(8,128)(2,1)S(1)} %collective-permute-done.14.rest_2_), channel_id=1, source_target_pairs={{0,4},{4,0},{8,12},{12,8},{16,20},{20,16},{24,28},{28,24},{1,5},{5... | collective-permute-start | bytes 786440 | tf_op jit(solution)/shard_map/ppermute | solution.py:37
  35.0 12.9 %collective-permute-start.17 = (bf16[512,256]{1,0:T(8,128)(2,1)S(1)}, bf16[512,256]{1,0:T(8,128)(2,1)}, u32[]{:S(2)}, u32[]{:S(2)}) collective-permute-start(bf16[512,256]{1,0:T(8,128)(2,1)S(1)} %collective-permute-done.16.rest_4_), channel_id=1, source_target_pairs={{0,4},{4,0},{8,12},{12,8},{16,20},{20,16},{24,28},{28,24},{1,5},{5... | collective-permute-start | bytes 786440 | tf_op jit(solution)/shard_map/ppermute | solution.py:37
  44.3 8.9 %collective-permute-start.11 = (bf16[512,256]{1,0:T(8,128)(2,1)}, bf16[512,256]{1,0:T(8,128)(2,1)S(1)}, u32[]{:S(2)}, u32[]{:S(2)}) collective-permute-start(bf16[512,256]{1,0:T(8,128)(2,1)} %get-tuple-element.89.rest_0_), channel_id=1, source_target_pairs={{0,8},{4,12},{8,0},{12,4},{1,9},{5,13},{9,1},{13,5},{2,10},{6,14},... | collective-permute-start | bytes 786440 | tf_op jit(solution)/shard_map/ppermute | solution.py:37
  46.3 9.7 %collective-permute-start.19 = (bf16[512,256]{1,0:T(8,128)(2,1)S(1)}, bf16[512,256]{1,0:T(8,128)(2,1)S(1)}, u32[]{:S(2)}, u32[]{:S(2)}) collective-permute-start(bf16[512,256]{1,0:T(8,128)(2,1)S(1)} %collective-permute-done.18.rest_6_), channel_id=1, source_target_pairs={{0,4},{4,0},{8,12},{12,8},{16,20},{20,16},{24,28},{28,24},{1,5},{5... | collective-permute-start | bytes 786440 | tf_op jit(solution)/shard_map/ppermute | solution.py:37
  46.3 130.2 %collective-permute-start.23 = (bf16[256,2048]{1,0:T(8,128)(2,1)}, bf16[256,2048]{1,0:T(8,128)(2,1)}, u32[]{:S(2)}, u32[]{:S(2)}) collective-permute-start(bf16[256,2048]{1,0:T(8,128)(2,1)} %rest_0_.4), channel_id=1, source_target_pairs={{0,16},{4,20},{8,24},{12,28},{16,0},{20,4},{24,8},{28,12},{1,17},{... | collective-permute-start | bytes 3145736 | tf_op jit(solution)/shard_map/ppermute | solution.py:37
  47.9 129.2 %collective-permute-start.30 = (bf16[256,2048]{1,0:T(8,128)(2,1)}, bf16[256,2048]{1,0:T(8,128)(2,1)}, u32[]{:S(2)}, u32[]{:S(2)}) collective-permute-start(bf16[256,2048]{1,0:T(8,128)(2,1)} %rest_8_.1), channel_id=1, source_target_pairs={{0,16},{4,20},{8,24},{12,28},{16,0},{20,4},{24,8},{28,12},{1,17},{... | collective-permute-start | bytes 3145736 | tf_op jit(solution)/shard_map/ppermute | solution.py:37
  48.4 10.0 %collective-permute-start.10 = (bf16[512,256]{1,0:T(8,128)(2,1)}, bf16[512,256]{1,0:T(8,128)(2,1)S(1)}, u32[]{:S(2)}, u32[]{:S(2)}) collective-permute-start(bf16[512,256]{1,0:T(8,128)(2,1)} %get-tuple-element.89.rest_0_), channel_id=1, source_target_pairs={{0,4},{4,0},{8,12},{12,8},{1,5},{5,1},{9,13},{13,9},{2,6},{6,2},{1... | collective-permute-start | bytes 786440 | tf_op jit(solution)/shard_map/ppermute | solution.py:37
  56.8 49.7 %collective-permute-start.37 = (bf16[1024,256]{1,0:T(8,128)(2,1)}, bf16[1024,256]{1,0:T(8,128)(2,1)}, u32[]{:S(2)}, u32[]{:S(2)}) collective-permute-start(bf16[1024,256]{1,0:T(8,128)(2,1)} %get-tuple-element.109.rest_16_), channel_id=1, source_target_pairs={{0,16},{4,20},{8,24},{12,28},{16,0},{20,4},{24,8},{28,12},{1,17},{... | collective-permute-start | bytes 1572872 | tf_op jit(solution)/shard_map/ppermute | solution.py:37
  58.5 116.5 %collective-permute-start.44 = (bf16[1024,256]{1,0:T(8,128)(2,1)S(1)}, bf16[1024,256]{1,0:T(8,128)(2,1)}, u32[]{:S(2)}, u32[]{:S(2)}) collective-permute-start(bf16[1024,256]{1,0:T(8,128)(2,1)S(1)} %get-tuple-element.115.rest_24_), channel_id=1, source_target_pairs={{0,16},{4,20},{8,24},{12,28},{16,0},{20,4},{24,8},{28,12},{1,17},{... | collective-permute-start | bytes 1572872 | tf_op jit(solution)/shard_map/ppermute | solution.py:37
  59.1 117.9 %collective-permute-start.42 = (bf16[1024,256]{1,0:T(8,128)(2,1)S(1)}, bf16[1024,256]{1,0:T(8,128)(2,1)}, u32[]{:S(2)}, u32[]{:S(2)}) collective-permute-start(bf16[1024,256]{1,0:T(8,128)(2,1)S(1)} %get-tuple-element.115.rest_24_), channel_id=1, source_target_pairs={{0,8},{4,12},{8,0},{12,4},{16,24},{20,28},{24,16},{28,20},{1,9},{5... | collective-permute-start | bytes 1572872 | tf_op jit(solution)/shard_map/ppermute | solution.py:37
  106.5 95.4 %collective-permute-start.28 = (bf16[256,2048]{1,0:T(8,128)(2,1)}, bf16[256,2048]{1,0:T(8,128)(2,1)}, u32[]{:S(2)}, u32[]{:S(2)}) collective-permute-start(bf16[256,2048]{1,0:T(8,128)(2,1)} %rest_8_.1), channel_id=1, source_target_pairs={{0,8},{4,12},{8,0},{12,4},{16,24},{20,28},{24,16},{28,20},{1,9},{5... | collective-permute-start | bytes 3145736 | tf_op jit(solution)/shard_map/ppermute | solution.py:37
  174.9 15.1 %collective-permute-start.35 = (bf16[1024,256]{1,0:T(8,128)(2,1)}, bf16[1024,256]{1,0:T(8,128)(2,1)S(1)}, u32[]{:S(2)}, u32[]{:S(2)}) collective-permute-start(bf16[1024,256]{1,0:T(8,128)(2,1)} %get-tuple-element.109.rest_16_), channel_id=1, source_target_pairs={{0,8},{4,12},{8,0},{12,4},{16,24},{20,28},{24,16},{28,20},{1,9},{5... | collective-permute-start | bytes 1572872 | tf_op jit(solution)/shard_map/ppermute | solution.py:37
  176.5 24.7 %collective-permute-start.39 = (bf16[1024,256]{1,0:T(8,128)(2,1)}, bf16[1024,256]{1,0:T(8,128)(2,1)S(1)}, u32[]{:S(2)}, u32[]{:S(2)}) collective-permute-start(bf16[1024,256]{1,0:T(8,128)(2,1)} %collective-permute-done.37.rest_20_), channel_id=1, source_target_pairs={{0,8},{4,12},{8,0},{12,4},{16,24},{20,28},{24,16},{28,20},{1,9},{5... | collective-permute-start | bytes 1572872 | tf_op jit(solution)/shard_map/ppermute | solution.py:37
  177.0 24.2 %collective-permute-start.38 = (bf16[1024,256]{1,0:T(8,128)(2,1)}, bf16[1024,256]{1,0:T(8,128)(2,1)S(1)}, u32[]{:S(2)}, u32[]{:S(2)}) collective-permute-start(bf16[1024,256]{1,0:T(8,128)(2,1)} %collective-permute-done.37.rest_20_), channel_id=1, source_target_pairs={{0,4},{4,0},{8,12},{12,8},{16,20},{20,16},{24,28},{28,24},{1,5},{5... | collective-permute-start | bytes 1572872 | tf_op jit(solution)/shard_map/ppermute | solution.py:37
  177.1 46.7 %collective-permute-start.21 = (bf16[256,2048]{1,0:T(8,128)(2,1)}, bf16[256,2048]{1,0:T(8,128)(2,1)S(1)}, u32[]{:S(2)}, u32[]{:S(2)}) collective-permute-start(bf16[256,2048]{1,0:T(8,128)(2,1)} %rest_0_.4), channel_id=1, source_target_pairs={{0,8},{4,12},{8,0},{12,4},{16,24},{20,28},{24,16},{28,20},{1,9},{5... | collective-permute-start | bytes 3145736 | tf_op jit(solution)/shard_map/ppermute | solution.py:37
  190.0 13.3 %collective-permute-start.45 = (bf16[1024,256]{1,0:T(8,128)(2,1)}, bf16[1024,256]{1,0:T(8,128)(2,1)S(1)}, u32[]{:S(2)}, u32[]{:S(2)}) collective-permute-start(bf16[1024,256]{1,0:T(8,128)(2,1)} %collective-permute-done.44.rest_28_), channel_id=1, source_target_pairs={{0,4},{4,0},{8,12},{12,8},{16,20},{20,16},{24,28},{28,24},{1,5},{5... | collective-permute-start | bytes 1572872 | tf_op jit(solution)/shard_map/ppermute | solution.py:37
  201.8 40.2 %collective-permute-start.25 = (bf16[256,2048]{1,0:T(8,128)(2,1)}, bf16[256,2048]{1,0:T(8,128)(2,1)}, u32[]{:S(2)}, u32[]{:S(2)}) collective-permute-start(bf16[256,2048]{1,0:T(8,128)(2,1)} %collective-permute-done.23.rest_4_), channel_id=1, source_target_pairs={{0,8},{4,12},{8,0},{12,4},{16,24},{20,28},{24,16},{28,20},{1,9},{5... | collective-permute-start | bytes 3145736 | tf_op jit(solution)/shard_map/ppermute | solution.py:37
  203.3 38.7 %collective-permute-start.32 = (bf16[256,2048]{1,0:T(8,128)(2,1)}, bf16[256,2048]{1,0:T(8,128)(2,1)}, u32[]{:S(2)}, u32[]{:S(2)}) collective-permute-start(bf16[256,2048]{1,0:T(8,128)(2,1)} %collective-permute-done.28.rest_10_), channel_id=1, source_target_pairs={{0,16},{4,20},{8,24},{12,28},{16,0},{20,4},{24,8},{28,12},{1,17},{... | collective-permute-start | bytes 3145736 | tf_op jit(solution)/shard_map/ppermute | solution.py:37
  204.9 34.8 %collective-permute-start.46 = (bf16[1024,256]{1,0:T(8,128)(2,1)}, bf16[1024,256]{1,0:T(8,128)(2,1)S(1)}, u32[]{:S(2)}, u32[]{:S(2)}) collective-permute-start(bf16[1024,256]{1,0:T(8,128)(2,1)} %collective-permute-done.42.rest_26_), channel_id=1, source_target_pairs={{0,16},{4,20},{8,24},{12,28},{16,0},{20,4},{24,8},{28,12},{1,17},{... | collective-permute-start | bytes 1572872 | tf_op jit(solution)/shard_map/ppermute | solution.py:37
  205.4 34.3 %collective-permute-start.36 = (bf16[1024,256]{1,0:T(8,128)(2,1)S(1)}, bf16[1024,256]{1,0:T(8,128)(2,1)S(1)}, u32[]{:S(2)}, u32[]{:S(2)}) collective-permute-start(bf16[1024,256]{1,0:T(8,128)(2,1)S(1)} %collective-permute-done.35.rest_18_), channel_id=1, source_target_pairs={{0,4},{4,0},{8,12},{12,8},{16,20},{20,16},{24,28},{28,24},{1,5},{5... | collective-permute-start | bytes 1572872 | tf_op jit(solution)/shard_map/ppermute | solution.py:37
  223.7 16.5 %collective-permute-start.43 = (bf16[1024,256]{1,0:T(8,128)(2,1)}, bf16[1024,256]{1,0:T(8,128)(2,1)S(1)}, u32[]{:S(2)}, u32[]{:S(2)}) collective-permute-start(bf16[1024,256]{1,0:T(8,128)(2,1)} %collective-permute-done.42.rest_26_), channel_id=1, source_target_pairs={{0,4},{4,0},{8,12},{12,8},{16,20},{20,16},{24,28},{28,24},{1,5},{5... | collective-permute-start | bytes 1572872 | tf_op jit(solution)/shard_map/ppermute | solution.py:37
  239.7 8.3 %collective-permute-start.20 = (bf16[256,2048]{1,0:T(8,128)(2,1)}, bf16[256,2048]{1,0:T(8,128)(2,1)S(1)}, u32[]{:S(2)}, u32[]{:S(2)}) collective-permute-start(bf16[256,2048]{1,0:T(8,128)(2,1)} %rest_0_.4), channel_id=1, source_target_pairs={{0,4},{4,0},{8,12},{12,8},{16,20},{20,16},{24,28},{28,24},{1,5},{5... | collective-permute-start | bytes 3145736 | tf_op jit(solution)/shard_map/ppermute | solution.py:37
  239.7 8.7 %collective-permute-start.27 = (bf16[256,2048]{1,0:T(8,128)(2,1)}, bf16[256,2048]{1,0:T(8,128)(2,1)}, u32[]{:S(2)}, u32[]{:S(2)}) collective-permute-start(bf16[256,2048]{1,0:T(8,128)(2,1)} %rest_8_.1), channel_id=1, source_target_pairs={{0,4},{4,0},{8,12},{12,8},{16,20},{20,16},{24,28},{28,24},{1,5},{5... | collective-permute-start | bytes 3145736 | tf_op jit(solution)/shard_map/ppermute | solution.py:37
  240.2 8.4 %collective-permute-start.24 = (bf16[256,2048]{1,0:T(8,128)(2,1)}, bf16[256,2048]{1,0:T(8,128)(2,1)}, u32[]{:S(2)}, u32[]{:S(2)}) collective-permute-start(bf16[256,2048]{1,0:T(8,128)(2,1)} %collective-permute-done.23.rest_4_), channel_id=1, source_target_pairs={{0,4},{4,0},{8,12},{12,8},{16,20},{20,16},{24,28},{28,24},{1,5},{5... | collective-permute-start | bytes 3145736 | tf_op jit(solution)/shard_map/ppermute | solution.py:37
  247.8 8.1 %collective-permute-start.29 = (bf16[256,2048]{1,0:T(8,128)(2,1)}, bf16[256,2048]{1,0:T(8,128)(2,1)}, u32[]{:S(2)}, u32[]{:S(2)}) collective-permute-start(bf16[256,2048]{1,0:T(8,128)(2,1)} %collective-permute-done.28.rest_10_), channel_id=1, source_target_pairs={{0,4},{4,0},{8,12},{12,8},{16,20},{20,16},{24,28},{28,24},{1,5},{5... | collective-permute-start | bytes 3145736 | tf_op jit(solution)/shard_map/ppermute | solution.py:37
  247.9 8.0 %collective-permute-start.22 = (bf16[256,2048]{1,0:T(8,128)(2,1)S(1)}, bf16[256,2048]{1,0:T(8,128)(2,1)}, u32[]{:S(2)}, u32[]{:S(2)}) collective-permute-start(bf16[256,2048]{1,0:T(8,128)(2,1)S(1)} %collective-permute-done.21.rest_2_), channel_id=1, source_target_pairs={{0,4},{4,0},{8,12},{12,8},{16,20},{20,16},{24,28},{28,24},{1,5},{5... | collective-permute-start | bytes 3145736 | tf_op jit(solution)/shard_map/ppermute | solution.py:37
  248.4 8.3 %collective-permute-start.26 = (bf16[256,2048]{1,0:T(8,128)(2,1)}, bf16[256,2048]{1,0:T(8,128)(2,1)}, u32[]{:S(2)}, u32[]{:S(2)}) collective-permute-start(bf16[256,2048]{1,0:T(8,128)(2,1)} %collective-permute-done.25.rest_6_), channel_id=1, source_target_pairs={{0,4},{4,0},{8,12},{12,8},{16,20},{20,16},{24,28},{28,24},{1,5},{5... | collective-permute-start | bytes 3145736 | tf_op jit(solution)/shard_map/ppermute | solution.py:37
  248.6 8.1 %collective-permute-start.33 = (bf16[256,2048]{1,0:T(8,128)(2,1)}, bf16[256,2048]{1,0:T(8,128)(2,1)}, u32[]{:S(2)}, u32[]{:S(2)}) collective-permute-start(bf16[256,2048]{1,0:T(8,128)(2,1)} %collective-permute-done.32.rest_14_), channel_id=1, source_target_pairs={{0,4},{4,0},{8,12},{12,8},{16,20},{20,16},{24,28},{28,24},{1,5},{5... | collective-permute-start | bytes 3145736 | tf_op jit(solution)/shard_map/ppermute | solution.py:37
  443.0 9.8 %collective-permute-start.54 = (bf16[512,256]{1,0:T(8,128)(2,1)}, bf16[512,256]{1,0:T(8,128)(2,1)S(1)}, u32[]{:S(2)}, u32[]{:S(2)}) collective-permute-start(bf16[512,256]{1,0:T(8,128)(2,1)} %get-tuple-element.131), channel_id=1, source_target_pairs={{0,4},{4,0},{8,12},{12,8},{1,5},{5,1},{9,13},{13,9},{2,6},{6,2},{1... | collective-permute-start | bytes 786440 | tf_op jit(solution)/shard_map/ppermute | solution.py:37
  447.4 8.4 %collective-permute-start.56 = (bf16[512,256]{1,0:T(8,128)(2,1)S(1)}, bf16[512,256]{1,0:T(8,128)(2,1)S(1)}, u32[]{:S(2)}, u32[]{:S(2)}) collective-permute-start(bf16[512,256]{1,0:T(8,128)(2,1)S(1)} %add_convert_fusion.7), channel_id=1, source_target_pairs={{0,8},{4,12},{8,0},{12,4},{1,9},{5,13},{9,1},{13,5},{2,10},{6,14},... | collective-permute-start | bytes 786440 | tf_op jit(solution)/shard_map/ppermute | solution.py:37
  448.9 106.8 %collective-permute-start.48 = (bf16[128,2048]{1,0:T(8,128)(2,1)}, bf16[128,2048]{1,0:T(8,128)(2,1)}, u32[]{:S(2)}, u32[]{:S(2)}) collective-permute-start(bf16[128,2048]{1,0:T(8,128)(2,1)} %get-tuple-element.200), channel_id=1, source_target_pairs={{0,1},{1,2},{2,3},{3,0},{4,5},{5,6},{6,7},{7,4},{8,9},{9,10},{10,1... | collective-permute-start | bytes 1572872 | tf_op jit(solution)/shard_map/ppermute | solution.py:125
  448.9 108.4 %collective-permute-start.49 = (bf16[128,2048]{1,0:T(8,128)(2,1)S(1)}, bf16[128,2048]{1,0:T(8,128)(2,1)}, u32[]{:S(2)}, u32[]{:S(2)}) collective-permute-start(bf16[128,2048]{1,0:T(8,128)(2,1)S(1)} %get-tuple-element.202), channel_id=1, source_target_pairs={{0,2},{1,3},{2,0},{3,1},{4,6},{5,7},{6,4},{7,5},{8,10},{9,11},{10,... | collective-permute-start | bytes 1572872 | tf_op jit(solution)/shard_map/ppermute | solution.py:125
  451.4 106.5 %collective-permute-start.50 = (bf16[128,2048]{1,0:T(8,128)(2,1)S(1)}, bf16[128,2048]{1,0:T(8,128)(2,1)}, u32[]{:S(2)}, u32[]{:S(2)}) collective-permute-start(bf16[128,2048]{1,0:T(8,128)(2,1)S(1)} %get-tuple-element.201), channel_id=1, source_target_pairs={{0,3},{1,0},{2,1},{3,2},{4,7},{5,4},{6,5},{7,6},{8,11},{9,8},{10,9... | collective-permute-start | bytes 1572872 | tf_op jit(solution)/shard_map/ppermute | solution.py:125
  550.5 15.1 %collective-permute-start.69 = (bf16[256,1024]{1,0:T(8,128)(2,1)}, bf16[256,1024]{1,0:T(8,128)(2,1)S(1)}, u32[]{:S(2)}, u32[]{:S(2)}) collective-permute-start(bf16[256,1024]{1,0:T(8,128)(2,1)} %get-tuple-element.157), channel_id=1, source_target_pairs={{0,16},{4,20},{8,24},{12,28},{16,0},{20,4},{24,8},{28,12},{1,17},{... | collective-permute-start | bytes 1572872 | tf_op jit(solution)/shard_map/ppermute | solution.py:37
  554.2 45.4 %collective-permute-start.71 = (bf16[256,1024]{1,0:T(8,128)(2,1)}, bf16[256,1024]{1,0:T(8,128)(2,1)S(1)}, u32[]{:S(2)}, u32[]{:S(2)}) collective-permute-start(bf16[256,1024]{1,0:T(8,128)(2,1)} %get-tuple-element.158), channel_id=1, source_target_pairs={{0,16},{4,20},{8,24},{12,28},{16,0},{20,4},{24,8},{28,12},{1,17},{... | collective-permute-start | bytes 1572872 | tf_op jit(solution)/shard_map/ppermute | solution.py:37
  555.7 15.1 %collective-permute-start.73 = (bf16[256,1024]{1,0:T(8,128)(2,1)}, bf16[256,1024]{1,0:T(8,128)(2,1)S(1)}, u32[]{:S(2)}, u32[]{:S(2)}) collective-permute-start(bf16[256,1024]{1,0:T(8,128)(2,1)} %get-tuple-element.162), channel_id=1, source_target_pairs={{0,8},{4,12},{8,0},{12,4},{16,24},{20,28},{24,16},{28,20},{1,9},{5... | collective-permute-start | bytes 1572872 | tf_op jit(solution)/shard_map/ppermute | solution.py:37
  557.3 63.0 %collective-permute-start.72 = (bf16[256,1024]{1,0:T(8,128)(2,1)}, bf16[256,1024]{1,0:T(8,128)(2,1)S(1)}, u32[]{:S(2)}, u32[]{:S(2)}) collective-permute-start(bf16[256,1024]{1,0:T(8,128)(2,1)} %get-tuple-element.160), channel_id=1, source_target_pairs={{0,8},{4,12},{8,0},{12,4},{16,24},{20,28},{24,16},{28,20},{1,9},{5... | collective-permute-start | bytes 1572872 | tf_op jit(solution)/shard_map/ppermute | solution.py:37
  562.5 37.1 %collective-permute-start.51 = (bf16[128,2048]{1,0:T(8,128)(2,1)}, bf16[128,2048]{1,0:T(8,128)(2,1)S(1)}, u32[]{:S(2)}, u32[]{:S(2)}) collective-permute-start(bf16[128,2048]{1,0:T(8,128)(2,1)} %get-tuple-element.199), channel_id=1, source_target_pairs={{0,1},{1,2},{2,3},{3,0},{4,5},{5,6},{6,7},{7,4},{8,9},{9,10},{10,1... | collective-permute-start | bytes 1572872 | tf_op jit(solution)/shard_map/ppermute | solution.py:136
  566.8 14.7 %collective-permute-start.78 = (f32[2,2048]{1,0:T(2,128)S(1)}, f32[2,2048]{1,0:T(2,128)S(1)}, u32[]{:S(2)}, u32[]{:S(2)}) collective-permute-start(f32[2,2048]{1,0:T(2,128)S(1)} %add.221), channel_id=1, source_target_pairs={{0,8},{1,9},{2,10},{3,11},{4,12},{5,13},{6,14},{7,15},{8,0},{9,1},... | collective-permute-start | bytes 49160 | tf_op jit(solution)/shard_map/ppermute | solution.py:37
  571.0 15.7 %collective-permute-start.61 = (bf16[256,512]{1,0:T(8,128)(2,1)S(1)}, bf16[256,512]{1,0:T(8,128)(2,1)S(1)}, u32[]{:S(2)}, u32[]{:S(2)}) collective-permute-start(bf16[256,512]{1,0:T(8,128)(2,1)S(1)} %copy-done.51), channel_id=1, source_target_pairs={{0,8},{4,12},{8,0},{12,4},{16,24},{20,28},{24,16},{28,20},{1,9},{5... | collective-permute-start | bytes 786440 | tf_op jit(solution)/shard_map/ppermute | solution.py:37
  585.3 10.9 %collective-permute-start.57 = (bf16[256,768]{1,0:T(8,128)(2,1)S(1)}, bf16[256,768]{1,0:T(8,128)(2,1)S(1)}, u32[]{:S(2)}, u32[]{:S(2)}) collective-permute-start(bf16[256,768]{1,0:T(8,128)(2,1)S(1)} %copy-done.47), channel_id=1, source_target_pairs={{0,16},{4,20},{8,24},{12,28},{16,0},{20,4},{24,8},{28,12},{1,17},{... | collective-permute-start | bytes 1179656 | tf_op jit(solution)/shard_map/ppermute | solution.py:37
  586.7 56.9 %collective-permute-start.67 = (bf16[256,2048]{1,0:T(8,128)(2,1)}, bf16[256,2048]{1,0:T(8,128)(2,1)}, u32[]{:S(2)}, u32[]{:S(2)}) collective-permute-start(bf16[256,2048]{1,0:T(8,128)(2,1)} %get-tuple-element.154), channel_id=1, source_target_pairs={{0,8},{4,12},{8,0},{12,4},{16,24},{20,28},{24,16},{28,20},{1,9},{5... | collective-permute-start | bytes 3145736 | tf_op jit(solution)/shard_map/ppermute | solution.py:37
  596.2 21.8 %collective-permute-start.70 = (bf16[256,1024]{1,0:T(8,128)(2,1)S(1)}, bf16[256,1024]{1,0:T(8,128)(2,1)S(1)}, u32[]{:S(2)}, u32[]{:S(2)}) collective-permute-start(bf16[256,1024]{1,0:T(8,128)(2,1)S(1)} %add_convert_fusion.3), channel_id=1, source_target_pairs={{0,8},{4,12},{8,0},{12,4},{16,24},{20,28},{24,16},{28,20},{1,9},{5... | collective-permute-start | bytes 1572872 | tf_op jit(solution)/shard_map/ppermute | solution.py:37
  599.5 19.2 %collective-permute-start.52 = (bf16[128,2048]{1,0:T(8,128)(2,1)}, bf16[128,2048]{1,0:T(8,128)(2,1)S(1)}, u32[]{:S(2)}, u32[]{:S(2)}) collective-permute-start(bf16[128,2048]{1,0:T(8,128)(2,1)} %get-tuple-element.199), channel_id=1, source_target_pairs={{0,2},{1,3},{2,0},{3,1},{4,6},{5,7},{6,4},{7,5},{8,10},{9,11},{10,... | collective-permute-start | bytes 1572872 | tf_op jit(solution)/shard_map/ppermute | solution.py:136
  599.6 39.3 %collective-permute-start.63 = (bf16[256,2048]{1,0:T(8,128)(2,1)}, bf16[256,2048]{1,0:T(8,128)(2,1)}, u32[]{:S(2)}, u32[]{:S(2)}) collective-permute-start(bf16[256,2048]{1,0:T(8,128)(2,1)} %get-tuple-element.149), channel_id=1, source_target_pairs={{0,16},{4,20},{8,24},{12,28},{16,0},{20,4},{24,8},{28,12},{1,17},{... | collective-permute-start | bytes 3145736 | tf_op jit(solution)/shard_map/ppermute | solution.py:37
  618.0 14.8 %collective-permute-start.74 = (bf16[256,1024]{1,0:T(8,128)(2,1)S(1)}, bf16[256,1024]{1,0:T(8,128)(2,1)S(1)}, u32[]{:S(2)}, u32[]{:S(2)}) collective-permute-start(bf16[256,1024]{1,0:T(8,128)(2,1)S(1)} %add_convert_fusion.2), channel_id=1, source_target_pairs={{0,16},{4,20},{8,24},{12,28},{16,0},{20,4},{24,8},{28,12},{1,17},{... | collective-permute-start | bytes 1572872 | tf_op jit(solution)/shard_map/ppermute | solution.py:37
  618.7 52.4 %collective-permute-start.65 = (bf16[256,2048]{1,0:T(8,128)(2,1)}, bf16[256,2048]{1,0:T(8,128)(2,1)}, u32[]{:S(2)}, u32[]{:S(2)}) collective-permute-start(bf16[256,2048]{1,0:T(8,128)(2,1)} %get-tuple-element.150), channel_id=1, source_target_pairs={{0,16},{4,20},{8,24},{12,28},{16,0},{20,4},{24,8},{28,12},{1,17},{... | collective-permute-start | bytes 3145736 | tf_op jit(solution)/shard_map/ppermute | solution.py:37
  620.4 16.1 %collective-permute-start.53 = (bf16[128,2048]{1,0:T(8,128)(2,1)}, bf16[128,2048]{1,0:T(8,128)(2,1)}, u32[]{:S(2)}, u32[]{:S(2)}) collective-permute-start(bf16[128,2048]{1,0:T(8,128)(2,1)} %get-tuple-element.199), channel_id=1, source_target_pairs={{0,3},{1,0},{2,1},{3,2},{4,7},{5,4},{6,5},{7,6},{8,11},{9,8},{10,9... | collective-permute-start | bytes 1572872 | tf_op jit(solution)/shard_map/ppermute | solution.py:136
  632.7 9.4 %collective-permute-start.60 = (bf16[256,512]{1,0:T(8,128)(2,1)}, bf16[256,512]{1,0:T(8,128)(2,1)S(1)}, u32[]{:S(2)}, u32[]{:S(2)}) collective-permute-start(bf16[256,512]{1,0:T(8,128)(2,1)} %get-tuple-element.145), channel_id=1, source_target_pairs={{0,8},{4,12},{8,0},{12,4},{16,24},{20,28},{24,16},{28,20},{1,9},{5... | collective-permute-start | bytes 786440 | tf_op jit(solution)/shard_map/ppermute | solution.py:37
  636.5 31.2 %collective-permute-start.59 = (bf16[256,768]{1,0:T(8,128)(2,1)}, bf16[256,768]{1,0:T(8,128)(2,1)}, u32[]{:S(2)}, u32[]{:S(2)}) collective-permute-start(bf16[256,768]{1,0:T(8,128)(2,1)} %get-tuple-element.143), channel_id=1, source_target_pairs={{0,16},{4,20},{8,24},{12,28},{16,0},{20,4},{24,8},{28,12},{1,17},{... | collective-permute-start | bytes 1179656 | tf_op jit(solution)/shard_map/ppermute | solution.py:37
  638.9 24.4 %collective-permute-start.62 = (bf16[256,512]{1,0:T(8,128)(2,1)}, bf16[256,512]{1,0:T(8,128)(2,1)S(1)}, u32[]{:S(2)}, u32[]{:S(2)}) collective-permute-start(bf16[256,512]{1,0:T(8,128)(2,1)} %add_convert_fusion.6), channel_id=1, source_target_pairs={{0,16},{4,20},{8,24},{12,28},{16,0},{20,4},{24,8},{28,12},{1,17},{... | collective-permute-start | bytes 786440 | tf_op jit(solution)/shard_map/ppermute | solution.py:37
  642.1 26.1 %collective-permute-start.58 = (bf16[256,768]{1,0:T(8,128)(2,1)}, bf16[256,768]{1,0:T(8,128)(2,1)}, u32[]{:S(2)}, u32[]{:S(2)}) collective-permute-start(bf16[256,768]{1,0:T(8,128)(2,1)} %add_convert_fusion.5), channel_id=1, source_target_pairs={{0,8},{4,12},{8,0},{12,4},{16,24},{20,28},{24,16},{28,20},{1,9},{5... | collective-permute-start | bytes 1179656 | tf_op jit(solution)/shard_map/ppermute | solution.py:37
  643.7 28.1 %collective-permute-start.64 = (bf16[256,2048]{1,0:T(8,128)(2,1)S(1)}, bf16[256,2048]{1,0:T(8,128)(2,1)}, u32[]{:S(2)}, u32[]{:S(2)}) collective-permute-start(bf16[256,2048]{1,0:T(8,128)(2,1)S(1)} %add_convert_fusion.1), channel_id=1, source_target_pairs={{0,8},{4,12},{8,0},{12,4},{16,24},{20,28},{24,16},{28,20},{1,9},{5... | collective-permute-start | bytes 3145736 | tf_op jit(solution)/shard_map/ppermute | solution.py:37
  663.3 25.3 %collective-permute-start.66 = (bf16[256,2048]{1,0:T(8,128)(2,1)}, bf16[256,2048]{1,0:T(8,128)(2,1)}, u32[]{:S(2)}, u32[]{:S(2)}) collective-permute-start(bf16[256,2048]{1,0:T(8,128)(2,1)} %get-tuple-element.152), channel_id=1, source_target_pairs={{0,8},{4,12},{8,0},{12,4},{16,24},{20,28},{24,16},{28,20},{1,9},{5... | collective-permute-start | bytes 3145736 | tf_op jit(solution)/shard_map/ppermute | solution.py:37
  667.7 20.8 %collective-permute-start.68 = (bf16[256,2048]{1,0:T(8,128)(2,1)S(1)}, bf16[256,2048]{1,0:T(8,128)(2,1)S(1)}, u32[]{:S(2)}, u32[]{:S(2)}) collective-permute-start(bf16[256,2048]{1,0:T(8,128)(2,1)S(1)} %add_convert_fusion), channel_id=1, source_target_pairs={{0,16},{4,20},{8,24},{12,28},{16,0},{20,4},{24,8},{28,12},{1,17},{... | collective-permute-start | bytes 3145736 | tf_op jit(solution)/shard_map/ppermute | solution.py:37
  (68 other events, 1016.0 us)
where the time goes:
time: 701 us; the launch traced here: 692 us
  Pallas kernels  374 us (53%)
  waiting for transfers between devices  202 us (29%)
  starting transfers between devices  60.7 us (9%)
  other arithmetic  30.9 us (4%)
  local copies, waits for them, and re-layouts  22.1 us (3%)
    ppermute x74, waiting for transfers between devices, swap(): return lax.ppermute(value, axes, [(i, i ^ bit) for i in range(size)])  202 us
    pallas_call x3, Pallas kernels, line_sum(): pl.pallas_call(functools.partial(line_body, finish, keep_state, gain_sum,...  201 us
    ppermute x74, starting transfers between devices, swap(): return lax.ppermute(value, axes, [(i, i ^ bit) for i in range(size)])  54.9 us
    pallas_call x1, Pallas kernels, ffn(): pl.pallas_call(functools.partial(ffn_body, count, len(low_pieces), tile),...  48.5 us
    pallas_call x2, Pallas kernels, plane_grads(): pl.pallas_call(functools.partial(grads_body, count, jobs), in_specs=[pl.B...  42 us
    pallas_call x1, Pallas kernels, attend_back(): pl.pallas_call(functools.partial(attend_back_body, len(pieces)), grid=gri...  35.5 us
    pallas_call x1, Pallas kernels, attend(): pl.pallas_call(functools.partial(attend_body, len(pieces)), grid=grid, in...  21.3 us
  transfers between devices with their start and end apart: 80, of which 29 were waited for; matrix products, arithmetic and copies ran while one was open for 6% of the time, Pallas kernels for 28%

commit v1 on v0

--- a/solution.py
+++ b/solution.py
@@ -37,7 +37,7 @@
     return lax.ppermute(value, axes, [(i, i ^ bit) for i in range(size)])
 
 
-def gather_pair(first, second, far_after=(), near_after=(), cross_after=(), core_after=()):
+def gather_pair(first, second, far_after=(), near_after=(), cross_after=(), core_after=(), core=True):
     size = plane_size()
     bits = [1 << b for b in range(1, size.bit_length() - 1)]
     sides = [{0: first}, {0: second}]
@@ -54,6 +54,8 @@
             for bit in bits:
                 for r in list(side):
                     side[r | bit] = swap(side[r], PLANE, size, bit)
+    if not core:
+        return [[side[r] for r in range(0, size, 2)] for side in sides]
     for side in sides:
         for r in list(side):
             side[r | 1] = swap(after(side[r], *core_after), PLANE, size, 1)
@@ -320,24 +322,7 @@
     )(left, *pieces)
 
 
-def ffn_body(count, narrow, tile, normed, d_ffn, *rest):
-    gate_pieces, up_pieces, rest = rest[:count], rest[count : 2 * count], rest[2 * count :]
-    low_pieces, high_pieces, rest = rest[:narrow], rest[narrow : 2 * narrow], rest[2 * narrow :]
-    active, d_gate, d_up, out, d_normed, gate, up, down, out_sum, d_sum, sems = rest
-    f_step = pl.program_id(1)
-    half = down.shape[0] // 2
-
-    @pl.when((pl.program_id(0) == 0) & (f_step == 0))
-    def _():
-        place_pieces(gate_pieces, gate, sems.at[0], 0)
-        place_pieces(up_pieces, up, sems.at[1], 0)
-        place_pieces(low_pieces, down.at[pl.ds(0, half)], sems.at[2], 1)
-        place_pieces(high_pieces, down.at[pl.ds(half, half)], sems.at[3], 1)
-        await_whole(gate, sems.at[0])
-        await_whole(up, sems.at[1])
-        await_whole(down.at[pl.ds(0, half)], sems.at[2])
-        await_whole(down.at[pl.ds(half, half)], sems.at[3])
-
+def ffn_tile(f_step, tile, normed, d_ffn, gate, up, down, active, d_gate, d_up, out, d_normed, out_sum, d_sum):
     units = pl.ds(pl.multiple_of(f_step * tile, tile), tile)
     gate_tile, up_tile, down_tile = gate[:, units], up[:, units], down[units, :]
     gate_in = jnp.dot(normed[...], gate_tile, preferred_element_type=F32)
@@ -371,7 +356,28 @@
         d_normed[...] = d_sum[...].astype(BF16)
 
 
-def ffn(normed, d_ffn, gate_pieces, up_pieces, low_pieces, high_pieces):
+def ffn_body(count, narrow, tile, normed, d_ffn, *rest):
+    gate_pieces, up_pieces, rest = rest[:count], rest[count : 2 * count], rest[2 * count :]
+    low_pieces, high_pieces, rest = rest[:narrow], rest[narrow : 2 * narrow], rest[2 * narrow :]
+    active, d_gate, d_up, out, d_normed, gate, up, down, out_sum, d_sum, sems = rest
+    f_step = pl.program_id(1)
+    half = down.shape[0] // 2
+
+    @pl.when((pl.program_id(0) == 0) & (f_step == 0))
+    def _():
+        place_pieces(gate_pieces, gate, sems.at[0], 0)
+        place_pieces(up_pieces, up, sems.at[1], 0)
+        place_pieces(low_pieces, down.at[pl.ds(0, half)], sems.at[2], 1)
+        place_pieces(high_pieces, down.at[pl.ds(half, half)], sems.at[3], 1)
+        await_whole(gate, sems.at[0])
+        await_whole(up, sems.at[1])
+        await_whole(down.at[pl.ds(0, half)], sems.at[2])
+        await_whole(down.at[pl.ds(half, half)], sems.at[3])
+
+    ffn_tile(f_step, tile, normed, d_ffn, gate, up, down, active, d_gate, d_up, out, d_normed, out_sum, d_sum)
+
+
+def ffn(normed, d_ffn, gate_pieces, up_pieces, low_pieces, high_pieces, pushed):
     rows, width = normed.shape
     units = gate_pieces[0].shape[1]
     count = len(gate_pieces)
@@ -382,8 +388,19 @@
     unit_spec = pl.BlockSpec((row_tile, tile), lambda i, f: (i, f))
     unit_shape = jax.ShapeDtypeStruct((rows, units), BF16)
     row_shape = jax.ShapeDtypeStruct((rows, width), BF16)
+    body = functools.partial(ffn_body, count, len(low_pieces), tile)
+    settings, sems = params(2), [pltpu.SemaphoreType.DMA((4,))]
+    if pushed:
+        body = functools.partial(pushed_body, count, tile)
+        sems = [pltpu.SemaphoreType.DMA((3, units // tile))] * 3
+        settings = pltpu.CompilerParams(
+            dimension_semantics=("arbitrary",) * 2,
+            vmem_limit_bytes=VMEM_BYTES,
+            collective_id=5,
+            has_side_effects=True,
+        )
     return pl.pallas_call(
-        functools.partial(ffn_body, count, len(low_pieces), tile),
+        body,
         grid=(rows // row_tile, units // tile),
         in_specs=[row_spec, row_spec] + [ANYWHERE] * (2 * count + 2 * len(low_pieces)),
         out_specs=[unit_spec, unit_spec, unit_spec, row_spec, row_spec],
@@ -394,14 +411,86 @@
             pltpu.VMEM((units, width), BF16),
             pltpu.VMEM((row_tile, width), F32),
             pltpu.VMEM((row_tile, width), F32),
-            pltpu.SemaphoreType.DMA((4,)),
-        ],
-        compiler_params=params(2),
+        ]
+        + sems,
+        compiler_params=settings,
         cost_estimate=pl.CostEstimate(
             flops=12 * rows * width * units, bytes_accessed=6 * width * units + 14 * rows * width, transcendentals=rows * units
         ),
         name="feed_forward",
     )(normed, d_ffn, *gate_pieces, *up_pieces, *low_pieces, *high_pieces)
+
+
+def pushed_body(count, tile, normed, d_ffn, *refs):
+    groups, rest = [refs[k * count : (k + 1) * count] for k in range(4)], refs[4 * count :]
+    active, d_gate, d_up, out, d_normed, gate, up, down, out_sum, d_sum, near, send, recv = rest
+    f_step = pl.program_id(1)
+    first = (pl.program_id(0) == 0) & (f_step == 0)
+    last = (pl.program_id(0) == pl.num_programs(0) - 1) & (f_step == pl.num_programs(1) - 1)
+    steps = down.shape[0] // tile
+    width = down.shape[1]
+    extent = width // (2 * count)
+    me = plane_index()
+    mate = {"context": lax.axis_index("context") ^ 1}
+    mesh_ids = pl.DeviceIdType.MESH
+
+    def push(source, target, w, t):
+        return pltpu.make_async_remote_copy(
+            src_ref=source,
+            dst_ref=target,
+            send_sem=send.at[w, t],
+            recv_sem=recv.at[w, t],
+            device_id=mate,
+            device_id_type=mesh_ids,
+        )
+
+    def halves(t):
+        units = pl.ds(pl.multiple_of(t * tile, tile), tile)
+        half = pl.ds(0, width // 2)
+        return [gate.at[half, units], up.at[half, units], down.at[units, half]]
+
+    @pl.when(first)
+    def _():
+        barrier = pltpu.get_barrier_semaphore()
+        pl.semaphore_signal(barrier, inc=1, device_id=mate, device_id_type=mesh_ids)
+        pl.semaphore_wait(barrier, 1)
+
+        def start(t, carry):
+            units = pl.ds(pl.multiple_of(t * tile, tile), tile)
+            for i in range(count):
+                base = pl.multiple_of((me ^ (2 * i)) * extent, extent)
+                rows = pl.ds(base, extent)
+                left = pl.ds(base, extent // 2)
+                right = pl.ds(pl.multiple_of(base + extent // 2, extent // 2), extent // 2)
+                moves = (
+                    (0, groups[0][i].at[:, units], gate.at[rows, units]),
+                    (1, groups[1][i].at[:, units], up.at[rows, units]),
+                    (2, groups[2][i].at[units, :], down.at[units, left]),
+                    (2, groups[3][i].at[units, :], down.at[units, right]),
+                )
+                for w, source, target in moves:
+                    push(source, target, w, t).start()
+                    pltpu.make_async_copy(source, target, near.at[w, t]).start()
+            return carry
+
+        lax.fori_loop(0, steps, start, 0)
+
+    @pl.when(pl.program_id(0) == 0)
+    def _():
+        for w, half in enumerate(halves(f_step)):
+            pltpu.make_async_copy(half, half, near.at[w, f_step]).wait()
+            push(half, half, w, f_step).wait_recv()
+
+    ffn_tile(f_step, tile, normed, d_ffn, gate, up, down, active, d_gate, d_up, out, d_normed, out_sum, d_sum)
+
+    @pl.when(last)
+    def _():
+        def drain(t, carry):
+            for w, half in enumerate(halves(t)):
+                push(half, half, w, t).wait_send()
+            return carry
+
+        lax.fori_loop(0, steps, drain, 0)
 
 
 def doubled(values, lane, head):
@@ -927,12 +1016,19 @@
     output_pieces = widened(output_pieces)
     branch = gathered_matmul(mixture, output_pieces, 1, False)
     normed_ffn, hidden = line_sum(branch, [token_rows, gain_ffn], finish_attention, True, False, 0)
-    gate_pieces, up_pieces = gather_pair(w_gate, w_up, early, late, [mixture], [normed_ffn])
-    low_pieces, high_pieces = gather_pair(w_down[:half], w_down[half:], early, late, [normed_ffn], [normed_ffn])
-    low_pieces, high_pieces = widened(low_pieces), widened(high_pieces)
+    extent = width // size
+    pushed = extent % (2 * LANES) == 0
+    order = (early, late, [mixture], [normed_ffn], not pushed)
+    gate_pieces, up_pieces = gather_pair(w_gate, w_up, *order)
+    order = (early, late, [normed_ffn], [normed_ffn], not pushed)
+    if pushed:
+        low_pieces, high_pieces = gather_pair(w_down[:, : extent // 2], w_down[:, extent // 2 :], *order)
+    else:
+        low_pieces, high_pieces = gather_pair(w_down[:half], w_down[half:], *order)
+        low_pieces, high_pieces = widened(low_pieces), widened(high_pieces)
     d_ffn = (RESIDUAL_SCALE * grad_rows.astype(F32)).astype(BF16)
     active, d_gate, d_up, ffn_out, d_normed_ffn = ffn(
-        normed_ffn, d_ffn, gate_pieces, up_pieces, low_pieces, high_pieces
+        normed_ffn, d_ffn, gate_pieces, up_pieces, low_pieces, high_pieces, pushed
     )
     grad_gate, grad_up, grad_low, grad_high = plane_grads(
         [(normed_ffn, d_gate), (normed_ffn, d_up), (d_ffn, active[:, :half]), (d_ffn, active[:, half:])], 3

time: 701 us -> 621 us (0.89)
  waiting for transfers between devices: 202 us -> 134 us
    ppermute x74 -> x58, waiting for transfers between devices: 202 us -> 134 us  [swap(): return lax.ppermute(value, axes, [(i, i ^ bit) for i in range(size)])]
    ppermute x74 -> x58, starting transfers between devices: 54.9 us -> 49 us  [swap(): return lax.ppermute(value, axes, [(i, i ^ bit) for i in range(size)])]
  transfers between devices with their start and end apart: 80 -> 64, of which waited for: 29 -> 27; matrix products, arithmetic and copies ran while one was open for 6% -> 7% of each run, Pallas kernels for 28% -> 31%
where the time goes in v1:
time: 621 us; the launch traced here: 614 us
  Pallas kernels  369 us (59%)
  waiting for transfers between devices  134 us (22%)
  starting transfers between devices  54.7 us (9%)
  other arithmetic  30.9 us (5%)
  local copies, waits for them, and re-layouts  23.4 us (4%)
    pallas_call x3, Pallas kernels, line_sum(): pl.pallas_call(functools.partial(line_body, finish, keep_state, gain_sum,...  201 us
    ppermute x58, waiting for transfers between devices, swap(): return lax.ppermute(value, axes, [(i, i ^ bit) for i in range(size)])  134 us
    ppermute x58, starting transfers between devices, swap(): return lax.ppermute(value, axes, [(i, i ^ bit) for i in range(size)])  49 us
    pallas_call x1, Pallas kernels, ffn(): pl.pallas_call(body, grid=(rows // row_tile, units // tile), in_specs=[ro...  44.4 us
    pallas_call x2, Pallas kernels, plane_grads(): pl.pallas_call(functools.partial(grads_body, count, jobs), in_specs=[pl.B...  42.1 us
    pallas_call x1, Pallas kernels, attend_back(): pl.pallas_call(functools.partial(attend_back_body, len(pieces)), grid=gri...  35.5 us
    pallas_call x1, Pallas kernels, attend(): pl.pallas_call(functools.partial(attend_body, len(pieces)), grid=grid, in...  21.3 us
  transfers between devices with their start and end apart: 64, of which 27 were waited for; matrix products, arithmetic and copies ran while one was open for 7% of the time, Pallas kernels for 31%

profile of v1, /device:TPU:0, one launch (start us, length us, event | category | flops | bytes accessed | tf_op | source)
XLA Modules:
  0.0 613.7 jit_solution(17642059721249857733)
XLA Ops:
  3.3 3.0 collective-permute-start.6
  6.4 1.5 collective-permute-start.4
  11.2 1.6 collective-permute-start.1
  12.8 2.7 collective-permute-done.6.rest_4_
  15.5 1.8 collective-permute-start.8
  17.3 1.8 multiply_sine_fusion
  19.1 5.0 collective-permute-done.1
  24.2 3.5 collective-permute-done.2
  28.2 2.8 collective-permute-done.8.rest_6_
  32.2 1.7 collective-permute-start.18
  34.9 8.4 %project_qkv.1 = (bf16[512,2048]{1,0:T(8,128)(2,1)}, bf16[512,512]{1,0:T(8,128)(2,1)}, bf16[512,256]{1,0:T(8,128)(2,1)}) custom-call(bf16[512,2048]{1,0:T(8,128)(2,1)} %bitcast.39, f32[1,2048]{1,0:T(1,128)} %bitcast.50, f32[512,128]{1,0:T(8,128)} %get-tuple-element.184.cosine, f32[512,128]{1,0:T(8,128)} %get-tuple-element.183.sine, ...), custom_call_target="tpu_custom_call" | custom-call | flops 1610612736 | bytes 7340032 | tf_op jit(solution)/shard_map/project_qkv/pallas_call | solution.py:211
  43.4 1.6 collective-permute-start.11
  45.0 1.4 collective-permute-done.18.rest_6_
  46.8 5.0 collective-permute-done.11.rest_2_
  51.8 1.5 collective-permute-start.23
  56.8 2.2 fusion.19
  59.6 1.5 collective-permute-start.30
  61.8 10.9 %collective-permute-done.21.refs_2_ = bf16[256,2048]{1,0:T(8,128)(2,1)} collective-permute-done((bf16[256,2048]{1,0:T(8,128)(2,1)}, bf16[256,2048]{1,0:T(8,128)(2,1)}, u32[]{:S(2)}, u32[]{:S(2)}) %collective-permute-start.21) | collective-permute-done | bytes 1048608 | tf_op jit(solution)/shard_map/ppermute | solution.py:37
  72.8 1.5 collective-permute-start.29
  74.3 3.9 collective-permute-done.23.refs_5_
  78.2 1.5 collective-permute-start.26
  79.7 21.3 %attend.1 = (bf16[512,512]{1,0:T(8,128)(2,1)}, f32[4,2,512]{2,1,0:T(2,128)}) custom-call(s32[1,8]{1,0:T(1,128)} %order.3, bf16[512,512]{1,0:T(8,128)(2,1)} %get-tuple-element.74.query_ref, bf16[512,256]{1,0:T(8,128)(2,1)} %get-tuple-element.75.rest_0_, bf16[512,256]{1,0:T(8,128)(2,1)} %copy-done.41, bf16[512,256]{1,0:T(8,128)(2,1)} %copy-done.40, ...), custom_call_target="tpu_custom_call" | custom-call | flops 8589934592 | bytes 2097152 | tf_op jit(solution)/shard_map/attend/pallas_call | solution.py:558
  101.6 1.5 collective-permute-start.22
  104.2 4.9 shard_map.203.refs_0_
  109.2 61.8 %shard_map.204 = (bf16[512,2048]{1,0:T(8,128)(2,1)}, f32[256,2048]{1,0:T(8,128)}) custom-call(bf16[512,2048]{1,0:T(8,128)(2,1)} %shard_map.203.refs_0_, bf16[512,2048]{1,0:T(8,128)(2,1)} %bitcast.40, f32[1,2048]{1,0:T(1,128)} %bitcast.48), custom_call_target="tpu_custom_call" | custom-call | bytes 104857600 | tf_op jit(solution)/shard_map/pallas_call | solution.py:786
  171.5 1.5 collective-permute-start.31
  173.0 3.4 multiply_convert_fusion.d_ffn.refs_4_.refs_6_
  176.4 3.9 collective-permute-done.28.refs_11_
  182.3 44.4 %feed_forward.1 = (bf16[512,2048]{1,0:T(8,128)(2,1)}, bf16[512,2048]{1,0:T(8,128)(2,1)}, bf16[512,2048]{1,0:T(8,128)(2,1)}, bf16[512,2048]{1,0:T(8,128)(2,1)}, bf16[512,2048]{1,0:T(8,128)(2,1)}) custom-call(bf16[512,2048]{1,0:T(8,128)(2,1)} %get-tuple-element.77.normed.refs_0_.refs_2_, bf16[512,2048]{1,0:T(8,128)(2,1)} %multiply_convert_fusion.d_ffn.refs_4_.refs_6_, ...), custom_call_target="tpu_custom_call" | custom-call | flops 25769803776 | bytes 39845888 | tf_op jit(solution)/shard_map/feed_forward/pallas_call | solution.py:402
  226.7 3.0 fusion.18
  229.7 31.3 %shard_map.205 = (f32[256,2048]{1,0:T(8,128)}, f32[256,2048]{1,0:T(8,128)}, f32[256,1024]{1,0:T(8,128)}, f32[256,1024]{1,0:T(8,128)}, bf16[256,2048]{1,0:T(8,128...) custom-call(bf16[512,2048]{1,0:T(8,128)(2,1)} %get-tuple-element.77., ...), custom_call_target="tpu_custom_call" | custom-call | flops 12884901888 | bytes 25165824 | tf_op jit(solution)/shard_map/pallas_call | solution.py:921
  261.1 63.0 %shard_map.206 = (bf16[512,2048]{1,0:T(8,128)(2,1)}, f32[256,2048]{1,0:T(8,128)}, f32[8,2048]{1,0:T(8,128)}) custom-call(bf16[512,2048]{1,0:T(8,128)(2,1)} %get-tuple-element.96.refs_0_, f32[256,2048]{1,0:T(8,128)} %get-tuple-element.97.refs_1_, bf16[512,2048]{1,0:T(8,128)(2,1)} %bitcast.38, f32[1,2048]{1,0:T(1,128)} %bitcast.49), custom_call_target="tpu_custom_call" | custom-call | bytes 104857600 | tf_op jit(solution)/shard_map/pallas_call | solution.py:786
  324.1 5.1 shard_map.207.grad_ref
  329.2 35.5 %attend_back.1 = (f32[512,512]{1,0:T(8,128)}, f32[512,256]{1,0:T(8,128)}, bf16[512,256]{1,0:T(8,128)(2,1)}, f32[512,256]{1,0:T(8,128)}, bf16[512,256]{1,0:T(8,128)(2,1)}) custom-call(s32[1,8]{1,0:T(1,128)} %order.3, bf16[512,512]{1,0:T(8,128)(2,1)} %get-tuple-element.74.query_ref, bf16[512,512]{1,0:T(8,128)(2,1)} %shard_map.207.grad_ref, ...), custom_call_target="tpu_custom_call" | custom-call | flops 21474836480 | bytes 3145728 | tf_op jit(solution)/shard_map/attend_back/pallas_call | solution.py:633
  365.3 2.3 convert_multiply_fusion
  371.1 2.5 collective-permute-start.33
  373.6 1.4 collective-permute-start.34
  375.0 2.6 collective-permute-done.40
  378.5 6.8 %project_qkv_back.1 = (bf16[512,768]{1,0:T(8,128)(2,1)}, bf16[512,2048]{1,0:T(8,128)(2,1)}) custom-call(f32[512,512]{1,0:T(8,128)} %get-tuple-element.101.d_queries, f32[512,256]{1,0:T(8,128)} %convert_add_fusion.3.d_keys_values, f32[512,128]{1,0:T(8,128)} %get-tuple-element.184.cosine, f32[512,128]{1,0:T(8,128)} %get-tuple-element.183.sine, ...), custom_call_target="tpu_custom_call" | custom-call | flops 1610612736 | bytes 7340032 | tf_op jit(solution)/shard_map/project_qkv_back/pallas_call | solution.py:268
  385.3 10.7 %shard_map.208 = (f32[256,768]{1,0:T(8,128)}, f32[256,512]{1,0:T(8,128)}, bf16[256,768]{1,0:T(8,128)(2,1)}, bf16[256,512]{1,0:T(8,128)(2,1)}, bf16[256,768]{1,0:...) custom-call(bf16[512,2048]{1,0:T(8,128)(2,1)} %get-tuple-element.107.refs_0_, ...), custom_call_target="tpu_custom_call" | custom-call | flops 2684354560 | bytes 5242880 | tf_op jit(solution)/shard_map/pallas_call | solution.py:921
  396.0 75.9 %shard_map.209 = (bf16[512,2048]{1,0:T(8,128)(2,1)}, f32[8,2048]{1,0:T(8,128)}) custom-call(bf16[512,2048]{1,0:T(8,128)(2,1)} %get-tuple-element.110.refs_0_, bf16[512,2048]{1,0:T(8,128)(2,1)} %bitcast.41, f32[256,2048]{1,0:T(8,128)} %get-tuple-element.111.refs_2_, f32[1,2048]{1,0:T(1,128)} %bitcast.51), custom_call_target="tpu_custom_call" | custom-call | bytes 104857600 | tf_op jit(solution)/shard_map/pallas_call | solution.py:786
  472.9 1.6 collective-permute-start.53
  474.4 2.2 collective-permute-done.59
  476.6 1.5 collective-permute-start.55
  480.7 2.8 bitcast_dynamic-update-slice_fusion.3
  483.5 1.4 collective-permute-done.60
  485.6 2.3 collective-permute-done.53
  490.3 2.9 collective-permute-done.57
  494.5 9.3 %collective-permute-done.62 = f32[2,2048]{1,0:T(2,128)S(1)} collective-permute-done((f32[2,2048]{1,0:T(2,128)S(1)}, f32[2,2048]{1,0:T(2,128)S(1)}, u32[]{:S(2)}, u32[]{:S(2)}) %collective-permute-start.62) | collective-permute-done | bytes 16416 | tf_op jit(solution)/shard_map/ppermute | solution.py:37
  504.4 2.5 bitcast_convert_fusion
  511.0 8.1 %collective-permute-done.41 = bf16[256,768]{1,0:T(8,128)(2,1)S(1)} collective-permute-done((bf16[256,768]{1,0:T(8,128)(2,1)S(1)}, bf16[256,768]{1,0:T(8,128)(2,1)S(1)}, u32[]{:S(2)}, u32[]{:S(2)}) %collective-permute-start.41) | collective-permute-done | bytes 393248 | tf_op jit(solution)/shard_map/ppermute | solution.py:37
  521.6 18.7 %collective-permute-done.54 = bf16[256,1024]{1,0:T(8,128)(2,1)S(1)} collective-permute-done((bf16[256,1024]{1,0:T(8,128)(2,1)S(1)}, bf16[256,1024]{1,0:T(8,128)(2,1)S(1)}, u32[]{:S(2)}, u32[]{:S(2)}) %collective-permute-start.54) | collective-permute-done | bytes 524320 | tf_op jit(solution)/shard_map/ppermute | solution.py:37
  541.1 1.6 collective-permute-start.49
  543.9 11.2 %collective-permute-done.58 = bf16[256,1024]{1,0:T(8,128)(2,1)S(1)} collective-permute-done((bf16[256,1024]{1,0:T(8,128)(2,1)S(1)}, bf16[256,1024]{1,0:T(8,128)(2,1)S(1)}, u32[]{:S(2)}, u32[]{:S(2)}) %collective-permute-start.58) | collective-permute-done | bytes 524320 | tf_op jit(solution)/shard_map/ppermute | solution.py:37
  556.6 1.8 copy.36
  559.0 1.9 bitcast_dynamic-update-slice_fusion
  560.8 1.5 collective-permute-start.46
  562.3 1.6 add_convert_fusion.1
  566.6 1.6 add_convert_fusion
  568.2 17.8 %collective-permute-done.46 = bf16[256,512]{1,0:T(8,128)(2,1)S(1)} collective-permute-done((bf16[256,512]{1,0:T(8,128)(2,1)}, bf16[256,512]{1,0:T(8,128)(2,1)S(1)}, u32[]{:S(2)}, u32[]{:S(2)}) %collective-permute-start.46) | collective-permute-done | bytes 262176 | tf_op jit(solution)/shard_map/ppermute | solution.py:37
  589.8 1.3 convert_add_fusion.2
  593.3 3.3 convert_add_fusion.1
  596.6 13.9 %collective-permute-done.50 = bf16[256,2048]{1,0:T(8,128)(2,1)} collective-permute-done((bf16[256,2048]{1,0:T(8,128)(2,1)}, bf16[256,2048]{1,0:T(8,128)(2,1)}, u32[]{:S(2)}, u32[]{:S(2)}) %collective-permute-start.50) | collective-permute-done | bytes 1048608 | tf_op jit(solution)/shard_map/ppermute | solution.py:37
  610.5 3.0 convert_add_fusion
  (226 shorter events, 50.8 us)
Async XLA Ops:
  3.3 12.1 %collective-permute-start.6 = (bf16[256,768]{1,0:T(8,128)(2,1)S(1)}, bf16[256,768]{1,0:T(8,128)(2,1)S(1)}, u32[]{:S(2)}, u32[]{:S(2)}) collective-permute-start(bf16[256,768]{1,0:T(8,128)(2,1)S(1)} %constant_dynamic-update-slice_fusion.rest_0_), channel_id=1, source_target_pairs={{0,16},{4,20},{8,24},{12,28},{16,0},{20,4},{24,8},{28,12},{1,17},{... | collective-permute-start | bytes 1179656 | tf_op jit(solution)/shard_map/ppermute | solution.py:37
  6.4 21.3 %collective-permute-start.4 = (bf16[256,768]{1,0:T(8,128)(2,1)S(1)}, bf16[256,768]{1,0:T(8,128)(2,1)S(1)}, u32[]{:S(2)}, u32[]{:S(2)}) collective-permute-start(bf16[256,768]{1,0:T(8,128)(2,1)S(1)} %constant_dynamic-update-slice_fusion.rest_0_), channel_id=1, source_target_pairs={{0,8},{4,12},{8,0},{12,4},{16,24},{20,28},{24,16},{28,20},{1,9},{5... | collective-permute-start | bytes 1179656 | tf_op jit(solution)/shard_map/ppermute | solution.py:37
  7.9 24.3 %collective-permute-start.3 = (bf16[256,768]{1,0:T(8,128)(2,1)S(1)}, bf16[256,768]{1,0:T(8,128)(2,1)S(1)}, u32[]{:S(2)}, u32[]{:S(2)}) collective-permute-start(bf16[256,768]{1,0:T(8,128)(2,1)S(1)} %constant_dynamic-update-slice_fusion.rest_0_), channel_id=1, source_target_pairs={{0,4},{4,0},{8,12},{12,8},{16,20},{20,16},{24,28},{28,24},{1,5},{5... | collective-permute-start | bytes 1179656 | tf_op jit(solution)/shard_map/ppermute | solution.py:37
  9.2 2.0 collective-permute-start
  9.8 22.0 %collective-permute-start.14 = (bf16[512,256]{1,0:T(8,128)(2,1)}, bf16[512,256]{1,0:T(8,128)(2,1)S(1)}, u32[]{:S(2)}, u32[]{:S(2)}) collective-permute-start(bf16[512,256]{1,0:T(8,128)(2,1)} %rest_0_.3), channel_id=1, source_target_pairs={{0,8},{4,12},{8,0},{12,4},{16,24},{20,28},{24,16},{28,20},{1,9},{5... | collective-permute-start | bytes 786440 | tf_op jit(solution)/shard_map/ppermute | solution.py:37
  11.2 12.8 %collective-permute-start.1 = (bf16[2,2,256]{2,0,1:T(2,128)(2,1)S(1)}, bf16[2,2,256]{2,0,1:T(2,128)(2,1)S(1)}, u32[]{:S(2)}, u32[]{:S(2)}) collective-permute-start(bf16[2,2,256]{2,0,1:T(2,128)(2,1)S(1)} %pad_maximum_fusion.3), channel_id=1, source_target_pairs={{0,8},{4,12},{8,0},{12,4},{16,24},{20,28},{24,16},{28,20},{1,9},{5... | collective-permute-start | bytes 6152 | tf_op jit(solution)/shard_map/ppermute | solution.py:37
  15.5 15.5 %collective-permute-start.8 = (bf16[256,768]{1,0:T(8,128)(2,1)S(1)}, bf16[256,768]{1,0:T(8,128)(2,1)S(1)}, u32[]{:S(2)}, u32[]{:S(2)}) collective-permute-start(bf16[256,768]{1,0:T(8,128)(2,1)S(1)} %collective-permute-done.6.rest_4_), channel_id=1, source_target_pairs={{0,8},{4,12},{8,0},{12,4},{16,24},{20,28},{24,16},{28,20},{1,9},{5... | collective-permute-start | bytes 1179656 | tf_op jit(solution)/shard_map/ppermute | solution.py:37
  24.0 3.7 collective-permute-start.2
  27.7 6.2 %collective-permute-start.7 = (bf16[256,768]{1,0:T(8,128)(2,1)S(1)}, bf16[256,768]{1,0:T(8,128)(2,1)S(1)}, u32[]{:S(2)}, u32[]{:S(2)}) collective-permute-start(bf16[256,768]{1,0:T(8,128)(2,1)S(1)} %collective-permute-done.6.rest_4_), channel_id=1, source_target_pairs={{0,4},{4,0},{8,12},{12,8},{16,20},{20,16},{24,28},{28,24},{1,5},{5... | collective-permute-start | bytes 1179656 | tf_op jit(solution)/shard_map/ppermute | solution.py:37
  27.7 6.2 %collective-permute-start.5 = (bf16[256,768]{1,0:T(8,128)(2,1)S(1)}, bf16[256,768]{1,0:T(8,128)(2,1)S(1)}, u32[]{:S(2)}, u32[]{:S(2)}) collective-permute-start(bf16[256,768]{1,0:T(8,128)(2,1)S(1)} %collective-permute-done.4.rest_2_), channel_id=1, source_target_pairs={{0,4},{4,0},{8,12},{12,8},{16,20},{20,16},{24,28},{28,24},{1,5},{5... | collective-permute-start | bytes 1179656 | tf_op jit(solution)/shard_map/ppermute | solution.py:37
  31.0 2.9 collective-permute-start.9
  31.9 13.1 %collective-permute-start.16 = (bf16[512,256]{1,0:T(8,128)(2,1)}, bf16[512,256]{1,0:T(8,128)(2,1)S(1)}, u32[]{:S(2)}, u32[]{:S(2)}) collective-permute-start(bf16[512,256]{1,0:T(8,128)(2,1)} %rest_0_.3), channel_id=1, source_target_pairs={{0,16},{4,20},{8,24},{12,28},{16,0},{20,4},{24,8},{28,12},{1,17},{... | collective-permute-start | bytes 786440 | tf_op jit(solution)/shard_map/ppermute | solution.py:37
  32.2 14.2 %collective-permute-start.18 = (bf16[512,256]{1,0:T(8,128)(2,1)S(1)}, bf16[512,256]{1,0:T(8,128)(2,1)S(1)}, u32[]{:S(2)}, u32[]{:S(2)}) collective-permute-start(bf16[512,256]{1,0:T(8,128)(2,1)S(1)} %collective-permute-done.14.rest_2_), channel_id=1, source_target_pairs={{0,16},{4,20},{8,24},{12,28},{16,0},{20,4},{24,8},{28,12},{1,17},{... | collective-permute-start | bytes 786440 | tf_op jit(solution)/shard_map/ppermute | solution.py:37
  43.4 8.4 %collective-permute-start.11 = (bf16[512,256]{1,0:T(8,128)(2,1)}, bf16[512,256]{1,0:T(8,128)(2,1)S(1)}, u32[]{:S(2)}, u32[]{:S(2)}) collective-permute-start(bf16[512,256]{1,0:T(8,128)(2,1)} %get-tuple-element.75.rest_0_), channel_id=1, source_target_pairs={{0,8},{4,12},{8,0},{12,4},{1,9},{5,13},{9,1},{13,5},{2,10},{6,14},... | collective-permute-start | bytes 786440 | tf_op jit(solution)/shard_map/ppermute | solution.py:37
  46.4 26.3 %collective-permute-start.21 = (bf16[256,2048]{1,0:T(8,128)(2,1)}, bf16[256,2048]{1,0:T(8,128)(2,1)}, u32[]{:S(2)}, u32[]{:S(2)}) collective-permute-start(bf16[256,2048]{1,0:T(8,128)(2,1)} %refs_0_.1), channel_id=1, source_target_pairs={{0,16},{4,20},{8,24},{12,28},{16,0},{20,4},{24,8},{28,12},{1,17},{... | collective-permute-start | bytes 3145736 | tf_op jit(solution)/shard_map/ppermute | solution.py:37
  51.8 26.3 %collective-permute-start.23 = (bf16[256,2048]{1,0:T(8,128)(2,1)}, bf16[256,2048]{1,0:T(8,128)(2,1)}, u32[]{:S(2)}, u32[]{:S(2)}) collective-permute-start(bf16[256,2048]{1,0:T(8,128)(2,1)} %refs_4_.1), channel_id=1, source_target_pairs={{0,8},{4,12},{8,0},{12,4},{16,24},{20,28},{24,16},{28,20},{1,9},{5... | collective-permute-start | bytes 3145736 | tf_op jit(solution)/shard_map/ppermute | solution.py:37
  53.3 1.5 collective-permute-start.13
  53.3 1.9 collective-permute-start.17
  53.8 1.8 collective-permute-start.15
  54.9 4.1 collective-permute-start.19
  55.2 4.4 collective-permute-start.10
  56.6 4.5 collective-permute-start.12
  59.0 42.0 %collective-permute-start.27 = (bf16[2048,128]{1,0:T(8,128)(2,1)}, bf16[2048,128]{1,0:T(8,128)(2,1)}, u32[]{:S(2)}, u32[]{:S(2)}) collective-permute-start(bf16[2048,128]{1,0:T(8,128)(2,1)} %get-tuple-element.85.refs_8_), channel_id=1, source_target_pairs={{0,16},{4,20},{8,24},{12,28},{16,0},{20,4},{24,8},{28,12},{1,17},{... | collective-permute-start | bytes 1572872 | tf_op jit(solution)/shard_map/ppermute | solution.py:37
  59.6 41.9 %collective-permute-start.30 = (bf16[2048,128]{1,0:T(8,128)(2,1)}, bf16[2048,128]{1,0:T(8,128)(2,1)}, u32[]{:S(2)}, u32[]{:S(2)}) collective-permute-start(bf16[2048,128]{1,0:T(8,128)(2,1)} %get-tuple-element.88.refs_12_), channel_id=1, source_target_pairs={{0,16},{4,20},{8,24},{12,28},{16,0},{20,4},{24,8},{28,12},{1,17},{... | collective-permute-start | bytes 1572872 | tf_op jit(solution)/shard_map/ppermute | solution.py:37
  61.1 109.8 %collective-permute-start.24 = (bf16[256,2048]{1,0:T(8,128)(2,1)}, bf16[256,2048]{1,0:T(8,128)(2,1)}, u32[]{:S(2)}, u32[]{:S(2)}) collective-permute-start(bf16[256,2048]{1,0:T(8,128)(2,1)} %refs_4_.1), channel_id=1, source_target_pairs={{0,16},{4,20},{8,24},{12,28},{16,0},{20,4},{24,8},{28,12},{1,17},{... | collective-permute-start | bytes 3145736 | tf_op jit(solution)/shard_map/ppermute | solution.py:37
  72.8 30.3 %collective-permute-start.29 = (bf16[2048,128]{1,0:T(8,128)(2,1)}, bf16[2048,128]{1,0:T(8,128)(2,1)}, u32[]{:S(2)}, u32[]{:S(2)}) collective-permute-start(bf16[2048,128]{1,0:T(8,128)(2,1)} %get-tuple-element.88.refs_12_), channel_id=1, source_target_pairs={{0,8},{4,12},{8,0},{12,4},{16,24},{20,28},{24,16},{28,20},{1,9},{5... | collective-permute-start | bytes 1572872 | tf_op jit(solution)/shard_map/ppermute | solution.py:37
  78.2 93.4 %collective-permute-start.26 = (bf16[2048,128]{1,0:T(8,128)(2,1)}, bf16[2048,128]{1,0:T(8,128)(2,1)}, u32[]{:S(2)}, u32[]{:S(2)}) collective-permute-start(bf16[2048,128]{1,0:T(8,128)(2,1)} %get-tuple-element.85.refs_8_), channel_id=1, source_target_pairs={{0,8},{4,12},{8,0},{12,4},{16,24},{20,28},{24,16},{28,20},{1,9},{5... | collective-permute-start | bytes 1572872 | tf_op jit(solution)/shard_map/ppermute | solution.py:37
  101.0 79.4 %collective-permute-start.20 = (bf16[256,2048]{1,0:T(8,128)(2,1)}, bf16[256,2048]{1,0:T(8,128)(2,1)S(1)}, u32[]{:S(2)}, u32[]{:S(2)}) collective-permute-start(bf16[256,2048]{1,0:T(8,128)(2,1)} %refs_0_.1), channel_id=1, source_target_pairs={{0,8},{4,12},{8,0},{12,4},{16,24},{20,28},{24,16},{28,20},{1,9},{5... | collective-permute-start | bytes 3145736 | tf_op jit(solution)/shard_map/ppermute | solution.py:37
  101.6 80.5 %collective-permute-start.22 = (bf16[256,2048]{1,0:T(8,128)(2,1)}, bf16[256,2048]{1,0:T(8,128)(2,1)}, u32[]{:S(2)}, u32[]{:S(2)}) collective-permute-start(bf16[256,2048]{1,0:T(8,128)(2,1)} %collective-permute-done.21.refs_2_), channel_id=1, source_target_pairs={{0,8},{4,12},{8,0},{12,4},{16,24},{20,28},{24,16},{28,20},{1,9},{5... | collective-permute-start | bytes 3145736 | tf_op jit(solution)/shard_map/ppermute | solution.py:37
  103.1 79.0 %collective-permute-start.25 = (bf16[256,2048]{1,0:T(8,128)(2,1)}, bf16[256,2048]{1,0:T(8,128)(2,1)}, u32[]{:S(2)}, u32[]{:S(2)}) collective-permute-start(bf16[256,2048]{1,0:T(8,128)(2,1)} %collective-permute-done.23.refs_5_), channel_id=1, source_target_pairs={{0,16},{4,20},{8,24},{12,28},{16,0},{20,4},{24,8},{28,12},{1,17},{... | collective-permute-start | bytes 3145736 | tf_op jit(solution)/shard_map/ppermute | solution.py:37
  170.9 9.5 %collective-permute-start.28 = (bf16[2048,128]{1,0:T(8,128)(2,1)}, bf16[2048,128]{1,0:T(8,128)(2,1)S(1)}, u32[]{:S(2)}, u32[]{:S(2)}) collective-permute-start(bf16[2048,128]{1,0:T(8,128)(2,1)} %collective-permute-done.27.refs_10_), channel_id=1, source_target_pairs={{0,8},{4,12},{8,0},{12,4},{16,24},{20,28},{24,16},{28,20},{1,9},{5... | collective-permute-start | bytes 1572872 | tf_op jit(solution)/shard_map/ppermute | solution.py:37
  171.5 9.7 %collective-permute-start.31 = (bf16[2048,128]{1,0:T(8,128)(2,1)}, bf16[2048,128]{1,0:T(8,128)(2,1)S(1)}, u32[]{:S(2)}, u32[]{:S(2)}) collective-permute-start(bf16[2048,128]{1,0:T(8,128)(2,1)} %collective-permute-done.29.refs_13_), channel_id=1, source_target_pairs={{0,16},{4,20},{8,24},{12,28},{16,0},{20,4},{24,8},{28,12},{1,17},{... | collective-permute-start | bytes 1572872 | tf_op jit(solution)/shard_map/ppermute | solution.py:37
  364.7 3.7 collective-permute-start.39
  364.8 10.2 %collective-permute-start.38 = (bf16[512,256]{1,0:T(8,128)(2,1)}, bf16[512,256]{1,0:T(8,128)(2,1)S(1)}, u32[]{:S(2)}, u32[]{:S(2)}) collective-permute-start(bf16[512,256]{1,0:T(8,128)(2,1)} %get-tuple-element.103), channel_id=1, source_target_pairs={{0,4},{4,0},{8,12},{12,8},{1,5},{5,1},{9,13},{13,9},{2,6},{6,2},{1... | collective-permute-start | bytes 786440 | tf_op jit(solution)/shard_map/ppermute | solution.py:37
  369.2 8.4 %collective-permute-start.40 = (bf16[512,256]{1,0:T(8,128)(2,1)S(1)}, bf16[512,256]{1,0:T(8,128)(2,1)S(1)}, u32[]{:S(2)}, u32[]{:S(2)}) collective-permute-start(bf16[512,256]{1,0:T(8,128)(2,1)S(1)} %add_convert_fusion.7), channel_id=1, source_target_pairs={{0,8},{4,12},{8,0},{12,4},{1,9},{5,13},{9,1},{13,5},{2,10},{6,14},... | collective-permute-start | bytes 786440 | tf_op jit(solution)/shard_map/ppermute | solution.py:37
  371.1 107.0 %collective-permute-start.32 = (bf16[128,2048]{1,0:T(8,128)(2,1)}, bf16[128,2048]{1,0:T(8,128)(2,1)}, u32[]{:S(2)}, u32[]{:S(2)}) collective-permute-start(bf16[128,2048]{1,0:T(8,128)(2,1)} %get-tuple-element.172), channel_id=1, source_target_pairs={{0,1},{1,2},{2,3},{3,0},{4,5},{5,6},{6,7},{7,4},{8,9},{9,10},{10,1... | collective-permute-start | bytes 1572872 | tf_op jit(solution)/shard_map/ppermute | solution.py:127
  371.1 108.1 %collective-permute-start.33 = (bf16[128,2048]{1,0:T(8,128)(2,1)S(1)}, bf16[128,2048]{1,0:T(8,128)(2,1)}, u32[]{:S(2)}, u32[]{:S(2)}) collective-permute-start(bf16[128,2048]{1,0:T(8,128)(2,1)S(1)} %get-tuple-element.174), channel_id=1, source_target_pairs={{0,2},{1,3},{2,0},{3,1},{4,6},{5,7},{6,4},{7,5},{8,10},{9,11},{10,... | collective-permute-start | bytes 1572872 | tf_op jit(solution)/shard_map/ppermute | solution.py:127
  373.6 106.6 %collective-permute-start.34 = (bf16[128,2048]{1,0:T(8,128)(2,1)S(1)}, bf16[128,2048]{1,0:T(8,128)(2,1)}, u32[]{:S(2)}, u32[]{:S(2)}) collective-permute-start(bf16[128,2048]{1,0:T(8,128)(2,1)S(1)} %get-tuple-element.173), channel_id=1, source_target_pairs={{0,3},{1,0},{2,1},{3,2},{4,7},{5,4},{6,5},{7,6},{8,11},{9,8},{10,9... | collective-permute-start | bytes 1572872 | tf_op jit(solution)/shard_map/ppermute | solution.py:127
  472.8 3.8 collective-permute-start.59
  472.9 15.1 %collective-permute-start.53 = (bf16[256,1024]{1,0:T(8,128)(2,1)}, bf16[256,1024]{1,0:T(8,128)(2,1)S(1)}, u32[]{:S(2)}, u32[]{:S(2)}) collective-permute-start(bf16[256,1024]{1,0:T(8,128)(2,1)} %get-tuple-element.129), channel_id=1, source_target_pairs={{0,16},{4,20},{8,24},{12,28},{16,0},{20,4},{24,8},{28,12},{1,17},{... | collective-permute-start | bytes 1572872 | tf_op jit(solution)/shard_map/ppermute | solution.py:37
  476.6 44.5 %collective-permute-start.55 = (bf16[256,1024]{1,0:T(8,128)(2,1)}, bf16[256,1024]{1,0:T(8,128)(2,1)S(1)}, u32[]{:S(2)}, u32[]{:S(2)}) collective-permute-start(bf16[256,1024]{1,0:T(8,128)(2,1)} %get-tuple-element.130), channel_id=1, source_target_pairs={{0,16},{4,20},{8,24},{12,28},{16,0},{20,4},{24,8},{28,12},{1,17},{... | collective-permute-start | bytes 1572872 | tf_op jit(solution)/shard_map/ppermute | solution.py:37
  478.1 15.1 %collective-permute-start.57 = (bf16[256,1024]{1,0:T(8,128)(2,1)}, bf16[256,1024]{1,0:T(8,128)(2,1)S(1)}, u32[]{:S(2)}, u32[]{:S(2)}) collective-permute-start(bf16[256,1024]{1,0:T(8,128)(2,1)} %get-tuple-element.134), channel_id=1, source_target_pairs={{0,8},{4,12},{8,0},{12,4},{16,24},{20,28},{24,16},{28,20},{1,9},{5... | collective-permute-start | bytes 1572872 | tf_op jit(solution)/shard_map/ppermute | solution.py:37
  479.3 63.5 %collective-permute-start.56 = (bf16[256,1024]{1,0:T(8,128)(2,1)}, bf16[256,1024]{1,0:T(8,128)(2,1)S(1)}, u32[]{:S(2)}, u32[]{:S(2)}) collective-permute-start(bf16[256,1024]{1,0:T(8,128)(2,1)} %get-tuple-element.132), channel_id=1, source_target_pairs={{0,8},{4,12},{8,0},{12,4},{16,24},{20,28},{24,16},{28,20},{1,9},{5... | collective-permute-start | bytes 1572872 | tf_op jit(solution)/shard_map/ppermute | solution.py:37
  480.2 4.6 collective-permute-start.60
  484.9 36.2 %collective-permute-start.35 = (bf16[128,2048]{1,0:T(8,128)(2,1)}, bf16[128,2048]{1,0:T(8,128)(2,1)S(1)}, u32[]{:S(2)}, u32[]{:S(2)}) collective-permute-start(bf16[128,2048]{1,0:T(8,128)(2,1)} %get-tuple-element.171), channel_id=1, source_target_pairs={{0,1},{1,2},{2,3},{3,0},{4,5},{5,6},{6,7},{7,4},{8,9},{9,10},{10,1... | collective-permute-start | bytes 1572872 | tf_op jit(solution)/shard_map/ppermute | solution.py:138
  488.0 1.2 collective-permute-start.61
  489.2 14.7 %collective-permute-start.62 = (f32[2,2048]{1,0:T(2,128)S(1)}, f32[2,2048]{1,0:T(2,128)S(1)}, u32[]{:S(2)}, u32[]{:S(2)}) collective-permute-start(f32[2,2048]{1,0:T(2,128)S(1)} %add.221), channel_id=1, source_target_pairs={{0,8},{1,9},{2,10},{3,11},{4,12},{5,13},{6,14},{7,15},{8,0},{9,1},... | collective-permute-start | bytes 49160 | tf_op jit(solution)/shard_map/ppermute | solution.py:37
  493.4 15.7 %collective-permute-start.45 = (bf16[256,512]{1,0:T(8,128)(2,1)S(1)}, bf16[256,512]{1,0:T(8,128)(2,1)S(1)}, u32[]{:S(2)}, u32[]{:S(2)}) collective-permute-start(bf16[256,512]{1,0:T(8,128)(2,1)S(1)} %copy-done.43), channel_id=1, source_target_pairs={{0,8},{4,12},{8,0},{12,4},{16,24},{20,28},{24,16},{28,20},{1,9},{5... | collective-permute-start | bytes 786440 | tf_op jit(solution)/shard_map/ppermute | solution.py:37
  503.8 3.8 collective-permute-start.63
  507.6 11.4 %collective-permute-start.41 = (bf16[256,768]{1,0:T(8,128)(2,1)S(1)}, bf16[256,768]{1,0:T(8,128)(2,1)S(1)}, u32[]{:S(2)}, u32[]{:S(2)}) collective-permute-start(bf16[256,768]{1,0:T(8,128)(2,1)S(1)} %copy-done.39), channel_id=1, source_target_pairs={{0,16},{4,20},{8,24},{12,28},{16,0},{20,4},{24,8},{28,12},{1,17},{... | collective-permute-start | bytes 1179656 | tf_op jit(solution)/shard_map/ppermute | solution.py:37
  509.1 56.5 %collective-permute-start.51 = (bf16[256,2048]{1,0:T(8,128)(2,1)}, bf16[256,2048]{1,0:T(8,128)(2,1)}, u32[]{:S(2)}, u32[]{:S(2)}) collective-permute-start(bf16[256,2048]{1,0:T(8,128)(2,1)} %get-tuple-element.126), channel_id=1, source_target_pairs={{0,8},{4,12},{8,0},{12,4},{16,24},{20,28},{24,16},{28,20},{1,9},{5... | collective-permute-start | bytes 3145736 | tf_op jit(solution)/shard_map/ppermute | solution.py:37
  519.0 21.3 %collective-permute-start.54 = (bf16[256,1024]{1,0:T(8,128)(2,1)S(1)}, bf16[256,1024]{1,0:T(8,128)(2,1)S(1)}, u32[]{:S(2)}, u32[]{:S(2)}) collective-permute-start(bf16[256,1024]{1,0:T(8,128)(2,1)S(1)} %add_convert_fusion.3), channel_id=1, source_target_pairs={{0,8},{4,12},{8,0},{12,4},{16,24},{20,28},{24,16},{28,20},{1,9},{5... | collective-permute-start | bytes 1572872 | tf_op jit(solution)/shard_map/ppermute | solution.py:37
  521.0 20.1 %collective-permute-start.36 = (bf16[128,2048]{1,0:T(8,128)(2,1)}, bf16[128,2048]{1,0:T(8,128)(2,1)S(1)}, u32[]{:S(2)}, u32[]{:S(2)}) collective-permute-start(bf16[128,2048]{1,0:T(8,128)(2,1)} %get-tuple-element.171), channel_id=1, source_target_pairs={{0,2},{1,3},{2,0},{3,1},{4,6},{5,7},{6,4},{7,5},{8,10},{9,11},{10,... | collective-permute-start | bytes 1572872 | tf_op jit(solution)/shard_map/ppermute | solution.py:138
  521.1 39.7 %collective-permute-start.47 = (bf16[256,2048]{1,0:T(8,128)(2,1)}, bf16[256,2048]{1,0:T(8,128)(2,1)}, u32[]{:S(2)}, u32[]{:S(2)}) collective-permute-start(bf16[256,2048]{1,0:T(8,128)(2,1)} %get-tuple-element.121), channel_id=1, source_target_pairs={{0,16},{4,20},{8,24},{12,28},{16,0},{20,4},{24,8},{28,12},{1,17},{... | collective-permute-start | bytes 3145736 | tf_op jit(solution)/shard_map/ppermute | solution.py:37
  540.3 14.8 %collective-permute-start.58 = (bf16[256,1024]{1,0:T(8,128)(2,1)S(1)}, bf16[256,1024]{1,0:T(8,128)(2,1)S(1)}, u32[]{:S(2)}, u32[]{:S(2)}) collective-permute-start(bf16[256,1024]{1,0:T(8,128)(2,1)S(1)} %add_convert_fusion.2), channel_id=1, source_target_pairs={{0,16},{4,20},{8,24},{12,28},{16,0},{20,4},{24,8},{28,12},{1,17},{... | collective-permute-start | bytes 1572872 | tf_op jit(solution)/shard_map/ppermute | solution.py:37
  541.1 51.5 %collective-permute-start.49 = (bf16[256,2048]{1,0:T(8,128)(2,1)}, bf16[256,2048]{1,0:T(8,128)(2,1)}, u32[]{:S(2)}, u32[]{:S(2)}) collective-permute-start(bf16[256,2048]{1,0:T(8,128)(2,1)} %get-tuple-element.122), channel_id=1, source_target_pairs={{0,16},{4,20},{8,24},{12,28},{16,0},{20,4},{24,8},{28,12},{1,17},{... | collective-permute-start | bytes 3145736 | tf_op jit(solution)/shard_map/ppermute | solution.py:37
  542.8 15.7 %collective-permute-start.37 = (bf16[128,2048]{1,0:T(8,128)(2,1)}, bf16[128,2048]{1,0:T(8,128)(2,1)}, u32[]{:S(2)}, u32[]{:S(2)}) collective-permute-start(bf16[128,2048]{1,0:T(8,128)(2,1)} %get-tuple-element.171), channel_id=1, source_target_pairs={{0,3},{1,0},{2,1},{3,2},{4,7},{5,4},{6,5},{7,6},{8,11},{9,8},{10,9... | collective-permute-start | bytes 1572872 | tf_op jit(solution)/shard_map/ppermute | solution.py:138
  555.1 9.4 %collective-permute-start.44 = (bf16[256,512]{1,0:T(8,128)(2,1)}, bf16[256,512]{1,0:T(8,128)(2,1)S(1)}, u32[]{:S(2)}, u32[]{:S(2)}) collective-permute-start(bf16[256,512]{1,0:T(8,128)(2,1)} %get-tuple-element.117), channel_id=1, source_target_pairs={{0,8},{4,12},{8,0},{12,4},{16,24},{20,28},{24,16},{28,20},{1,9},{5... | collective-permute-start | bytes 786440 | tf_op jit(solution)/shard_map/ppermute | solution.py:37
  558.4 30.8 %collective-permute-start.43 = (bf16[256,768]{1,0:T(8,128)(2,1)}, bf16[256,768]{1,0:T(8,128)(2,1)}, u32[]{:S(2)}, u32[]{:S(2)}) collective-permute-start(bf16[256,768]{1,0:T(8,128)(2,1)} %get-tuple-element.115), channel_id=1, source_target_pairs={{0,16},{4,20},{8,24},{12,28},{16,0},{20,4},{24,8},{28,12},{1,17},{... | collective-permute-start | bytes 1179656 | tf_op jit(solution)/shard_map/ppermute | solution.py:37
  560.8 25.2 %collective-permute-start.46 = (bf16[256,512]{1,0:T(8,128)(2,1)}, bf16[256,512]{1,0:T(8,128)(2,1)S(1)}, u32[]{:S(2)}, u32[]{:S(2)}) collective-permute-start(bf16[256,512]{1,0:T(8,128)(2,1)} %add_convert_fusion.6), channel_id=1, source_target_pairs={{0,16},{4,20},{8,24},{12,28},{16,0},{20,4},{24,8},{28,12},{1,17},{... | collective-permute-start | bytes 786440 | tf_op jit(solution)/shard_map/ppermute | solution.py:37
  564.5 25.2 %collective-permute-start.42 = (bf16[256,768]{1,0:T(8,128)(2,1)}, bf16[256,768]{1,0:T(8,128)(2,1)}, u32[]{:S(2)}, u32[]{:S(2)}) collective-permute-start(bf16[256,768]{1,0:T(8,128)(2,1)} %add_convert_fusion.5), channel_id=1, source_target_pairs={{0,8},{4,12},{8,0},{12,4},{16,24},{20,28},{24,16},{28,20},{1,9},{5... | collective-permute-start | bytes 1179656 | tf_op jit(solution)/shard_map/ppermute | solution.py:37
  565.6 27.7 %collective-permute-start.48 = (bf16[256,2048]{1,0:T(8,128)(2,1)S(1)}, bf16[256,2048]{1,0:T(8,128)(2,1)}, u32[]{:S(2)}, u32[]{:S(2)}) collective-permute-start(bf16[256,2048]{1,0:T(8,128)(2,1)S(1)} %add_convert_fusion.1), channel_id=1, source_target_pairs={{0,8},{4,12},{8,0},{12,4},{16,24},{20,28},{24,16},{28,20},{1,9},{5... | collective-permute-start | bytes 3145736 | tf_op jit(solution)/shard_map/ppermute | solution.py:37
  586.0 24.5 %collective-permute-start.50 = (bf16[256,2048]{1,0:T(8,128)(2,1)}, bf16[256,2048]{1,0:T(8,128)(2,1)}, u32[]{:S(2)}, u32[]{:S(2)}) collective-permute-start(bf16[256,2048]{1,0:T(8,128)(2,1)} %get-tuple-element.124), channel_id=1, source_target_pairs={{0,8},{4,12},{8,0},{12,4},{16,24},{20,28},{24,16},{28,20},{1,9},{5... | collective-permute-start | bytes 3145736 | tf_op jit(solution)/shard_map/ppermute | solution.py:37
  589.2 21.3 %collective-permute-start.52 = (bf16[256,2048]{1,0:T(8,128)(2,1)S(1)}, bf16[256,2048]{1,0:T(8,128)(2,1)S(1)}, u32[]{:S(2)}, u32[]{:S(2)}) collective-permute-start(bf16[256,2048]{1,0:T(8,128)(2,1)S(1)} %add_convert_fusion), channel_id=1, source_target_pairs={{0,16},{4,20},{8,24},{12,28},{16,0},{20,4},{24,8},{28,12},{1,17},{... | collective-permute-start | bytes 3145736 | tf_op jit(solution)/shard_map/ppermute | solution.py:37
  (44 other events, 574.8 us)

commit v2 on v1

--- a/solution.py
+++ b/solution.py
@@ -78,7 +78,7 @@
     return total if kept == 0 else total.astype(BF16)
 
 
-def reduce_pair(first, second):
+def reduce_pair(first, second, last_after=()):
     size = plane_size()
     bits = [1 << b for b in range(1, size.bit_length() - 1)]
     sides = [dict(first), dict(second)]
@@ -88,8 +88,9 @@
         sides[1][far] = take_sum(sides[1], near, far)
         done = []
         for side in sides:
-            a = swap(side[near].astype(BF16), PLANE, size, near).astype(F32)
-            b = swap(side[far].astype(BF16), PLANE, size, far).astype(F32)
+            sent = [after(side[bit].astype(BF16), *last_after) for bit in bits]
+            a = swap(sent[0], PLANE, size, near).astype(F32)
+            b = swap(sent[1], PLANE, size, far).astype(F32)
             done.append(side[0] + a + b)
         return done
     done = []
@@ -116,15 +117,12 @@
     return lax.dynamic_slice_in_dim(rows, index * count, count, 0)
 
 
-def rows_sum(partial):
+def rows_sum(chunks):
     size = lax.axis_size("tensor")
-    me = lax.axis_index("tensor")
-    count = partial.shape[0] // size
-    total = chunk_of(partial, me, count).astype(F32)
+    total = chunks[0].astype(F32)
     for shift in range(1, size):
-        sent = chunk_of(partial, lax.rem(me + shift, size), count)
         pairs = [(i, (i + shift) % size) for i in range(size)]
-        total = total + lax.ppermute(sent, "tensor", pairs).astype(F32)
+        total = total + lax.ppermute(chunks[shift], "tensor", pairs).astype(F32)
     return total
 
 
@@ -141,6 +139,19 @@
         place = lax.rem(me - shift + size, size) * count
         whole = lax.dynamic_update_slice_in_dim(whole, parts[shift], place, 0)
     return whole
+
+
+def gains_sum(values):
+    size, tensor, me = plane_size(), lax.axis_size("tensor"), plane_index()
+    extent = values.shape[1] // size
+    total = values
+    for shift in range(1, tensor):
+        total = total + lax.ppermute(values, "tensor", [(i, (i + shift) % tensor) for i in range(tensor)])
+    own = 0.0
+    for r in range(size):
+        sent = lax.dynamic_slice_in_dim(total, (me ^ r) * extent, extent, 1)
+        own = own + (swap(sent, PLANE, size, r) if r else sent)
+    return own
 
 
 def params(steps):
@@ -652,12 +663,18 @@
     return half, sub, half // sub
 
 
-def line_body(finish, keep_state, gain_sum, n_in, *refs):
+def line_body(finish, keep_state, gain_sum, n_in, extra, *refs):
     partial, ins, rest = refs[0], refs[1 : 1 + n_in], refs[1 + n_in :]
+    if extra:
+        world, n_grad, plan = extra
+        ffn_out, grad_ins, rest = rest[0], rest[1 : 1 + n_grad], rest[1 + n_grad :]
     result, rest = rest[0], rest[1:]
     state_out, rest = (rest[0], rest[1:]) if keep_state else (None, rest)
     gain_out, rest = (rest[0], rest[1:]) if gain_sum else (None, rest)
-    from_outer, from_peer, staged, send, recv = rest
+    if extra:
+        spread = world // 2 * len(plan)
+        out_parts, grad_outs, rest = rest[0], rest[1 : 1 + spread], rest[1 + spread :]
+    from_outer, from_peer, staged, send, recv = rest[:5]
     half, sub, count = line_steps(partial.shape[0])
     me = lax.axis_index("tensor")
     side = me // 2
@@ -701,6 +718,30 @@
     def greet(where):
         pl.semaphore_signal(barrier, inc=1, device_id={"tensor": where}, device_id_type=pl.DeviceIdType.MESH)
 
+    if extra:
+        mate = {"context": lax.axis_index("context") ^ 1}
+        pl.semaphore_signal(barrier, inc=1, device_id=mate, device_id_type=pl.DeviceIdType.MESH)
+        grad_work, grad_finish = grads_parts(world, plan, grad_ins, grad_outs, rest[5:])
+    block = partial.shape[0] // world if extra else 0
+
+    def work(q):
+        grad_work(q)
+        rows_q = pl.ds(pl.multiple_of(q * block, block), block)
+        value = RESIDUAL_SCALE * ffn_out[rows_q, :].astype(F32)
+        quarter = 2 * block * world // 8
+        chunk = lax.rem(q * 4 // world - me + 4, 4)
+        place = pl.ds(pl.multiple_of(lax.rem(q * block, quarter), block), block)
+        owned = inner & (q * 2 // world == side)
+
+        @pl.when(owned)
+        def _():
+            mine = pl.ds(pl.multiple_of(lax.rem(q * block, half), block), block)
+            out_parts[chunk, place, :] = (value + ins[0][mine, :]).astype(BF16)
+
+        @pl.when(jnp.logical_not(owned))
+        def _():
+            out_parts[chunk, place, :] = value.astype(BF16)
+
     if gain_sum:
         gain_out[...] = jnp.zeros_like(gain_out)
 
@@ -708,7 +749,7 @@
     def _():
         greet(to_outer)
         greet(to_peer)
-        pl.semaphore_wait(barrier, 2)
+        pl.semaphore_wait(barrier, 3 if extra else 2)
 
         def step(k, carry):
             @pl.when(k < count)
@@ -739,6 +780,12 @@
                 over(k - 3, far).wait_recv()
                 down_far(k - 3).start()
 
+            if extra:
+
+                @pl.when((lax.rem(k, count // world) == 0) & (k < count))
+                def _():
+                    work(k // (count // world))
+
             return carry
 
         lax.fori_loop(0, count + 3, step, 0)
@@ -755,7 +802,7 @@
     @pl.when(jnp.logical_not(inner))
     def _():
         greet(to_inner)
-        pl.semaphore_wait(barrier, 1)
+        pl.semaphore_wait(barrier, 2 if extra else 1)
 
         def step(k, carry):
             up_far(k).start()
@@ -763,6 +810,13 @@
             return carry
 
         lax.fori_loop(0, count, step, 0)
+        if extra:
+
+            def busy(q, carry):
+                work(q)
+                return carry
+
+            lax.fori_loop(0, world, busy, 0)
 
         def drain(k, carry):
             down_near(k).wait_recv()
@@ -773,8 +827,11 @@
 
         lax.fori_loop(0, count, drain, 0)
 
-
-def line_sum(partial, ins, finish, keep_state, gain_sum, identity):
+    if extra:
+        grad_finish()
+
+
+def line_sum(partial, ins, finish, keep_state, gain_sum, identity, ffn_out=None, pairs=()):
     rows, width = partial.shape
     half, _, count = line_steps(rows)
     vmem = pl.BlockSpec(memory_space=pltpu.VMEM)
@@ -783,10 +840,18 @@
         shapes.append(jax.ShapeDtypeStruct((half, width), F32))
     if gain_sum:
         shapes.append(jax.ShapeDtypeStruct((8, width), F32))
+    specs, more, scratch, extra = [vmem] * len(shapes), [], [], None
+    if pairs:
+        arrays, plan = unique_arrays(pairs)
+        extra = (plane_size(), len(arrays), plan)
+        more = [ffn_out] + arrays
+        outs, scratch = grads_shapes(pairs)
+        shapes += [jax.ShapeDtypeStruct((4, rows // 4, width), BF16)] + outs
+        specs += [vmem] + [ANYWHERE] * len(outs)
     return pl.pallas_call(
-        functools.partial(line_body, finish, keep_state, gain_sum, len(ins)),
-        in_specs=[vmem] * (1 + len(ins)),
-        out_specs=[vmem] * len(shapes),
+        functools.partial(line_body, finish, keep_state, gain_sum, len(ins), extra),
+        in_specs=[vmem] * (1 + len(ins) + len(more)),
+        out_specs=specs,
         out_shape=shapes,
         scratch_shapes=[
             pltpu.VMEM((2, half, width), BF16),
@@ -794,12 +859,13 @@
             pltpu.VMEM((half, width), BF16),
             pltpu.SemaphoreType.DMA((4, count)),
             pltpu.SemaphoreType.DMA((5, count)),
-        ],
+        ]
+        + scratch,
         compiler_params=pltpu.CompilerParams(
             collective_id=identity, has_side_effects=True, vmem_limit_bytes=VMEM_BYTES
         ),
         cost_estimate=pl.CostEstimate(flops=0, bytes_accessed=100 * rows * width, transcendentals=0),
-    )(partial, *ins)
+    )(partial, *ins, *more)
 
 
 def mean_square(values):
@@ -832,21 +898,33 @@
     return (d_hidden[own, :] + pulled).astype(BF16), None, gains
 
 
-def grads_body(count, jobs, *refs):
-    ins, rest = refs[: 2 * jobs], refs[2 * jobs :]
-    halves = count // 2
-    outs, rest = rest[: halves * jobs], rest[halves * jobs :]
-    sent, got, own = rest[:jobs], rest[jobs : 2 * jobs], rest[2 * jobs : 3 * jobs]
-    send, recv, done = rest[3 * jobs :]
+def unique_arrays(pairs):
+    arrays, plan = [], []
+    for left, right, low, high in pairs:
+        spots = []
+        for value in (left, right):
+            known = [i for i, array in enumerate(arrays) if array is value]
+            if not known:
+                arrays.append(value)
+            spots.append(known[0] if known else len(arrays) - 1)
+        plan.append((spots[0], spots[1], low, high))
+    return arrays, tuple(plan)
+
+
+def grads_parts(count, plan, ins, outs, scratch):
+    halves, jobs = count // 2, len(plan)
+    sent, got, own = scratch[:jobs], scratch[jobs : 2 * jobs], scratch[2 * jobs : 3 * jobs]
+    send, recv, done = scratch[3 * jobs :]
     me = plane_index()
     mate = {"context": lax.axis_index("context") ^ 1}
-    mesh_ids = pl.DeviceIdType.MESH
 
     def piece(j, r):
-        left, right = ins[2 * j], ins[2 * j + 1]
-        extent = left.shape[1] // count
+        left, right, low, high = plan[j]
+        extent = ins[left].shape[1] // count
         columns = pl.ds(pl.multiple_of((me ^ r) * extent, extent), extent)
-        return lax.dot_general(left[:, columns], right[...], (((0,), (0,)), ((), ())), preferred_element_type=F32)
+        return lax.dot_general(
+            ins[left][:, columns], ins[right][:, low:high], (((0,), (0,)), ((), ())), preferred_element_type=F32
+        )
 
     def across(j, i):
         return pltpu.make_async_remote_copy(
@@ -855,24 +933,15 @@
             send_sem=send.at[j, i],
             recv_sem=recv.at[j, i],
             device_id=mate,
-            device_id_type=mesh_ids,
+            device_id_type=pl.DeviceIdType.MESH,
         )
 
-    barrier = pltpu.get_barrier_semaphore()
-    pl.semaphore_signal(barrier, inc=1, device_id=mate, device_id_type=mesh_ids)
-    pl.semaphore_wait(barrier, 1)
-
-    def odd(step, carry):
-        i = halves - 1 - step
+    def odd(i):
         for j in range(jobs):
             sent[j][i] = piece(j, 2 * i + 1).astype(BF16)
             across(j, i).start()
-        return carry
-
-    lax.fori_loop(0, halves, odd, 0)
-
-    def even(step, carry):
-        i = halves - 1 - step
+
+    def even(i):
         for j in range(jobs):
             value = piece(j, 2 * i)
             across(j, i).wait_recv()
@@ -894,52 +963,92 @@
                     source = got[j].at[known] if known else own[j]
                     pltpu.make_async_copy(source, outs[known * jobs + j], done.at[known, j]).start()
 
+    def work(q):
+        @pl.when(q < halves)
+        def _():
+            odd(halves - 1 - q)
+
+        @pl.when(q >= halves)
+        def _():
+            even(count - 1 - q)
+
+    def finish():
+        for known in range(halves):
+            for j in range(jobs):
+                source = got[j].at[known] if known else own[j]
+                pltpu.make_async_copy(source, outs[known * jobs + j], done.at[known, j]).wait()
+                across(j, known).wait_send()
+
+    return work, finish
+
+
+def grads_body(count, n_in, plan, *refs):
+    ins, rest = refs[:n_in], refs[n_in:]
+    spread = count // 2 * len(plan)
+    outs, scratch = rest[:spread], rest[spread:]
+    work, finish = grads_parts(count, plan, ins, outs, scratch)
+    barrier = pltpu.get_barrier_semaphore()
+    mate = {"context": lax.axis_index("context") ^ 1}
+    pl.semaphore_signal(barrier, inc=1, device_id=mate, device_id_type=pl.DeviceIdType.MESH)
+    pl.semaphore_wait(barrier, 1)
+
+    def step(q, carry):
+        work(q)
         return carry
 
-    lax.fori_loop(0, halves, even, 0)
-    for known in range(halves):
-        for j in range(jobs):
-            source = got[j].at[known] if known else own[j]
-            pltpu.make_async_copy(source, outs[known * jobs + j], done.at[known, j]).wait()
-            across(j, known).wait_send()
+    lax.fori_loop(0, count, step, 0)
+    finish()
+
+
+def grads_shapes(pairs):
+    count = plane_size()
+    halves = count // 2
+    shapes = [(left.shape[1] // count, high - low) for left, right, low, high in pairs]
+    outs = [jax.ShapeDtypeStruct(shape, BF16 if i else F32) for i in range(halves) for shape in shapes]
+    scratch = [pltpu.VMEM((halves,) + shape, BF16) for shape in shapes] * 2
+    scratch += [pltpu.VMEM(shape, F32) for shape in shapes]
+    sems = [(len(pairs), halves), (len(pairs), halves), (halves, len(pairs))]
+    return outs, scratch + [pltpu.SemaphoreType.DMA(shape) for shape in sems]
+
+
+def grads_named(flat, jobs):
+    return [{2 * i: flat[i * jobs + j] for i in range(len(flat) // jobs)} for j in range(jobs)]
+
+
+def grads_fit(pairs):
+    return all((pair[0].shape[1] // plane_size()) % LANES == 0 for pair in pairs)
 
 
 def plane_grads(pairs, identity):
     count = plane_size()
-    halves = count // 2
     jobs = len(pairs)
-    extents = [left.shape[1] // count for left, _ in pairs]
-    if any(extent % LANES for extent in extents):
+    extents = [pair[0].shape[1] // count for pair in pairs]
+    arrays, plan = unique_arrays(pairs)
+    if not grads_fit(pairs):
         me = plane_index()
         sides = []
-        for (left, right), e in zip(pairs, extents):
+        for (left, right, low, high), e in zip(pairs, extents):
             columns = lambda r: lax.dynamic_slice_in_dim(left, (me ^ r) * e, e, 1)
-            whole = {r: weight_grad(columns(r), right).astype(BF16) for r in range(count)}
+            whole = {r: weight_grad(columns(r), right[:, low:high]).astype(BF16) for r in range(count)}
             sides.append({r: take_sum(whole, 1, r) for r in range(0, count, 2)})
         return sides
-    shapes = [(e, right.shape[1]) for e, (_, right) in zip(extents, pairs)]
+    outs, scratch = grads_shapes(pairs)
     flat = pl.pallas_call(
-        functools.partial(grads_body, count, jobs),
-        in_specs=[pl.BlockSpec(memory_space=pltpu.VMEM)] * (2 * jobs),
-        out_specs=[ANYWHERE] * (halves * jobs),
-        out_shape=[jax.ShapeDtypeStruct(shape, BF16 if i else F32) for i in range(halves) for shape in shapes],
-        scratch_shapes=[pltpu.VMEM((halves,) + shape, BF16) for shape in shapes] * 2
-        + [pltpu.VMEM(shape, F32) for shape in shapes]
-        + [
-            pltpu.SemaphoreType.DMA((jobs, halves)),
-            pltpu.SemaphoreType.DMA((jobs, halves)),
-            pltpu.SemaphoreType.DMA((halves, jobs)),
-        ],
+        functools.partial(grads_body, count, len(arrays), plan),
+        in_specs=[pl.BlockSpec(memory_space=pltpu.VMEM)] * len(arrays),
+        out_specs=[ANYWHERE] * len(outs),
+        out_shape=outs,
+        scratch_shapes=scratch,
         compiler_params=pltpu.CompilerParams(
             collective_id=identity, has_side_effects=True, vmem_limit_bytes=VMEM_BYTES
         ),
         cost_estimate=pl.CostEstimate(
-            flops=sum(2 * left.shape[0] * left.shape[1] * right.shape[1] for left, right in pairs),
-            bytes_accessed=sum(2 * left.shape[1] * right.shape[1] for left, right in pairs),
+            flops=sum(2 * left.shape[0] * left.shape[1] * (high - low) for left, _, low, high in pairs),
+            bytes_accessed=sum(2 * left.shape[1] * (high - low) for left, _, low, high in pairs),
             transcendentals=0,
         ),
-    )(*[value for pair in pairs for value in pair])
-    return [{2 * i: flat[i * jobs + j] for i in range(halves)} for j in range(jobs)]
+    )(*arrays)
+    return grads_named(flat, jobs)
 
 
 def after(value, *others):
@@ -996,7 +1105,6 @@
     seqs, local_len, width = tokens.shape
     rows = seqs * local_len
     size = plane_size()
-    me = plane_index()
     z = lax.axis_index("tensor")
     token_rows = tokens.reshape(rows, width)
     grad_rows = grad_out.reshape(rows, width)
@@ -1030,25 +1138,36 @@
     active, d_gate, d_up, ffn_out, d_normed_ffn = ffn(
         normed_ffn, d_ffn, gate_pieces, up_pieces, low_pieces, high_pieces, pushed
     )
-    grad_gate, grad_up, grad_low, grad_high = plane_grads(
-        [(normed_ffn, d_gate), (normed_ffn, d_up), (d_ffn, active[:, :half]), (d_ffn, active[:, half:])], 3
-    )
-    d_normed_ffn = after(d_normed_ffn, grad_gate[0])
-    d_branch, d_hidden, ffn_gain = line_sum(d_normed_ffn, [hidden, grad_rows, gain_ffn], finish_ffn_back, True, True, 1)
-
-    grad_gate, grad_up = reduce_pair(grad_gate, grad_up)
-    grad_low, grad_high = reduce_pair(grad_low, grad_high)
-
-    owner = lax.rem(z, 3) != 0
-    padded = lax.dynamic_update_slice_in_dim(jnp.zeros((rows, width), F32), hidden, (z // 2) * (rows // 2), 0)
-    out_part = RESIDUAL_SCALE * after(ffn_out, d_branch).astype(F32) + jnp.where(owner, padded, 0.0)
-    layer_out = rows_gather(rows_sum(out_part.astype(BF16)).astype(BF16))
+    pairs = [
+        (normed_ffn, d_gate, 0, units),
+        (normed_ffn, d_up, 0, units),
+        (d_ffn, active, 0, half),
+        (d_ffn, active, half, units),
+    ]
+    sum_ins = [hidden, grad_rows, gain_ffn]
+    if grads_fit(pairs):
+        d_branch, d_hidden, ffn_gain, out_parts, *flat = line_sum(
+            d_normed_ffn, sum_ins, finish_ffn_back, True, True, 1, ffn_out, pairs
+        )
+        grad_gate, grad_up, grad_low, grad_high = grads_named(flat, len(pairs))
+        out_chunks = [out_parts[shift] for shift in range(4)]
+    else:
+        grad_gate, grad_up, grad_low, grad_high = plane_grads(pairs, 3)
+        d_branch, d_hidden, ffn_gain = line_sum(
+            after(d_normed_ffn, grad_gate[0]), sum_ins, finish_ffn_back, True, True, 1
+        )
+        padded = lax.dynamic_update_slice_in_dim(jnp.zeros((rows, width), F32), hidden, (z // 2) * (rows // 2), 0)
+        out_part = RESIDUAL_SCALE * ffn_out.astype(F32) + jnp.where(lax.rem(z, 3) != 0, padded, 0.0)
+        out_chunks = [chunk_of(out_part.astype(BF16), lax.rem(z + shift, 4), rows // 4) for shift in range(4)]
+    layer_out = rows_gather(rows_sum(out_chunks).astype(BF16))
 
     d_mixture = gathered_matmul(d_branch, output_pieces, 1, True)
     d_queries, *d_pieces = attend_back(block_order, queries, d_mixture, logs, kv_pieces)
     d_keys_values = reduce_context(d_pieces)
+    grad_gate, grad_up = reduce_pair(grad_gate, grad_up, [d_keys_values])
+    grad_low, grad_high = reduce_pair(grad_low, grad_high, [d_keys_values])
     d_qkv, d_normed = project_qkv_back(d_queries, d_keys_values, cosine, sine, qkv_pieces)
-    grad_qkv, grad_output = plane_grads([(normed, d_qkv), (d_branch, mixture)], 4)
+    grad_qkv, grad_output = plane_grads([(normed, d_qkv, 0, d_qkv.shape[1]), (d_branch, mixture, 0, q_width)], 4)
     d_normed = after(d_normed, grad_qkv[0])
     grad_tokens, attn_gain = line_sum(
         d_normed, [token_rows, d_hidden, gain_attn], finish_attention_back, False, True, 2
@@ -1057,13 +1176,7 @@
     grad_qkv, grad_output = reduce_pair(grad_qkv, grad_output)
     attn_gain, ffn_gain = jnp.sum(attn_gain, axis=0), jnp.sum(ffn_gain, axis=0)
     gain_grads = jnp.stack([attn_gain, ffn_gain])
-    everyone = ("shard", "context", "tensor")
-    world = size * lax.axis_size("tensor")
-    bit = 1
-    while bit < world:
-        gain_grads = gain_grads + swap(gain_grads, everyone, world, bit)
-        bit *= 2
-    gain_grads = lax.dynamic_slice_in_dim(gain_grads, me * (width // size), width // size, 1)
+    gain_grads = gains_sum(gain_grads)
     return (
         layer_out.reshape(seqs, local_len, width),
         grad_tokens.reshape(seqs, local_len, width),

time: 621 us -> 636 us (1.024)
  the two profiles are of different devices: /device:TPU:0 before, /device:TPU:24 now
where the time goes in v2:
time: 636 us; the launch traced here: 629 us
  Pallas kernels  336 us (53%)
  waiting for transfers between devices  179 us (28%)
  starting transfers between devices  59.6 us (9%)
  other arithmetic  29.2 us (5%)
  local copies, waits for them, and re-layouts  23.2 us (4%)
    pallas_call x3, Pallas kernels, line_sum(): pl.pallas_call(functools.partial(line_body, finish, keep_state, gain_sum,...  199 us
    ppermute x60, waiting for transfers between devices, swap(): return lax.ppermute(value, axes, [(i, i ^ bit) for i in range(size)])  147 us
    ppermute x60, starting transfers between devices, swap(): return lax.ppermute(value, axes, [(i, i ^ bit) for i in range(size)])  52.4 us
    pallas_call x1, Pallas kernels, ffn(): pl.pallas_call(body, grid=(rows // row_tile, units // tile), in_specs=[ro...  44.3 us
    pallas_call x1, Pallas kernels, attend_back(): pl.pallas_call(functools.partial(attend_back_body, len(pieces)), grid=gri...  35.6 us
    ppermute x3, waiting for transfers between devices, rows_gather(): parts.append(lax.ppermute(chunk, 'tensor', pairs))  29.3 us
    pallas_call x1, Pallas kernels, attend(): pl.pallas_call(functools.partial(attend_body, len(pieces)), grid=grid, in...  21.3 us
  transfers between devices with their start and end apart: 69, of which 25 were waited for; matrix products, arithmetic and copies ran while one was open for 6% of the time, Pallas kernels for 35%

profile of v2, /device:TPU:24, one launch (start us, length us, event | category | flops | bytes accessed | tf_op | source)
XLA Modules:
  0.0 629.0 jit_solution(2988524450310808729)
XLA Ops:
  3.3 1.6 collective-permute-start.6
  4.9 1.5 collective-permute-start.4
  9.7 1.6 collective-permute-start.1
  11.3 2.9 collective-permute-done.6.rest_4_
  14.3 1.5 collective-permute-start.8
  15.8 1.8 multiply_sine_fusion
  17.6 5.0 collective-permute-done.1
  23.2 3.1 collective-permute-done.2
  26.8 2.8 collective-permute-done.8.rest_6_
  30.9 1.5 collective-permute-start.18
  33.4 8.4 %project_qkv.1 = (bf16[512,2048]{1,0:T(8,128)(2,1)}, bf16[512,512]{1,0:T(8,128)(2,1)}, bf16[512,256]{1,0:T(8,128)(2,1)}) custom-call(bf16[512,2048]{1,0:T(8,128)(2,1)} %bitcast.49, f32[1,2048]{1,0:T(1,128)} %bitcast.58, f32[512,128]{1,0:T(8,128)} %get-tuple-element.203.cosine, f32[512,128]{1,0:T(8,128)} %get-tuple-element.202.sine, ...), custom_call_target="tpu_custom_call" | custom-call | flops 1610612736 | bytes 7340032 | tf_op jit(solution)/shard_map/project_qkv/pallas_call | solution.py:222
  41.9 1.6 collective-permute-start.11
  43.5 1.5 collective-permute-done.18.rest_6_
  45.5 4.8 collective-permute-done.11.rest_2_
  50.3 1.5 collective-permute-start.23
  55.3 2.2 fusion.27
  58.1 1.5 collective-permute-start.30
  60.3 10.9 %collective-permute-done.21.refs_2_ = bf16[256,2048]{1,0:T(8,128)(2,1)} collective-permute-done((bf16[256,2048]{1,0:T(8,128)(2,1)}, bf16[256,2048]{1,0:T(8,128)(2,1)}, u32[]{:S(2)}, u32[]{:S(2)}) %collective-permute-start.21) | collective-permute-done | bytes 1048608 | tf_op jit(solution)/shard_map/ppermute | solution.py:37
  71.3 1.5 collective-permute-start.29
  72.8 3.8 collective-permute-done.23.refs_5_
  76.6 1.5 collective-permute-start.26
  78.2 21.3 %attend.1 = (bf16[512,512]{1,0:T(8,128)(2,1)}, f32[4,2,512]{2,1,0:T(2,128)}) custom-call(s32[1,8]{1,0:T(1,128)} %order.3, bf16[512,512]{1,0:T(8,128)(2,1)} %get-tuple-element.81.query_ref, bf16[512,256]{1,0:T(8,128)(2,1)} %get-tuple-element.82.rest_0_, bf16[512,256]{1,0:T(8,128)(2,1)} %copy-done.43, bf16[512,256]{1,0:T(8,128)(2,1)} %copy-done.42, ...), custom_call_target="tpu_custom_call" | custom-call | flops 8589934592 | bytes 2097152 | tf_op jit(solution)/shard_map/attend/pallas_call | solution.py:569
  100.1 1.5 collective-permute-start.22
  102.7 4.9 shard_map.203.refs_0_
  107.6 59.7 %shard_map.204 = (bf16[512,2048]{1,0:T(8,128)(2,1)}, f32[256,2048]{1,0:T(8,128)}) custom-call(bf16[512,2048]{1,0:T(8,128)(2,1)} %shard_map.203.refs_0_, bf16[512,2048]{1,0:T(8,128)(2,1)} %bitcast.50, f32[1,2048]{1,0:T(1,128)} %bitcast.52), custom_call_target="tpu_custom_call" | custom-call | bytes 104857600 | tf_op jit(solution)/shard_map/pallas_call | solution.py:851
  168.0 1.5 collective-permute-start.31
  169.5 3.4 multiply_convert_fusion.d_ffn.refs_8_
  172.9 3.9 collective-permute-done.28.refs_11_
  178.8 44.3 %feed_forward.1 = (bf16[512,2048]{1,0:T(8,128)(2,1)}, bf16[512,2048]{1,0:T(8,128)(2,1)}, bf16[512,2048]{1,0:T(8,128)(2,1)}, bf16[512,2048]{1,0:T(8,128)(2,1)}, bf16[512,2048]{1,0:T(8,128)(2,1)}) custom-call(bf16[512,2048]{1,0:T(8,128)(2,1)} %get-tuple-element.84.normed.refs_5_, bf16[512,2048]{1,0:T(8,128)(2,1)} %multiply_convert_fusion.d_ffn.refs_8_, ...), custom_call_target="tpu_custom_call" | custom-call | flops 25769803776 | bytes 39845888 | tf_op jit(solution)/shard_map/feed_forward/pallas_call | solution.py:413
  223.1 74.1 %shard_map.205 = (bf16[512,2048]{1,0:T(8,128)(2,1)}, f32[256,2048]{1,0:T(8,128)}, f32[8,2048]{1,0:T(8,128)}, bf16[4,128,2048]{2,1,0:T(8,128)(2,1)}, f32[256,2048...) custom-call(bf16[512,2048]{1,0:T(8,128)(2,1)} %get-tuple-element.97., ...), custom_call_target="tpu_custom_call" | custom-call | bytes 104857600 | tf_op jit(solution)/shard_map/pallas_call | solution.py:851
  297.3 2.5 slice_bitcast_fusion.2
  299.8 2.0 collective-permute-start.32
  302.4 5.0 shard_map.206.grad_ref
  307.5 35.6 %attend_back.1 = (f32[512,512]{1,0:T(8,128)}, f32[512,256]{1,0:T(8,128)}, bf16[512,256]{1,0:T(8,128)(2,1)}, f32[512,256]{1,0:T(8,128)}, bf16[512,256]{1,0:T(8,128)(2,1)}) custom-call(s32[1,8]{1,0:T(1,128)} %order.3, bf16[512,512]{1,0:T(8,128)(2,1)} %get-tuple-element.81.query_ref, bf16[512,512]{1,0:T(8,128)(2,1)} %shard_map.206.grad_ref, ...), custom_call_target="tpu_custom_call" | custom-call | flops 21474836480 | bytes 3145728 | tf_op jit(solution)/shard_map/attend_back/pallas_call | solution.py:644
  344.9 1.5 collective-permute-start.53
  349.6 1.6 reshape.106
  351.1 2.6 bitcast_dynamic-update-slice_fusion.3
  353.7 13.3 %collective-permute-done.40 = bf16[512,256]{1,0:T(8,128)(2,1)S(1)} collective-permute-done((bf16[512,256]{1,0:T(8,128)(2,1)S(1)}, bf16[512,256]{1,0:T(8,128)(2,1)S(1)}, u32[]{:S(2)}, u32[]{:S(2)}) %collective-permute-start.40) | collective-permute-done | bytes 262176 | tf_op jit(solution)/shard_map/ppermute | solution.py:37
  367.9 6.8 %project_qkv_back.1 = (bf16[512,768]{1,0:T(8,128)(2,1)}, bf16[512,2048]{1,0:T(8,128)(2,1)}) custom-call(f32[512,512]{1,0:T(8,128)} %get-tuple-element.106.d_queries, f32[512,256]{1,0:T(8,128)} %convert_add_fusion.4.d_keys_values, f32[512,128]{1,0:T(8,128)} %get-tuple-element.203.cosine, f32[512,128]{1,0:T(8,128)} %get-tuple-element.202.sine, ...), custom_call_target="tpu_custom_call" | custom-call | flops 1610612736 | bytes 7340032 | tf_op jit(solution)/shard_map/project_qkv_back/pallas_call | solution.py:279
  374.8 10.7 %shard_map.207 = (f32[256,768]{1,0:T(8,128)}, f32[256,512]{1,0:T(8,128)}, bf16[256,768]{1,0:T(8,128)(2,1)}, bf16[256,512]{1,0:T(8,128)(2,1)}, bf16[256,768]{1,0:...) custom-call(bf16[512,2048]{1,0:T(8,128)(2,1)} %get-tuple-element.112.refs_0_, ...), custom_call_target="tpu_custom_call" | custom-call | flops 2684354560 | bytes 5242880 | tf_op jit(solution)/shard_map/pallas_call | solution.py:1036
  385.5 64.7 %shard_map.208 = (bf16[512,2048]{1,0:T(8,128)(2,1)}, f32[8,2048]{1,0:T(8,128)}) custom-call(bf16[512,2048]{1,0:T(8,128)(2,1)} %get-tuple-element.115.refs_0_, bf16[512,2048]{1,0:T(8,128)(2,1)} %bitcast.51, f32[256,2048]{1,0:T(8,128)} %get-tuple-element.116.refs_2_, f32[1,2048]{1,0:T(1,128)} %bitcast.59), custom_call_target="tpu_custom_call" | custom-call | bytes 104857600 | tf_op jit(solution)/shard_map/pallas_call | solution.py:851
  451.3 2.1 collective-permute-start.59
  454.0 1.2 add_convert_fusion.3
  455.3 2.7 collective-permute-done.60
  460.0 1.2 add_convert_fusion.2
  464.7 1.9 collective-permute-start.68
  466.7 2.6 bitcast_convert_fusion
  472.8 1.4 collective-permute-start.41
  474.9 25.6 %collective-permute-done.45 = bf16[256,512]{1,0:T(8,128)(2,1)S(1)} collective-permute-done((bf16[256,512]{1,0:T(8,128)(2,1)S(1)}, bf16[256,512]{1,0:T(8,128)(2,1)S(1)}, u32[]{:S(2)}, u32[]{:S(2)}) %collective-permute-start.45) | collective-permute-done | bytes 262176 | tf_op jit(solution)/shard_map/ppermute | solution.py:37
  501.6 2.2 collective-permute-done.41
  506.7 29.3 %collective-permute-done.36 = bf16[128,2048]{1,0:T(8,128)(2,1)S(1)} collective-permute-done((bf16[128,2048]{1,0:T(8,128)(2,1)S(1)}, bf16[128,2048]{1,0:T(8,128)(2,1)S(1)}, u32[]{:S(2)}, u32[]{:S(2)}) %collective-permute-start.36) | collective-permute-done | bytes 524320 | tf_op jit(solution)/shard_map/ppermute | solution.py:136
  539.1 1.5 collective-permute-start.58
  542.3 8.5 %collective-permute-done.55 = bf16[256,1024]{1,0:T(8,128)(2,1)S(1)} collective-permute-done((bf16[256,1024]{1,0:T(8,128)(2,1)S(1)}, bf16[256,1024]{1,0:T(8,128)(2,1)S(1)}, u32[]{:S(2)}, u32[]{:S(2)}) %collective-permute-start.55) | collective-permute-done | bytes 524320 | tf_op jit(solution)/shard_map/ppermute | solution.py:37
  552.5 1.4 add_convert_fusion.1
  553.8 1.5 collective-permute-start.46
  555.4 6.7 %collective-permute-done.58 = bf16[256,1024]{1,0:T(8,128)(2,1)S(1)} collective-permute-done((bf16[256,1024]{1,0:T(8,128)(2,1)S(1)}, bf16[256,1024]{1,0:T(8,128)(2,1)S(1)}, u32[]{:S(2)}, u32[]{:S(2)}) %collective-permute-start.58) | collective-permute-done | bytes 524320 | tf_op jit(solution)/shard_map/ppermute | solution.py:37
  563.1 17.2 %collective-permute-done.44 = bf16[256,512]{1,0:T(8,128)(2,1)S(1)} collective-permute-done((bf16[256,512]{1,0:T(8,128)(2,1)S(1)}, bf16[256,512]{1,0:T(8,128)(2,1)S(1)}, u32[]{:S(2)}, u32[]{:S(2)}) %collective-permute-start.44) | collective-permute-done | bytes 262176 | tf_op jit(solution)/shard_map/ppermute | solution.py:37
  580.3 1.5 collective-permute-start.52
  581.9 1.8 copy.36
  584.5 1.3 add_bitcast_fusion.2
  591.1 15.4 %collective-permute-done.52 = bf16[256,2048]{1,0:T(8,128)(2,1)} collective-permute-done((bf16[256,2048]{1,0:T(8,128)(2,1)S(1)}, bf16[256,2048]{1,0:T(8,128)(2,1)}, u32[]{:S(2)}, u32[]{:S(2)}) %collective-permute-start.52) | collective-permute-done | bytes 1048608 | tf_op jit(solution)/shard_map/ppermute | solution.py:37
  606.4 3.5 convert_add_fusion
  609.9 15.7 %collective-permute-done.49 = bf16[256,2048]{1,0:T(8,128)(2,1)} collective-permute-done((bf16[256,2048]{1,0:T(8,128)(2,1)}, bf16[256,2048]{1,0:T(8,128)(2,1)}, u32[]{:S(2)}, u32[]{:S(2)}) %collective-permute-start.49) | collective-permute-done | bytes 1048608 | tf_op jit(solution)/shard_map/ppermute | solution.py:37
  625.6 3.0 convert_add_fusion.1
  (233 shorter events, 54.4 us)
Async XLA Ops:
  3.3 10.9 %collective-permute-start.6 = (bf16[256,768]{1,0:T(8,128)(2,1)S(1)}, bf16[256,768]{1,0:T(8,128)(2,1)S(1)}, u32[]{:S(2)}, u32[]{:S(2)}) collective-permute-start(bf16[256,768]{1,0:T(8,128)(2,1)S(1)} %constant_dynamic-update-slice_fusion.rest_0_), channel_id=1, source_target_pairs={{0,16},{4,20},{8,24},{12,28},{16,0},{20,4},{24,8},{28,12},{1,17},{... | collective-permute-start | bytes 1179656 | tf_op jit(solution)/shard_map/ppermute | solution.py:37
  4.9 21.3 %collective-permute-start.4 = (bf16[256,768]{1,0:T(8,128)(2,1)S(1)}, bf16[256,768]{1,0:T(8,128)(2,1)S(1)}, u32[]{:S(2)}, u32[]{:S(2)}) collective-permute-start(bf16[256,768]{1,0:T(8,128)(2,1)S(1)} %constant_dynamic-update-slice_fusion.rest_0_), channel_id=1, source_target_pairs={{0,8},{4,12},{8,0},{12,4},{16,24},{20,28},{24,16},{28,20},{1,9},{5... | collective-permute-start | bytes 1179656 | tf_op jit(solution)/shard_map/ppermute | solution.py:37
  6.4 24.5 %collective-permute-start.3 = (bf16[256,768]{1,0:T(8,128)(2,1)S(1)}, bf16[256,768]{1,0:T(8,128)(2,1)S(1)}, u32[]{:S(2)}, u32[]{:S(2)}) collective-permute-start(bf16[256,768]{1,0:T(8,128)(2,1)S(1)} %constant_dynamic-update-slice_fusion.rest_0_), channel_id=1, source_target_pairs={{0,4},{4,0},{8,12},{12,8},{16,20},{20,16},{24,28},{28,24},{1,5},{5... | collective-permute-start | bytes 1179656 | tf_op jit(solution)/shard_map/ppermute | solution.py:37
  8.3 22.0 %collective-permute-start.14 = (bf16[512,256]{1,0:T(8,128)(2,1)}, bf16[512,256]{1,0:T(8,128)(2,1)S(1)}, u32[]{:S(2)}, u32[]{:S(2)}) collective-permute-start(bf16[512,256]{1,0:T(8,128)(2,1)} %rest_0_.3), channel_id=1, source_target_pairs={{0,8},{4,12},{8,0},{12,4},{16,24},{20,28},{24,16},{28,20},{1,9},{5... | collective-permute-start | bytes 786440 | tf_op jit(solution)/shard_map/ppermute | solution.py:37
  9.7 12.8 %collective-permute-start.1 = (bf16[2,2,256]{2,0,1:T(2,128)(2,1)S(1)}, bf16[2,2,256]{2,0,1:T(2,128)(2,1)S(1)}, u32[]{:S(2)}, u32[]{:S(2)}) collective-permute-start(bf16[2,2,256]{2,0,1:T(2,128)(2,1)S(1)} %pad_maximum_fusion.3), channel_id=1, source_target_pairs={{0,8},{4,12},{8,0},{12,4},{16,24},{20,28},{24,16},{28,20},{1,9},{5... | collective-permute-start | bytes 6152 | tf_op jit(solution)/shard_map/ppermute | solution.py:37
  14.3 15.3 %collective-permute-start.8 = (bf16[256,768]{1,0:T(8,128)(2,1)S(1)}, bf16[256,768]{1,0:T(8,128)(2,1)S(1)}, u32[]{:S(2)}, u32[]{:S(2)}) collective-permute-start(bf16[256,768]{1,0:T(8,128)(2,1)S(1)} %collective-permute-done.6.rest_4_), channel_id=1, source_target_pairs={{0,8},{4,12},{8,0},{12,4},{16,24},{20,28},{24,16},{28,20},{1,9},{5... | collective-permute-start | bytes 1179656 | tf_op jit(solution)/shard_map/ppermute | solution.py:37
  22.6 3.7 collective-permute-start.2
  26.2 6.2 collective-permute-start.7
  26.3 6.2 collective-permute-start.5
  29.6 2.9 collective-permute-start.9
  30.4 13.1 %collective-permute-start.16 = (bf16[512,256]{1,0:T(8,128)(2,1)}, bf16[512,256]{1,0:T(8,128)(2,1)S(1)}, u32[]{:S(2)}, u32[]{:S(2)}) collective-permute-start(bf16[512,256]{1,0:T(8,128)(2,1)} %rest_0_.3), channel_id=1, source_target_pairs={{0,16},{4,20},{8,24},{12,28},{16,0},{20,4},{24,8},{28,12},{1,17},{... | collective-permute-start | bytes 786440 | tf_op jit(solution)/shard_map/ppermute | solution.py:37
  30.9 14.0 %collective-permute-start.18 = (bf16[512,256]{1,0:T(8,128)(2,1)S(1)}, bf16[512,256]{1,0:T(8,128)(2,1)S(1)}, u32[]{:S(2)}, u32[]{:S(2)}) collective-permute-start(bf16[512,256]{1,0:T(8,128)(2,1)S(1)} %collective-permute-done.14.rest_2_), channel_id=1, source_target_pairs={{0,16},{4,20},{8,24},{12,28},{16,0},{20,4},{24,8},{28,12},{1,17},{... | collective-permute-start | bytes 786440 | tf_op jit(solution)/shard_map/ppermute | solution.py:37
  41.9 8.4 %collective-permute-start.11 = (bf16[512,256]{1,0:T(8,128)(2,1)}, bf16[512,256]{1,0:T(8,128)(2,1)S(1)}, u32[]{:S(2)}, u32[]{:S(2)}) collective-permute-start(bf16[512,256]{1,0:T(8,128)(2,1)} %get-tuple-element.82.rest_0_), channel_id=1, source_target_pairs={{0,8},{4,12},{8,0},{12,4},{1,9},{5,13},{9,1},{13,5},{2,10},{6,14},... | collective-permute-start | bytes 786440 | tf_op jit(solution)/shard_map/ppermute | solution.py:37
  44.9 26.3 %collective-permute-start.21 = (bf16[256,2048]{1,0:T(8,128)(2,1)}, bf16[256,2048]{1,0:T(8,128)(2,1)}, u32[]{:S(2)}, u32[]{:S(2)}) collective-permute-start(bf16[256,2048]{1,0:T(8,128)(2,1)} %refs_0_.1), channel_id=1, source_target_pairs={{0,16},{4,20},{8,24},{12,28},{16,0},{20,4},{24,8},{28,12},{1,17},{... | collective-permute-start | bytes 3145736 | tf_op jit(solution)/shard_map/ppermute | solution.py:37
  50.3 26.3 %collective-permute-start.23 = (bf16[256,2048]{1,0:T(8,128)(2,1)}, bf16[256,2048]{1,0:T(8,128)(2,1)}, u32[]{:S(2)}, u32[]{:S(2)}) collective-permute-start(bf16[256,2048]{1,0:T(8,128)(2,1)} %refs_4_.1), channel_id=1, source_target_pairs={{0,8},{4,12},{8,0},{12,4},{16,24},{20,28},{24,16},{28,20},{1,9},{5... | collective-permute-start | bytes 3145736 | tf_op jit(solution)/shard_map/ppermute | solution.py:37
  53.4 4.2 collective-permute-start.19
  53.7 4.4 collective-permute-start.10
  55.2 4.5 collective-permute-start.12
  57.5 41.9 %collective-permute-start.27 = (bf16[2048,128]{1,0:T(8,128)(2,1)}, bf16[2048,128]{1,0:T(8,128)(2,1)}, u32[]{:S(2)}, u32[]{:S(2)}) collective-permute-start(bf16[2048,128]{1,0:T(8,128)(2,1)} %get-tuple-element.92.refs_8_), channel_id=1, source_target_pairs={{0,16},{4,20},{8,24},{12,28},{16,0},{20,4},{24,8},{28,12},{1,17},{... | collective-permute-start | bytes 1572872 | tf_op jit(solution)/shard_map/ppermute | solution.py:37
  58.1 41.9 %collective-permute-start.30 = (bf16[2048,128]{1,0:T(8,128)(2,1)}, bf16[2048,128]{1,0:T(8,128)(2,1)}, u32[]{:S(2)}, u32[]{:S(2)}) collective-permute-start(bf16[2048,128]{1,0:T(8,128)(2,1)} %get-tuple-element.95.refs_12_), channel_id=1, source_target_pairs={{0,16},{4,20},{8,24},{12,28},{16,0},{20,4},{24,8},{28,12},{1,17},{... | collective-permute-start | bytes 1572872 | tf_op jit(solution)/shard_map/ppermute | solution.py:37
  59.6 107.8 %collective-permute-start.24 = (bf16[256,2048]{1,0:T(8,128)(2,1)}, bf16[256,2048]{1,0:T(8,128)(2,1)}, u32[]{:S(2)}, u32[]{:S(2)}) collective-permute-start(bf16[256,2048]{1,0:T(8,128)(2,1)} %refs_4_.1), channel_id=1, source_target_pairs={{0,16},{4,20},{8,24},{12,28},{16,0},{20,4},{24,8},{28,12},{1,17},{... | collective-permute-start | bytes 3145736 | tf_op jit(solution)/shard_map/ppermute | solution.py:37
  71.3 30.3 %collective-permute-start.29 = (bf16[2048,128]{1,0:T(8,128)(2,1)}, bf16[2048,128]{1,0:T(8,128)(2,1)}, u32[]{:S(2)}, u32[]{:S(2)}) collective-permute-start(bf16[2048,128]{1,0:T(8,128)(2,1)} %get-tuple-element.95.refs_12_), channel_id=1, source_target_pairs={{0,8},{4,12},{8,0},{12,4},{16,24},{20,28},{24,16},{28,20},{1,9},{5... | collective-permute-start | bytes 1572872 | tf_op jit(solution)/shard_map/ppermute | solution.py:37
  76.6 91.3 %collective-permute-start.26 = (bf16[2048,128]{1,0:T(8,128)(2,1)}, bf16[2048,128]{1,0:T(8,128)(2,1)}, u32[]{:S(2)}, u32[]{:S(2)}) collective-permute-start(bf16[2048,128]{1,0:T(8,128)(2,1)} %get-tuple-element.92.refs_8_), channel_id=1, source_target_pairs={{0,8},{4,12},{8,0},{12,4},{16,24},{20,28},{24,16},{28,20},{1,9},{5... | collective-permute-start | bytes 1572872 | tf_op jit(solution)/shard_map/ppermute | solution.py:37
  99.5 77.4 %collective-permute-start.20 = (bf16[256,2048]{1,0:T(8,128)(2,1)}, bf16[256,2048]{1,0:T(8,128)(2,1)S(1)}, u32[]{:S(2)}, u32[]{:S(2)}) collective-permute-start(bf16[256,2048]{1,0:T(8,128)(2,1)} %refs_0_.1), channel_id=1, source_target_pairs={{0,8},{4,12},{8,0},{12,4},{16,24},{20,28},{24,16},{28,20},{1,9},{5... | collective-permute-start | bytes 3145736 | tf_op jit(solution)/shard_map/ppermute | solution.py:37
  100.1 78.5 %collective-permute-start.22 = (bf16[256,2048]{1,0:T(8,128)(2,1)}, bf16[256,2048]{1,0:T(8,128)(2,1)}, u32[]{:S(2)}, u32[]{:S(2)}) collective-permute-start(bf16[256,2048]{1,0:T(8,128)(2,1)} %collective-permute-done.21.refs_2_), channel_id=1, source_target_pairs={{0,8},{4,12},{8,0},{12,4},{16,24},{20,28},{24,16},{28,20},{1,9},{5... | collective-permute-start | bytes 3145736 | tf_op jit(solution)/shard_map/ppermute | solution.py:37
  101.6 76.9 %collective-permute-start.25 = (bf16[256,2048]{1,0:T(8,128)(2,1)}, bf16[256,2048]{1,0:T(8,128)(2,1)}, u32[]{:S(2)}, u32[]{:S(2)}) collective-permute-start(bf16[256,2048]{1,0:T(8,128)(2,1)} %collective-permute-done.23.refs_5_), channel_id=1, source_target_pairs={{0,16},{4,20},{8,24},{12,28},{16,0},{20,4},{24,8},{28,12},{1,17},{... | collective-permute-start | bytes 3145736 | tf_op jit(solution)/shard_map/ppermute | solution.py:37
  167.4 9.5 %collective-permute-start.28 = (bf16[2048,128]{1,0:T(8,128)(2,1)}, bf16[2048,128]{1,0:T(8,128)(2,1)S(1)}, u32[]{:S(2)}, u32[]{:S(2)}) collective-permute-start(bf16[2048,128]{1,0:T(8,128)(2,1)} %collective-permute-done.27.refs_10_), channel_id=1, source_target_pairs={{0,8},{4,12},{8,0},{12,4},{16,24},{20,28},{24,16},{28,20},{1,9},{5... | collective-permute-start | bytes 1572872 | tf_op jit(solution)/shard_map/ppermute | solution.py:37
  168.0 9.7 %collective-permute-start.31 = (bf16[2048,128]{1,0:T(8,128)(2,1)}, bf16[2048,128]{1,0:T(8,128)(2,1)S(1)}, u32[]{:S(2)}, u32[]{:S(2)}) collective-permute-start(bf16[2048,128]{1,0:T(8,128)(2,1)} %collective-permute-done.29.refs_13_), channel_id=1, source_target_pairs={{0,16},{4,20},{8,24},{12,28},{16,0},{20,4},{24,8},{28,12},{1,17},{... | collective-permute-start | bytes 1572872 | tf_op jit(solution)/shard_map/ppermute | solution.py:37
  299.8 47.6 %collective-permute-start.32 = (bf16[128,2048]{1,0:T(8,128)(2,1)}, bf16[128,2048]{1,0:T(8,128)(2,1)S(1)}, u32[]{:S(2)}, u32[]{:S(2)}) collective-permute-start(bf16[128,2048]{1,0:T(8,128)(2,1)} %get-tuple-element.186), channel_id=1, source_target_pairs={{0,1},{1,2},{2,3},{3,0},{4,5},{5,6},{6,7},{7,4},{8,9},{9,10},{10,1... | collective-permute-start | bytes 1572872 | tf_op jit(solution)/shard_map/ppermute | solution.py:125
  301.9 46.5 %collective-permute-start.33 = (bf16[128,2048]{1,0:T(8,128)(2,1)}, bf16[128,2048]{1,0:T(8,128)(2,1)S(1)}, u32[]{:S(2)}, u32[]{:S(2)}) collective-permute-start(bf16[128,2048]{1,0:T(8,128)(2,1)} %get-tuple-element.188), channel_id=1, source_target_pairs={{0,2},{1,3},{2,0},{3,1},{4,6},{5,7},{6,4},{7,5},{8,10},{9,11},{10,... | collective-permute-start | bytes 1572872 | tf_op jit(solution)/shard_map/ppermute | solution.py:125
  301.9 47.7 %collective-permute-start.34 = (bf16[128,2048]{1,0:T(8,128)(2,1)}, bf16[128,2048]{1,0:T(8,128)(2,1)}, u32[]{:S(2)}, u32[]{:S(2)}) collective-permute-start(bf16[128,2048]{1,0:T(8,128)(2,1)} %get-tuple-element.187), channel_id=1, source_target_pairs={{0,3},{1,0},{2,1},{3,2},{4,7},{5,4},{6,5},{7,6},{8,11},{9,8},{10,9... | collective-permute-start | bytes 1572872 | tf_op jit(solution)/shard_map/ppermute | solution.py:125
  343.2 10.5 %collective-permute-start.38 = (bf16[512,256]{1,0:T(8,128)(2,1)}, bf16[512,256]{1,0:T(8,128)(2,1)S(1)}, u32[]{:S(2)}, u32[]{:S(2)}) collective-permute-start(bf16[512,256]{1,0:T(8,128)(2,1)} %get-tuple-element.108), channel_id=1, source_target_pairs={{0,4},{4,0},{8,12},{12,8},{1,5},{5,1},{9,13},{13,9},{2,6},{6,2},{1... | collective-permute-start | bytes 786440 | tf_op jit(solution)/shard_map/ppermute | solution.py:37
  344.9 109.2 %collective-permute-start.53 = (bf16[256,1024]{1,0:T(8,128)(2,1)}, bf16[256,1024]{1,0:T(8,128)(2,1)}, u32[]{:S(2)}, u32[]{:S(2)}) collective-permute-start(bf16[256,1024]{1,0:T(8,128)(2,1)} %get-tuple-element.139), channel_id=1, source_target_pairs={{0,16},{4,20},{8,24},{12,28},{16,0},{20,4},{24,8},{28,12},{1,17},{... | collective-permute-start | bytes 1572872 | tf_op jit(solution)/shard_map/ppermute | solution.py:37
  347.5 112.5 %collective-permute-start.57 = (bf16[256,1024]{1,0:T(8,128)(2,1)}, bf16[256,1024]{1,0:T(8,128)(2,1)}, u32[]{:S(2)}, u32[]{:S(2)}) collective-permute-start(bf16[256,1024]{1,0:T(8,128)(2,1)} %get-tuple-element.147), channel_id=1, source_target_pairs={{0,8},{4,12},{8,0},{12,4},{16,24},{20,28},{24,16},{28,20},{1,9},{5... | collective-permute-start | bytes 1572872 | tf_op jit(solution)/shard_map/ppermute | solution.py:37
  348.4 18.6 %collective-permute-start.40 = (bf16[512,256]{1,0:T(8,128)(2,1)S(1)}, bf16[512,256]{1,0:T(8,128)(2,1)S(1)}, u32[]{:S(2)}, u32[]{:S(2)}) collective-permute-start(bf16[512,256]{1,0:T(8,128)(2,1)S(1)} %add_convert_fusion.6), channel_id=1, source_target_pairs={{0,8},{4,12},{8,0},{12,4},{1,9},{5,13},{9,1},{13,5},{2,10},{6,14},... | collective-permute-start | bytes 786440 | tf_op jit(solution)/shard_map/ppermute | solution.py:37
  451.3 4.0 collective-permute-start.59
  453.4 4.6 collective-permute-start.60
  453.4 5.5 collective-permute-start.61
  459.0 5.0 collective-permute-start.62
  459.1 5.7 collective-permute-start.63
  461.2 8.1 %collective-permute-start.64 = (f32[2,256]{1,0:T(2,128)S(1)}, f32[2,256]{1,0:T(2,128)S(1)}, u32[]{:S(2)}, u32[]{:S(2)}) collective-permute-start(f32[2,256]{1,0:T(2,128)S(1)} %get-tuple-element.198), channel_id=1, source_target_pairs={{0,12},{4,8},{8,4},{12,0},{16,28},{20,24},{24,20},{28,16},{1,13},{... | collective-permute-start | bytes 6152 | tf_op jit(solution)/shard_map/ppermute | solution.py:37
  462.2 8.0 %collective-permute-start.65 = (f32[2,256]{1,0:T(2,128)S(1)}, f32[2,256]{1,0:T(2,128)S(1)}, u32[]{:S(2)}, u32[]{:S(2)}) collective-permute-start(f32[2,256]{1,0:T(2,128)S(1)} %get-tuple-element.197), channel_id=1, source_target_pairs={{0,16},{4,20},{8,24},{12,28},{16,0},{20,4},{24,8},{28,12},{1,17},{... | collective-permute-start | bytes 6152 | tf_op jit(solution)/shard_map/ppermute | solution.py:37
  462.8 8.0 %collective-permute-start.66 = (f32[2,256]{1,0:T(2,128)S(1)}, f32[2,256]{1,0:T(2,128)S(1)}, u32[]{:S(2)}, u32[]{:S(2)}) collective-permute-start(f32[2,256]{1,0:T(2,128)S(1)} %get-tuple-element.196), channel_id=1, source_target_pairs={{0,20},{4,16},{8,28},{12,24},{16,4},{20,0},{24,12},{28,8},{1,21},{... | collective-permute-start | bytes 6152 | tf_op jit(solution)/shard_map/ppermute | solution.py:37
  463.9 7.7 %collective-permute-start.67 = (f32[2,256]{1,0:T(2,128)S(1)}, f32[2,256]{1,0:T(2,128)S(1)}, u32[]{:S(2)}, u32[]{:S(2)}) collective-permute-start(f32[2,256]{1,0:T(2,128)S(1)} %get-tuple-element.195), channel_id=1, source_target_pairs={{0,24},{4,28},{8,16},{12,20},{16,8},{20,12},{24,0},{28,4},{1,25},{... | collective-permute-start | bytes 6152 | tf_op jit(solution)/shard_map/ppermute | solution.py:37
  464.7 8.1 %collective-permute-start.68 = (f32[2,256]{1,0:T(2,128)S(1)}, f32[2,256]{1,0:T(2,128)S(1)}, u32[]{:S(2)}, u32[]{:S(2)}) collective-permute-start(f32[2,256]{1,0:T(2,128)S(1)} %get-tuple-element.194), channel_id=1, source_target_pairs={{0,28},{4,24},{8,20},{12,16},{16,12},{20,8},{24,4},{28,0},{1,29},{... | collective-permute-start | bytes 6152 | tf_op jit(solution)/shard_map/ppermute | solution.py:37
  469.3 69.7 %collective-permute-start.51 = (bf16[256,2048]{1,0:T(8,128)(2,1)S(1)}, bf16[256,2048]{1,0:T(8,128)(2,1)S(1)}, u32[]{:S(2)}, u32[]{:S(2)}) collective-permute-start(bf16[256,2048]{1,0:T(8,128)(2,1)S(1)} %copy-done.27), channel_id=1, source_target_pairs={{0,8},{4,12},{8,0},{12,4},{16,24},{20,28},{24,16},{28,20},{1,9},{5... | collective-permute-start | bytes 3145736 | tf_op jit(solution)/shard_map/ppermute | solution.py:37
  470.3 81.6 %collective-permute-start.47 = (bf16[256,2048]{1,0:T(8,128)(2,1)S(1)}, bf16[256,2048]{1,0:T(8,128)(2,1)S(1)}, u32[]{:S(2)}, u32[]{:S(2)}) collective-permute-start(bf16[256,2048]{1,0:T(8,128)(2,1)S(1)} %copy-done.26), channel_id=1, source_target_pairs={{0,16},{4,20},{8,24},{12,28},{16,0},{20,4},{24,8},{28,12},{1,17},{... | collective-permute-start | bytes 3145736 | tf_op jit(solution)/shard_map/ppermute | solution.py:37
  470.8 33.9 %collective-permute-start.35 = (bf16[128,2048]{1,0:T(8,128)(2,1)S(1)}, bf16[128,2048]{1,0:T(8,128)(2,1)S(1)}, u32[]{:S(2)}, u32[]{:S(2)}) collective-permute-start(bf16[128,2048]{1,0:T(8,128)(2,1)S(1)} %copy-done.20), channel_id=1, source_target_pairs={{0,1},{1,2},{2,3},{3,0},{4,5},{5,6},{6,7},{7,4},{8,9},{9,10},{10,1... | collective-permute-start | bytes 1572872 | tf_op jit(solution)/shard_map/ppermute | solution.py:136
  471.6 28.8 %collective-permute-start.45 = (bf16[256,512]{1,0:T(8,128)(2,1)S(1)}, bf16[256,512]{1,0:T(8,128)(2,1)S(1)}, u32[]{:S(2)}, u32[]{:S(2)}) collective-permute-start(bf16[256,512]{1,0:T(8,128)(2,1)S(1)} %copy-done.45), channel_id=1, source_target_pairs={{0,8},{4,12},{8,0},{12,4},{16,24},{20,28},{24,16},{28,20},{1,9},{5... | collective-permute-start | bytes 786440 | tf_op jit(solution)/shard_map/ppermute | solution.py:37
  472.8 31.0 %collective-permute-start.41 = (bf16[256,768]{1,0:T(8,128)(2,1)S(1)}, bf16[256,768]{1,0:T(8,128)(2,1)S(1)}, u32[]{:S(2)}, u32[]{:S(2)}) collective-permute-start(bf16[256,768]{1,0:T(8,128)(2,1)S(1)} %copy-done.40), channel_id=1, source_target_pairs={{0,16},{4,20},{8,24},{12,28},{16,0},{20,4},{24,8},{28,12},{1,17},{... | collective-permute-start | bytes 1179656 | tf_op jit(solution)/shard_map/ppermute | solution.py:37
  500.4 35.5 %collective-permute-start.36 = (bf16[128,2048]{1,0:T(8,128)(2,1)S(1)}, bf16[128,2048]{1,0:T(8,128)(2,1)S(1)}, u32[]{:S(2)}, u32[]{:S(2)}) collective-permute-start(bf16[128,2048]{1,0:T(8,128)(2,1)S(1)} %copy-done.20), channel_id=1, source_target_pairs={{0,2},{1,3},{2,0},{3,1},{4,6},{5,7},{6,4},{7,5},{8,10},{9,11},{10,... | collective-permute-start | bytes 1572872 | tf_op jit(solution)/shard_map/ppermute | solution.py:136
  503.8 33.5 %collective-permute-start.37 = (bf16[128,2048]{1,0:T(8,128)(2,1)S(1)}, bf16[128,2048]{1,0:T(8,128)(2,1)S(1)}, u32[]{:S(2)}, u32[]{:S(2)}) collective-permute-start(bf16[128,2048]{1,0:T(8,128)(2,1)S(1)} %copy-done.20), channel_id=1, source_target_pairs={{0,3},{1,0},{2,1},{3,2},{4,7},{5,4},{6,5},{7,6},{8,11},{9,8},{10,9... | collective-permute-start | bytes 1572872 | tf_op jit(solution)/shard_map/ppermute | solution.py:136
  504.7 36.4 %collective-permute-start.54 = (bf16[256,1024]{1,0:T(8,128)(2,1)S(1)}, bf16[256,1024]{1,0:T(8,128)(2,1)S(1)}, u32[]{:S(2)}, u32[]{:S(2)}) collective-permute-start(bf16[256,1024]{1,0:T(8,128)(2,1)S(1)} %add_convert_fusion.3), channel_id=1, source_target_pairs={{0,8},{4,12},{8,0},{12,4},{16,24},{20,28},{24,16},{28,20},{1,9},{5... | collective-permute-start | bytes 1572872 | tf_op jit(solution)/shard_map/ppermute | solution.py:37
  536.0 14.8 %collective-permute-start.55 = (bf16[256,1024]{1,0:T(8,128)(2,1)S(1)}, bf16[256,1024]{1,0:T(8,128)(2,1)S(1)}, u32[]{:S(2)}, u32[]{:S(2)}) collective-permute-start(bf16[256,1024]{1,0:T(8,128)(2,1)S(1)} %copy-done.30), channel_id=1, source_target_pairs={{0,16},{4,20},{8,24},{12,28},{16,0},{20,4},{24,8},{28,12},{1,17},{... | collective-permute-start | bytes 1572872 | tf_op jit(solution)/shard_map/ppermute | solution.py:37
  537.4 16.5 %collective-permute-start.56 = (bf16[256,1024]{1,0:T(8,128)(2,1)S(1)}, bf16[256,1024]{1,0:T(8,128)(2,1)S(1)}, u32[]{:S(2)}, u32[]{:S(2)}) collective-permute-start(bf16[256,1024]{1,0:T(8,128)(2,1)S(1)} %copy-done.29), channel_id=1, source_target_pairs={{0,8},{4,12},{8,0},{12,4},{16,24},{20,28},{24,16},{28,20},{1,9},{5... | collective-permute-start | bytes 1572872 | tf_op jit(solution)/shard_map/ppermute | solution.py:37
  539.1 22.9 %collective-permute-start.58 = (bf16[256,1024]{1,0:T(8,128)(2,1)S(1)}, bf16[256,1024]{1,0:T(8,128)(2,1)S(1)}, u32[]{:S(2)}, u32[]{:S(2)}) collective-permute-start(bf16[256,1024]{1,0:T(8,128)(2,1)S(1)} %add_convert_fusion.2), channel_id=1, source_target_pairs={{0,16},{4,20},{8,24},{12,28},{16,0},{20,4},{24,8},{28,12},{1,17},{... | collective-permute-start | bytes 1572872 | tf_op jit(solution)/shard_map/ppermute | solution.py:37
  541.1 50.0 %collective-permute-start.50 = (bf16[256,2048]{1,0:T(8,128)(2,1)}, bf16[256,2048]{1,0:T(8,128)(2,1)}, u32[]{:S(2)}, u32[]{:S(2)}) collective-permute-start(bf16[256,2048]{1,0:T(8,128)(2,1)} %get-tuple-element.133), channel_id=1, source_target_pairs={{0,8},{4,12},{8,0},{12,4},{16,24},{20,28},{24,16},{28,20},{1,9},{5... | collective-permute-start | bytes 3145736 | tf_op jit(solution)/shard_map/ppermute | solution.py:37
  550.8 29.5 %collective-permute-start.44 = (bf16[256,512]{1,0:T(8,128)(2,1)S(1)}, bf16[256,512]{1,0:T(8,128)(2,1)S(1)}, u32[]{:S(2)}, u32[]{:S(2)}) collective-permute-start(bf16[256,512]{1,0:T(8,128)(2,1)S(1)} %copy-done.41), channel_id=1, source_target_pairs={{0,8},{4,12},{8,0},{12,4},{16,24},{20,28},{24,16},{28,20},{1,9},{5... | collective-permute-start | bytes 786440 | tf_op jit(solution)/shard_map/ppermute | solution.py:37
  551.9 34.9 %collective-permute-start.43 = (bf16[256,768]{1,0:T(8,128)(2,1)}, bf16[256,768]{1,0:T(8,128)(2,1)}, u32[]{:S(2)}, u32[]{:S(2)}) collective-permute-start(bf16[256,768]{1,0:T(8,128)(2,1)} %get-tuple-element.120), channel_id=1, source_target_pairs={{0,16},{4,20},{8,24},{12,28},{16,0},{20,4},{24,8},{28,12},{1,17},{... | collective-permute-start | bytes 1179656 | tf_op jit(solution)/shard_map/ppermute | solution.py:37
  553.8 29.9 %collective-permute-start.46 = (bf16[256,512]{1,0:T(8,128)(2,1)S(1)}, bf16[256,512]{1,0:T(8,128)(2,1)}, u32[]{:S(2)}, u32[]{:S(2)}) collective-permute-start(bf16[256,512]{1,0:T(8,128)(2,1)S(1)} %add_convert_fusion.5), channel_id=1, source_target_pairs={{0,16},{4,20},{8,24},{12,28},{16,0},{20,4},{24,8},{28,12},{1,17},{... | collective-permute-start | bytes 786440 | tf_op jit(solution)/shard_map/ppermute | solution.py:37
  562.0 26.3 %collective-permute-start.42 = (bf16[256,768]{1,0:T(8,128)(2,1)}, bf16[256,768]{1,0:T(8,128)(2,1)}, u32[]{:S(2)}, u32[]{:S(2)}) collective-permute-start(bf16[256,768]{1,0:T(8,128)(2,1)} %add_convert_fusion.4), channel_id=1, source_target_pairs={{0,8},{4,12},{8,0},{12,4},{16,24},{20,28},{24,16},{28,20},{1,9},{5... | collective-permute-start | bytes 1179656 | tf_op jit(solution)/shard_map/ppermute | solution.py:37
  580.3 26.1 %collective-permute-start.52 = (bf16[256,2048]{1,0:T(8,128)(2,1)S(1)}, bf16[256,2048]{1,0:T(8,128)(2,1)}, u32[]{:S(2)}, u32[]{:S(2)}) collective-permute-start(bf16[256,2048]{1,0:T(8,128)(2,1)S(1)} %add_convert_fusion), channel_id=1, source_target_pairs={{0,16},{4,20},{8,24},{12,28},{16,0},{20,4},{24,8},{28,12},{1,17},{... | collective-permute-start | bytes 3145736 | tf_op jit(solution)/shard_map/ppermute | solution.py:37
  583.8 41.8 %collective-permute-start.49 = (bf16[256,2048]{1,0:T(8,128)(2,1)}, bf16[256,2048]{1,0:T(8,128)(2,1)}, u32[]{:S(2)}, u32[]{:S(2)}) collective-permute-start(bf16[256,2048]{1,0:T(8,128)(2,1)} %get-tuple-element.130), channel_id=1, source_target_pairs={{0,16},{4,20},{8,24},{12,28},{16,0},{20,4},{24,8},{28,12},{1,17},{... | collective-permute-start | bytes 3145736 | tf_op jit(solution)/shard_map/ppermute | solution.py:37
  586.8 38.8 %collective-permute-start.48 = (bf16[256,2048]{1,0:T(8,128)(2,1)S(1)}, bf16[256,2048]{1,0:T(8,128)(2,1)S(1)}, u32[]{:S(2)}, u32[]{:S(2)}) collective-permute-start(bf16[256,2048]{1,0:T(8,128)(2,1)S(1)} %copy-done.7), channel_id=1, source_target_pairs={{0,8},{4,12},{8,0},{12,4},{16,24},{20,28},{24,16},{28,20},{1,9},{5... | collective-permute-start | bytes 3145736 | tf_op jit(solution)/shard_map/ppermute | solution.py:37
  (51 other events, 914.6 us)

commit v3 on v2

--- a/solution.py
+++ b/solution.py
@@ -550,26 +550,27 @@
     mixture[...] = jnp.where(row < HD, parts[0], parts[1]).T.astype(BF16)
 
 
-def attend_specs(order, queries, group_pairs):
+def attend_specs(order, queries, pieces, group_pairs):
     seqs = order.shape[0]
     rows = queries.shape[0] // seqs
     tiles = rows // BLK
     grid = (seqs, 2, group_pairs, tiles)
     q_spec = pl.BlockSpec((BLK, LANES), lambda s, h, g, t: (s * tiles + t, h * group_pairs + g))
     kv_spec = pl.BlockSpec((rows, 2 * LANES), lambda s, h, g, t: (s, 0))
+    kv_ins = [pl.BlockSpec((None, rows, 2 * LANES), lambda s, h, g, t, r=r: (r, s, 0)) for r in range(pieces.shape[0])]
     log_spec = pl.BlockSpec((None, 2, BLK), lambda s, h, g, t: (h * group_pairs + g, 0, s * tiles + t))
-    return grid, q_spec, kv_spec, log_spec
+    return grid, q_spec, kv_spec, kv_ins, log_spec
 
 
 def attend(order, queries, pieces):
     rows, q_width = queries.shape
     pairs = q_width // LANES
-    grid, q_spec, kv_spec, log_spec = attend_specs(order, queries, pairs // 2)
-    keys = rows * len(pieces) // order.shape[0]
+    grid, q_spec, _, kv_ins, log_spec = attend_specs(order, queries, pieces, pairs // 2)
+    keys = rows * pieces.shape[0] // order.shape[0]
     return pl.pallas_call(
-        functools.partial(attend_body, len(pieces)),
+        functools.partial(attend_body, pieces.shape[0]),
         grid=grid,
-        in_specs=[pl.BlockSpec(memory_space=pltpu.SMEM), q_spec] + [kv_spec] * len(pieces),
+        in_specs=[pl.BlockSpec(memory_space=pltpu.SMEM), q_spec] + kv_ins,
         out_specs=[q_spec, log_spec],
         out_shape=[jax.ShapeDtypeStruct((rows, q_width), BF16), jax.ShapeDtypeStruct((pairs, 2, rows), F32)],
         compiler_params=params(4),
@@ -577,7 +578,7 @@
             flops=8 * rows * keys * q_width * 2, bytes_accessed=8 * rows * q_width, transcendentals=rows * keys * q_width // HD
         ),
         name="attend",
-    )(order, queries, *pieces)
+    )(order, queries, *[pieces] * pieces.shape[0])
 
 
 def attend_back_body(count, order, query_ref, grad_ref, logs, *rest):
@@ -639,22 +640,22 @@
 def attend_back(order, queries, grads, logs, pieces):
     rows, q_width = queries.shape
     pairs = q_width // LANES
-    grid, q_spec, kv_spec, log_spec = attend_specs(order, queries, pairs // 2)
-    keys = rows * len(pieces) // order.shape[0]
+    grid, q_spec, kv_spec, kv_ins, log_spec = attend_specs(order, queries, pieces, pairs // 2)
+    keys = rows * pieces.shape[0] // order.shape[0]
     return pl.pallas_call(
-        functools.partial(attend_back_body, len(pieces)),
+        functools.partial(attend_back_body, pieces.shape[0]),
         grid=grid,
-        in_specs=[pl.BlockSpec(memory_space=pltpu.SMEM), q_spec, q_spec, log_spec] + [kv_spec] * len(pieces),
-        out_specs=[q_spec] + [kv_spec] * len(pieces),
+        in_specs=[pl.BlockSpec(memory_space=pltpu.SMEM), q_spec, q_spec, log_spec] + kv_ins,
+        out_specs=[q_spec] + [kv_spec] * pieces.shape[0],
         out_shape=[jax.ShapeDtypeStruct((rows, q_width), F32)]
-        + [jax.ShapeDtypeStruct((rows, 2 * LANES), F32 if r % 2 == 0 else BF16) for r in range(len(pieces))],
+        + [jax.ShapeDtypeStruct((rows, 2 * LANES), F32 if r % 2 == 0 else BF16) for r in range(pieces.shape[0])],
         scratch_shapes=[pltpu.VMEM((keys, LANES), F32), pltpu.VMEM((keys, LANES), F32)],
         compiler_params=params(4),
         cost_estimate=pl.CostEstimate(
             flops=20 * rows * keys * q_width * 2, bytes_accessed=12 * rows * q_width, transcendentals=rows * keys * q_width // HD
         ),
         name="attend_back",
-    )(order, queries, grads, logs, *pieces)
+    )(order, queries, grads, logs, *[pieces] * pieces.shape[0])
 
 
 def line_steps(rows):
@@ -898,6 +899,193 @@
     return (d_hidden[own, :] + pulled).astype(BF16), None, gains
 
 
+def front_fits():
+    return lax.axis_size("shard") == 2 and lax.axis_size("context") == 4
+
+
+def front_body(*refs):
+    tokens, gain_piece, cosine, sine, w_query, w_key, w_value, w_output = refs[:8]
+    normed, queries, kv, weight, output, gains = refs[8:14]
+    local_sem, send, recv = refs[14:]
+    me = plane_index()
+    extent = weight.shape[0] // 8
+    q_width = queries.shape[1]
+    k_width = kv.shape[2] // 2
+    context, shard = lax.axis_index("context"), lax.axis_index("shard")
+    peers = {1: {"context": context ^ 1}, 2: {"context": context ^ 2}, 4: {"shard": shard ^ 1}}
+    mesh_ids = pl.DeviceIdType.MESH
+    barrier = pltpu.get_barrier_semaphore()
+    for bit in (1, 2, 4):
+        pl.semaphore_signal(barrier, inc=1, device_id=peers[bit], device_id_type=mesh_ids)
+
+    def start(r):
+        return pl.multiple_of((me ^ r) * extent, extent)
+
+    def qkv_at(r, part=None):
+        size = extent if part is None else extent // 2
+        base = start(r) + (part or 0) * size
+        return weight.at[pl.ds(pl.multiple_of(base, size), size)]
+
+    def output_at(r, part=None):
+        columns = pl.ds(start(r), extent)
+        if part is None:
+            return output.at[:, columns]
+        size = output.shape[0] // 2
+        return output.at[pl.ds(part * size, size), columns]
+
+    def gains_at(r):
+        return gains.at[:, pl.ds(start(r), extent)]
+
+    spots = {}
+
+    def remote(name, ref, bit, target=None):
+        index = spots.setdefault(name, len(spots))
+        return pltpu.make_async_remote_copy(
+            src_ref=ref,
+            dst_ref=ref if target is None else target,
+            send_sem=send.at[index],
+            recv_sem=recv.at[index],
+            device_id=peers[bit],
+            device_id_type=mesh_ids,
+        )
+
+    locals_ = [
+        pltpu.make_async_copy(gain_piece, gains_at(0), local_sem.at[0]),
+        pltpu.make_async_copy(w_query, weight.at[pl.ds(start(0), extent), pl.ds(0, q_width)], local_sem.at[1]),
+        pltpu.make_async_copy(w_key, weight.at[pl.ds(start(0), extent), pl.ds(q_width, k_width)], local_sem.at[2]),
+        pltpu.make_async_copy(
+            w_value, weight.at[pl.ds(start(0), extent), pl.ds(q_width + k_width, k_width)], local_sem.at[3]
+        ),
+        pltpu.make_async_copy(w_output, output_at(0), local_sem.at[4]),
+    ]
+    for copy in locals_:
+        copy.start()
+
+    begun = []
+
+    def begin(copy):
+        copy.start()
+        begun.append(copy)
+        return copy
+
+    pl.semaphore_wait(barrier, 3)
+    locals_[0].wait()
+    gain_in = [begin(remote("g2", gains_at(0), 2)), begin(remote("g4", gains_at(0), 4))]
+    gain_core = [begin(remote("gc0", gains_at(0), 1))]
+    for copy in locals_[1:4]:
+        copy.wait()
+    near, far = begin(remote("q2", qkv_at(0), 2)), begin(remote("q4", qkv_at(0), 4))
+    core = [begin(remote("qc0", qkv_at(0), 1))]
+    locals_[4].wait()
+    out_near, out_far = begin(remote("o2", output_at(0), 2)), begin(remote("o4", output_at(0), 4))
+    out_core = [begin(remote("oc0", output_at(0), 1))]
+
+    gain_in[0].wait_recv()
+    gain_in[1].wait_recv()
+    diagonal = begin(remote("g6", gains_at(4), 2))
+    gain_core += [begin(remote("gc2", gains_at(2), 1)), begin(remote("gc4", gains_at(4), 1))]
+    diagonal.wait_recv()
+    gain_core.append(begin(remote("gc6", gains_at(6), 1)))
+    for copy in gain_core:
+        copy.wait_recv()
+
+    rows = tokens.shape[0]
+    tile = 128
+
+    def norm(i, carry):
+        spot = pl.ds(pl.multiple_of(i * tile, tile), tile)
+        values = tokens[spot, :].astype(F32)
+        normed[spot, :] = (values * mean_square(values) * gains[0:1, :]).astype(BF16)
+        return carry
+
+    lax.fori_loop(0, rows // tile, norm, 0)
+
+    far.wait_recv()
+    cross = [begin(remote("q6a", qkv_at(4, 0), 2))]
+    core.append(begin(remote("qc4", qkv_at(4), 1)))
+    near.wait_recv()
+    cross.append(begin(remote("q6b", qkv_at(2, 1), 4)))
+    core.append(begin(remote("qc2", qkv_at(2), 1)))
+    cross[0].wait_recv()
+    cross[1].wait_recv()
+    core.append(begin(remote("qc6", qkv_at(6), 1)))
+    out_far.wait_recv()
+    out_cross = [begin(remote("o6a", output_at(4, 0), 2))]
+    out_core.append(begin(remote("oc4", output_at(4), 1)))
+    out_near.wait_recv()
+    out_cross.append(begin(remote("o6b", output_at(2, 1), 4)))
+    out_core.append(begin(remote("oc2", output_at(2), 1)))
+    for copy in core:
+        copy.wait_recv()
+
+    lane = lax.broadcasted_iota(jnp.int32, (1, LANES), 1)
+
+    def rotated(part, spot):
+        return part * cosine[spot, :] + turned(part, lane, 1.0) * sine[spot, :]
+
+    def keys(i, carry):
+        spot = pl.ds(pl.multiple_of(i * 256, 256), 256)
+        part = jnp.dot(normed[spot, :], weight[:, q_width:], preferred_element_type=F32)
+        kv[0, spot, :k_width] = rotated(part[:, :k_width], spot).astype(BF16)
+        kv[0, spot, k_width:] = part[:, k_width:].astype(BF16)
+        return carry
+
+    lax.fori_loop(0, rows // 256, keys, 0)
+    kv_near = begin(remote("k2", kv.at[0], 2, kv.at[2]))
+    kv_core = begin(remote("k1", kv.at[0], 1, kv.at[1]))
+
+    def query(i, carry):
+        spot = pl.ds(pl.multiple_of(i * 256, 256), 256)
+        part = jnp.dot(normed[spot, :], weight[:, :q_width], preferred_element_type=F32)
+        for base in range(0, q_width, LANES):
+            turned_part = rotated(part[:, base : base + LANES], spot).astype(BF16)
+            queries[spot, base : base + LANES] = (turned_part * SCORE_SCALE).astype(BF16)
+        return carry
+
+    lax.fori_loop(0, rows // 256, query, 0)
+    kv_near.wait_recv()
+    kv_last = begin(remote("k3", kv.at[2], 1, kv.at[3]))
+    out_cross[0].wait_recv()
+    out_cross[1].wait_recv()
+    out_core.append(begin(remote("oc6", output_at(6), 1)))
+    for copy in out_core:
+        copy.wait_recv()
+    kv_core.wait_recv()
+    kv_last.wait_recv()
+    for copy in begun:
+        copy.wait_send()
+
+
+def front(tokens, gains, cosine, sine, w_query, w_key, w_value, w_output):
+    rows, width = tokens.shape
+    q_width, k_width = w_query.shape[1], w_key.shape[1]
+    total = q_width + 2 * k_width
+    vmem = pl.BlockSpec(memory_space=pltpu.VMEM)
+    return pl.pallas_call(
+        front_body,
+        in_specs=[vmem] * 4 + [ANYWHERE] * 4,
+        out_specs=[vmem] * 6,
+        out_shape=[
+            jax.ShapeDtypeStruct((rows, width), BF16),
+            jax.ShapeDtypeStruct((rows, q_width), BF16),
+            jax.ShapeDtypeStruct((4, rows, 2 * k_width), BF16),
+            jax.ShapeDtypeStruct((width, total), BF16),
+            jax.ShapeDtypeStruct((w_output.shape[0], width), BF16),
+            jax.ShapeDtypeStruct((8, width), F32),
+        ],
+        scratch_shapes=[
+            pltpu.SemaphoreType.DMA((5,)),
+            pltpu.SemaphoreType.DMA((27,)),
+            pltpu.SemaphoreType.DMA((27,)),
+        ],
+        compiler_params=pltpu.CompilerParams(collective_id=6, has_side_effects=True, vmem_limit_bytes=VMEM_BYTES),
+        cost_estimate=pl.CostEstimate(
+            flops=2 * rows * width * total, bytes_accessed=10 * rows * width, transcendentals=0
+        ),
+        name="front",
+    )(tokens, gains, cosine, sine, w_query, w_key, w_value, w_output)
+
+
 def unique_arrays(pairs):
     arrays, plan = [], []
     for left, right, low, high in pairs:
@@ -1112,16 +1300,25 @@
     units = w_down.shape[0]
     half = units // 2
 
-    gains = gather_small(jnp.stack([norm_attn, norm_ffn])).reshape(2, width)
-    gain_attn, gain_ffn = gains[0:1], gains[1:2]
-    w_qkv = jnp.concatenate([w_query, w_key, w_value], axis=1)
-    qkv_pieces, output_pieces = gather_pair(w_qkv, w_output)
     cosine, sine = rope_tables(block_order, local_len)
-    normed, queries, keys_values = project_qkv(token_rows, gain_attn, cosine, sine, qkv_pieces, q_width)
-    kv_pieces = gather_context(keys_values)
-    early, late = [qkv_pieces[-2], output_pieces[-2], output_pieces[size // 2]], [kv_pieces[-2]]
+    if front_fits():
+        gain_piece = jnp.pad(jnp.stack([norm_attn, norm_ffn]).astype(F32), ((0, 6), (0, 0)))
+        normed, queries, kv_pieces, w_qkv, w_out, gains = front(
+            token_rows, gain_piece, cosine, sine, w_query, w_key, w_value, w_output
+        )
+        qkv_pieces, output_pieces = [w_qkv], [w_out]
+        early, late = [queries], [queries]
+        gain_attn, gain_ffn = gains[0:1], gains[1:2]
+    else:
+        gains = gather_small(jnp.stack([norm_attn, norm_ffn])).reshape(2, width)
+        gain_attn, gain_ffn = gains[0:1], gains[1:2]
+        w_qkv = jnp.concatenate([w_query, w_key, w_value], axis=1)
+        qkv_pieces, output_pieces = gather_pair(w_qkv, w_output)
+        normed, queries, keys_values = project_qkv(token_rows, gain_attn, cosine, sine, qkv_pieces, q_width)
+        kv_pieces = jnp.stack(gather_context(keys_values))
+        early, late = [qkv_pieces[-2]], [kv_pieces]
+        output_pieces = widened(output_pieces)
     mixture, logs = attend(block_order, queries, kv_pieces)
-    output_pieces = widened(output_pieces)
     branch = gathered_matmul(mixture, output_pieces, 1, False)
     normed_ffn, hidden = line_sum(branch, [token_rows, gain_ffn], finish_attention, True, False, 0)
     extent = width // size

time: 636 us -> 638 us (level)
  the two profiles are of different devices: /device:TPU:24 before, /device:TPU:0 now
where the time goes in v3:
time: 638 us; the launch traced here: 633 us
  Pallas kernels  377 us (59%)
  waiting for transfers between devices  156 us (24%)
  starting transfers between devices  47.7 us (7%)
  other arithmetic  34.7 us (5%)
  local copies, waits for them, and re-layouts  15.8 us (2%)
    pallas_call x3, Pallas kernels, line_sum(): pl.pallas_call(functools.partial(line_body, finish, keep_state, gain_sum,...  204 us
    ppermute x40, waiting for transfers between devices, swap(): return lax.ppermute(value, axes, [(i, i ^ bit) for i in range(size)])  144 us
    pallas_call x1, Pallas kernels, ffn(): pl.pallas_call(body, grid=(rows // row_tile, units // tile), in_specs=[ro...  44.3 us
    pallas_call x1, Pallas kernels, front(): pl.pallas_call(front_body, in_specs=[vmem] * 4 + [ANYWHERE] * 4, out_spec...  44.3 us
    ppermute x40, starting transfers between devices, swap(): return lax.ppermute(value, axes, [(i, i ^ bit) for i in range(size)])  38.7 us
    pallas_call x1, Pallas kernels, attend_back(): pl.pallas_call(functools.partial(attend_back_body, pieces.shape[0]), grid...  35.6 us
    pallas_call x1, Pallas kernels, attend(): pl.pallas_call(functools.partial(attend_body, pieces.shape[0]), grid=grid...  21.3 us
  transfers between devices with their start and end apart: 49, of which 13 were waited for; matrix products, arithmetic and copies ran while one was open for 6% of the time, Pallas kernels for 27%

profile of v3, /device:TPU:0, one launch (start us, length us, event | category | flops | bytes accessed | tf_op | source)
XLA Modules:
  0.0 632.8 jit_solution(4375222583845772469)
XLA Ops:
  2.8 1.3 fusion.20
  4.1 1.8 multiply_sine_fusion
  6.6 44.3 %front.1 = (bf16[512,2048]{1,0:T(8,128)(2,1)}, bf16[512,512]{1,0:T(8,128)(2,1)}, bf16[4,512,256]{2,1,0:T(8,128)(2,1)}, bf16[2048,768]{1,0:T(8,128)(2,1)}, bf16[512,2048]{1,0:T(8,128)(2,1)}, /*index=5*/f32[8,2048]{1,0:T(8,128)}) custom-call(bf16[512,2048]{1,0:T(8,128)(2,1)} %bitcast.36, f32[8,256]{1,0:T(8,128)} %fusion.6.refs_1_, ...), custom_call_target="tpu_custom_call" | custom-call | flops 1610612736 | bytes 10485760 | tf_op jit(solution)/shard_map/front/pallas_call | solution.py:1064
  50.8 1.2 collective-permute-start.9
  52.9 1.1 collective-permute-start.7
  54.9 1.1 collective-permute-start.1
  56.1 21.3 %attend.1 = (bf16[512,512]{1,0:T(8,128)(2,1)}, f32[4,2,512]{2,1,0:T(2,128)}) custom-call(s32[1,8]{1,0:T(1,128)} %order.3, bf16[512,512]{1,0:T(8,128)(2,1)} %get-tuple-element.80.query_ref, bf16[4,512,256]{2,1,0:T(8,128)(2,1)} %get-tuple-element.81.rest_0_.rest_1_.rest_2_.rest_3_, bf16[4,512,256]{2,1,0:T(8,128)(2,1)} %get-tuple-element.81.rest_0_.rest_1_.rest_2_.rest_3_, ...), custom_call_target="tpu_custom_call" | custom-call | flops 8589934592 | bytes 2097152 | tf_op jit(solution)/shard_map/attend/pallas_call | solution.py:570
  78.3 5.0 shard_map.203.refs_0_
  83.3 1.5 fusion.22
  84.8 63.4 %shard_map.204 = (bf16[512,2048]{1,0:T(8,128)(2,1)}, f32[256,2048]{1,0:T(8,128)}) custom-call(bf16[512,2048]{1,0:T(8,128)(2,1)} %shard_map.203.refs_0_, bf16[512,2048]{1,0:T(8,128)(2,1)} %bitcast.37, f32[1,2048]{1,0:T(1,128)} %get-tuple-element.181.refs_2_.refs_3_), custom_call_target="tpu_custom_call" | custom-call | bytes 104857600 | tf_op jit(solution)/shard_map/pallas_call | solution.py:852
  148.3 1.2 collective-permute-start.11
  150.4 1.1 collective-permute-start.4
  152.4 1.1 collective-permute-start.2
  153.6 9.9 %collective-permute-done.11.refs_15_ = bf16[2048,128]{1,0:T(8,128)(2,1)} collective-permute-done((bf16[2048,128]{1,0:T(8,128)(2,1)}, bf16[2048,128]{1,0:T(8,128)(2,1)}, u32[]{:S(2)}, u32[]{:S(2)}) %collective-permute-start.11) | collective-permute-done | bytes 524320 | tf_op jit(solution)/shard_map/ppermute | solution.py:37
  163.4 1.1 collective-permute-start.8
  164.6 3.4 multiply_convert_fusion.d_ffn.refs_8_
  168.0 36.9 %collective-permute-done.8.refs_11_ = bf16[2048,128]{1,0:T(8,128)(2,1)S(1)} collective-permute-done((bf16[2048,128]{1,0:T(8,128)(2,1)}, bf16[2048,128]{1,0:T(8,128)(2,1)S(1)}, u32[]{:S(2)}, u32[]{:S(2)}) %collective-permute-start.8) | collective-permute-done | bytes 524320 | tf_op jit(solution)/shard_map/ppermute | solution.py:37
  206.7 44.3 %feed_forward.1 = (bf16[512,2048]{1,0:T(8,128)(2,1)}, bf16[512,2048]{1,0:T(8,128)(2,1)}, bf16[512,2048]{1,0:T(8,128)(2,1)}, bf16[512,2048]{1,0:T(8,128)(2,1)}, bf16[512,2048]{1,0:T(8,128)(2,1)}) custom-call(bf16[512,2048]{1,0:T(8,128)(2,1)} %get-tuple-element.85.normed.refs_5_, bf16[512,2048]{1,0:T(8,128)(2,1)} %multiply_convert_fusion.d_ffn.refs_8_, ...), custom_call_target="tpu_custom_call" | custom-call | flops 25769803776 | bytes 39845888 | tf_op jit(solution)/shard_map/feed_forward/pallas_call | solution.py:413
  251.0 74.4 %shard_map.205 = (bf16[512,2048]{1,0:T(8,128)(2,1)}, f32[256,2048]{1,0:T(8,128)}, f32[8,2048]{1,0:T(8,128)}, bf16[4,128,2048]{2,1,0:T(8,128)(2,1)}, f32[256,2048...) custom-call(bf16[512,2048]{1,0:T(8,128)(2,1)} %get-tuple-element.94., ...), custom_call_target="tpu_custom_call" | custom-call | bytes 104857600 | tf_op jit(solution)/shard_map/pallas_call | solution.py:852
  325.3 5.1 shard_map.206.grad_ref
  330.5 35.6 %attend_back.1 = (f32[512,512]{1,0:T(8,128)}, f32[512,256]{1,0:T(8,128)}, bf16[512,256]{1,0:T(8,128)(2,1)}, f32[512,256]{1,0:T(8,128)}, bf16[512,256]{1,0:T(8,128)(2,1)}) custom-call(s32[1,8]{1,0:T(1,128)} %order.3, bf16[512,512]{1,0:T(8,128)(2,1)} %get-tuple-element.80.query_ref, bf16[512,512]{1,0:T(8,128)(2,1)} %shard_map.206.grad_ref, ...), custom_call_target="tpu_custom_call" | custom-call | flops 21474836480 | bytes 3145728 | tf_op jit(solution)/shard_map/attend_back/pallas_call | solution.py:645
  368.4 1.2 add_convert_fusion.6
  369.6 1.1 collective-permute-start.20
  370.7 2.6 slice_bitcast_fusion.2
  373.3 2.3 collective-permute-start.13
  375.7 11.3 %collective-permute-done.20 = bf16[512,256]{1,0:T(8,128)(2,1)S(1)} collective-permute-done((bf16[512,256]{1,0:T(8,128)(2,1)S(1)}, bf16[512,256]{1,0:T(8,128)(2,1)S(1)}, u32[]{:S(2)}, u32[]{:S(2)}) %collective-permute-start.20) | collective-permute-done | bytes 262176 | tf_op jit(solution)/shard_map/ppermute | solution.py:37
  387.0 1.9 collective-permute-start.14
  389.8 6.9 %project_qkv_back.1 = (bf16[512,768]{1,0:T(8,128)(2,1)}, bf16[512,2048]{1,0:T(8,128)(2,1)}) custom-call(f32[512,512]{1,0:T(8,128)} %get-tuple-element.103.d_queries, f32[512,256]{1,0:T(8,128)} %convert_add_fusion.4.d_keys_values, f32[512,128]{1,0:T(8,128)} %get-tuple-element.190.refs_2_.cosine, f32[512,128]{1,0:T(8,128)} %get-tuple-element.189.refs_3_.sine, ...), custom_call_target="tpu_custom_call" | custom-call | flops 1610612736 | bytes 7340032 | tf_op jit(solution)/shard_map/project_qkv_back/pallas_call | solution.py:279
  396.7 10.7 %shard_map.207 = (f32[256,768]{1,0:T(8,128)}, f32[256,512]{1,0:T(8,128)}, bf16[256,768]{1,0:T(8,128)(2,1)}, bf16[256,512]{1,0:T(8,128)(2,1)}, bf16[256,768]{1,0:...) custom-call(bf16[512,2048]{1,0:T(8,128)(2,1)} %get-tuple-element.110.refs_0_, ...), custom_call_target="tpu_custom_call" | custom-call | flops 2684354560 | bytes 5242880 | tf_op jit(solution)/shard_map/pallas_call | solution.py:1224
  407.4 66.1 %shard_map.208 = (bf16[512,2048]{1,0:T(8,128)(2,1)}, f32[8,2048]{1,0:T(8,128)}) custom-call(bf16[512,2048]{1,0:T(8,128)(2,1)} %get-tuple-element.113.refs_0_, bf16[512,2048]{1,0:T(8,128)(2,1)} %bitcast.38, f32[256,2048]{1,0:T(8,128)} %get-tuple-element.114.refs_2_, f32[1,2048]{1,0:T(1,128)} %get-tuple-element.180.refs_3_), custom_call_target="tpu_custom_call" | custom-call | bytes 104857600 | tf_op jit(solution)/shard_map/pallas_call | solution.py:852
  474.4 4.1 bitcast_convert_fusion
  478.6 2.2 collective-permute-start.40
  480.8 1.6 collective-permute-start.41
  482.7 2.8 bitcast_dynamic-update-slice_fusion.3
  485.5 1.0 collective-permute-start.25
  486.7 1.1 collective-permute-start.43
  492.0 1.3 collective-permute-start.47
  495.0 1.1 collective-permute-start.31
  496.0 1.1 collective-permute-start.27
  497.9 1.2 collective-permute-start.21
  500.6 30.1 %collective-permute-done.21 = bf16[256,768]{1,0:T(8,128)(2,1)S(1)} collective-permute-done((bf16[256,768]{1,0:T(8,128)(2,1)S(1)}, bf16[256,768]{1,0:T(8,128)(2,1)S(1)}, u32[]{:S(2)}, u32[]{:S(2)}) %collective-permute-start.21) | collective-permute-done | bytes 393248 | tf_op jit(solution)/shard_map/ppermute | solution.py:37
  530.7 1.1 collective-permute-start.35
  533.3 3.0 collective-permute-done.26
  537.4 1.0 copy.25
  538.4 1.1 collective-permute-start.34
  539.5 2.9 add_convert_fusion
  542.9 1.7 add_convert_fusion.1
  544.6 12.6 %collective-permute-done.15 = bf16[128,2048]{1,0:T(8,128)(2,1)S(1)} collective-permute-done((bf16[128,2048]{1,0:T(8,128)(2,1)}, bf16[128,2048]{1,0:T(8,128)(2,1)S(1)}, u32[]{:S(2)}, u32[]{:S(2)}) %collective-permute-start.15) | collective-permute-done | bytes 524320 | tf_op jit(solution)/shard_map/ppermute | solution.py:136
  558.5 20.9 %collective-permute-done.34 = bf16[256,1024]{1,0:T(8,128)(2,1)S(1)} collective-permute-done((bf16[256,1024]{1,0:T(8,128)(2,1)}, bf16[256,1024]{1,0:T(8,128)(2,1)S(1)}, u32[]{:S(2)}, u32[]{:S(2)}) %collective-permute-start.34) | collective-permute-done | bytes 524320 | tf_op jit(solution)/shard_map/ppermute | solution.py:37
  579.4 1.3 collective-permute-start.38
  580.7 1.4 add_bitcast_fusion.1
  583.2 11.0 %collective-permute-done.38 = bf16[256,1024]{1,0:T(8,128)(2,1)S(1)} collective-permute-done((bf16[256,1024]{1,0:T(8,128)(2,1)S(1)}, bf16[256,1024]{1,0:T(8,128)(2,1)S(1)}, u32[]{:S(2)}, u32[]{:S(2)}) %collective-permute-start.38) | collective-permute-done | bytes 524320 | tf_op jit(solution)/shard_map/ppermute | solution.py:37
  594.2 1.3 collective-permute-start.32
  595.5 1.3 add_bitcast_fusion
  596.9 1.8 copy.26
  598.7 1.2 collective-permute-start.22
  599.9 1.9 bitcast_dynamic-update-slice_fusion
  602.6 1.7 collective-permute-start.28
  604.4 6.6 %collective-permute-done.22 = bf16[256,768]{1,0:T(8,128)(2,1)S(1)} collective-permute-done((bf16[256,768]{1,0:T(8,128)(2,1)}, bf16[256,768]{1,0:T(8,128)(2,1)S(1)}, u32[]{:S(2)}, u32[]{:S(2)}) %collective-permute-start.22) | collective-permute-done | bytes 393248 | tf_op jit(solution)/shard_map/ppermute | solution.py:37
  610.9 1.3 convert_add_fusion.3
  613.8 9.4 %collective-permute-done.32 = bf16[256,2048]{1,0:T(8,128)(2,1)} collective-permute-done((bf16[256,2048]{1,0:T(8,128)(2,1)}, bf16[256,2048]{1,0:T(8,128)(2,1)}, u32[]{:S(2)}, u32[]{:S(2)}) %collective-permute-start.32) | collective-permute-done | bytes 1048608 | tf_op jit(solution)/shard_map/ppermute | solution.py:37
  623.1 3.5 convert_add_fusion
  626.6 2.9 collective-permute-done.28
  629.6 3.0 convert_add_fusion.1
  (133 shorter events, 29.6 us)
Async XLA Ops:
  4.1 47.9 %copy-start.11 = (bf16[2048,128]{1,0:T(8,128)(2,1)}, bf16[2048,128]{1,0:T(8,128)(2,1)S(1)}, u32[]{:S(2)}) copy-start(bf16[2048,128]{1,0:T(8,128)(2,1)S(1)} %get-tuple-element.92.refs_12_) | copy-start | bytes 1572868
  4.1 73.2 %copy-start.12 = (bf16[2048,128]{1,0:T(8,128)(2,1)}, bf16[2048,128]{1,0:T(8,128)(2,1)S(1)}, u32[]{:S(2)}) copy-start(bf16[2048,128]{1,0:T(8,128)(2,1)S(1)} %get-tuple-element.90.refs_8_) | copy-start | bytes 1572868
  50.8 26.5 %collective-permute-start.9 = (bf16[2048,128]{1,0:T(8,128)(2,1)S(1)}, bf16[2048,128]{1,0:T(8,128)(2,1)}, u32[]{:S(2)}, u32[]{:S(2)}) collective-permute-start(bf16[2048,128]{1,0:T(8,128)(2,1)S(1)} %get-tuple-element.92.refs_12_), channel_id=1, source_target_pairs={{0,8},{4,12},{8,0},{12,4},{16,24},{20,28},{24,16},{28,20},{1,9},{5... | collective-permute-start | bytes 1572872 | tf_op jit(solution)/shard_map/ppermute | solution.py:37
  52.0 99.5 %collective-permute-start.10 = (bf16[2048,128]{1,0:T(8,128)(2,1)S(1)}, bf16[2048,128]{1,0:T(8,128)(2,1)}, u32[]{:S(2)}, u32[]{:S(2)}) collective-permute-start(bf16[2048,128]{1,0:T(8,128)(2,1)S(1)} %get-tuple-element.92.refs_12_), channel_id=1, source_target_pairs={{0,16},{4,20},{8,24},{12,28},{16,0},{20,4},{24,8},{28,12},{1,17},{... | collective-permute-start | bytes 1572872 | tf_op jit(solution)/shard_map/ppermute | solution.py:37
  52.9 97.4 %collective-permute-start.7 = (bf16[2048,128]{1,0:T(8,128)(2,1)S(1)}, bf16[2048,128]{1,0:T(8,128)(2,1)}, u32[]{:S(2)}, u32[]{:S(2)}) collective-permute-start(bf16[2048,128]{1,0:T(8,128)(2,1)S(1)} %get-tuple-element.90.refs_8_), channel_id=1, source_target_pairs={{0,16},{4,20},{8,24},{12,28},{16,0},{20,4},{24,8},{28,12},{1,17},{... | collective-permute-start | bytes 1572872 | tf_op jit(solution)/shard_map/ppermute | solution.py:37
  54.1 94.2 %collective-permute-start.3 = (bf16[256,2048]{1,0:T(8,128)(2,1)}, bf16[256,2048]{1,0:T(8,128)(2,1)}, u32[]{:S(2)}, u32[]{:S(2)}) collective-permute-start(bf16[256,2048]{1,0:T(8,128)(2,1)} %refs_4_.3), channel_id=1, source_target_pairs={{0,8},{4,12},{8,0},{12,4},{16,24},{20,28},{24,16},{28,20},{1,9},{5... | collective-permute-start | bytes 3145736 | tf_op jit(solution)/shard_map/ppermute | solution.py:37
  54.9 94.5 %collective-permute-start.1 = (bf16[256,2048]{1,0:T(8,128)(2,1)}, bf16[256,2048]{1,0:T(8,128)(2,1)}, u32[]{:S(2)}, u32[]{:S(2)}) collective-permute-start(bf16[256,2048]{1,0:T(8,128)(2,1)} %refs_0_.1), channel_id=1, source_target_pairs={{0,16},{4,20},{8,24},{12,28},{16,0},{20,4},{24,8},{28,12},{1,17},{... | collective-permute-start | bytes 3145736 | tf_op jit(solution)/shard_map/ppermute | solution.py:37
  77.4 75.0 %collective-permute-start.6 = (bf16[2048,128]{1,0:T(8,128)(2,1)S(1)}, bf16[2048,128]{1,0:T(8,128)(2,1)}, u32[]{:S(2)}, u32[]{:S(2)}) collective-permute-start(bf16[2048,128]{1,0:T(8,128)(2,1)S(1)} %get-tuple-element.90.refs_8_), channel_id=1, source_target_pairs={{0,8},{4,12},{8,0},{12,4},{16,24},{20,28},{24,16},{28,20},{1,9},{5... | collective-permute-start | bytes 1572872 | tf_op jit(solution)/shard_map/ppermute | solution.py:37
  148.3 15.2 %collective-permute-start.11 = (bf16[2048,128]{1,0:T(8,128)(2,1)}, bf16[2048,128]{1,0:T(8,128)(2,1)}, u32[]{:S(2)}, u32[]{:S(2)}) collective-permute-start(bf16[2048,128]{1,0:T(8,128)(2,1)} %collective-permute-done.9.refs_13_), channel_id=1, source_target_pairs={{0,16},{4,20},{8,24},{12,28},{16,0},{20,4},{24,8},{28,12},{1,17},{... | collective-permute-start | bytes 1572872 | tf_op jit(solution)/shard_map/ppermute | solution.py:37
  149.5 55.4 %collective-permute-start = (bf16[256,2048]{1,0:T(8,128)(2,1)}, bf16[256,2048]{1,0:T(8,128)(2,1)}, u32[]{:S(2)}, u32[]{:S(2)}) collective-permute-start(bf16[256,2048]{1,0:T(8,128)(2,1)} %refs_0_.1), channel_id=1, source_target_pairs={{0,8},{4,12},{8,0},{12,4},{16,24},{20,28},{24,16},{28,20},{1,9},{5... | collective-permute-start | bytes 3145736 | tf_op jit(solution)/shard_map/ppermute | solution.py:37
  150.4 54.5 %collective-permute-start.4 = (bf16[256,2048]{1,0:T(8,128)(2,1)}, bf16[256,2048]{1,0:T(8,128)(2,1)}, u32[]{:S(2)}, u32[]{:S(2)}) collective-permute-start(bf16[256,2048]{1,0:T(8,128)(2,1)} %refs_4_.3), channel_id=1, source_target_pairs={{0,16},{4,20},{8,24},{12,28},{16,0},{20,4},{24,8},{28,12},{1,17},{... | collective-permute-start | bytes 3145736 | tf_op jit(solution)/shard_map/ppermute | solution.py:37
  151.5 54.2 %collective-permute-start.5 = (bf16[256,2048]{1,0:T(8,128)(2,1)}, bf16[256,2048]{1,0:T(8,128)(2,1)}, u32[]{:S(2)}, u32[]{:S(2)}) collective-permute-start(bf16[256,2048]{1,0:T(8,128)(2,1)} %collective-permute-done.3.refs_5_), channel_id=1, source_target_pairs={{0,16},{4,20},{8,24},{12,28},{16,0},{20,4},{24,8},{28,12},{1,17},{... | collective-permute-start | bytes 3145736 | tf_op jit(solution)/shard_map/ppermute | solution.py:37
  152.4 53.3 %collective-permute-start.2 = (bf16[256,2048]{1,0:T(8,128)(2,1)}, bf16[256,2048]{1,0:T(8,128)(2,1)S(1)}, u32[]{:S(2)}, u32[]{:S(2)}) collective-permute-start(bf16[256,2048]{1,0:T(8,128)(2,1)} %collective-permute-done.1.refs_2_), channel_id=1, source_target_pairs={{0,8},{4,12},{8,0},{12,4},{16,24},{20,28},{24,16},{28,20},{1,9},{5... | collective-permute-start | bytes 3145736 | tf_op jit(solution)/shard_map/ppermute | solution.py:37
  163.4 41.4 %collective-permute-start.8 = (bf16[2048,128]{1,0:T(8,128)(2,1)}, bf16[2048,128]{1,0:T(8,128)(2,1)S(1)}, u32[]{:S(2)}, u32[]{:S(2)}) collective-permute-start(bf16[2048,128]{1,0:T(8,128)(2,1)} %collective-permute-done.7.refs_10_), channel_id=1, source_target_pairs={{0,8},{4,12},{8,0},{12,4},{16,24},{20,28},{24,16},{28,20},{1,9},{5... | collective-permute-start | bytes 1572872 | tf_op jit(solution)/shard_map/ppermute | solution.py:37
  366.0 2.4 collective-permute-start.19
  366.2 7.2 %collective-permute-start.18 = (bf16[512,256]{1,0:T(8,128)(2,1)}, bf16[512,256]{1,0:T(8,128)(2,1)S(1)}, u32[]{:S(2)}, u32[]{:S(2)}) collective-permute-start(bf16[512,256]{1,0:T(8,128)(2,1)} %get-tuple-element.105), channel_id=1, source_target_pairs={{0,4},{4,0},{8,12},{12,8},{1,5},{5,1},{9,13},{13,9},{2,6},{6,2},{1... | collective-permute-start | bytes 786440 | tf_op jit(solution)/shard_map/ppermute | solution.py:37
  366.6 121.3 %collective-permute-start.33 = (bf16[256,1024]{1,0:T(8,128)(2,1)}, bf16[256,1024]{1,0:T(8,128)(2,1)S(1)}, u32[]{:S(2)}, u32[]{:S(2)}) collective-permute-start(bf16[256,1024]{1,0:T(8,128)(2,1)} %get-tuple-element.137), channel_id=1, source_target_pairs={{0,16},{4,20},{8,24},{12,28},{16,0},{20,4},{24,8},{28,12},{1,17},{... | collective-permute-start | bytes 1572872 | tf_op jit(solution)/shard_map/ppermute | solution.py:37
  367.5 122.1 %collective-permute-start.37 = (bf16[256,1024]{1,0:T(8,128)(2,1)}, bf16[256,1024]{1,0:T(8,128)(2,1)S(1)}, u32[]{:S(2)}, u32[]{:S(2)}) collective-permute-start(bf16[256,1024]{1,0:T(8,128)(2,1)} %get-tuple-element.145), channel_id=1, source_target_pairs={{0,8},{4,12},{8,0},{12,4},{16,24},{20,28},{24,16},{28,20},{1,9},{5... | collective-permute-start | bytes 1572872 | tf_op jit(solution)/shard_map/ppermute | solution.py:37
  368.4 20.5 %copy-start.8 = (f32[512,256]{1,0:T(8,128)S(1)}, f32[512,256]{1,0:T(8,128)}, u32[]{:S(2)}) copy-start(f32[512,256]{1,0:T(8,128)} %get-tuple-element.104) | copy-start | bytes 1572868
  369.6 17.4 %collective-permute-start.20 = (bf16[512,256]{1,0:T(8,128)(2,1)S(1)}, bf16[512,256]{1,0:T(8,128)(2,1)S(1)}, u32[]{:S(2)}, u32[]{:S(2)}) collective-permute-start(bf16[512,256]{1,0:T(8,128)(2,1)S(1)} %add_convert_fusion.6), channel_id=1, source_target_pairs={{0,8},{4,12},{8,0},{12,4},{1,9},{5,13},{9,1},{13,5},{2,10},{6,14},... | collective-permute-start | bytes 786440 | tf_op jit(solution)/shard_map/ppermute | solution.py:37
  373.3 105.3 %collective-permute-start.12 = (bf16[128,2048]{1,0:T(8,128)(2,1)}, bf16[128,2048]{1,0:T(8,128)(2,1)}, u32[]{:S(2)}, u32[]{:S(2)}) collective-permute-start(bf16[128,2048]{1,0:T(8,128)(2,1)} %get-tuple-element.173), channel_id=1, source_target_pairs={{0,1},{1,2},{2,3},{3,0},{4,5},{5,6},{6,7},{7,4},{8,9},{9,10},{10,1... | collective-permute-start | bytes 1572872 | tf_op jit(solution)/shard_map/ppermute | solution.py:125
  373.3 105.2 %collective-permute-start.13 = (bf16[128,2048]{1,0:T(8,128)(2,1)}, bf16[128,2048]{1,0:T(8,128)(2,1)}, u32[]{:S(2)}, u32[]{:S(2)}) collective-permute-start(bf16[128,2048]{1,0:T(8,128)(2,1)} %get-tuple-element.175), channel_id=1, source_target_pairs={{0,2},{1,3},{2,0},{3,1},{4,6},{5,7},{6,4},{7,5},{8,10},{9,11},{10,... | collective-permute-start | bytes 1572872 | tf_op jit(solution)/shard_map/ppermute | solution.py:125
  387.0 93.8 %collective-permute-start.14 = (bf16[128,2048]{1,0:T(8,128)(2,1)}, bf16[128,2048]{1,0:T(8,128)(2,1)}, u32[]{:S(2)}, u32[]{:S(2)}) collective-permute-start(bf16[128,2048]{1,0:T(8,128)(2,1)} %get-tuple-element.174), channel_id=1, source_target_pairs={{0,3},{1,0},{2,1},{3,2},{4,7},{5,4},{6,5},{7,6},{8,11},{9,8},{10,9... | collective-permute-start | bytes 1572872 | tf_op jit(solution)/shard_map/ppermute | solution.py:125
  478.5 7.0 %collective-permute-start.39 = (f32[2,2048]{1,0:T(2,128)S(1)}, f32[2,2048]{1,0:T(2,128)S(1)}, u32[]{:S(2)}, u32[]{:S(2)}) collective-permute-start(f32[2,2048]{1,0:T(2,128)S(1)} %pad_maximum_fusion.1), channel_id=1, source_target_pairs={{0,1},{1,2},{2,3},{3,0},{4,5},{5,6},{6,7},{7,4},{8,9},{9,10},{10,1... | collective-permute-start | bytes 49160 | tf_op jit(solution)/shard_map/ppermute | solution.py:149
  478.6 8.0 %collective-permute-start.40 = (f32[2,2048]{1,0:T(2,128)S(1)}, f32[2,2048]{1,0:T(2,128)S(1)}, u32[]{:S(2)}, u32[]{:S(2)}) collective-permute-start(f32[2,2048]{1,0:T(2,128)S(1)} %pad_maximum_fusion.1), channel_id=1, source_target_pairs={{0,2},{1,3},{2,0},{3,1},{4,6},{5,7},{6,4},{7,5},{8,10},{9,11},{10,... | collective-permute-start | bytes 49160 | tf_op jit(solution)/shard_map/ppermute | solution.py:149
  480.8 5.8 collective-permute-start.41
  482.7 11.3 %copy-start.6 = (bf16[256,1024]{1,0:T(8,128)(2,1)S(1)}, bf16[256,1024]{1,0:T(8,128)(2,1)}, u32[]{:S(2)}) copy-start(bf16[256,1024]{1,0:T(8,128)(2,1)} %get-tuple-element.144) | copy-start | bytes 1572868
  485.5 11.7 %copy-start.19 = (bf16[256,512]{1,0:T(8,128)(2,1)S(1)}, bf16[256,512]{1,0:T(8,128)(2,1)}, u32[]{:S(2)}) copy-start(bf16[256,512]{1,0:T(8,128)(2,1)} %get-tuple-element.120) | copy-start | bytes 786436
  485.5 12.4 %copy-start.18 = (bf16[256,768]{1,0:T(8,128)(2,1)S(1)}, bf16[256,768]{1,0:T(8,128)(2,1)}, u32[]{:S(2)}) copy-start(bf16[256,768]{1,0:T(8,128)(2,1)} %get-tuple-element.117) | copy-start | bytes 1179652
  485.5 13.6 %copy-start.14 = (bf16[256,512]{1,0:T(8,128)(2,1)S(1)}, bf16[256,512]{1,0:T(8,128)(2,1)}, u32[]{:S(2)}) copy-start(bf16[256,512]{1,0:T(8,128)(2,1)} %get-tuple-element.121) | copy-start | bytes 786436
  485.5 46.3 %copy-start.13 = (bf16[256,768]{1,0:T(8,128)(2,1)S(1)}, bf16[256,768]{1,0:T(8,128)(2,1)}, u32[]{:S(2)}) copy-start(bf16[256,768]{1,0:T(8,128)(2,1)} %get-tuple-element.116) | copy-start | bytes 1179652
  485.5 13.5 %collective-permute-start.25 = (bf16[256,512]{1,0:T(8,128)(2,1)S(1)}, bf16[256,512]{1,0:T(8,128)(2,1)S(1)}, u32[]{:S(2)}, u32[]{:S(2)}) collective-permute-start(bf16[256,512]{1,0:T(8,128)(2,1)S(1)} %copy-done.20), channel_id=1, source_target_pairs={{0,8},{4,12},{8,0},{12,4},{16,24},{20,28},{24,16},{28,20},{1,9},{5... | collective-permute-start | bytes 786440 | tf_op jit(solution)/shard_map/ppermute | solution.py:37
  486.6 3.8 collective-permute-start.42
  486.7 5.3 collective-permute-start.43
  487.8 5.5 collective-permute-start.44
  489.6 47.7 %copy-start.9 = (f32[256,512]{1,0:T(8,128)S(1)}, f32[256,512]{1,0:T(8,128)}, u32[]{:S(2)}) copy-start(f32[256,512]{1,0:T(8,128)} %get-tuple-element.119) | copy-start | bytes 1572868
  489.6 5.4 collective-permute-start.45
  490.4 5.6 collective-permute-start.46
  492.0 5.1 collective-permute-start.47
  493.3 4.6 collective-permute-start.48
  495.0 43.4 %collective-permute-start.31 = (bf16[256,2048]{1,0:T(8,128)(2,1)}, bf16[256,2048]{1,0:T(8,128)(2,1)}, u32[]{:S(2)}, u32[]{:S(2)}) collective-permute-start(bf16[256,2048]{1,0:T(8,128)(2,1)} %get-tuple-element.133), channel_id=1, source_target_pairs={{0,8},{4,12},{8,0},{12,4},{16,24},{20,28},{24,16},{28,20},{1,9},{5... | collective-permute-start | bytes 3145736 | tf_op jit(solution)/shard_map/ppermute | solution.py:37
  496.0 46.3 %collective-permute-start.27 = (bf16[256,2048]{1,0:T(8,128)(2,1)}, bf16[256,2048]{1,0:T(8,128)(2,1)}, u32[]{:S(2)}, u32[]{:S(2)}) collective-permute-start(bf16[256,2048]{1,0:T(8,128)(2,1)} %get-tuple-element.125), channel_id=1, source_target_pairs={{0,16},{4,20},{8,24},{12,28},{16,0},{20,4},{24,8},{28,12},{1,17},{... | collective-permute-start | bytes 3145736 | tf_op jit(solution)/shard_map/ppermute | solution.py:37
  497.2 35.5 %collective-permute-start.24 = (bf16[256,512]{1,0:T(8,128)(2,1)S(1)}, bf16[256,512]{1,0:T(8,128)(2,1)S(1)}, u32[]{:S(2)}, u32[]{:S(2)}) collective-permute-start(bf16[256,512]{1,0:T(8,128)(2,1)S(1)} %copy-done.19), channel_id=1, source_target_pairs={{0,8},{4,12},{8,0},{12,4},{16,24},{20,28},{24,16},{28,20},{1,9},{5... | collective-permute-start | bytes 786440 | tf_op jit(solution)/shard_map/ppermute | solution.py:37
  497.9 32.8 %collective-permute-start.21 = (bf16[256,768]{1,0:T(8,128)(2,1)S(1)}, bf16[256,768]{1,0:T(8,128)(2,1)S(1)}, u32[]{:S(2)}, u32[]{:S(2)}) collective-permute-start(bf16[256,768]{1,0:T(8,128)(2,1)S(1)} %copy-done.18), channel_id=1, source_target_pairs={{0,16},{4,20},{8,24},{12,28},{16,0},{20,4},{24,8},{28,12},{1,17},{... | collective-permute-start | bytes 1179656 | tf_op jit(solution)/shard_map/ppermute | solution.py:37
  499.1 37.2 %collective-permute-start.26 = (bf16[256,512]{1,0:T(8,128)(2,1)S(1)}, bf16[256,512]{1,0:T(8,128)(2,1)S(1)}, u32[]{:S(2)}, u32[]{:S(2)}) collective-permute-start(bf16[256,512]{1,0:T(8,128)(2,1)S(1)} %add_convert_fusion.5), channel_id=1, source_target_pairs={{0,16},{4,20},{8,24},{12,28},{16,0},{20,4},{24,8},{28,12},{1,17},{... | collective-permute-start | bytes 786440 | tf_op jit(solution)/shard_map/ppermute | solution.py:37
  530.7 26.8 %collective-permute-start.35 = (bf16[256,1024]{1,0:T(8,128)(2,1)}, bf16[256,1024]{1,0:T(8,128)(2,1)}, u32[]{:S(2)}, u32[]{:S(2)}) collective-permute-start(bf16[256,1024]{1,0:T(8,128)(2,1)} %get-tuple-element.140), channel_id=1, source_target_pairs={{0,16},{4,20},{8,24},{12,28},{16,0},{20,4},{24,8},{28,12},{1,17},{... | collective-permute-start | bytes 1572872 | tf_op jit(solution)/shard_map/ppermute | solution.py:37
  532.7 50.2 %collective-permute-start.36 = (bf16[256,1024]{1,0:T(8,128)(2,1)}, bf16[256,1024]{1,0:T(8,128)(2,1)}, u32[]{:S(2)}, u32[]{:S(2)}) collective-permute-start(bf16[256,1024]{1,0:T(8,128)(2,1)} %get-tuple-element.143), channel_id=1, source_target_pairs={{0,8},{4,12},{8,0},{12,4},{16,24},{20,28},{24,16},{28,20},{1,9},{5... | collective-permute-start | bytes 1572872 | tf_op jit(solution)/shard_map/ppermute | solution.py:37
  536.3 77.4 %collective-permute-start.30 = (bf16[256,2048]{1,0:T(8,128)(2,1)}, bf16[256,2048]{1,0:T(8,128)(2,1)}, u32[]{:S(2)}, u32[]{:S(2)}) collective-permute-start(bf16[256,2048]{1,0:T(8,128)(2,1)} %get-tuple-element.131), channel_id=1, source_target_pairs={{0,8},{4,12},{8,0},{12,4},{16,24},{20,28},{24,16},{28,20},{1,9},{5... | collective-permute-start | bytes 3145736 | tf_op jit(solution)/shard_map/ppermute | solution.py:37
  538.4 41.0 %collective-permute-start.34 = (bf16[256,1024]{1,0:T(8,128)(2,1)}, bf16[256,1024]{1,0:T(8,128)(2,1)S(1)}, u32[]{:S(2)}, u32[]{:S(2)}) collective-permute-start(bf16[256,1024]{1,0:T(8,128)(2,1)} %add_convert_fusion.3), channel_id=1, source_target_pairs={{0,8},{4,12},{8,0},{12,4},{16,24},{20,28},{24,16},{28,20},{1,9},{5... | collective-permute-start | bytes 1572872 | tf_op jit(solution)/shard_map/ppermute | solution.py:37
  542.4 14.9 %collective-permute-start.15 = (bf16[128,2048]{1,0:T(8,128)(2,1)}, bf16[128,2048]{1,0:T(8,128)(2,1)S(1)}, u32[]{:S(2)}, u32[]{:S(2)}) collective-permute-start(bf16[128,2048]{1,0:T(8,128)(2,1)} %get-tuple-element.172), channel_id=1, source_target_pairs={{0,1},{1,2},{2,3},{3,0},{4,5},{5,6},{6,7},{7,4},{8,9},{9,10},{10,1... | collective-permute-start | bytes 1572872 | tf_op jit(solution)/shard_map/ppermute | solution.py:136
  542.9 36.5 %copy-start.10 = (bf16[256,1024]{1,0:T(8,128)(2,1)S(1)}, bf16[256,1024]{1,0:T(8,128)(2,1)}, u32[]{:S(2)}) copy-start(bf16[256,1024]{1,0:T(8,128)(2,1)} %add_convert_fusion.2) | copy-start | bytes 1572868
  542.9 37.8 %copy-start.4 = (f32[256,1024]{1,0:T(8,128)S(1)}, f32[256,1024]{1,0:T(8,128)}, u32[]{:S(2)}) copy-start(f32[256,1024]{1,0:T(8,128)} %get-tuple-element.135) | copy-start | bytes 3145732
  557.3 24.8 %collective-permute-start.16 = (bf16[128,2048]{1,0:T(8,128)(2,1)}, bf16[128,2048]{1,0:T(8,128)(2,1)S(1)}, u32[]{:S(2)}, u32[]{:S(2)}) collective-permute-start(bf16[128,2048]{1,0:T(8,128)(2,1)} %get-tuple-element.172), channel_id=1, source_target_pairs={{0,2},{1,3},{2,0},{3,1},{4,6},{5,7},{6,4},{7,5},{8,10},{9,11},{10,... | collective-permute-start | bytes 1572872 | tf_op jit(solution)/shard_map/ppermute | solution.py:136
  557.5 69.1 %collective-permute-start.29 = (bf16[256,2048]{1,0:T(8,128)(2,1)}, bf16[256,2048]{1,0:T(8,128)(2,1)}, u32[]{:S(2)}, u32[]{:S(2)}) collective-permute-start(bf16[256,2048]{1,0:T(8,128)(2,1)} %get-tuple-element.128), channel_id=1, source_target_pairs={{0,16},{4,20},{8,24},{12,28},{16,0},{20,4},{24,8},{28,12},{1,17},{... | collective-permute-start | bytes 3145736 | tf_op jit(solution)/shard_map/ppermute | solution.py:37
  579.4 14.8 %collective-permute-start.38 = (bf16[256,1024]{1,0:T(8,128)(2,1)S(1)}, bf16[256,1024]{1,0:T(8,128)(2,1)S(1)}, u32[]{:S(2)}, u32[]{:S(2)}) collective-permute-start(bf16[256,1024]{1,0:T(8,128)(2,1)S(1)} %copy-done.10), channel_id=1, source_target_pairs={{0,16},{4,20},{8,24},{12,28},{16,0},{20,4},{24,8},{28,12},{1,17},{... | collective-permute-start | bytes 1572872 | tf_op jit(solution)/shard_map/ppermute | solution.py:37
  580.7 14.8 %copy-start.3 = (f32[256,1024]{1,0:T(8,128)S(1)}, f32[256,1024]{1,0:T(8,128)}, u32[]{:S(2)}) copy-start(f32[256,1024]{1,0:T(8,128)} %get-tuple-element.141) | copy-start | bytes 3145732
  582.1 20.5 %collective-permute-start.23 = (bf16[256,768]{1,0:T(8,128)(2,1)}, bf16[256,768]{1,0:T(8,128)(2,1)S(1)}, u32[]{:S(2)}, u32[]{:S(2)}) collective-permute-start(bf16[256,768]{1,0:T(8,128)(2,1)} %get-tuple-element.118), channel_id=1, source_target_pairs={{0,16},{4,20},{8,24},{12,28},{16,0},{20,4},{24,8},{28,12},{1,17},{... | collective-permute-start | bytes 1179656 | tf_op jit(solution)/shard_map/ppermute | solution.py:37
  582.9 12.6 %copy-start.2 = (bf16[1,512,2048]{2,1,0:T(8,128)(2,1)}, bf16[1,512,2048]{2,1,0:T(8,128)(2,1)S(1)}, u32[]{:S(2)}) copy-start(bf16[1,512,2048]{2,1,0:T(8,128)(2,1)S(1)} %bitcast_dynamic-update-slice_fusion.1) | copy-start | bytes 6291460
  583.0 15.8 %collective-permute-start.17 = (bf16[128,2048]{1,0:T(8,128)(2,1)}, bf16[128,2048]{1,0:T(8,128)(2,1)}, u32[]{:S(2)}, u32[]{:S(2)}) collective-permute-start(bf16[128,2048]{1,0:T(8,128)(2,1)} %get-tuple-element.172), channel_id=1, source_target_pairs={{0,3},{1,0},{2,1},{3,2},{4,7},{5,4},{6,5},{7,6},{8,11},{9,8},{10,9... | collective-permute-start | bytes 1572872 | tf_op jit(solution)/shard_map/ppermute | solution.py:136
  594.2 28.9 %collective-permute-start.32 = (bf16[256,2048]{1,0:T(8,128)(2,1)}, bf16[256,2048]{1,0:T(8,128)(2,1)}, u32[]{:S(2)}, u32[]{:S(2)}) collective-permute-start(bf16[256,2048]{1,0:T(8,128)(2,1)} %add_convert_fusion), channel_id=1, source_target_pairs={{0,16},{4,20},{8,24},{12,28},{16,0},{20,4},{24,8},{28,12},{1,17},{... | collective-permute-start | bytes 3145736 | tf_op jit(solution)/shard_map/ppermute | solution.py:37
  598.7 12.2 %collective-permute-start.22 = (bf16[256,768]{1,0:T(8,128)(2,1)}, bf16[256,768]{1,0:T(8,128)(2,1)S(1)}, u32[]{:S(2)}, u32[]{:S(2)}) collective-permute-start(bf16[256,768]{1,0:T(8,128)(2,1)} %add_convert_fusion.4), channel_id=1, source_target_pairs={{0,8},{4,12},{8,0},{12,4},{16,24},{20,28},{24,16},{28,20},{1,9},{5... | collective-permute-start | bytes 1179656 | tf_op jit(solution)/shard_map/ppermute | solution.py:37
  601.8 21.3 %copy-start.1 = (f32[256,2048]{1,0:T(8,128)S(1)}, f32[256,2048]{1,0:T(8,128)}, u32[]{:S(2)}) copy-start(f32[256,2048]{1,0:T(8,128)} %get-tuple-element.129) | copy-start | bytes 6291460
  602.6 26.9 %collective-permute-start.28 = (bf16[256,2048]{1,0:T(8,128)(2,1)S(1)}, bf16[256,2048]{1,0:T(8,128)(2,1)S(1)}, u32[]{:S(2)}, u32[]{:S(2)}) collective-permute-start(bf16[256,2048]{1,0:T(8,128)(2,1)S(1)} %add_convert_fusion.1), channel_id=1, source_target_pairs={{0,8},{4,12},{8,0},{12,4},{16,24},{20,28},{24,16},{28,20},{1,9},{5... | collective-permute-start | bytes 3145736 | tf_op jit(solution)/shard_map/ppermute | solution.py:37
  623.1 6.4 %copy-start = (f32[256,2048]{1,0:T(8,128)S(1)}, f32[256,2048]{1,0:T(8,128)}, u32[]{:S(2)}) copy-start(f32[256,2048]{1,0:T(8,128)} %get-tuple-element.123) | copy-start | bytes 6291460
  (6 other events, 19.8 us)

commit v4 on v3

--- a/solution.py
+++ b/solution.py
@@ -128,17 +128,31 @@
 
 def rows_gather(chunk):
     size = lax.axis_size("tensor")
-    me = lax.axis_index("tensor")
     count = chunk.shape[0]
     parts = [chunk]
     for shift in range(1, size):
         pairs = [(i, (i + shift) % size) for i in range(size)]
         parts.append(lax.ppermute(chunk, "tensor", pairs))
-    whole = jnp.zeros((size * count,) + chunk.shape[1:], chunk.dtype)
-    for shift in range(size):
-        place = lax.rem(me - shift + size, size) * count
-        whole = lax.dynamic_update_slice_in_dim(whole, parts[shift], place, 0)
-    return whole
+    return pl.pallas_call(
+        assemble_body,
+        in_specs=[ANYWHERE] * size,
+        out_specs=pl.BlockSpec(memory_space=pltpu.VMEM),
+        out_shape=jax.ShapeDtypeStruct((size * count,) + chunk.shape[1:], chunk.dtype),
+        scratch_shapes=[pltpu.SemaphoreType.DMA],
+        compiler_params=pltpu.CompilerParams(vmem_limit_bytes=8 << 20),
+        cost_estimate=pl.CostEstimate(flops=0, bytes_accessed=4 * size * chunk.size, transcendentals=0),
+        name="assemble",
+    )(*parts)
+
+
+def assemble_body(*refs):
+    parts, whole, sem = refs[:-2], refs[-2], refs[-1]
+    count = parts[0].shape[0]
+    me = lax.axis_index("tensor")
+    for shift, part in enumerate(parts):
+        place = pl.multiple_of(lax.rem(me - shift + len(parts), len(parts)) * count, count)
+        pltpu.make_async_copy(part, whole.at[pl.ds(place, count)], sem).start()
+    pltpu.make_async_copy(whole, whole, sem).wait()
 
 
 def gains_sum(values):
@@ -667,14 +681,16 @@
 def line_body(finish, keep_state, gain_sum, n_in, extra, *refs):
     partial, ins, rest = refs[0], refs[1 : 1 + n_in], refs[1 + n_in :]
     if extra:
-        world, n_grad, plan = extra
-        ffn_out, grad_ins, rest = rest[0], rest[1 : 1 + n_grad], rest[1 + n_grad :]
+        world, n_grad, plan, whole_plane = extra
+        ffn_out, rest = (None, rest) if whole_plane else (rest[0], rest[1:])
+        grad_ins, rest = rest[:n_grad], rest[n_grad:]
     result, rest = rest[0], rest[1:]
     state_out, rest = (rest[0], rest[1:]) if keep_state else (None, rest)
     gain_out, rest = (rest[0], rest[1:]) if gain_sum else (None, rest)
     if extra:
-        spread = world // 2 * len(plan)
-        out_parts, grad_outs, rest = rest[0], rest[1 : 1 + spread], rest[1 + spread :]
+        spread = len(plan) if whole_plane else world // 2 * len(plan)
+        n_parts = 0 if whole_plane else 4
+        out_parts, grad_outs, rest = rest[:n_parts], rest[n_parts : n_parts + spread], rest[n_parts + spread :]
     from_outer, from_peer, staged, send, recv = rest[:5]
     half, sub, count = line_steps(partial.shape[0])
     me = lax.axis_index("tensor")
@@ -722,11 +738,22 @@
     if extra:
         mate = {"context": lax.axis_index("context") ^ 1}
         pl.semaphore_signal(barrier, inc=1, device_id=mate, device_id_type=pl.DeviceIdType.MESH)
-        grad_work, grad_finish = grads_parts(world, plan, grad_ins, grad_outs, rest[5:])
+        if whole_plane:
+            for where in ({"context": lax.axis_index("context") ^ 2}, {"shard": lax.axis_index("shard") ^ 1}):
+                pl.semaphore_signal(barrier, inc=1, device_id=where, device_id_type=pl.DeviceIdType.MESH)
+            grad_work, grad_rest, grad_finish = plane_parts(world, plan, grad_ins, grad_outs, rest[5:])
+        else:
+            grad_work, grad_finish = grads_parts(world, plan, grad_ins, grad_outs, rest[5:])
+            grad_rest = lambda: None
     block = partial.shape[0] // world if extra else 0
+    more_greetings = (3 if whole_plane else 1) if extra else 0
 
     def work(q):
         grad_work(q)
+        if not whole_plane:
+            out_work(q)
+
+    def out_work(q):
         rows_q = pl.ds(pl.multiple_of(q * block, block), block)
         value = RESIDUAL_SCALE * ffn_out[rows_q, :].astype(F32)
         quarter = 2 * block * world // 8
@@ -734,14 +761,16 @@
         place = pl.ds(pl.multiple_of(lax.rem(q * block, quarter), block), block)
         owned = inner & (q * 2 // world == side)
 
-        @pl.when(owned)
-        def _():
-            mine = pl.ds(pl.multiple_of(lax.rem(q * block, half), block), block)
-            out_parts[chunk, place, :] = (value + ins[0][mine, :]).astype(BF16)
-
-        @pl.when(jnp.logical_not(owned))
-        def _():
-            out_parts[chunk, place, :] = value.astype(BF16)
+        for part in range(4):
+
+            @pl.when(owned & (chunk == part))
+            def _():
+                mine = pl.ds(pl.multiple_of(lax.rem(q * block, half), block), block)
+                out_parts[part][place, :] = (value + ins[0][mine, :]).astype(BF16)
+
+            @pl.when(jnp.logical_not(owned) & (chunk == part))
+            def _():
+                out_parts[part][place, :] = value.astype(BF16)
 
     if gain_sum:
         gain_out[...] = jnp.zeros_like(gain_out)
@@ -750,7 +779,7 @@
     def _():
         greet(to_outer)
         greet(to_peer)
-        pl.semaphore_wait(barrier, 3 if extra else 2)
+        pl.semaphore_wait(barrier, 2 + more_greetings)
 
         def step(k, carry):
             @pl.when(k < count)
@@ -803,7 +832,7 @@
     @pl.when(jnp.logical_not(inner))
     def _():
         greet(to_inner)
-        pl.semaphore_wait(barrier, 2 if extra else 1)
+        pl.semaphore_wait(barrier, 1 + more_greetings)
 
         def step(k, carry):
             up_far(k).start()
@@ -829,6 +858,7 @@
         lax.fori_loop(0, count, drain, 0)
 
     if extra:
+        grad_rest()
         grad_finish()
 
 
@@ -844,11 +874,20 @@
     specs, more, scratch, extra = [vmem] * len(shapes), [], [], None
     if pairs:
         arrays, plan = unique_arrays(pairs)
-        extra = (plane_size(), len(arrays), plan)
-        more = [ffn_out] + arrays
+        whole_plane = ffn_out is None
+        extra = (plane_size(), len(arrays), plan, whole_plane)
         outs, scratch = grads_shapes(pairs)
-        shapes += [jax.ShapeDtypeStruct((4, rows // 4, width), BF16)] + outs
-        specs += [vmem] + [ANYWHERE] * len(outs)
+        if whole_plane:
+            more = arrays
+            pieces = [(left.shape[1] // plane_size(), high - low) for left, right, low, high in pairs]
+            shapes += [jax.ShapeDtypeStruct(shape, F32) for shape in pieces]
+            specs += [vmem] * len(pieces)
+            scratch = scratch[:-1] + [pltpu.VMEM((3,) + shape, BF16) for shape in pieces]
+            scratch += [pltpu.SemaphoreType.DMA((3, len(pairs)))] * 2
+        else:
+            more = [ffn_out] + arrays
+            shapes += [jax.ShapeDtypeStruct((rows // 4, width), BF16)] * 4 + outs
+            specs += [vmem] * 4 + [ANYWHERE] * len(outs)
     return pl.pallas_call(
         functools.partial(line_body, finish, keep_state, gain_sum, len(ins), extra),
         in_specs=[vmem] * (1 + len(ins) + len(more)),
@@ -1168,6 +1207,104 @@
                 across(j, known).wait_send()
 
     return work, finish
+
+
+def plane_parts(count, plan, ins, outs, scratch):
+    jobs = len(plan)
+    sent, got, own = scratch[:jobs], scratch[jobs : 2 * jobs], scratch[2 * jobs : 3 * jobs]
+    send, recv = scratch[3 * jobs : 3 * jobs + 2]
+    landed = scratch[3 * jobs + 2 : 4 * jobs + 2]
+    plane_send, plane_recv = scratch[4 * jobs + 2 :]
+    me = plane_index()
+    core = {"context": lax.axis_index("context") ^ 1}
+    peers = ({"context": lax.axis_index("context") ^ 2}, {"shard": lax.axis_index("shard") ^ 1})
+
+    def piece(j, r):
+        left, right, low, high = plan[j]
+        extent = ins[left].shape[1] // count
+        columns = pl.ds(pl.multiple_of((me ^ r) * extent, extent), extent)
+        return lax.dot_general(
+            ins[left][:, columns], ins[right][:, low:high], (((0,), (0,)), ((), ())), preferred_element_type=F32
+        )
+
+    def across(j, i):
+        return pltpu.make_async_remote_copy(
+            src_ref=sent[j].at[i],
+            dst_ref=got[j].at[i],
+            send_sem=send.at[j, i],
+            recv_sem=recv.at[j, i],
+            device_id=core,
+            device_id_type=pl.DeviceIdType.MESH,
+        )
+
+    def move(j, i, slot, way):
+        return pltpu.make_async_remote_copy(
+            src_ref=got[j].at[i],
+            dst_ref=landed[j].at[slot],
+            send_sem=plane_send.at[slot, j],
+            recv_sem=plane_recv.at[slot, j],
+            device_id=peers[way],
+            device_id_type=pl.DeviceIdType.MESH,
+        )
+
+    first = [(j + 1) % 2 for j in range(jobs)]
+    cross = [move(j, 3, 2, first[j]) for j in range(jobs)]
+    early = [move(j, 2 if first[j] else 1, 1 if first[j] else 0, first[j]) for j in range(jobs)]
+    late = [move(j, 1 if first[j] else 2, 0 if first[j] else 1, 1 - first[j]) for j in range(jobs)]
+
+    def work(q):
+        @pl.when(q < 4)
+        def _():
+            i = 3 - q
+            for j in range(jobs):
+                sent[j][i] = piece(j, 2 * i + 1).astype(BF16)
+                across(j, i).start()
+
+        @pl.when(q >= 4)
+        def _():
+            i = 7 - q
+            for j in range(jobs):
+                value = piece(j, 2 * i)
+                across(j, i).wait_recv()
+                value = value + got[j][i].astype(F32)
+
+                @pl.when(i > 0)
+                def _():
+                    got[j][i] = value.astype(BF16)
+
+                @pl.when(i == 0)
+                def _():
+                    own[j][...] = value
+
+        @pl.when(q == 4)
+        def _():
+            for j in range(jobs):
+                cross[j].start()
+
+        @pl.when(q == 7)
+        def _():
+            for j in range(jobs):
+                early[j].start()
+
+    def rest():
+        for j in range(jobs):
+            kept = 1 if first[j] else 2
+            cross[j].wait_recv()
+            got[j][kept] = (got[j][kept].astype(F32) + landed[j][2].astype(F32)).astype(BF16)
+            late[j].start()
+        for j in range(jobs):
+            early[j].wait_recv()
+            late[j].wait_recv()
+            outs[j][...] = own[j][...] + landed[j][0].astype(F32) + landed[j][1].astype(F32)
+
+    def finish():
+        for j in range(jobs):
+            for copy in (cross[j], early[j], late[j]):
+                copy.wait_send()
+            for i in range(4):
+                across(j, i).wait_send()
+
+    return work, rest, finish
 
 
 def grads_body(count, n_in, plan, *refs):
@@ -1343,11 +1480,11 @@
     ]
     sum_ins = [hidden, grad_rows, gain_ffn]
     if grads_fit(pairs):
-        d_branch, d_hidden, ffn_gain, out_parts, *flat = line_sum(
+        d_branch, d_hidden, ffn_gain, *flat = line_sum(
             d_normed_ffn, sum_ins, finish_ffn_back, True, True, 1, ffn_out, pairs
         )
-        grad_gate, grad_up, grad_low, grad_high = grads_named(flat, len(pairs))
-        out_chunks = [out_parts[shift] for shift in range(4)]
+        out_chunks = flat[:4]
+        grad_gate, grad_up, grad_low, grad_high = grads_named(flat[4:], len(pairs))
     else:
         grad_gate, grad_up, grad_low, grad_high = plane_grads(pairs, 3)
         d_branch, d_hidden, ffn_gain = line_sum(
@@ -1364,13 +1501,17 @@
     grad_gate, grad_up = reduce_pair(grad_gate, grad_up, [d_keys_values])
     grad_low, grad_high = reduce_pair(grad_low, grad_high, [d_keys_values])
     d_qkv, d_normed = project_qkv_back(d_queries, d_keys_values, cosine, sine, qkv_pieces)
-    grad_qkv, grad_output = plane_grads([(normed, d_qkv, 0, d_qkv.shape[1]), (d_branch, mixture, 0, q_width)], 4)
-    d_normed = after(d_normed, grad_qkv[0])
-    grad_tokens, attn_gain = line_sum(
-        d_normed, [token_rows, d_hidden, gain_attn], finish_attention_back, False, True, 2
-    )
+    pairs = [(normed, d_qkv, 0, d_qkv.shape[1]), (d_branch, mixture, 0, q_width)]
+    sum_ins = [token_rows, d_hidden, gain_attn]
+    if grads_fit(pairs) and front_fits():
+        grad_tokens, attn_gain, grad_qkv, grad_output = line_sum(
+            d_normed, sum_ins, finish_attention_back, False, True, 2, None, pairs
+        )
+    else:
+        grad_qkv, grad_output = plane_grads(pairs, 4)
+        grad_tokens, attn_gain = line_sum(after(d_normed, grad_qkv[0]), sum_ins, finish_attention_back, False, True, 2)
+        grad_qkv, grad_output = reduce_pair(grad_qkv, grad_output)
     grad_tokens = grad_tokens.astype(F32)
-    grad_qkv, grad_output = reduce_pair(grad_qkv, grad_output)
     attn_gain, ffn_gain = jnp.sum(attn_gain, axis=0), jnp.sum(ffn_gain, axis=0)
     gain_grads = jnp.stack([attn_gain, ffn_gain])
     gain_grads = gains_sum(gain_grads)

time: 638 us -> 631 us (0.989)
  Pallas kernels: 377 us -> 395 us
  waiting for transfers between devices: 156 us -> 142 us
  other arithmetic: 34.7 us -> 25.8 us
    pallas_call x3, Pallas kernels: 204 us -> 231 us  [line_sum(): pl.pallas_call(functools.partial(line_body, finish, keep_state, gain_sum,...]
    pallas_call x1, Pallas kernels: 10.7 us -> 1.48 us  [rows_gather(): pl.pallas_call(assemble_body, in_specs=[ANYWHERE] * size, out_specs=pl.Bl...]
    ppermute x3, waiting for transfers between devices: 12.6 us -> 4.74 us  [rows_gather(): parts.append(lax.ppermute(chunk, 'tensor', pairs))]
    ppermute x40 -> x34, waiting for transfers between devices: 144 us -> 137 us  [swap(): return lax.ppermute(value, axes, [(i, i ^ bit) for i in range(size)])]
    ppermute x40 -> x34, starting transfers between devices: 38.7 us -> 32.9 us  [swap(): return lax.ppermute(value, axes, [(i, i ^ bit) for i in range(size)])]
  transfers between devices with their start and end apart: 49 -> 43, of which waited for: 13 -> 13; matrix products, arithmetic and copies ran while one was open for 6% -> 5% of each run, Pallas kernels for 27% -> 30%
where the time goes in v4:
time: 631 us; the launch traced here: 626 us
  Pallas kernels  395 us (63%)
  waiting for transfers between devices  142 us (23%)
  starting transfers between devices  46.6 us (7%)
  other arithmetic  25.8 us (4%)
  local copies, waits for them, and re-layouts  15.2 us (2%)
    pallas_call x3, Pallas kernels, line_sum(): pl.pallas_call(functools.partial(line_body, finish, keep_state, gain_sum,...  231 us
    ppermute x34, waiting for transfers between devices, swap(): return lax.ppermute(value, axes, [(i, i ^ bit) for i in range(size)])  137 us
    pallas_call x1, Pallas kernels, ffn(): pl.pallas_call(body, grid=(rows // row_tile, units // tile), in_specs=[ro...  44.4 us
    pallas_call x1, Pallas kernels, front(): pl.pallas_call(front_body, in_specs=[vmem] * 4 + [ANYWHERE] * 4, out_spec...  44.2 us
    pallas_call x1, Pallas kernels, attend_back(): pl.pallas_call(functools.partial(attend_back_body, pieces.shape[0]), grid...  35.6 us
    ppermute x34, starting transfers between devices, swap(): return lax.ppermute(value, axes, [(i, i ^ bit) for i in range(size)])  32.9 us
    pallas_call x1, Pallas kernels, attend(): pl.pallas_call(functools.partial(attend_body, pieces.shape[0]), grid=grid...  21.3 us
  transfers between devices with their start and end apart: 43, of which 13 were waited for; matrix products, arithmetic and copies ran while one was open for 5% of the time, Pallas kernels for 30%

profile of v4, /device:TPU:0, one launch (start us, length us, event | category | flops | bytes accessed | tf_op | source)
XLA Modules:
  0.0 625.6 jit_solution(2078907739058522577)
XLA Ops:
  2.8 1.3 fusion.9
  4.1 1.8 multiply_sine_fusion
  6.5 44.2 %front.1 = (bf16[512,2048]{1,0:T(8,128)(2,1)}, bf16[512,512]{1,0:T(8,128)(2,1)}, bf16[4,512,256]{2,1,0:T(8,128)(2,1)}, bf16[2048,768]{1,0:T(8,128)(2,1)}, bf16[512,2048]{1,0:T(8,128)(2,1)}, /*index=5*/f32[8,2048]{1,0:T(8,128)}) custom-call(bf16[512,2048]{1,0:T(8,128)(2,1)} %bitcast.18, f32[8,256]{1,0:T(8,128)} %fusion.3.refs_1_, ...), custom_call_target="tpu_custom_call" | custom-call | flops 1610612736 | bytes 10485760 | tf_op jit(solution)/shard_map/front/pallas_call | solution.py:1103
  50.7 1.2 collective-permute-start.9
  52.8 1.1 collective-permute-start.7
  54.9 1.1 collective-permute-start.1
  56.0 21.3 %attend.1 = (bf16[512,512]{1,0:T(8,128)(2,1)}, f32[4,2,512]{2,1,0:T(2,128)}) custom-call(s32[1,8]{1,0:T(1,128)} %order.3, bf16[512,512]{1,0:T(8,128)(2,1)} %get-tuple-element.76.query_ref, bf16[4,512,256]{2,1,0:T(8,128)(2,1)} %get-tuple-element.77.rest_0_.rest_1_.rest_2_.rest_3_, bf16[4,512,256]{2,1,0:T(8,128)(2,1)} %get-tuple-element.77.rest_0_.rest_1_.rest_2_.rest_3_, ...), custom_call_target="tpu_custom_call" | custom-call | flops 8589934592 | bytes 2097152 | tf_op jit(solution)/shard_map/attend/pallas_call | solution.py:584
  78.2 5.0 shard_map.203.refs_0_
  83.2 1.5 fusion.11
  84.8 63.3 %shard_map.204 = (bf16[512,2048]{1,0:T(8,128)(2,1)}, f32[256,2048]{1,0:T(8,128)}) custom-call(bf16[512,2048]{1,0:T(8,128)(2,1)} %shard_map.203.refs_0_, bf16[512,2048]{1,0:T(8,128)(2,1)} %bitcast.19, f32[1,2048]{1,0:T(1,128)} %get-tuple-element.168.refs_2_.refs_3_), custom_call_target="tpu_custom_call" | custom-call | bytes 104857600 | tf_op jit(solution)/shard_map/pallas_call | solution.py:891
  148.1 1.2 collective-permute-start.11
  150.2 1.1 collective-permute-start.4
  152.2 1.1 collective-permute-start.2
  153.4 9.9 %collective-permute-done.11.refs_15_ = bf16[2048,128]{1,0:T(8,128)(2,1)} collective-permute-done((bf16[2048,128]{1,0:T(8,128)(2,1)}, bf16[2048,128]{1,0:T(8,128)(2,1)}, u32[]{:S(2)}, u32[]{:S(2)}) %collective-permute-start.11) | collective-permute-done | bytes 524320 | tf_op jit(solution)/shard_map/ppermute | solution.py:37
  163.3 1.1 collective-permute-start.8
  164.4 3.4 multiply_convert_fusion.d_ffn.refs_8_
  167.9 36.9 %collective-permute-done.8.refs_11_ = bf16[2048,128]{1,0:T(8,128)(2,1)S(1)} collective-permute-done((bf16[2048,128]{1,0:T(8,128)(2,1)}, bf16[2048,128]{1,0:T(8,128)(2,1)S(1)}, u32[]{:S(2)}, u32[]{:S(2)}) %collective-permute-start.8) | collective-permute-done | bytes 524320 | tf_op jit(solution)/shard_map/ppermute | solution.py:37
  206.5 44.4 %feed_forward.1 = (bf16[512,2048]{1,0:T(8,128)(2,1)}, bf16[512,2048]{1,0:T(8,128)(2,1)}, bf16[512,2048]{1,0:T(8,128)(2,1)}, bf16[512,2048]{1,0:T(8,128)(2,1)}, bf16[512,2048]{1,0:T(8,128)(2,1)}) custom-call(bf16[512,2048]{1,0:T(8,128)(2,1)} %get-tuple-element.81.normed.refs_5_, bf16[512,2048]{1,0:T(8,128)(2,1)} %multiply_convert_fusion.d_ffn.refs_8_, ...), custom_call_target="tpu_custom_call" | custom-call | flops 25769803776 | bytes 39845888 | tf_op jit(solution)/shard_map/feed_forward/pallas_call | solution.py:427
  250.9 74.8 %shard_map.205 = (bf16[512,2048]{1,0:T(8,128)(2,1)}, f32[256,2048]{1,0:T(8,128)}, f32[8,2048]{1,0:T(8,128)}, bf16[128,2048]{1,0:T(8,128)(2,1)}, bf16[128,2048]{1...) custom-call(bf16[512,2048]{1,0:T(8,128)(2,1)} %get-tuple-element.90., ...), custom_call_target="tpu_custom_call" | custom-call | bytes 104857600 | tf_op jit(solution)/shard_map/pallas_call | solution.py:891
  325.6 5.1 shard_map.206.grad_ref
  330.8 35.6 %attend_back.1 = (f32[512,512]{1,0:T(8,128)}, f32[512,256]{1,0:T(8,128)}, bf16[512,256]{1,0:T(8,128)(2,1)}, f32[512,256]{1,0:T(8,128)}, bf16[512,256]{1,0:T(8,128)(2,1)}) custom-call(s32[1,8]{1,0:T(1,128)} %order.3, bf16[512,512]{1,0:T(8,128)(2,1)} %get-tuple-element.76.query_ref, bf16[512,512]{1,0:T(8,128)(2,1)} %shard_map.206.grad_ref, ...), custom_call_target="tpu_custom_call" | custom-call | flops 21474836480 | bytes 3145728 | tf_op jit(solution)/shard_map/attend_back/pallas_call | solution.py:659
  366.9 1.2 collective-permute-done.19
  368.1 1.1 add_convert_fusion.5
  370.0 1.2 collective-permute-start.27
  371.1 1.0 collective-permute-start.31
  372.2 2.4 collective-permute-start.13
  374.6 3.9 collective-permute-done.20
  378.5 1.9 collective-permute-start.14
  380.4 1.9 convert_add_fusion.2.d_keys_values
  382.3 6.9 %project_qkv_back.1 = (bf16[512,768]{1,0:T(8,128)(2,1)}, bf16[512,2048]{1,0:T(8,128)(2,1)}) custom-call(f32[512,512]{1,0:T(8,128)} %get-tuple-element.102.d_queries, f32[512,256]{1,0:T(8,128)} %convert_add_fusion.2.d_keys_values, f32[512,128]{1,0:T(8,128)} %get-tuple-element.177.refs_2_.cosine, f32[512,128]{1,0:T(8,128)} %get-tuple-element.176.refs_3_.sine, ...), custom_call_target="tpu_custom_call" | custom-call | flops 1610612736 | bytes 7340032 | tf_op jit(solution)/shard_map/project_qkv_back/pallas_call | solution.py:293
  389.2 92.6 %shard_map.207 = (bf16[512,2048]{1,0:T(8,128)(2,1)}, f32[8,2048]{1,0:T(8,128)}, f32[256,768]{1,0:T(8,128)}, f32[256,512]{1,0:T(8,128)}) custom-call(bf16[512,2048]{1,0:T(8,128)(2,1)} %get-tuple-element.108.refs_0_, bf16[512,2048]{1,0:T(8,128)(2,1)} %bitcast.20, f32[256,2048]{1,0:T(8,128)} %get-tuple-element.109.refs_2_, ...), custom_call_target="tpu_custom_call" | custom-call | bytes 104857600 | tf_op jit(solution)/shard_map/pallas_call | solution.py:891
  481.8 2.0 slice.31
  483.9 1.7 fusion.10
  486.4 2.0 copy.25
  488.5 2.5 bitcast_convert_fusion
  491.1 1.9 collective-permute-start.34
  493.0 2.0 collective-permute-start.35
  494.9 1.8 add_convert_fusion.4.refs_0_
  496.8 1.1 collective-permute-start.25
  498.0 1.1 collective-permute-start.37
  499.9 1.2 collective-permute-start.39
  502.2 16.9 %collective-permute-done.37 = f32[2,256]{1,0:T(2,128)S(1)} collective-permute-done((f32[2,256]{1,0:T(2,128)S(1)}, f32[2,256]{1,0:T(2,128)S(1)}, u32[]{:S(2)}, u32[]{:S(2)}) %collective-permute-start.37) | collective-permute-done | bytes 2080 | tf_op jit(solution)/shard_map/ppermute | solution.py:37
  519.1 1.6 collective-permute-start.41
  520.7 1.6 collective-permute-start.42
  522.5 3.2 collective-permute-done.40
  526.7 1.3 collective-permute-start.30
  529.4 1.3 collective-permute-start.28
  531.2 9.2 %collective-permute-done.29 = bf16[256,1024]{1,0:T(8,128)(2,1)S(1)} collective-permute-done((bf16[256,1024]{1,0:T(8,128)(2,1)S(1)}, bf16[256,1024]{1,0:T(8,128)(2,1)S(1)}, u32[]{:S(2)}, u32[]{:S(2)}) %collective-permute-start.29) | collective-permute-done | bytes 524320 | tf_op jit(solution)/shard_map/ppermute | solution.py:37
  540.4 1.0 collective-permute-start.15
  541.5 2.0 collective-permute-start.16
  543.5 1.2 collective-permute-start.32
  544.7 30.1 %collective-permute-done.28 = bf16[256,1024]{1,0:T(8,128)(2,1)S(1)} collective-permute-done((bf16[256,1024]{1,0:T(8,128)(2,1)S(1)}, bf16[256,1024]{1,0:T(8,128)(2,1)S(1)}, u32[]{:S(2)}, u32[]{:S(2)}) %collective-permute-start.28) | collective-permute-done | bytes 524320 | tf_op jit(solution)/shard_map/ppermute | solution.py:37
  574.8 1.2 collective-permute-start.26
  576.0 1.4 add_convert_fusion.1
  578.5 2.6 collective-permute-start.17
  581.1 1.0 collective-permute-start.22
  582.3 1.5 pad_maximum_fusion
  583.8 2.9 copy.26
  586.7 4.7 collective-permute-done.17.refs_3_
  591.4 1.5 assemble.1
  592.9 8.0 %collective-permute-done.26 = bf16[256,2048]{1,0:T(8,128)(2,1)} collective-permute-done((bf16[256,2048]{1,0:T(8,128)(2,1)S(1)}, bf16[256,2048]{1,0:T(8,128)(2,1)}, u32[]{:S(2)}, u32[]{:S(2)}) %collective-permute-start.26) | collective-permute-done | bytes 1048608 | tf_op jit(solution)/shard_map/ppermute | solution.py:37
  600.9 3.5 convert_add_fusion
  604.4 17.7 %collective-permute-done.23 = bf16[256,2048]{1,0:T(8,128)(2,1)} collective-permute-done((bf16[256,2048]{1,0:T(8,128)(2,1)}, bf16[256,2048]{1,0:T(8,128)(2,1)}, u32[]{:S(2)}, u32[]{:S(2)}) %collective-permute-start.23) | collective-permute-done | bytes 1048608 | tf_op jit(solution)/shard_map/ppermute | solution.py:37
  622.1 3.3 convert_add_fusion.1
  (108 shorter events, 17.8 us)
Async XLA Ops:
  4.1 47.8 %copy-start.10 = (bf16[2048,128]{1,0:T(8,128)(2,1)}, bf16[2048,128]{1,0:T(8,128)(2,1)S(1)}, u32[]{:S(2)}) copy-start(bf16[2048,128]{1,0:T(8,128)(2,1)S(1)} %get-tuple-element.88.refs_12_) | copy-start | bytes 1572868
  4.1 73.1 %copy-start.11 = (bf16[2048,128]{1,0:T(8,128)(2,1)}, bf16[2048,128]{1,0:T(8,128)(2,1)S(1)}, u32[]{:S(2)}) copy-start(bf16[2048,128]{1,0:T(8,128)(2,1)S(1)} %get-tuple-element.86.refs_8_) | copy-start | bytes 1572868
  50.7 26.5 %collective-permute-start.9 = (bf16[2048,128]{1,0:T(8,128)(2,1)S(1)}, bf16[2048,128]{1,0:T(8,128)(2,1)}, u32[]{:S(2)}, u32[]{:S(2)}) collective-permute-start(bf16[2048,128]{1,0:T(8,128)(2,1)S(1)} %get-tuple-element.88.refs_12_), channel_id=1, source_target_pairs={{0,8},{4,12},{8,0},{12,4},{16,24},{20,28},{24,16},{28,20},{1,9},{5... | collective-permute-start | bytes 1572872 | tf_op jit(solution)/shard_map/ppermute | solution.py:37
  52.0 99.4 %collective-permute-start.10 = (bf16[2048,128]{1,0:T(8,128)(2,1)S(1)}, bf16[2048,128]{1,0:T(8,128)(2,1)}, u32[]{:S(2)}, u32[]{:S(2)}) collective-permute-start(bf16[2048,128]{1,0:T(8,128)(2,1)S(1)} %get-tuple-element.88.refs_12_), channel_id=1, source_target_pairs={{0,16},{4,20},{8,24},{12,28},{16,0},{20,4},{24,8},{28,12},{1,17},{... | collective-permute-start | bytes 1572872 | tf_op jit(solution)/shard_map/ppermute | solution.py:37
  52.8 97.4 %collective-permute-start.7 = (bf16[2048,128]{1,0:T(8,128)(2,1)S(1)}, bf16[2048,128]{1,0:T(8,128)(2,1)}, u32[]{:S(2)}, u32[]{:S(2)}) collective-permute-start(bf16[2048,128]{1,0:T(8,128)(2,1)S(1)} %get-tuple-element.86.refs_8_), channel_id=1, source_target_pairs={{0,16},{4,20},{8,24},{12,28},{16,0},{20,4},{24,8},{28,12},{1,17},{... | collective-permute-start | bytes 1572872 | tf_op jit(solution)/shard_map/ppermute | solution.py:37
  54.0 94.1 %collective-permute-start.3 = (bf16[256,2048]{1,0:T(8,128)(2,1)}, bf16[256,2048]{1,0:T(8,128)(2,1)}, u32[]{:S(2)}, u32[]{:S(2)}) collective-permute-start(bf16[256,2048]{1,0:T(8,128)(2,1)} %refs_4_.3), channel_id=1, source_target_pairs={{0,8},{4,12},{8,0},{12,4},{16,24},{20,28},{24,16},{28,20},{1,9},{5... | collective-permute-start | bytes 3145736 | tf_op jit(solution)/shard_map/ppermute | solution.py:37
  54.9 94.5 %collective-permute-start.1 = (bf16[256,2048]{1,0:T(8,128)(2,1)}, bf16[256,2048]{1,0:T(8,128)(2,1)}, u32[]{:S(2)}, u32[]{:S(2)}) collective-permute-start(bf16[256,2048]{1,0:T(8,128)(2,1)} %refs_0_.1), channel_id=1, source_target_pairs={{0,16},{4,20},{8,24},{12,28},{16,0},{20,4},{24,8},{28,12},{1,17},{... | collective-permute-start | bytes 3145736 | tf_op jit(solution)/shard_map/ppermute | solution.py:37
  77.3 75.0 %collective-permute-start.6 = (bf16[2048,128]{1,0:T(8,128)(2,1)S(1)}, bf16[2048,128]{1,0:T(8,128)(2,1)}, u32[]{:S(2)}, u32[]{:S(2)}) collective-permute-start(bf16[2048,128]{1,0:T(8,128)(2,1)S(1)} %get-tuple-element.86.refs_8_), channel_id=1, source_target_pairs={{0,8},{4,12},{8,0},{12,4},{16,24},{20,28},{24,16},{28,20},{1,9},{5... | collective-permute-start | bytes 1572872 | tf_op jit(solution)/shard_map/ppermute | solution.py:37
  148.1 15.2 %collective-permute-start.11 = (bf16[2048,128]{1,0:T(8,128)(2,1)}, bf16[2048,128]{1,0:T(8,128)(2,1)}, u32[]{:S(2)}, u32[]{:S(2)}) collective-permute-start(bf16[2048,128]{1,0:T(8,128)(2,1)} %collective-permute-done.9.refs_13_), channel_id=1, source_target_pairs={{0,16},{4,20},{8,24},{12,28},{16,0},{20,4},{24,8},{28,12},{1,17},{... | collective-permute-start | bytes 1572872 | tf_op jit(solution)/shard_map/ppermute | solution.py:37
  149.3 55.4 %collective-permute-start = (bf16[256,2048]{1,0:T(8,128)(2,1)}, bf16[256,2048]{1,0:T(8,128)(2,1)}, u32[]{:S(2)}, u32[]{:S(2)}) collective-permute-start(bf16[256,2048]{1,0:T(8,128)(2,1)} %refs_0_.1), channel_id=1, source_target_pairs={{0,8},{4,12},{8,0},{12,4},{16,24},{20,28},{24,16},{28,20},{1,9},{5... | collective-permute-start | bytes 3145736 | tf_op jit(solution)/shard_map/ppermute | solution.py:37
  150.2 54.5 %collective-permute-start.4 = (bf16[256,2048]{1,0:T(8,128)(2,1)}, bf16[256,2048]{1,0:T(8,128)(2,1)}, u32[]{:S(2)}, u32[]{:S(2)}) collective-permute-start(bf16[256,2048]{1,0:T(8,128)(2,1)} %refs_4_.3), channel_id=1, source_target_pairs={{0,16},{4,20},{8,24},{12,28},{16,0},{20,4},{24,8},{28,12},{1,17},{... | collective-permute-start | bytes 3145736 | tf_op jit(solution)/shard_map/ppermute | solution.py:37
  151.3 54.2 %collective-permute-start.5 = (bf16[256,2048]{1,0:T(8,128)(2,1)}, bf16[256,2048]{1,0:T(8,128)(2,1)}, u32[]{:S(2)}, u32[]{:S(2)}) collective-permute-start(bf16[256,2048]{1,0:T(8,128)(2,1)} %collective-permute-done.3.refs_5_), channel_id=1, source_target_pairs={{0,16},{4,20},{8,24},{12,28},{16,0},{20,4},{24,8},{28,12},{1,17},{... | collective-permute-start | bytes 3145736 | tf_op jit(solution)/shard_map/ppermute | solution.py:37
  152.2 53.3 %collective-permute-start.2 = (bf16[256,2048]{1,0:T(8,128)(2,1)}, bf16[256,2048]{1,0:T(8,128)(2,1)S(1)}, u32[]{:S(2)}, u32[]{:S(2)}) collective-permute-start(bf16[256,2048]{1,0:T(8,128)(2,1)} %collective-permute-done.1.refs_2_), channel_id=1, source_target_pairs={{0,8},{4,12},{8,0},{12,4},{16,24},{20,28},{24,16},{28,20},{1,9},{5... | collective-permute-start | bytes 3145736 | tf_op jit(solution)/shard_map/ppermute | solution.py:37
  163.3 41.4 %collective-permute-start.8 = (bf16[2048,128]{1,0:T(8,128)(2,1)}, bf16[2048,128]{1,0:T(8,128)(2,1)S(1)}, u32[]{:S(2)}, u32[]{:S(2)}) collective-permute-start(bf16[2048,128]{1,0:T(8,128)(2,1)} %collective-permute-done.7.refs_10_), channel_id=1, source_target_pairs={{0,8},{4,12},{8,0},{12,4},{16,24},{20,28},{24,16},{28,20},{1,9},{5... | collective-permute-start | bytes 1572872 | tf_op jit(solution)/shard_map/ppermute | solution.py:37
  204.7 0.8 copy-start.18
  205.5 1.0 copy-start.15
  330.8 41.4 %copy-start.12 = (f32[8,2048]{1,0:T(8,128)S(1)}, f32[8,2048]{1,0:T(8,128)}, u32[]{:S(2)}) copy-start(f32[8,2048]{1,0:T(8,128)} %get-tuple-element.140) | copy-start | bytes 196612
  366.3 1.8 collective-permute-start.19
  366.4 5.8 collective-permute-start.18
  369.2 9.2 %collective-permute-start.20 = (bf16[512,256]{1,0:T(8,128)(2,1)S(1)}, bf16[512,256]{1,0:T(8,128)(2,1)S(1)}, u32[]{:S(2)}, u32[]{:S(2)}) collective-permute-start(bf16[512,256]{1,0:T(8,128)(2,1)S(1)} %add_convert_fusion.5), channel_id=1, source_target_pairs={{0,8},{4,12},{8,0},{12,4},{1,9},{5,13},{9,1},{13,5},{2,10},{6,14},... | collective-permute-start | bytes 786440 | tf_op jit(solution)/shard_map/ppermute | solution.py:37
  370.0 129.1 %collective-permute-start.27 = (bf16[256,1024]{1,0:T(8,128)(2,1)}, bf16[256,1024]{1,0:T(8,128)(2,1)S(1)}, u32[]{:S(2)}, u32[]{:S(2)}) collective-permute-start(bf16[256,1024]{1,0:T(8,128)(2,1)} %get-tuple-element.129), channel_id=1, source_target_pairs={{0,16},{4,20},{8,24},{12,28},{16,0},{20,4},{24,8},{28,12},{1,17},{... | collective-permute-start | bytes 1572872 | tf_op jit(solution)/shard_map/ppermute | solution.py:37
  371.1 128.8 %collective-permute-start.31 = (bf16[256,1024]{1,0:T(8,128)(2,1)}, bf16[256,1024]{1,0:T(8,128)(2,1)S(1)}, u32[]{:S(2)}, u32[]{:S(2)}) collective-permute-start(bf16[256,1024]{1,0:T(8,128)(2,1)} %get-tuple-element.137), channel_id=1, source_target_pairs={{0,8},{4,12},{8,0},{12,4},{16,24},{20,28},{24,16},{28,20},{1,9},{5... | collective-permute-start | bytes 1572872 | tf_op jit(solution)/shard_map/ppermute | solution.py:37
  372.2 118.9 %collective-permute-start.12 = (bf16[128,2048]{1,0:T(8,128)(2,1)}, bf16[128,2048]{1,0:T(8,128)(2,1)}, u32[]{:S(2)}, u32[]{:S(2)}) collective-permute-start(bf16[128,2048]{1,0:T(8,128)(2,1)} %get-tuple-element.97), channel_id=1, source_target_pairs={{0,1},{1,2},{2,3},{3,0},{4,5},{5,6},{6,7},{7,4},{8,9},{9,10},{10,1... | collective-permute-start | bytes 1572872 | tf_op jit(solution)/shard_map/ppermute | solution.py:125
  372.2 118.8 %collective-permute-start.13 = (bf16[128,2048]{1,0:T(8,128)(2,1)}, bf16[128,2048]{1,0:T(8,128)(2,1)}, u32[]{:S(2)}, u32[]{:S(2)}) collective-permute-start(bf16[128,2048]{1,0:T(8,128)(2,1)} %get-tuple-element.98), channel_id=1, source_target_pairs={{0,2},{1,3},{2,0},{3,1},{4,6},{5,7},{6,4},{7,5},{8,10},{9,11},{10,... | collective-permute-start | bytes 1572872 | tf_op jit(solution)/shard_map/ppermute | solution.py:125
  378.5 114.5 %collective-permute-start.14 = (bf16[128,2048]{1,0:T(8,128)(2,1)}, bf16[128,2048]{1,0:T(8,128)(2,1)}, u32[]{:S(2)}, u32[]{:S(2)}) collective-permute-start(bf16[128,2048]{1,0:T(8,128)(2,1)} %get-tuple-element.99), channel_id=1, source_target_pairs={{0,3},{1,0},{2,1},{3,2},{4,7},{5,4},{6,5},{7,6},{8,11},{9,8},{10,9... | collective-permute-start | bytes 1572872 | tf_op jit(solution)/shard_map/ppermute | solution.py:125
  481.8 6.6 %copy-start.2 = (bf16[512,2048]{1,0:T(8,128)(2,1)S(1)}, bf16[512,2048]{1,0:T(8,128)(2,1)}, u32[]{:S(2)}) copy-start(bf16[512,2048]{1,0:T(8,128)(2,1)} %get-tuple-element.112) | copy-start | bytes 6291460
  488.5 6.5 %copy-start.9 = (bf16[128,2048]{1,0:T(8,128)(2,1)S(1)}, bf16[128,2048]{1,0:T(8,128)(2,1)}, u32[]{:S(2)}) copy-start(bf16[128,2048]{1,0:T(8,128)(2,1)} %get-tuple-element.96) | copy-start | bytes 1572868
  491.0 5.8 copy-start.14
  491.0 10.1 %copy-start.8 = (bf16[256,1024]{1,0:T(8,128)(2,1)S(1)}, bf16[256,1024]{1,0:T(8,128)(2,1)}, u32[]{:S(2)}) copy-start(bf16[256,1024]{1,0:T(8,128)(2,1)} %get-tuple-element.128) | copy-start | bytes 1572868
  491.0 5.7 collective-permute-start.33
  491.1 6.8 %collective-permute-start.34 = (f32[2,2048]{1,0:T(2,128)S(1)}, f32[2,2048]{1,0:T(2,128)S(1)}, u32[]{:S(2)}, u32[]{:S(2)}) collective-permute-start(f32[2,2048]{1,0:T(2,128)S(1)} %pad_maximum_fusion.1), channel_id=1, source_target_pairs={{0,2},{1,3},{2,0},{3,1},{4,6},{5,7},{6,4},{7,5},{8,10},{9,11},{10,... | collective-permute-start | bytes 49160 | tf_op jit(solution)/shard_map/ppermute | solution.py:163
  493.0 4.9 collective-permute-start.35
  494.9 6.4 %copy-start.13 = (bf16[256,2048]{1,0:T(8,128)(2,1)S(1)}, bf16[256,2048]{1,0:T(8,128)(2,1)}, u32[]{:S(2)}) copy-start(bf16[256,2048]{1,0:T(8,128)(2,1)} %get-tuple-element.117) | copy-start | bytes 3145732
  494.9 27.4 %copy-start.7 = (bf16[256,1024]{1,0:T(8,128)(2,1)S(1)}, bf16[256,1024]{1,0:T(8,128)(2,1)}, u32[]{:S(2)}) copy-start(bf16[256,1024]{1,0:T(8,128)(2,1)} %get-tuple-element.136) | copy-start | bytes 1572868
  496.7 28.9 %copy-start.17 = (bf16[256,1024]{1,0:T(8,128)(2,1)S(1)}, bf16[256,1024]{1,0:T(8,128)(2,1)}, u32[]{:S(2)}) copy-start(bf16[256,1024]{1,0:T(8,128)(2,1)} %get-tuple-element.132) | copy-start | bytes 1572868
  496.8 30.0 %copy-start.16 = (bf16[256,1024]{1,0:T(8,128)(2,1)S(1)}, bf16[256,1024]{1,0:T(8,128)(2,1)}, u32[]{:S(2)}) copy-start(bf16[256,1024]{1,0:T(8,128)(2,1)} %get-tuple-element.135) | copy-start | bytes 1572868
  496.8 34.0 %copy-start.6 = (bf16[256,2048]{1,0:T(8,128)(2,1)S(1)}, bf16[256,2048]{1,0:T(8,128)(2,1)}, u32[]{:S(2)}) copy-start(bf16[256,2048]{1,0:T(8,128)(2,1)} %get-tuple-element.124) | copy-start | bytes 3145732
  496.8 32.6 %collective-permute-start.25 = (bf16[256,2048]{1,0:T(8,128)(2,1)S(1)}, bf16[256,2048]{1,0:T(8,128)(2,1)S(1)}, u32[]{:S(2)}, u32[]{:S(2)}) collective-permute-start(bf16[256,2048]{1,0:T(8,128)(2,1)S(1)} %copy-done.14), channel_id=1, source_target_pairs={{0,8},{4,12},{8,0},{12,4},{16,24},{20,28},{24,16},{28,20},{1,9},{5... | collective-permute-start | bytes 3145736 | tf_op jit(solution)/shard_map/ppermute | solution.py:37
  497.9 3.3 collective-permute-start.36
  498.0 21.0 %collective-permute-start.37 = (f32[2,256]{1,0:T(2,128)S(1)}, f32[2,256]{1,0:T(2,128)S(1)}, u32[]{:S(2)}, u32[]{:S(2)}) collective-permute-start(f32[2,256]{1,0:T(2,128)S(1)} %get-tuple-element.175), channel_id=1, source_target_pairs={{0,8},{4,12},{8,0},{12,4},{16,24},{20,28},{24,16},{28,20},{1,9},{5... | collective-permute-start | bytes 6152 | tf_op jit(solution)/shard_map/ppermute | solution.py:37
  499.1 20.0 %collective-permute-start.38 = (f32[2,256]{1,0:T(2,128)S(1)}, f32[2,256]{1,0:T(2,128)S(1)}, u32[]{:S(2)}, u32[]{:S(2)}) collective-permute-start(f32[2,256]{1,0:T(2,128)S(1)} %get-tuple-element.174), channel_id=1, source_target_pairs={{0,12},{4,8},{8,4},{12,0},{16,28},{20,24},{24,20},{28,16},{1,13},{... | collective-permute-start | bytes 6152 | tf_op jit(solution)/shard_map/ppermute | solution.py:37
  499.9 20.8 %collective-permute-start.39 = (f32[2,256]{1,0:T(2,128)S(1)}, f32[2,256]{1,0:T(2,128)S(1)}, u32[]{:S(2)}, u32[]{:S(2)}) collective-permute-start(f32[2,256]{1,0:T(2,128)S(1)} %get-tuple-element.173), channel_id=1, source_target_pairs={{0,16},{4,20},{8,24},{12,28},{16,0},{20,4},{24,8},{28,12},{1,17},{... | collective-permute-start | bytes 6152 | tf_op jit(solution)/shard_map/ppermute | solution.py:37
  501.3 42.2 %collective-permute-start.21 = (bf16[256,2048]{1,0:T(8,128)(2,1)S(1)}, bf16[256,2048]{1,0:T(8,128)(2,1)S(1)}, u32[]{:S(2)}, u32[]{:S(2)}) collective-permute-start(bf16[256,2048]{1,0:T(8,128)(2,1)S(1)} %copy-done.13), channel_id=1, source_target_pairs={{0,16},{4,20},{8,24},{12,28},{16,0},{20,4},{24,8},{28,12},{1,17},{... | collective-permute-start | bytes 3145736 | tf_op jit(solution)/shard_map/ppermute | solution.py:37
  519.1 6.6 %collective-permute-start.40 = (f32[2,256]{1,0:T(2,128)S(1)}, f32[2,256]{1,0:T(2,128)S(1)}, u32[]{:S(2)}, u32[]{:S(2)}) collective-permute-start(f32[2,256]{1,0:T(2,128)S(1)} %get-tuple-element.172), channel_id=1, source_target_pairs={{0,20},{4,16},{8,28},{12,24},{16,4},{20,0},{24,12},{28,8},{1,21},{... | collective-permute-start | bytes 6152 | tf_op jit(solution)/shard_map/ppermute | solution.py:37
  519.1 7.7 %collective-permute-start.41 = (f32[2,256]{1,0:T(2,128)S(1)}, f32[2,256]{1,0:T(2,128)S(1)}, u32[]{:S(2)}, u32[]{:S(2)}) collective-permute-start(f32[2,256]{1,0:T(2,128)S(1)} %get-tuple-element.171), channel_id=1, source_target_pairs={{0,24},{4,28},{8,16},{12,20},{16,8},{20,12},{24,0},{28,4},{1,25},{... | collective-permute-start | bytes 6152 | tf_op jit(solution)/shard_map/ppermute | solution.py:37
  520.7 7.4 %collective-permute-start.42 = (f32[2,256]{1,0:T(2,128)S(1)}, f32[2,256]{1,0:T(2,128)S(1)}, u32[]{:S(2)}, u32[]{:S(2)}) collective-permute-start(f32[2,256]{1,0:T(2,128)S(1)} %get-tuple-element.170), channel_id=1, source_target_pairs={{0,28},{4,24},{8,20},{12,16},{16,12},{20,8},{24,4},{28,0},{1,29},{... | collective-permute-start | bytes 6152 | tf_op jit(solution)/shard_map/ppermute | solution.py:37
  522.3 53.7 %copy-start.5 = (bf16[256,2048]{1,0:T(8,128)(2,1)S(1)}, bf16[256,2048]{1,0:T(8,128)(2,1)}, u32[]{:S(2)}) copy-start(bf16[256,2048]{1,0:T(8,128)(2,1)} %get-tuple-element.116) | copy-start | bytes 3145732
  525.7 14.7 %collective-permute-start.29 = (bf16[256,1024]{1,0:T(8,128)(2,1)S(1)}, bf16[256,1024]{1,0:T(8,128)(2,1)S(1)}, u32[]{:S(2)}, u32[]{:S(2)}) collective-permute-start(bf16[256,1024]{1,0:T(8,128)(2,1)S(1)} %copy-done.17), channel_id=1, source_target_pairs={{0,16},{4,20},{8,24},{12,28},{16,0},{20,4},{24,8},{28,12},{1,17},{... | collective-permute-start | bytes 1572872 | tf_op jit(solution)/shard_map/ppermute | solution.py:37
  526.7 14.8 %collective-permute-start.30 = (bf16[256,1024]{1,0:T(8,128)(2,1)S(1)}, bf16[256,1024]{1,0:T(8,128)(2,1)S(1)}, u32[]{:S(2)}, u32[]{:S(2)}) collective-permute-start(bf16[256,1024]{1,0:T(8,128)(2,1)S(1)} %copy-done.16), channel_id=1, source_target_pairs={{0,8},{4,12},{8,0},{12,4},{16,24},{20,28},{24,16},{28,20},{1,9},{5... | collective-permute-start | bytes 1572872 | tf_op jit(solution)/shard_map/ppermute | solution.py:37
  528.1 64.8 %collective-permute-start.24 = (bf16[256,2048]{1,0:T(8,128)(2,1)}, bf16[256,2048]{1,0:T(8,128)(2,1)}, u32[]{:S(2)}, u32[]{:S(2)}) collective-permute-start(bf16[256,2048]{1,0:T(8,128)(2,1)} %get-tuple-element.123), channel_id=1, source_target_pairs={{0,8},{4,12},{8,0},{12,4},{16,24},{20,28},{24,16},{28,20},{1,9},{5... | collective-permute-start | bytes 3145736 | tf_op jit(solution)/shard_map/ppermute | solution.py:37
  529.4 45.4 %collective-permute-start.28 = (bf16[256,1024]{1,0:T(8,128)(2,1)S(1)}, bf16[256,1024]{1,0:T(8,128)(2,1)S(1)}, u32[]{:S(2)}, u32[]{:S(2)}) collective-permute-start(bf16[256,1024]{1,0:T(8,128)(2,1)S(1)} %add_convert_fusion.3), channel_id=1, source_target_pairs={{0,8},{4,12},{8,0},{12,4},{16,24},{20,28},{24,16},{28,20},{1,9},{5... | collective-permute-start | bytes 1572872 | tf_op jit(solution)/shard_map/ppermute | solution.py:37
  531.2 46.2 %copy-start.4 = (f32[256,1024]{1,0:T(8,128)S(1)}, f32[256,1024]{1,0:T(8,128)}, u32[]{:S(2)}) copy-start(f32[256,1024]{1,0:T(8,128)} %get-tuple-element.127) | copy-start | bytes 3145732
  540.4 38.1 %collective-permute-start.15 = (bf16[128,2048]{1,0:T(8,128)(2,1)S(1)}, bf16[128,2048]{1,0:T(8,128)(2,1)S(1)}, u32[]{:S(2)}, u32[]{:S(2)}) collective-permute-start(bf16[128,2048]{1,0:T(8,128)(2,1)S(1)} %add_convert_fusion.4.refs_0_), channel_id=1, source_target_pairs={{0,1},{1,2},{2,3},{3,0},{4,5},{5,6},{6,7},{7,4},{8,9},{9,10},{10,1... | collective-permute-start | bytes 1572872 | tf_op jit(solution)/shard_map/ppermute | solution.py:135
  541.5 39.5 %collective-permute-start.16 = (bf16[128,2048]{1,0:T(8,128)(2,1)S(1)}, bf16[128,2048]{1,0:T(8,128)(2,1)S(1)}, u32[]{:S(2)}, u32[]{:S(2)}) collective-permute-start(bf16[128,2048]{1,0:T(8,128)(2,1)S(1)} %add_convert_fusion.4.refs_0_), channel_id=1, source_target_pairs={{0,2},{1,3},{2,0},{3,1},{4,6},{5,7},{6,4},{7,5},{8,10},{9,11},{10,... | collective-permute-start | bytes 1572872 | tf_op jit(solution)/shard_map/ppermute | solution.py:135
  543.5 34.1 %collective-permute-start.32 = (bf16[256,1024]{1,0:T(8,128)(2,1)S(1)}, bf16[256,1024]{1,0:T(8,128)(2,1)S(1)}, u32[]{:S(2)}, u32[]{:S(2)}) collective-permute-start(bf16[256,1024]{1,0:T(8,128)(2,1)S(1)} %add_convert_fusion.2), channel_id=1, source_target_pairs={{0,16},{4,20},{8,24},{12,28},{16,0},{20,4},{24,8},{28,12},{1,17},{... | collective-permute-start | bytes 1572872 | tf_op jit(solution)/shard_map/ppermute | solution.py:37
  574.8 26.1 %collective-permute-start.26 = (bf16[256,2048]{1,0:T(8,128)(2,1)S(1)}, bf16[256,2048]{1,0:T(8,128)(2,1)}, u32[]{:S(2)}, u32[]{:S(2)}) collective-permute-start(bf16[256,2048]{1,0:T(8,128)(2,1)S(1)} %add_convert_fusion), channel_id=1, source_target_pairs={{0,16},{4,20},{8,24},{12,28},{16,0},{20,4},{24,8},{28,12},{1,17},{... | collective-permute-start | bytes 3145736 | tf_op jit(solution)/shard_map/ppermute | solution.py:37
  577.4 4.7 copy-start.3
  577.6 44.5 %collective-permute-start.23 = (bf16[256,2048]{1,0:T(8,128)(2,1)}, bf16[256,2048]{1,0:T(8,128)(2,1)}, u32[]{:S(2)}, u32[]{:S(2)}) collective-permute-start(bf16[256,2048]{1,0:T(8,128)(2,1)} %get-tuple-element.120), channel_id=1, source_target_pairs={{0,16},{4,20},{8,24},{12,28},{16,0},{20,4},{24,8},{28,12},{1,17},{... | collective-permute-start | bytes 3145736 | tf_op jit(solution)/shard_map/ppermute | solution.py:37
  578.5 12.9 %collective-permute-start.17 = (bf16[128,2048]{1,0:T(8,128)(2,1)S(1)}, bf16[128,2048]{1,0:T(8,128)(2,1)S(1)}, u32[]{:S(2)}, u32[]{:S(2)}) collective-permute-start(bf16[128,2048]{1,0:T(8,128)(2,1)S(1)} %add_convert_fusion.4.refs_0_), channel_id=1, source_target_pairs={{0,3},{1,0},{2,1},{3,2},{4,7},{5,4},{6,5},{7,6},{8,11},{9,8},{10,9... | collective-permute-start | bytes 1572872 | tf_op jit(solution)/shard_map/ppermute | solution.py:135
  581.1 41.0 %collective-permute-start.22 = (bf16[256,2048]{1,0:T(8,128)(2,1)}, bf16[256,2048]{1,0:T(8,128)(2,1)}, u32[]{:S(2)}, u32[]{:S(2)}) collective-permute-start(bf16[256,2048]{1,0:T(8,128)(2,1)} %add_convert_fusion.1), channel_id=1, source_target_pairs={{0,8},{4,12},{8,0},{12,4},{16,24},{20,28},{24,16},{28,20},{1,9},{5... | collective-permute-start | bytes 3145736 | tf_op jit(solution)/shard_map/ppermute | solution.py:37
  586.7 14.2 %copy-start.1 = (f32[256,2048]{1,0:T(8,128)S(1)}, f32[256,2048]{1,0:T(8,128)}, u32[]{:S(2)}) copy-start(f32[256,2048]{1,0:T(8,128)} %get-tuple-element.121) | copy-start | bytes 6291460
  600.9 21.2 %copy-start = (f32[256,2048]{1,0:T(8,128)S(1)}, f32[256,2048]{1,0:T(8,128)}, u32[]{:S(2)}) copy-start(f32[256,2048]{1,0:T(8,128)} %get-tuple-element.115) | copy-start | bytes 6291460

commit v5 on v4

--- a/solution.py
+++ b/solution.py
@@ -76,6 +76,19 @@
     sent = side[kept | bit].astype(BF16)
     total = side[kept].astype(F32) + swap(sent, PLANE, plane_size(), bit).astype(F32)
     return total if kept == 0 else total.astype(BF16)
+
+
+def crossed_pair(first, second, second_after):
+    size, near, far = plane_size(), 2, 4
+    first, second = dict(first), dict(second)
+    first[near] = (first[near].astype(F32) + first[6].astype(F32)).astype(BF16)
+    second[far] = (second[far].astype(F32) + second[6].astype(F32)).astype(BF16)
+    done = []
+    for side, waits in ((first, ()), (second, second_after)):
+        a = swap(after(side[near], *waits), PLANE, size, near).astype(F32)
+        b = swap(side[far], PLANE, size, far).astype(F32)
+        done.append(side[0] + a + b)
+    return done
 
 
 def reduce_pair(first, second, last_after=()):
@@ -738,15 +751,20 @@
     if extra:
         mate = {"context": lax.axis_index("context") ^ 1}
         pl.semaphore_signal(barrier, inc=1, device_id=mate, device_id_type=pl.DeviceIdType.MESH)
+        for where in ({"context": lax.axis_index("context") ^ 2}, {"shard": lax.axis_index("shard") ^ 1}):
+            pl.semaphore_signal(barrier, inc=1, device_id=where, device_id_type=pl.DeviceIdType.MESH)
         if whole_plane:
-            for where in ({"context": lax.axis_index("context") ^ 2}, {"shard": lax.axis_index("shard") ^ 1}):
-                pl.semaphore_signal(barrier, inc=1, device_id=where, device_id_type=pl.DeviceIdType.MESH)
             grad_work, grad_rest, grad_finish = plane_parts(world, plan, grad_ins, grad_outs, rest[5:])
         else:
-            grad_work, grad_finish = grads_parts(world, plan, grad_ins, grad_outs, rest[5:])
+            jobs = len(plan)
+            crossed, grad_outs = grad_outs[-jobs:], grad_outs[:-jobs]
+            grad_work, grad_finish = grads_parts(
+                world, plan, grad_ins, grad_outs, rest[5:-2], crossed, rest[-2:]
+            )
             grad_rest = lambda: None
     block = partial.shape[0] // world if extra else 0
-    more_greetings = (3 if whole_plane else 1) if extra else 0
+    more_greetings = 3 if extra else 0
+    last_work = world + 1 if extra and whole_plane else world if extra else 0
 
     def work(q):
         grad_work(q)
@@ -812,7 +830,7 @@
 
             if extra:
 
-                @pl.when((lax.rem(k, count // world) == 0) & (k < count))
+                @pl.when((lax.rem(k, count // world) == 0) & (k < last_work * (count // world)))
                 def _():
                     work(k // (count // world))
 
@@ -846,7 +864,7 @@
                 work(q)
                 return carry
 
-            lax.fori_loop(0, world, busy, 0)
+            lax.fori_loop(0, last_work, busy, 0)
 
         def drain(k, carry):
             down_near(k).wait_recv()
@@ -888,6 +906,7 @@
             more = [ffn_out] + arrays
             shapes += [jax.ShapeDtypeStruct((rows // 4, width), BF16)] * 4 + outs
             specs += [vmem] * 4 + [ANYWHERE] * len(outs)
+            scratch = scratch + [pltpu.SemaphoreType.DMA((len(pairs),))] * 2
     return pl.pallas_call(
         functools.partial(line_body, finish, keep_state, gain_sum, len(ins), extra),
         in_specs=[vmem] * (1 + len(ins) + len(more)),
@@ -1138,10 +1157,24 @@
     return arrays, tuple(plan)
 
 
-def grads_parts(count, plan, ins, outs, scratch):
+def grads_parts(count, plan, ins, outs, scratch, crossed=(), cross_sems=()):
     halves, jobs = count // 2, len(plan)
     sent, got, own = scratch[:jobs], scratch[jobs : 2 * jobs], scratch[2 * jobs : 3 * jobs]
-    send, recv, done = scratch[3 * jobs :]
+    send, recv, done = scratch[3 * jobs : 3 * jobs + 3]
+    kept = halves - 1 if crossed else halves
+    cross = []
+    for j, landed in enumerate(crossed):
+        ways = ({"shard": lax.axis_index("shard") ^ 1}, {"context": lax.axis_index("context") ^ 2})
+        cross.append(
+            pltpu.make_async_remote_copy(
+                src_ref=got[j].at[halves - 1],
+                dst_ref=landed,
+                send_sem=cross_sems[0].at[j],
+                recv_sem=cross_sems[1].at[j],
+                device_id=ways[j % 2],
+                device_id_type=pl.DeviceIdType.MESH,
+            )
+        )
     me = plane_index()
     mate = {"context": lax.axis_index("context") ^ 1}
 
@@ -1182,7 +1215,7 @@
             def _():
                 own[j][...] = value
 
-        for known in range(halves):
+        for known in range(kept):
 
             @pl.when(i == known)
             def _():
@@ -1190,6 +1223,13 @@
                     source = got[j].at[known] if known else own[j]
                     pltpu.make_async_copy(source, outs[known * jobs + j], done.at[known, j]).start()
 
+        if crossed:
+
+            @pl.when(i == halves - 1)
+            def _():
+                for copy in cross:
+                    copy.start()
+
     def work(q):
         @pl.when(q < halves)
         def _():
@@ -1203,8 +1243,11 @@
         for known in range(halves):
             for j in range(jobs):
                 source = got[j].at[known] if known else own[j]
-                pltpu.make_async_copy(source, outs[known * jobs + j], done.at[known, j]).wait()
+                if known < kept:
+                    pltpu.make_async_copy(source, outs[known * jobs + j], done.at[known, j]).wait()
                 across(j, known).wait_send()
+        for copy in cross:
+            copy.wait()
 
     return work, finish
 
@@ -1260,7 +1303,15 @@
                 sent[j][i] = piece(j, 2 * i + 1).astype(BF16)
                 across(j, i).start()
 
-        @pl.when(q >= 4)
+        @pl.when(q == 8)
+        def _():
+            for j in range(jobs):
+                kept = 1 if first[j] else 2
+                cross[j].wait_recv()
+                got[j][kept] = (got[j][kept].astype(F32) + landed[j][2].astype(F32)).astype(BF16)
+                late[j].start()
+
+        @pl.when((q >= 4) & (q < 8))
         def _():
             i = 7 - q
             for j in range(jobs):
@@ -1287,11 +1338,6 @@
                 early[j].start()
 
     def rest():
-        for j in range(jobs):
-            kept = 1 if first[j] else 2
-            cross[j].wait_recv()
-            got[j][kept] = (got[j][kept].astype(F32) + landed[j][2].astype(F32)).astype(BF16)
-            late[j].start()
         for j in range(jobs):
             early[j].wait_recv()
             late[j].wait_recv()
@@ -1479,12 +1525,13 @@
         (d_ffn, active, half, units),
     ]
     sum_ins = [hidden, grad_rows, gain_ffn]
-    if grads_fit(pairs):
+    fused = grads_fit(pairs) and front_fits()
+    if fused:
         d_branch, d_hidden, ffn_gain, *flat = line_sum(
             d_normed_ffn, sum_ins, finish_ffn_back, True, True, 1, ffn_out, pairs
         )
-        out_chunks = flat[:4]
-        grad_gate, grad_up, grad_low, grad_high = grads_named(flat[4:], len(pairs))
+        out_chunks, jobs = flat[:4], len(pairs)
+        grad_gate, grad_up, grad_low, grad_high = grads_named(flat[4:], jobs)
     else:
         grad_gate, grad_up, grad_low, grad_high = plane_grads(pairs, 3)
         d_branch, d_hidden, ffn_gain = line_sum(
@@ -1498,8 +1545,12 @@
     d_mixture = gathered_matmul(d_branch, output_pieces, 1, True)
     d_queries, *d_pieces = attend_back(block_order, queries, d_mixture, logs, kv_pieces)
     d_keys_values = reduce_context(d_pieces)
-    grad_gate, grad_up = reduce_pair(grad_gate, grad_up, [d_keys_values])
-    grad_low, grad_high = reduce_pair(grad_low, grad_high, [d_keys_values])
+    if fused:
+        grad_gate, grad_up = crossed_pair(grad_gate, grad_up, [d_keys_values])
+        grad_low, grad_high = crossed_pair(grad_low, grad_high, [d_keys_values])
+    else:
+        grad_gate, grad_up = reduce_pair(grad_gate, grad_up, [d_keys_values])
+        grad_low, grad_high = reduce_pair(grad_low, grad_high, [d_keys_values])
     d_qkv, d_normed = project_qkv_back(d_queries, d_keys_values, cosine, sine, qkv_pieces)
     pairs = [(normed, d_qkv, 0, d_qkv.shape[1]), (d_branch, mixture, 0, q_width)]
     sum_ins = [token_rows, d_hidden, gain_attn]

time: 631 us -> 639 us (1.013)
  the two profiles are of different devices: /device:TPU:0 before, /device:TPU:9 now
where the time goes in v5:
time: 639 us; the launch traced here: 633 us
  Pallas kernels  385 us (60%)
  waiting for transfers between devices  137 us (21%)
  starting transfers between devices  68.5 us (11%)
  other arithmetic  29.8 us (5%)
  local copies, waits for them, and re-layouts  12.1 us (2%)
    pallas_call x3, Pallas kernels, line_sum(): pl.pallas_call(functools.partial(line_body, finish, keep_state, gain_sum,...  217 us
    ppermute x30, waiting for transfers between devices, swap(): return lax.ppermute(value, axes, [(i, i ^ bit) for i in range(size)])  90.3 us
    ppermute x30, starting transfers between devices, swap(): return lax.ppermute(value, axes, [(i, i ^ bit) for i in range(size)])  60.1 us
    pallas_call x1, Pallas kernels, ffn(): pl.pallas_call(body, grid=(rows // row_tile, units // tile), in_specs=[ro...  48.8 us
    pallas_call x1, Pallas kernels, front(): pl.pallas_call(front_body, in_specs=[vmem] * 4 + [ANYWHERE] * 4, out_spec...  43.3 us
    ppermute x3, waiting for transfers between devices, rows_gather(): parts.append(lax.ppermute(chunk, 'tensor', pairs))  38.5 us
    pallas_call x1, Pallas kernels, attend_back(): pl.pallas_call(functools.partial(attend_back_body, pieces.shape[0]), grid...  35.6 us
    pallas_call x1, Pallas kernels, attend(): pl.pallas_call(functools.partial(attend_body, pieces.shape[0]), grid=grid...  21.3 us
  transfers between devices with their start and end apart: 39, of which 9 were waited for; matrix products, arithmetic and copies ran while one was open for 5% of the time, Pallas kernels for 25%

profile of v5, /device:TPU:9, one launch (start us, length us, event | category | flops | bytes accessed | tf_op | source)
XLA Modules:
  0.0 633.1 jit_solution(16045055161356162828)
XLA Ops:
  2.8 1.3 fusion.9
  4.1 1.8 multiply_sine_fusion
  6.6 43.3 %front.1 = (bf16[512,2048]{1,0:T(8,128)(2,1)}, bf16[512,512]{1,0:T(8,128)(2,1)}, bf16[4,512,256]{2,1,0:T(8,128)(2,1)}, bf16[2048,768]{1,0:T(8,128)(2,1)}, bf16[512,2048]{1,0:T(8,128)(2,1)}, /*index=5*/f32[8,2048]{1,0:T(8,128)}) custom-call(bf16[512,2048]{1,0:T(8,128)(2,1)} %bitcast.18, f32[8,256]{1,0:T(8,128)} %fusion.3.refs_1_, ...), custom_call_target="tpu_custom_call" | custom-call | flops 1610612736 | bytes 10485760 | tf_op jit(solution)/shard_map/front/pallas_call | solution.py:1122
  49.9 0.9 collective-permute-start.9
  51.4 0.9 collective-permute-start.7
  52.9 0.9 collective-permute-start.1
  53.8 21.3 %attend.1 = (bf16[512,512]{1,0:T(8,128)(2,1)}, f32[4,2,512]{2,1,0:T(2,128)}) custom-call(s32[1,8]{1,0:T(1,128)} %order.3, bf16[512,512]{1,0:T(8,128)(2,1)} %get-tuple-element.70.query_ref, bf16[4,512,256]{2,1,0:T(8,128)(2,1)} %get-tuple-element.71.rest_0_.rest_1_.rest_2_.rest_3_, bf16[4,512,256]{2,1,0:T(8,128)(2,1)} %get-tuple-element.71.rest_0_.rest_1_.rest_2_.rest_3_, ...), custom_call_target="tpu_custom_call" | custom-call | flops 8589934592 | bytes 2097152 | tf_op jit(solution)/shard_map/attend/pallas_call | solution.py:597
  75.7 5.0 shard_map.203.refs_0_
  80.7 1.5 fusion.11
  82.2 59.2 %shard_map.204 = (bf16[512,2048]{1,0:T(8,128)(2,1)}, f32[256,2048]{1,0:T(8,128)}) custom-call(bf16[512,2048]{1,0:T(8,128)(2,1)} %shard_map.203.refs_0_, bf16[512,2048]{1,0:T(8,128)(2,1)} %bitcast.19, f32[1,2048]{1,0:T(1,128)} %get-tuple-element.156.refs_2_.refs_3_), custom_call_target="tpu_custom_call" | custom-call | bytes 104857600 | tf_op jit(solution)/shard_map/pallas_call | solution.py:910
  141.4 0.9 collective-permute-start.11
  142.9 0.8 collective-permute-start.4
  144.4 0.9 collective-permute-start.2
  145.3 6.0 collective-permute-done.11.refs_15_
  151.3 0.8 collective-permute-start.8
  152.2 3.4 multiply_convert_fusion.d_ffn.refs_8_
  155.6 41.2 %collective-permute-done.8.refs_11_ = bf16[2048,128]{1,0:T(8,128)(2,1)S(1)} collective-permute-done((bf16[2048,128]{1,0:T(8,128)(2,1)}, bf16[2048,128]{1,0:T(8,128)(2,1)S(1)}, u32[]{:S(2)}, u32[]{:S(2)}) %collective-permute-start.8) | collective-permute-done | bytes 524320 | tf_op jit(solution)/shard_map/ppermute | solution.py:37
  196.9 0.8 copy-done.19
  197.7 1.0 copy-done.17
  198.6 48.8 %feed_forward.1 = (bf16[512,2048]{1,0:T(8,128)(2,1)}, bf16[512,2048]{1,0:T(8,128)(2,1)}, bf16[512,2048]{1,0:T(8,128)(2,1)}, bf16[512,2048]{1,0:T(8,128)(2,1)}, bf16[512,2048]{1,0:T(8,128)(2,1)}) custom-call(bf16[512,2048]{1,0:T(8,128)(2,1)} %get-tuple-element.75.normed.refs_5_, bf16[512,2048]{1,0:T(8,128)(2,1)} %multiply_convert_fusion.d_ffn.refs_8_, ...), custom_call_target="tpu_custom_call" | custom-call | flops 25769803776 | bytes 39845888 | tf_op jit(solution)/shard_map/feed_forward/pallas_call | solution.py:440
  247.5 92.5 %shard_map.205 = (bf16[512,2048]{1,0:T(8,128)(2,1)}, f32[256,2048]{1,0:T(8,128)}, f32[8,2048]{1,0:T(8,128)}, bf16[128,2048]{1,0:T(8,128)(2,1)}, bf16[128,2048]{1...) custom-call(bf16[512,2048]{1,0:T(8,128)(2,1)} %get-tuple-element.84., ...), custom_call_target="tpu_custom_call" | custom-call | bytes 104857600 | tf_op jit(solution)/shard_map/pallas_call | solution.py:910
  340.0 5.1 shard_map.206.grad_ref
  345.2 35.6 %attend_back.1 = (f32[512,512]{1,0:T(8,128)}, f32[512,256]{1,0:T(8,128)}, bf16[512,256]{1,0:T(8,128)(2,1)}, f32[512,256]{1,0:T(8,128)}, bf16[512,256]{1,0:T(8,128)(2,1)}) custom-call(s32[1,8]{1,0:T(1,128)} %order.3, bf16[512,512]{1,0:T(8,128)(2,1)} %get-tuple-element.70.query_ref, bf16[512,512]{1,0:T(8,128)(2,1)} %shard_map.206.grad_ref, ...), custom_call_target="tpu_custom_call" | custom-call | flops 21474836480 | bytes 3145728 | tf_op jit(solution)/shard_map/attend_back/pallas_call | solution.py:672
  380.8 5.7 collective-permute-start.19
  386.5 2.4 add_convert_fusion.3
  389.6 0.9 collective-permute-start.26
  390.4 1.4 add_convert_fusion
  391.9 1.4 add_convert_fusion.1
  393.3 1.1 add_convert_fusion.5
  394.3 0.7 collective-permute-start.20
  395.3 12.5 %collective-permute-done.20 = bf16[512,256]{1,0:T(8,128)(2,1)S(1)} collective-permute-done((bf16[512,256]{1,0:T(8,128)(2,1)S(1)}, bf16[512,256]{1,0:T(8,128)(2,1)S(1)}, u32[]{:S(2)}, u32[]{:S(2)}) %collective-permute-start.20) | collective-permute-done | bytes 262176 | tf_op jit(solution)/shard_map/ppermute | solution.py:37
  407.8 0.9 convert_add_fusion.2.d_keys_values
  408.6 6.9 %project_qkv_back.1 = (bf16[512,768]{1,0:T(8,128)(2,1)}, bf16[512,2048]{1,0:T(8,128)(2,1)}) custom-call(f32[512,512]{1,0:T(8,128)} %get-tuple-element.96.d_queries, f32[512,256]{1,0:T(8,128)} %convert_add_fusion.2.d_keys_values, f32[512,128]{1,0:T(8,128)} %get-tuple-element.165.refs_2_.cosine, f32[512,128]{1,0:T(8,128)} %get-tuple-element.164.refs_3_.sine, ...), custom_call_target="tpu_custom_call" | custom-call | flops 1610612736 | bytes 7340032 | tf_op jit(solution)/shard_map/project_qkv_back/pallas_call | solution.py:306
  415.5 65.7 %shard_map.207 = (bf16[512,2048]{1,0:T(8,128)(2,1)}, f32[8,2048]{1,0:T(8,128)}, f32[256,768]{1,0:T(8,128)}, f32[256,512]{1,0:T(8,128)}) custom-call(bf16[512,2048]{1,0:T(8,128)(2,1)} %get-tuple-element.102.refs_0_, bf16[512,2048]{1,0:T(8,128)(2,1)} %bitcast.20, f32[256,2048]{1,0:T(8,128)} %get-tuple-element.103.refs_2_, ...), custom_call_target="tpu_custom_call" | custom-call | bytes 104857600 | tf_op jit(solution)/shard_map/pallas_call | solution.py:910
  481.2 0.9 reduce_sum.28
  482.8 1.3 collective-permute-start.31
  484.1 4.2 bitcast_convert_fusion
  489.0 3.6 collective-permute-start.13
  492.7 4.7 collective-permute-start.32
  498.2 0.9 slice.31
  499.1 2.1 copy.25
  501.2 0.8 collective-permute-start.33
  502.0 26.9 %collective-permute-start.34 = (f32[2,256]{1,0:T(2,128)S(1)}, f32[2,256]{1,0:T(2,128)S(1)}, u32[]{:S(2)}, u32[]{:S(2)}) collective-permute-start(f32[2,256]{1,0:T(2,128)S(1)} %get-tuple-element.162), channel_id=1, source_target_pairs={{0,12},{4,8},{8,4},{12,0},{16,28},{20,24},{24,20},{28,16},{1,13},{... | collective-permute-start | bytes 6152 | tf_op jit(solution)/shard_map/ppermute | solution.py:37
  528.9 2.0 collective-permute-done.13
  530.8 0.9 collective-permute-start.35
  531.7 5.7 collective-permute-done.14
  537.5 2.1 collective-permute-start.36
  539.5 1.1 collective-permute-start.37
  540.7 1.7 add_convert_fusion.4.refs_0_
  542.4 0.8 collective-permute-start.28
  543.2 0.8 collective-permute-start.21
  544.6 0.8 collective-permute-start.27
  545.4 1.8 collective-permute-start.38
  547.2 1.4 add_bitcast_fusion.1
  548.6 30.5 %collective-permute-done.38 = f32[2,256]{1,0:T(2,128)S(1)} collective-permute-done((f32[2,256]{1,0:T(2,128)S(1)}, f32[2,256]{1,0:T(2,128)S(1)}, u32[]{:S(2)}, u32[]{:S(2)}) %collective-permute-start.38) | collective-permute-done | bytes 2080 | tf_op jit(solution)/shard_map/ppermute | solution.py:37
  579.1 1.0 collective-permute-start.24
  581.6 1.8 copy.26
  584.1 1.5 collective-permute-start.17
  585.5 4.0 convert_add_fusion.1
  589.5 4.4 collective-permute-done.15.refs_1_
  593.9 31.7 %collective-permute-done.16.refs_2_ = bf16[128,2048]{1,0:T(8,128)(2,1)S(1)} collective-permute-done((bf16[128,2048]{1,0:T(8,128)(2,1)S(1)}, bf16[128,2048]{1,0:T(8,128)(2,1)S(1)}, u32[]{:S(2)}, u32[]{:S(2)}) %collective-permute-start.16) | collective-permute-done | bytes 524320 | tf_op jit(solution)/shard_map/ppermute | solution.py:148
  625.6 2.4 collective-permute-done.17.refs_3_
  628.0 1.5 assemble.1
  629.5 3.3 convert_add_fusion
  (102 shorter events, 11.9 us)
Async XLA Ops:
  4.1 46.7 %copy-start.14 = (bf16[2048,128]{1,0:T(8,128)(2,1)}, bf16[2048,128]{1,0:T(8,128)(2,1)S(1)}, u32[]{:S(2)}) copy-start(bf16[2048,128]{1,0:T(8,128)(2,1)S(1)} %get-tuple-element.82.refs_12_) | copy-start | bytes 1572868
  4.1 70.9 %copy-start.15 = (bf16[2048,128]{1,0:T(8,128)(2,1)}, bf16[2048,128]{1,0:T(8,128)(2,1)S(1)}, u32[]{:S(2)}) copy-start(bf16[2048,128]{1,0:T(8,128)(2,1)S(1)} %get-tuple-element.80.refs_8_) | copy-start | bytes 1572868
  49.9 25.1 %collective-permute-start.9 = (bf16[2048,128]{1,0:T(8,128)(2,1)S(1)}, bf16[2048,128]{1,0:T(8,128)(2,1)}, u32[]{:S(2)}, u32[]{:S(2)}) collective-permute-start(bf16[2048,128]{1,0:T(8,128)(2,1)S(1)} %get-tuple-element.82.refs_12_), channel_id=1, source_target_pairs={{0,8},{4,12},{8,0},{12,4},{16,24},{20,28},{24,16},{28,20},{1,9},{5... | collective-permute-start | bytes 1572872 | tf_op jit(solution)/shard_map/ppermute | solution.py:37
  50.8 93.0 %collective-permute-start.10 = (bf16[2048,128]{1,0:T(8,128)(2,1)S(1)}, bf16[2048,128]{1,0:T(8,128)(2,1)}, u32[]{:S(2)}, u32[]{:S(2)}) collective-permute-start(bf16[2048,128]{1,0:T(8,128)(2,1)S(1)} %get-tuple-element.82.refs_12_), channel_id=1, source_target_pairs={{0,16},{4,20},{8,24},{12,28},{16,0},{20,4},{24,8},{28,12},{1,17},{... | collective-permute-start | bytes 1572872 | tf_op jit(solution)/shard_map/ppermute | solution.py:37
  51.4 91.5 %collective-permute-start.7 = (bf16[2048,128]{1,0:T(8,128)(2,1)S(1)}, bf16[2048,128]{1,0:T(8,128)(2,1)}, u32[]{:S(2)}, u32[]{:S(2)}) collective-permute-start(bf16[2048,128]{1,0:T(8,128)(2,1)S(1)} %get-tuple-element.80.refs_8_), channel_id=1, source_target_pairs={{0,16},{4,20},{8,24},{12,28},{16,0},{20,4},{24,8},{28,12},{1,17},{... | collective-permute-start | bytes 1572872 | tf_op jit(solution)/shard_map/ppermute | solution.py:37
  52.3 89.1 %collective-permute-start.3 = (bf16[256,2048]{1,0:T(8,128)(2,1)}, bf16[256,2048]{1,0:T(8,128)(2,1)}, u32[]{:S(2)}, u32[]{:S(2)}) collective-permute-start(bf16[256,2048]{1,0:T(8,128)(2,1)} %refs_4_.3), channel_id=1, source_target_pairs={{0,8},{4,12},{8,0},{12,4},{16,24},{20,28},{24,16},{28,20},{1,9},{5... | collective-permute-start | bytes 3145736 | tf_op jit(solution)/shard_map/ppermute | solution.py:37
  52.9 89.5 %collective-permute-start.1 = (bf16[256,2048]{1,0:T(8,128)(2,1)}, bf16[256,2048]{1,0:T(8,128)(2,1)}, u32[]{:S(2)}, u32[]{:S(2)}) collective-permute-start(bf16[256,2048]{1,0:T(8,128)(2,1)} %refs_0_.1), channel_id=1, source_target_pairs={{0,16},{4,20},{8,24},{12,28},{16,0},{20,4},{24,8},{28,12},{1,17},{... | collective-permute-start | bytes 3145736 | tf_op jit(solution)/shard_map/ppermute | solution.py:37
  75.0 69.4 %collective-permute-start.6 = (bf16[2048,128]{1,0:T(8,128)(2,1)S(1)}, bf16[2048,128]{1,0:T(8,128)(2,1)}, u32[]{:S(2)}, u32[]{:S(2)}) collective-permute-start(bf16[2048,128]{1,0:T(8,128)(2,1)S(1)} %get-tuple-element.80.refs_8_), channel_id=1, source_target_pairs={{0,8},{4,12},{8,0},{12,4},{16,24},{20,28},{24,16},{28,20},{1,9},{5... | collective-permute-start | bytes 1572872 | tf_op jit(solution)/shard_map/ppermute | solution.py:37
  141.4 9.9 %collective-permute-start.11 = (bf16[2048,128]{1,0:T(8,128)(2,1)}, bf16[2048,128]{1,0:T(8,128)(2,1)S(1)}, u32[]{:S(2)}, u32[]{:S(2)}) collective-permute-start(bf16[2048,128]{1,0:T(8,128)(2,1)} %collective-permute-done.9.refs_13_), channel_id=1, source_target_pairs={{0,16},{4,20},{8,24},{12,28},{16,0},{20,4},{24,8},{28,12},{1,17},{... | collective-permute-start | bytes 1572872 | tf_op jit(solution)/shard_map/ppermute | solution.py:37
  142.3 54.5 %collective-permute-start = (bf16[256,2048]{1,0:T(8,128)(2,1)}, bf16[256,2048]{1,0:T(8,128)(2,1)}, u32[]{:S(2)}, u32[]{:S(2)}) collective-permute-start(bf16[256,2048]{1,0:T(8,128)(2,1)} %refs_0_.1), channel_id=1, source_target_pairs={{0,8},{4,12},{8,0},{12,4},{16,24},{20,28},{24,16},{28,20},{1,9},{5... | collective-permute-start | bytes 3145736 | tf_op jit(solution)/shard_map/ppermute | solution.py:37
  142.9 53.9 %collective-permute-start.4 = (bf16[256,2048]{1,0:T(8,128)(2,1)}, bf16[256,2048]{1,0:T(8,128)(2,1)}, u32[]{:S(2)}, u32[]{:S(2)}) collective-permute-start(bf16[256,2048]{1,0:T(8,128)(2,1)} %refs_4_.3), channel_id=1, source_target_pairs={{0,16},{4,20},{8,24},{12,28},{16,0},{20,4},{24,8},{28,12},{1,17},{... | collective-permute-start | bytes 3145736 | tf_op jit(solution)/shard_map/ppermute | solution.py:37
  143.8 53.9 %collective-permute-start.5 = (bf16[256,2048]{1,0:T(8,128)(2,1)}, bf16[256,2048]{1,0:T(8,128)(2,1)}, u32[]{:S(2)}, u32[]{:S(2)}) collective-permute-start(bf16[256,2048]{1,0:T(8,128)(2,1)} %collective-permute-done.3.refs_5_), channel_id=1, source_target_pairs={{0,16},{4,20},{8,24},{12,28},{16,0},{20,4},{24,8},{28,12},{1,17},{... | collective-permute-start | bytes 3145736 | tf_op jit(solution)/shard_map/ppermute | solution.py:37
  144.4 53.2 %collective-permute-start.2 = (bf16[256,2048]{1,0:T(8,128)(2,1)}, bf16[256,2048]{1,0:T(8,128)(2,1)S(1)}, u32[]{:S(2)}, u32[]{:S(2)}) collective-permute-start(bf16[256,2048]{1,0:T(8,128)(2,1)} %collective-permute-done.1.refs_2_), channel_id=1, source_target_pairs={{0,8},{4,12},{8,0},{12,4},{16,24},{20,28},{24,16},{28,20},{1,9},{5... | collective-permute-start | bytes 3145736 | tf_op jit(solution)/shard_map/ppermute | solution.py:37
  151.3 4.3 copy-start.18
  151.3 45.5 %collective-permute-start.8 = (bf16[2048,128]{1,0:T(8,128)(2,1)}, bf16[2048,128]{1,0:T(8,128)(2,1)S(1)}, u32[]{:S(2)}, u32[]{:S(2)}) collective-permute-start(bf16[2048,128]{1,0:T(8,128)(2,1)} %collective-permute-done.7.refs_10_), channel_id=1, source_target_pairs={{0,8},{4,12},{8,0},{12,4},{16,24},{20,28},{24,16},{28,20},{1,9},{5... | collective-permute-start | bytes 1572872 | tf_op jit(solution)/shard_map/ppermute | solution.py:37
  196.9 0.8 copy-start.19
  197.7 1.0 copy-start.17
  345.1 45.3 %copy-start.6 = (bf16[256,2048]{1,0:T(8,128)(2,1)S(1)}, bf16[256,2048]{1,0:T(8,128)(2,1)}, u32[]{:S(2)}) copy-start(bf16[256,2048]{1,0:T(8,128)(2,1)} %get-tuple-element.117) | copy-start | bytes 3145732
  380.8 9.6 %copy-start.5 = (bf16[256,2048]{1,0:T(8,128)(2,1)S(1)}, bf16[256,2048]{1,0:T(8,128)(2,1)}, u32[]{:S(2)}) copy-start(bf16[256,2048]{1,0:T(8,128)(2,1)} %get-tuple-element.116) | copy-start | bytes 3145732
  380.8 12.4 %collective-permute-start.19 = (bf16[512,256]{1,0:T(8,128)(2,1)}, bf16[512,256]{1,0:T(8,128)(2,1)}, u32[]{:S(2)}, u32[]{:S(2)}) collective-permute-start(bf16[512,256]{1,0:T(8,128)(2,1)} %get-tuple-element.100), channel_id=1, source_target_pairs={{0,4},{4,0},{8,12},{12,8},{1,5},{5,1},{9,13},{13,9},{2,6},{6,2},{1... | collective-permute-start | bytes 786440 | tf_op jit(solution)/shard_map/ppermute | solution.py:37
  386.5 8.8 %collective-permute-start.18 = (bf16[512,256]{1,0:T(8,128)(2,1)}, bf16[512,256]{1,0:T(8,128)(2,1)S(1)}, u32[]{:S(2)}, u32[]{:S(2)}) collective-permute-start(bf16[512,256]{1,0:T(8,128)(2,1)} %get-tuple-element.98), channel_id=1, source_target_pairs={{0,4},{4,0},{8,12},{12,8},{1,5},{5,1},{9,13},{13,9},{2,6},{6,2},{1... | collective-permute-start | bytes 786440 | tf_op jit(solution)/shard_map/ppermute | solution.py:37
  386.5 5.3 copy-start.3
  386.5 5.3 copy-start.4
  388.9 103.8 %collective-permute-start.25 = (bf16[256,1024]{1,0:T(8,128)(2,1)}, bf16[256,1024]{1,0:T(8,128)(2,1)}, u32[]{:S(2)}, u32[]{:S(2)}) collective-permute-start(bf16[256,1024]{1,0:T(8,128)(2,1)} %add_convert_fusion.3), channel_id=1, source_target_pairs={{0,8},{4,12},{8,0},{12,4},{16,24},{20,28},{24,16},{28,20},{1,9},{5... | collective-permute-start | bytes 1572872 | tf_op jit(solution)/shard_map/ppermute | solution.py:37
  389.6 111.6 %collective-permute-start.26 = (bf16[256,1024]{1,0:T(8,128)(2,1)}, bf16[256,1024]{1,0:T(8,128)(2,1)}, u32[]{:S(2)}, u32[]{:S(2)}) collective-permute-start(bf16[256,1024]{1,0:T(8,128)(2,1)} %get-tuple-element.121), channel_id=1, source_target_pairs={{0,16},{4,20},{8,24},{12,28},{16,0},{20,4},{24,8},{28,12},{1,17},{... | collective-permute-start | bytes 1572872 | tf_op jit(solution)/shard_map/ppermute | solution.py:37
  391.8 1.4 copy-start.16
  391.8 1.4 copy-start.13
  391.8 3.2 copy-start.10
  391.8 3.2 copy-start.11
  393.2 14.6 %copy-start.12 = (f32[512,256]{1,0:T(8,128)S(1)}, f32[512,256]{1,0:T(8,128)}, u32[]{:S(2)}) copy-start(f32[512,256]{1,0:T(8,128)} %get-tuple-element.97) | copy-start | bytes 1572868
  394.3 13.5 %collective-permute-start.20 = (bf16[512,256]{1,0:T(8,128)(2,1)S(1)}, bf16[512,256]{1,0:T(8,128)(2,1)S(1)}, u32[]{:S(2)}, u32[]{:S(2)}) collective-permute-start(bf16[512,256]{1,0:T(8,128)(2,1)S(1)} %add_convert_fusion.5), channel_id=1, source_target_pairs={{0,8},{4,12},{8,0},{12,4},{1,9},{5,13},{9,1},{13,5},{2,10},{6,14},... | collective-permute-start | bytes 786440 | tf_op jit(solution)/shard_map/ppermute | solution.py:37
  482.1 6.2 collective-permute-start.29
  482.8 6.2 collective-permute-start.30
  482.8 9.8 %collective-permute-start.31 = (f32[2,2048]{1,0:T(2,128)S(1)}, f32[2,2048]{1,0:T(2,128)S(1)}, u32[]{:S(2)}, u32[]{:S(2)}) collective-permute-start(f32[2,2048]{1,0:T(2,128)S(1)} %pad_maximum_fusion.1), channel_id=1, source_target_pairs={{0,3},{1,0},{2,1},{3,2},{4,7},{5,4},{6,5},{7,6},{8,11},{9,8},{10,9... | collective-permute-start | bytes 49160 | tf_op jit(solution)/shard_map/ppermute | solution.py:176
  484.1 13.4 %copy-start.7 = (f32[256,768]{1,0:T(8,128)S(1)}, f32[256,768]{1,0:T(8,128)}, u32[]{:S(2)}) copy-start(f32[256,768]{1,0:T(8,128)} %get-tuple-element.107) | copy-start | bytes 2359300
  488.3 52.4 %copy-start.8 = (bf16[128,2048]{1,0:T(8,128)(2,1)S(1)}, bf16[128,2048]{1,0:T(8,128)(2,1)}, u32[]{:S(2)}) copy-start(bf16[128,2048]{1,0:T(8,128)(2,1)} %get-tuple-element.90) | copy-start | bytes 1572868
  488.3 13.7 %collective-permute-start.12 = (bf16[128,2048]{1,0:T(8,128)(2,1)}, bf16[128,2048]{1,0:T(8,128)(2,1)}, u32[]{:S(2)}, u32[]{:S(2)}) collective-permute-start(bf16[128,2048]{1,0:T(8,128)(2,1)} %get-tuple-element.91), channel_id=1, source_target_pairs={{0,1},{1,2},{2,3},{3,0},{4,5},{5,6},{6,7},{7,4},{8,9},{9,10},{10,1... | collective-permute-start | bytes 1572872 | tf_op jit(solution)/shard_map/ppermute | solution.py:138
  489.0 41.8 %collective-permute-start.13 = (bf16[128,2048]{1,0:T(8,128)(2,1)}, bf16[128,2048]{1,0:T(8,128)(2,1)S(1)}, u32[]{:S(2)}, u32[]{:S(2)}) collective-permute-start(bf16[128,2048]{1,0:T(8,128)(2,1)} %get-tuple-element.92), channel_id=1, source_target_pairs={{0,2},{1,3},{2,0},{3,1},{4,6},{5,7},{6,4},{7,5},{8,10},{9,11},{10,... | collective-permute-start | bytes 1572872 | tf_op jit(solution)/shard_map/ppermute | solution.py:138
  492.7 44.8 %collective-permute-start.14 = (bf16[128,2048]{1,0:T(8,128)(2,1)}, bf16[128,2048]{1,0:T(8,128)(2,1)}, u32[]{:S(2)}, u32[]{:S(2)}) collective-permute-start(bf16[128,2048]{1,0:T(8,128)(2,1)} %get-tuple-element.93), channel_id=1, source_target_pairs={{0,3},{1,0},{2,1},{3,2},{4,7},{5,4},{6,5},{7,6},{8,11},{9,8},{10,9... | collective-permute-start | bytes 1572872 | tf_op jit(solution)/shard_map/ppermute | solution.py:138
  492.7 46.8 %collective-permute-start.32 = (f32[2,256]{1,0:T(2,128)S(1)}, f32[2,256]{1,0:T(2,128)S(1)}, u32[]{:S(2)}, u32[]{:S(2)}) collective-permute-start(f32[2,256]{1,0:T(2,128)S(1)} %get-tuple-element.157), channel_id=1, source_target_pairs={{0,4},{4,0},{8,12},{12,8},{16,20},{20,16},{24,28},{28,24},{1,5},{5... | collective-permute-start | bytes 6152 | tf_op jit(solution)/shard_map/ppermute | solution.py:37
  499.1 48.1 %copy-start.2 = (f32[256,1024]{1,0:T(8,128)S(1)}, f32[256,1024]{1,0:T(8,128)}, u32[]{:S(2)}) copy-start(f32[256,1024]{1,0:T(8,128)} %get-tuple-element.118) | copy-start | bytes 3145732
  501.2 41.2 %collective-permute-start.33 = (f32[2,256]{1,0:T(2,128)S(1)}, f32[2,256]{1,0:T(2,128)S(1)}, u32[]{:S(2)}, u32[]{:S(2)}) collective-permute-start(f32[2,256]{1,0:T(2,128)S(1)} %get-tuple-element.163), channel_id=1, source_target_pairs={{0,8},{4,12},{8,0},{12,4},{16,24},{20,28},{24,16},{28,20},{1,9},{5... | collective-permute-start | bytes 6152 | tf_op jit(solution)/shard_map/ppermute | solution.py:37
  502.0 41.2 %collective-permute-start.34 = (f32[2,256]{1,0:T(2,128)S(1)}, f32[2,256]{1,0:T(2,128)S(1)}, u32[]{:S(2)}, u32[]{:S(2)}) collective-permute-start(f32[2,256]{1,0:T(2,128)S(1)} %get-tuple-element.162), channel_id=1, source_target_pairs={{0,12},{4,8},{8,4},{12,0},{16,28},{20,24},{24,20},{28,16},{1,13},{... | collective-permute-start | bytes 6152 | tf_op jit(solution)/shard_map/ppermute | solution.py:37
  530.8 9.8 %copy-start.9 = (bf16[128,2048]{1,0:T(8,128)(2,1)}, bf16[128,2048]{1,0:T(8,128)(2,1)S(1)}, u32[]{:S(2)}) copy-start(bf16[128,2048]{1,0:T(8,128)(2,1)S(1)} %collective-permute-done.13) | copy-start | bytes 1572868
  530.8 13.1 %collective-permute-start.35 = (f32[2,256]{1,0:T(2,128)S(1)}, f32[2,256]{1,0:T(2,128)S(1)}, u32[]{:S(2)}, u32[]{:S(2)}) collective-permute-start(f32[2,256]{1,0:T(2,128)S(1)} %get-tuple-element.161), channel_id=1, source_target_pairs={{0,16},{4,20},{8,24},{12,28},{16,0},{20,4},{24,8},{28,12},{1,17},{... | collective-permute-start | bytes 6152 | tf_op jit(solution)/shard_map/ppermute | solution.py:37
  537.5 7.1 %collective-permute-start.36 = (f32[2,256]{1,0:T(2,128)S(1)}, f32[2,256]{1,0:T(2,128)S(1)}, u32[]{:S(2)}, u32[]{:S(2)}) collective-permute-start(f32[2,256]{1,0:T(2,128)S(1)} %get-tuple-element.160), channel_id=1, source_target_pairs={{0,20},{4,16},{8,28},{12,24},{16,4},{20,0},{24,12},{28,8},{1,21},{... | collective-permute-start | bytes 6152 | tf_op jit(solution)/shard_map/ppermute | solution.py:37
  539.5 5.9 collective-permute-start.37
  542.4 38.9 %copy-start.1 = (f32[256,1024]{1,0:T(8,128)S(1)}, f32[256,1024]{1,0:T(8,128)}, u32[]{:S(2)}) copy-start(f32[256,1024]{1,0:T(8,128)} %get-tuple-element.122) | copy-start | bytes 3145732
  542.4 38.4 %collective-permute-start.28 = (bf16[256,1024]{1,0:T(8,128)(2,1)S(1)}, bf16[256,1024]{1,0:T(8,128)(2,1)S(1)}, u32[]{:S(2)}, u32[]{:S(2)}) collective-permute-start(bf16[256,1024]{1,0:T(8,128)(2,1)S(1)} %add_convert_fusion.2), channel_id=1, source_target_pairs={{0,16},{4,20},{8,24},{12,28},{16,0},{20,4},{24,8},{28,12},{1,17},{... | collective-permute-start | bytes 1572872 | tf_op jit(solution)/shard_map/ppermute | solution.py:37
  543.2 40.3 %collective-permute-start.21 = (bf16[256,2048]{1,0:T(8,128)(2,1)}, bf16[256,2048]{1,0:T(8,128)(2,1)}, u32[]{:S(2)}, u32[]{:S(2)}) collective-permute-start(bf16[256,2048]{1,0:T(8,128)(2,1)} %add_convert_fusion.1), channel_id=1, source_target_pairs={{0,8},{4,12},{8,0},{12,4},{16,24},{20,28},{24,16},{28,20},{1,9},{5... | collective-permute-start | bytes 3145736 | tf_op jit(solution)/shard_map/ppermute | solution.py:37
  544.0 40.1 %collective-permute-start.22 = (bf16[256,2048]{1,0:T(8,128)(2,1)}, bf16[256,2048]{1,0:T(8,128)(2,1)}, u32[]{:S(2)}, u32[]{:S(2)}) collective-permute-start(bf16[256,2048]{1,0:T(8,128)(2,1)} %get-tuple-element.112), channel_id=1, source_target_pairs={{0,16},{4,20},{8,24},{12,28},{16,0},{20,4},{24,8},{28,12},{1,17},{... | collective-permute-start | bytes 3145736 | tf_op jit(solution)/shard_map/ppermute | solution.py:37
  544.6 36.7 %collective-permute-start.27 = (bf16[256,1024]{1,0:T(8,128)(2,1)}, bf16[256,1024]{1,0:T(8,128)(2,1)S(1)}, u32[]{:S(2)}, u32[]{:S(2)}) collective-permute-start(bf16[256,1024]{1,0:T(8,128)(2,1)} %get-tuple-element.124), channel_id=1, source_target_pairs={{0,8},{4,12},{8,0},{12,4},{16,24},{20,28},{24,16},{28,20},{1,9},{5... | collective-permute-start | bytes 1572872 | tf_op jit(solution)/shard_map/ppermute | solution.py:37
  545.4 33.7 %collective-permute-start.38 = (f32[2,256]{1,0:T(2,128)S(1)}, f32[2,256]{1,0:T(2,128)S(1)}, u32[]{:S(2)}, u32[]{:S(2)}) collective-permute-start(f32[2,256]{1,0:T(2,128)S(1)} %get-tuple-element.158), channel_id=1, source_target_pairs={{0,28},{4,24},{8,20},{12,16},{16,12},{20,8},{24,4},{28,0},{1,29},{... | collective-permute-start | bytes 6152 | tf_op jit(solution)/shard_map/ppermute | solution.py:37
  579.1 50.4 %collective-permute-start.24 = (bf16[256,2048]{1,0:T(8,128)(2,1)}, bf16[256,2048]{1,0:T(8,128)(2,1)}, u32[]{:S(2)}, u32[]{:S(2)}) collective-permute-start(bf16[256,2048]{1,0:T(8,128)(2,1)} %add_convert_fusion), channel_id=1, source_target_pairs={{0,16},{4,20},{8,24},{12,28},{16,0},{20,4},{24,8},{28,12},{1,17},{... | collective-permute-start | bytes 3145736 | tf_op jit(solution)/shard_map/ppermute | solution.py:37
  580.7 48.8 %collective-permute-start.23 = (bf16[256,2048]{1,0:T(8,128)(2,1)}, bf16[256,2048]{1,0:T(8,128)(2,1)}, u32[]{:S(2)}, u32[]{:S(2)}) collective-permute-start(bf16[256,2048]{1,0:T(8,128)(2,1)} %get-tuple-element.115), channel_id=1, source_target_pairs={{0,8},{4,12},{8,0},{12,4},{16,24},{20,28},{24,16},{28,20},{1,9},{5... | collective-permute-start | bytes 3145736 | tf_op jit(solution)/shard_map/ppermute | solution.py:37
  581.3 12.6 %collective-permute-start.15 = (bf16[128,2048]{1,0:T(8,128)(2,1)S(1)}, bf16[128,2048]{1,0:T(8,128)(2,1)S(1)}, u32[]{:S(2)}, u32[]{:S(2)}) collective-permute-start(bf16[128,2048]{1,0:T(8,128)(2,1)S(1)} %add_convert_fusion.4.refs_0_), channel_id=1, source_target_pairs={{0,1},{1,2},{2,3},{3,0},{4,5},{5,6},{6,7},{7,4},{8,9},{9,10},{10,1... | collective-permute-start | bytes 1572872 | tf_op jit(solution)/shard_map/ppermute | solution.py:148
  583.5 42.1 %collective-permute-start.16 = (bf16[128,2048]{1,0:T(8,128)(2,1)S(1)}, bf16[128,2048]{1,0:T(8,128)(2,1)S(1)}, u32[]{:S(2)}, u32[]{:S(2)}) collective-permute-start(bf16[128,2048]{1,0:T(8,128)(2,1)S(1)} %add_convert_fusion.4.refs_0_), channel_id=1, source_target_pairs={{0,2},{1,3},{2,0},{3,1},{4,6},{5,7},{6,4},{7,5},{8,10},{9,11},{10,... | collective-permute-start | bytes 1572872 | tf_op jit(solution)/shard_map/ppermute | solution.py:148
  584.1 43.9 %collective-permute-start.17 = (bf16[128,2048]{1,0:T(8,128)(2,1)S(1)}, bf16[128,2048]{1,0:T(8,128)(2,1)S(1)}, u32[]{:S(2)}, u32[]{:S(2)}) collective-permute-start(bf16[128,2048]{1,0:T(8,128)(2,1)S(1)} %add_convert_fusion.4.refs_0_), channel_id=1, source_target_pairs={{0,3},{1,0},{2,1},{3,2},{4,7},{5,4},{6,5},{7,6},{8,11},{9,8},{10,9... | collective-permute-start | bytes 1572872 | tf_op jit(solution)/shard_map/ppermute | solution.py:148
  589.5 40.0 %copy-start = (f32[256,2048]{1,0:T(8,128)S(1)}, f32[256,2048]{1,0:T(8,128)}, u32[]{:S(2)}) copy-start(f32[256,2048]{1,0:T(8,128)} %get-tuple-element.113) | copy-start | bytes 6291460

commit v6 on v5

--- a/solution.py
+++ b/solution.py
@@ -78,17 +78,13 @@
     return total if kept == 0 else total.astype(BF16)
 
 
-def crossed_pair(first, second, second_after):
+def crossed_sum(side, own_bit, wait, waits):
     size, near, far = plane_size(), 2, 4
-    first, second = dict(first), dict(second)
-    first[near] = (first[near].astype(F32) + first[6].astype(F32)).astype(BF16)
-    second[far] = (second[far].astype(F32) + second[6].astype(F32)).astype(BF16)
-    done = []
-    for side, waits in ((first, ()), (second, second_after)):
-        a = swap(after(side[near], *waits), PLANE, size, near).astype(F32)
-        b = swap(side[far], PLANE, size, far).astype(F32)
-        done.append(side[0] + a + b)
-    return done
+    side = dict(side)
+    side[own_bit] = (side[own_bit].astype(F32) + after(side[6], wait).astype(F32)).astype(BF16)
+    a = swap(after(side[near], *waits), PLANE, size, near).astype(F32)
+    b = swap(side[far], PLANE, size, far).astype(F32)
+    return side[0] + a + b
 
 
 def reduce_pair(first, second, last_after=()):
@@ -691,18 +687,80 @@
     return half, sub, half // sub
 
 
+def plane_peer(r):
+    return {"shard": lax.axis_index("shard") ^ (r // 4), "context": lax.axis_index("context") ^ (r % 4)}
+
+
+def gains_parts(own_gain, other_gain, out, refs, inner, to_outer, to_peer):
+    held, total, landed, z_send, z_recv, send, recv = refs
+    me = plane_index()
+    extent = out.shape[1]
+    mesh_ids = pl.DeviceIdType.MESH
+
+    def along(source, target, where):
+        return pltpu.make_async_remote_copy(
+            src_ref=held.at[source],
+            dst_ref=held.at[target],
+            send_sem=z_send.at[source + target - 1],
+            recv_sem=z_recv.at[target],
+            device_id={"tensor": where},
+            device_id_type=mesh_ids,
+        )
+
+    def columns(r):
+        return pl.ds(pl.multiple_of((me ^ r) * extent, extent), extent)
+
+    def share(r):
+        return pltpu.make_async_remote_copy(
+            src_ref=total.at[:, columns(r)],
+            dst_ref=landed.at[r],
+            send_sem=send.at[r],
+            recv_sem=recv.at[r],
+            device_id=plane_peer(r),
+            device_id_type=mesh_ids,
+        )
+
+    @pl.when(inner)
+    def _():
+        held[0, 0:8, :] = own_gain[...]
+        held[0, 8:16, :] = other_gain[...]
+        to_mate = along(0, 1, to_peer)
+        to_mate.start()
+        to_mate.wait()
+        held[2] = held[0] + held[1]
+        down = along(2, 1, to_outer)
+        down.start()
+        total[...] = held[2]
+        down.wait_send()
+
+    @pl.when(jnp.logical_not(inner))
+    def _():
+        along(2, 1, to_outer).wait_recv()
+        total[...] = held[1]
+
+    for r in range(1, 8):
+        share(r).start()
+    value = total[:, columns(0)]
+    for r in range(1, 8):
+        share(r).wait_recv()
+        value = value + landed[r]
+    out[...] = value
+    for r in range(1, 8):
+        share(r).wait_send()
+
+
 def line_body(finish, keep_state, gain_sum, n_in, extra, *refs):
     partial, ins, rest = refs[0], refs[1 : 1 + n_in], refs[1 + n_in :]
     if extra:
         world, n_grad, plan, whole_plane = extra
-        ffn_out, rest = (None, rest) if whole_plane else (rest[0], rest[1:])
+        ffn_out, rest = rest[0], rest[1:]
         grad_ins, rest = rest[:n_grad], rest[n_grad:]
     result, rest = rest[0], rest[1:]
     state_out, rest = (rest[0], rest[1:]) if keep_state else (None, rest)
     gain_out, rest = (rest[0], rest[1:]) if gain_sum else (None, rest)
     if extra:
         spread = len(plan) if whole_plane else world // 2 * len(plan)
-        n_parts = 0 if whole_plane else 4
+        n_parts = 1 if whole_plane else 4
         out_parts, grad_outs, rest = rest[:n_parts], rest[n_parts : n_parts + spread], rest[n_parts + spread :]
     from_outer, from_peer, staged, send, recv = rest[:5]
     half, sub, count = line_steps(partial.shape[0])
@@ -751,9 +809,11 @@
     if extra:
         mate = {"context": lax.axis_index("context") ^ 1}
         pl.semaphore_signal(barrier, inc=1, device_id=mate, device_id_type=pl.DeviceIdType.MESH)
-        for where in ({"context": lax.axis_index("context") ^ 2}, {"shard": lax.axis_index("shard") ^ 1}):
-            pl.semaphore_signal(barrier, inc=1, device_id=where, device_id_type=pl.DeviceIdType.MESH)
+        known = (2, 3, 4, 5, 6, 7) if whole_plane else (2, 4)
+        for r in known:
+            pl.semaphore_signal(barrier, inc=1, device_id=plane_peer(r), device_id_type=pl.DeviceIdType.MESH)
         if whole_plane:
+            gain_refs, rest = rest[-7:], rest[:-7]
             grad_work, grad_rest, grad_finish = plane_parts(world, plan, grad_ins, grad_outs, rest[5:])
         else:
             jobs = len(plan)
@@ -763,7 +823,7 @@
             )
             grad_rest = lambda: None
     block = partial.shape[0] // world if extra else 0
-    more_greetings = 3 if extra else 0
+    more_greetings = (7 if whole_plane else 3) if extra else 0
     last_work = world + 1 if extra and whole_plane else world if extra else 0
 
     def work(q):
@@ -876,11 +936,13 @@
         lax.fori_loop(0, count, drain, 0)
 
     if extra:
+        if whole_plane:
+            gains_parts(gain_out, ffn_out, out_parts[0], gain_refs, inner, to_outer, to_peer)
         grad_rest()
         grad_finish()
 
 
-def line_sum(partial, ins, finish, keep_state, gain_sum, identity, ffn_out=None, pairs=()):
+def line_sum(partial, ins, finish, keep_state, gain_sum, identity, ffn_out=None, pairs=(), ffn_gain=None):
     rows, width = partial.shape
     half, _, count = line_steps(rows)
     vmem = pl.BlockSpec(memory_space=pltpu.VMEM)
@@ -892,16 +954,19 @@
     specs, more, scratch, extra = [vmem] * len(shapes), [], [], None
     if pairs:
         arrays, plan = unique_arrays(pairs)
-        whole_plane = ffn_out is None
+        whole_plane = ffn_gain is not None
         extra = (plane_size(), len(arrays), plan, whole_plane)
         outs, scratch = grads_shapes(pairs)
         if whole_plane:
-            more = arrays
+            more = [ffn_gain] + arrays
             pieces = [(left.shape[1] // plane_size(), high - low) for left, right, low, high in pairs]
-            shapes += [jax.ShapeDtypeStruct(shape, F32) for shape in pieces]
-            specs += [vmem] * len(pieces)
+            slots = (16, width // plane_size())
+            shapes += [jax.ShapeDtypeStruct(slots, F32)] + [jax.ShapeDtypeStruct(shape, F32) for shape in pieces]
+            specs += [vmem] * (1 + len(pieces))
             scratch = scratch[:-1] + [pltpu.VMEM((3,) + shape, BF16) for shape in pieces]
             scratch += [pltpu.SemaphoreType.DMA((3, len(pairs)))] * 2
+            scratch += [pltpu.VMEM((3, 16, width), F32), pltpu.VMEM((16, width), F32), pltpu.VMEM((8,) + slots, F32)]
+            scratch += [pltpu.SemaphoreType.DMA((3,))] * 2 + [pltpu.SemaphoreType.DMA((8,))] * 2
         else:
             more = [ffn_out] + arrays
             shapes += [jax.ShapeDtypeStruct((rows // 4, width), BF16)] * 4 + outs
@@ -1437,13 +1502,15 @@
     return [held[r] for r in range(size)]
 
 
-def reduce_context(pieces):
+def reduce_context(pieces, *waits):
     size = len(pieces)
     held = dict(enumerate(pieces))
     bit = 1
     while bit < size:
+        final = 2 * bit == size
         held = {
-            r: held[r].astype(F32) + swap(held[r | bit].astype(BF16), "context", size, bit).astype(F32)
+            r: after(held[r], *(waits if final else ())).astype(F32)
+            + swap(held[r | bit].astype(BF16), "context", size, bit).astype(F32)
             for r in held
             if not r & bit
         }
@@ -1544,28 +1611,30 @@
 
     d_mixture = gathered_matmul(d_branch, output_pieces, 1, True)
     d_queries, *d_pieces = attend_back(block_order, queries, d_mixture, logs, kv_pieces)
-    d_keys_values = reduce_context(d_pieces)
     if fused:
-        grad_gate, grad_up = crossed_pair(grad_gate, grad_up, [d_keys_values])
-        grad_low, grad_high = crossed_pair(grad_low, grad_high, [d_keys_values])
+        grad_gate = crossed_sum(grad_gate, 2, d_mixture, ())
+        grad_low = crossed_sum(grad_low, 2, d_mixture, ())
+        d_keys_values = reduce_context(d_pieces, grad_gate)
+        grad_up = crossed_sum(grad_up, 4, d_mixture, [d_keys_values])
+        grad_high = crossed_sum(grad_high, 4, d_mixture, [d_keys_values])
     else:
+        d_keys_values = reduce_context(d_pieces)
         grad_gate, grad_up = reduce_pair(grad_gate, grad_up, [d_keys_values])
         grad_low, grad_high = reduce_pair(grad_low, grad_high, [d_keys_values])
     d_qkv, d_normed = project_qkv_back(d_queries, d_keys_values, cosine, sine, qkv_pieces)
     pairs = [(normed, d_qkv, 0, d_qkv.shape[1]), (d_branch, mixture, 0, q_width)]
     sum_ins = [token_rows, d_hidden, gain_attn]
     if grads_fit(pairs) and front_fits():
-        grad_tokens, attn_gain, grad_qkv, grad_output = line_sum(
-            d_normed, sum_ins, finish_attention_back, False, True, 2, None, pairs
+        grad_tokens, attn_gain, gain_rows, grad_qkv, grad_output = line_sum(
+            d_normed, sum_ins, finish_attention_back, False, True, 2, None, pairs, ffn_gain
         )
+        gain_grads = jnp.sum(gain_rows.reshape(2, 8, width // size), axis=1)
     else:
         grad_qkv, grad_output = plane_grads(pairs, 4)
         grad_tokens, attn_gain = line_sum(after(d_normed, grad_qkv[0]), sum_ins, finish_attention_back, False, True, 2)
         grad_qkv, grad_output = reduce_pair(grad_qkv, grad_output)
+        gain_grads = gains_sum(jnp.stack([jnp.sum(attn_gain, axis=0), jnp.sum(ffn_gain, axis=0)]))
     grad_tokens = grad_tokens.astype(F32)
-    attn_gain, ffn_gain = jnp.sum(attn_gain, axis=0), jnp.sum(ffn_gain, axis=0)
-    gain_grads = jnp.stack([attn_gain, ffn_gain])
-    gain_grads = gains_sum(gain_grads)
     return (
         layer_out.reshape(seqs, local_len, width),
         grad_tokens.reshape(seqs, local_len, width),

time: 639 us -> 598 us (0.936)
  the two profiles are of different devices: /device:TPU:9 before, /device:TPU:0 now
where the time goes in v6:
time: 598 us; the launch traced here: 593 us
  Pallas kernels  413 us (69%)
  waiting for transfers between devices  87.1 us (15%)
  starting transfers between devices  51.1 us (9%)
  other arithmetic  27.7 us (5%)
  local copies, waits for them, and re-layouts  12.1 us (2%)
    pallas_call x3, Pallas kernels, line_sum(): pl.pallas_call(functools.partial(line_body, finish, keep_state, gain_sum,...  248 us
    ppermute x23, waiting for transfers between devices, swap(): return lax.ppermute(value, axes, [(i, i ^ bit) for i in range(size)])  70.3 us
    pallas_call x1, Pallas kernels, front(): pl.pallas_call(front_body, in_specs=[vmem] * 4 + [ANYWHERE] * 4, out_spec...  44.5 us
    pallas_call x1, Pallas kernels, ffn(): pl.pallas_call(body, grid=(rows // row_tile, units // tile), in_specs=[ro...  44.4 us
    pallas_call x1, Pallas kernels, attend_back(): pl.pallas_call(functools.partial(attend_back_body, pieces.shape[0]), grid...  35.6 us
    ppermute x23, starting transfers between devices, swap(): return lax.ppermute(value, axes, [(i, i ^ bit) for i in range(size)])  22.2 us
    pallas_call x1, Pallas kernels, attend(): pl.pallas_call(functools.partial(attend_body, pieces.shape[0]), grid=grid...  21.4 us
    ppermute x3, waiting for transfers between devices, rows_sum(): total = total + lax.ppermute(chunks[shift], 'tensor', pairs).astype(F32)  16.9 us
  transfers between devices with their start and end apart: 29, of which 7 were waited for; matrix products, arithmetic and copies ran while one was open for 5% of the time, Pallas kernels for 39%

profile of v6, /device:TPU:0, one launch (start us, length us, event | category | flops | bytes accessed | tf_op | source)
XLA Modules:
  0.0 592.6 jit_solution(2459433003911893211)
XLA Ops:
  2.1 0.7 select_reduce_fusion
  3.4 1.8 multiply_sine_fusion
  5.2 44.5 %front.1 = (bf16[512,2048]{1,0:T(8,128)(2,1)}, bf16[512,512]{1,0:T(8,128)(2,1)}, bf16[4,512,256]{2,1,0:T(8,128)(2,1)}, bf16[2048,768]{1,0:T(8,128)(2,1)}, bf16[512,2048]{1,0:T(8,128)(2,1)}, /*index=5*/f32[8,2048]{1,0:T(8,128)}) custom-call(bf16[512,2048]{1,0:T(8,128)(2,1)} %bitcast.18, f32[8,256]{1,0:T(8,128)} %fusion.3.refs_1_, ...), custom_call_target="tpu_custom_call" | custom-call | flops 1610612736 | bytes 10485760 | tf_op jit(solution)/shard_map/front/pallas_call | solution.py:1187
  49.7 1.2 collective-permute-start.1
  50.9 0.9 collective-permute-start.3
  51.8 1.0 fusion.9
  52.8 1.1 collective-permute-start.7
  54.0 0.9 collective-permute-start.6
  54.8 1.1 collective-permute-start
  56.0 20.0 %collective-permute-done.1.refs_2_ = bf16[256,2048]{1,0:T(8,128)(2,1)S(1)} collective-permute-done((bf16[256,2048]{1,0:T(8,128)(2,1)}, bf16[256,2048]{1,0:T(8,128)(2,1)S(1)}, u32[]{:S(2)}, u32[]{:S(2)}) %collective-permute-start.1) | collective-permute-done | bytes 1048608 | tf_op jit(solution)/shard_map/ppermute | solution.py:37
  76.0 1.1 collective-permute-start.9
  77.2 21.4 %attend.1 = (bf16[512,512]{1,0:T(8,128)(2,1)}, f32[4,2,512]{2,1,0:T(2,128)}) custom-call(s32[1,8]{1,0:T(1,128)} %order.3, bf16[512,512]{1,0:T(8,128)(2,1)} %get-tuple-element.75.query_ref, bf16[4,512,256]{2,1,0:T(8,128)(2,1)} %get-tuple-element.76.rest_0_.rest_1_.rest_2_.rest_3_, bf16[4,512,256]{2,1,0:T(8,128)(2,1)} %get-tuple-element.76.rest_0_.rest_1_.rest_2_.rest_3_, ...), custom_call_target="tpu_custom_call" | custom-call | flops 8589934592 | bytes 2097152 | tf_op jit(solution)/shard_map/attend/pallas_call | solution.py:593
  98.5 1.0 collective-permute-start.10
  99.5 1.1 collective-permute-start.4
  100.6 0.9 collective-permute-start.2
  101.6 20.6 %collective-permute-done.9.refs_13_ = bf16[2048,128]{1,0:T(8,128)(2,1)} collective-permute-done((bf16[2048,128]{1,0:T(8,128)(2,1)}, bf16[2048,128]{1,0:T(8,128)(2,1)}, u32[]{:S(2)}, u32[]{:S(2)}) %collective-permute-start.9) | collective-permute-done | bytes 524320 | tf_op jit(solution)/shard_map/ppermute | solution.py:37
  122.2 0.9 collective-permute-start.5
  123.1 5.0 shard_map.203.refs_0_
  128.1 1.5 fusion.11
  129.6 63.1 %shard_map.204 = (bf16[512,2048]{1,0:T(8,128)(2,1)}, f32[256,2048]{1,0:T(8,128)}) custom-call(bf16[512,2048]{1,0:T(8,128)(2,1)} %shard_map.203.refs_0_, bf16[512,2048]{1,0:T(8,128)(2,1)} %bitcast.19, f32[1,2048]{1,0:T(1,128)} %get-tuple-element.166.refs_2_.refs_3_), custom_call_target="tpu_custom_call" | custom-call | bytes 104857600 | tf_op jit(solution)/shard_map/pallas_call | solution.py:975
  192.7 1.2 collective-permute-start.8
  194.0 0.9 collective-permute-start.11
  194.8 3.4 multiply_convert_fusion.d_ffn.refs_8_
  198.3 4.0 collective-permute-done.8.refs_11_
  202.3 1.2 collective-permute-done.11.refs_15_
  203.5 44.4 %feed_forward.1 = (bf16[512,2048]{1,0:T(8,128)(2,1)}, bf16[512,2048]{1,0:T(8,128)(2,1)}, bf16[512,2048]{1,0:T(8,128)(2,1)}, bf16[512,2048]{1,0:T(8,128)(2,1)}, bf16[512,2048]{1,0:T(8,128)(2,1)}) custom-call(bf16[512,2048]{1,0:T(8,128)(2,1)} %get-tuple-element.80.normed.refs_5_, bf16[512,2048]{1,0:T(8,128)(2,1)} %multiply_convert_fusion.d_ffn.refs_8_, ...), custom_call_target="tpu_custom_call" | custom-call | flops 25769803776 | bytes 39845888 | tf_op jit(solution)/shard_map/feed_forward/pallas_call | solution.py:436
  247.8 86.5 %shard_map.205 = (bf16[512,2048]{1,0:T(8,128)(2,1)}, f32[256,2048]{1,0:T(8,128)}, f32[8,2048]{1,0:T(8,128)}, bf16[128,2048]{1,0:T(8,128)(2,1)}, bf16[128,2048]{1...) custom-call(bf16[512,2048]{1,0:T(8,128)(2,1)} %get-tuple-element.89., ...), custom_call_target="tpu_custom_call" | custom-call | bytes 104857600 | tf_op jit(solution)/shard_map/pallas_call | solution.py:975
  334.3 5.2 shard_map.206.grad_ref
  339.6 1.0 add_convert_fusion.3
  340.6 0.7 collective-permute-start.25
  341.3 11.6 %collective-permute-start.12 = (bf16[128,2048]{1,0:T(8,128)(2,1)}, bf16[128,2048]{1,0:T(8,128)(2,1)}, u32[]{:S(2)}, u32[]{:S(2)}) collective-permute-start(bf16[128,2048]{1,0:T(8,128)(2,1)} %get-tuple-element.96), channel_id=1, source_target_pairs={{0,1},{1,2},{2,3},{3,0},{4,5},{5,6},{6,7},{7,4},{8,9},{9,10},{10,1... | collective-permute-start | bytes 1572872 | tf_op jit(solution)/shard_map/ppermute | solution.py:134
  352.8 1.1 collective-permute-start.26
  354.0 35.6 %attend_back.1 = (f32[512,512]{1,0:T(8,128)}, f32[512,256]{1,0:T(8,128)}, bf16[512,256]{1,0:T(8,128)(2,1)}, f32[512,256]{1,0:T(8,128)}, bf16[512,256]{1,0:T(8,128)(2,1)}) custom-call(s32[1,8]{1,0:T(1,128)} %order.3, bf16[512,512]{1,0:T(8,128)(2,1)} %get-tuple-element.75.query_ref, bf16[512,512]{1,0:T(8,128)(2,1)} %shard_map.206.grad_ref, ...), custom_call_target="tpu_custom_call" | custom-call | flops 21474836480 | bytes 3145728 | tf_op jit(solution)/shard_map/attend_back/pallas_call | solution.py:668
  390.2 1.6 add_convert_fusion.1
  391.9 1.4 add_convert_fusion
  393.3 1.0 add_convert_fusion.2
  394.3 1.3 collective-permute-start.13
  395.7 3.0 collective-permute-start.14
  398.7 1.1 collective-permute-start.19
  399.7 1.2 collective-permute-start.20
  401.0 2.5 add_bitcast_fusion.1
  403.5 0.9 collective-permute-start.28
  404.4 16.9 %collective-permute-done.13 = bf16[128,2048]{1,0:T(8,128)(2,1)S(1)} collective-permute-done((bf16[128,2048]{1,0:T(8,128)(2,1)S(1)}, bf16[128,2048]{1,0:T(8,128)(2,1)S(1)}, u32[]{:S(2)}, u32[]{:S(2)}) %collective-permute-start.13) | collective-permute-done | bytes 524320 | tf_op jit(solution)/shard_map/ppermute | solution.py:134
  421.2 0.9 collective-permute-start.24
  422.1 1.3 collective-permute-start.22
  423.4 1.4 add_convert_fusion.4.refs_0_
  424.8 12.0 %collective-permute-start.17 = (bf16[128,2048]{1,0:T(8,128)(2,1)S(1)}, bf16[128,2048]{1,0:T(8,128)(2,1)S(1)}, u32[]{:S(2)}, u32[]{:S(2)}) collective-permute-start(bf16[128,2048]{1,0:T(8,128)(2,1)S(1)} %add_convert_fusion.4.refs_0_), channel_id=1, source_target_pairs={{0,3},{1,0},{2,1},{3,2},{4,7},{5,4},{6,5},{7,6},{8,11},{9,8},{10,9... | collective-permute-start | bytes 1572872 | tf_op jit(solution)/shard_map/ppermute | solution.py:144
  436.8 1.8 convert_add_fusion.1
  438.6 1.0 collective-permute-start.15
  439.6 0.8 convert_add_fusion.2.d_keys_values
  440.5 6.9 %project_qkv_back.1 = (bf16[512,768]{1,0:T(8,128)(2,1)}, bf16[512,2048]{1,0:T(8,128)(2,1)}) custom-call(f32[512,512]{1,0:T(8,128)} %get-tuple-element.101.d_queries, f32[512,256]{1,0:T(8,128)} %convert_add_fusion.2.d_keys_values, f32[512,128]{1,0:T(8,128)} %get-tuple-element.168.refs_2_.cosine, f32[512,128]{1,0:T(8,128)} %get-tuple-element.167.refs_3_.sine, ...), custom_call_target="tpu_custom_call" | custom-call | flops 1610612736 | bytes 7340032 | tf_op jit(solution)/shard_map/project_qkv_back/pallas_call | solution.py:302
  447.4 98.2 %shard_map.207 = (bf16[512,2048]{1,0:T(8,128)(2,1)}, f32[8,2048]{1,0:T(8,128)}, f32[16,256]{1,0:T(8,128)}, f32[256,768]{1,0:T(8,128)}, f32[256,512]{1,0:T(8,128)}) custom-call(bf16[512,2048]{1,0:T(8,128)(2,1)} %get-tuple-element.113.refs_0_, bf16[512,2048]{1,0:T(8,128)(2,1)} %bitcast.20, f32[256,2048]{1,0:T(8,128)} %get-tuple-element.114.refs_2_, ...), custom_call_target="tpu_custom_call" | custom-call | bytes 104857600 | tf_op jit(solution)/shard_map/pallas_call | solution.py:975
  545.5 2.1 copy.25
  547.6 1.9 slice.31
  550.1 1.7 fusion.10
  551.8 1.1 collective-permute-start.27
  552.9 1.0 collective-permute-start.23
  553.9 4.1 bitcast_convert_fusion
  558.0 2.6 assemble.1
  560.7 6.0 %collective-permute-done.27 = bf16[256,1024]{1,0:T(8,128)(2,1)S(1)} collective-permute-done((bf16[256,1024]{1,0:T(8,128)(2,1)S(1)}, bf16[256,1024]{1,0:T(8,128)(2,1)S(1)}, u32[]{:S(2)}, u32[]{:S(2)}) %collective-permute-start.27) | collective-permute-done | bytes 524320 | tf_op jit(solution)/shard_map/ppermute | solution.py:37
  566.6 1.3 add_bitcast_fusion
  568.1 1.8 copy.26
  569.9 18.5 %collective-permute-done.23 = bf16[256,2048]{1,0:T(8,128)(2,1)} collective-permute-done((bf16[256,2048]{1,0:T(8,128)(2,1)}, bf16[256,2048]{1,0:T(8,128)(2,1)}, u32[]{:S(2)}, u32[]{:S(2)}) %collective-permute-start.23) | collective-permute-done | bytes 1048608 | tf_op jit(solution)/shard_map/ppermute | solution.py:37
  588.4 4.0 convert_add_fusion
  (82 shorter events, 3.6 us)
Async XLA Ops:
  5.2 46.6 %copy-start.7 = (bf16[2048,256]{1,0:T(8,128)(2,1)S(1)}, bf16[2048,256]{1,0:T(8,128)(2,1)}, u32[]{:S(2)}) copy-start(bf16[2048,256]{1,0:T(8,128)(2,1)} %param.20) | copy-start | bytes 3145732
  49.7 26.3 %collective-permute-start.1 = (bf16[256,2048]{1,0:T(8,128)(2,1)}, bf16[256,2048]{1,0:T(8,128)(2,1)S(1)}, u32[]{:S(2)}, u32[]{:S(2)}) collective-permute-start(bf16[256,2048]{1,0:T(8,128)(2,1)} %refs_0_.1), channel_id=1, source_target_pairs={{0,16},{4,20},{8,24},{12,28},{16,0},{20,4},{24,8},{28,12},{1,17},{... | collective-permute-start | bytes 3145736 | tf_op jit(solution)/shard_map/ppermute | solution.py:37
  50.9 47.6 %collective-permute-start.3 = (bf16[256,2048]{1,0:T(8,128)(2,1)}, bf16[256,2048]{1,0:T(8,128)(2,1)}, u32[]{:S(2)}, u32[]{:S(2)}) collective-permute-start(bf16[256,2048]{1,0:T(8,128)(2,1)} %refs_4_.3), channel_id=1, source_target_pairs={{0,8},{4,12},{8,0},{12,4},{16,24},{20,28},{24,16},{28,20},{1,9},{5... | collective-permute-start | bytes 3145736 | tf_op jit(solution)/shard_map/ppermute | solution.py:37
  52.8 46.7 %collective-permute-start.7 = (bf16[2048,128]{1,0:T(8,128)(2,1)}, bf16[2048,128]{1,0:T(8,128)(2,1)}, u32[]{:S(2)}, u32[]{:S(2)}) collective-permute-start(bf16[2048,128]{1,0:T(8,128)(2,1)} %get-tuple-element.85.refs_8_), channel_id=1, source_target_pairs={{0,16},{4,20},{8,24},{12,28},{16,0},{20,4},{24,8},{28,12},{1,17},{... | collective-permute-start | bytes 1572872 | tf_op jit(solution)/shard_map/ppermute | solution.py:37
  54.0 46.6 %collective-permute-start.6 = (bf16[2048,128]{1,0:T(8,128)(2,1)}, bf16[2048,128]{1,0:T(8,128)(2,1)}, u32[]{:S(2)}, u32[]{:S(2)}) collective-permute-start(bf16[2048,128]{1,0:T(8,128)(2,1)} %get-tuple-element.85.refs_8_), channel_id=1, source_target_pairs={{0,8},{4,12},{8,0},{12,4},{16,24},{20,28},{24,16},{28,20},{1,9},{5... | collective-permute-start | bytes 1572872 | tf_op jit(solution)/shard_map/ppermute | solution.py:37
  54.8 139.1 %collective-permute-start = (bf16[256,2048]{1,0:T(8,128)(2,1)}, bf16[256,2048]{1,0:T(8,128)(2,1)}, u32[]{:S(2)}, u32[]{:S(2)}) collective-permute-start(bf16[256,2048]{1,0:T(8,128)(2,1)} %refs_0_.1), channel_id=1, source_target_pairs={{0,8},{4,12},{8,0},{12,4},{16,24},{20,28},{24,16},{28,20},{1,9},{5... | collective-permute-start | bytes 3145736 | tf_op jit(solution)/shard_map/ppermute | solution.py:37
  76.0 1.2 copy-start.18
  76.0 46.2 %collective-permute-start.9 = (bf16[2048,128]{1,0:T(8,128)(2,1)}, bf16[2048,128]{1,0:T(8,128)(2,1)}, u32[]{:S(2)}, u32[]{:S(2)}) collective-permute-start(bf16[2048,128]{1,0:T(8,128)(2,1)} %get-tuple-element.87.refs_12_), channel_id=1, source_target_pairs={{0,8},{4,12},{8,0},{12,4},{16,24},{20,28},{24,16},{28,20},{1,9},{5... | collective-permute-start | bytes 1572872 | tf_op jit(solution)/shard_map/ppermute | solution.py:37
  77.1 22.4 %copy-start.16 = (bf16[256,2048]{1,0:T(8,128)(2,1)S(1)}, bf16[256,2048]{1,0:T(8,128)(2,1)}, u32[]{:S(2)}) copy-start(bf16[256,2048]{1,0:T(8,128)(2,1)} %refs_4_.3) | copy-start | bytes 3145732
  98.5 94.2 %collective-permute-start.10 = (bf16[2048,128]{1,0:T(8,128)(2,1)}, bf16[2048,128]{1,0:T(8,128)(2,1)}, u32[]{:S(2)}, u32[]{:S(2)}) collective-permute-start(bf16[2048,128]{1,0:T(8,128)(2,1)} %get-tuple-element.87.refs_12_), channel_id=1, source_target_pairs={{0,16},{4,20},{8,24},{12,28},{16,0},{20,4},{24,8},{28,12},{1,17},{... | collective-permute-start | bytes 1572872 | tf_op jit(solution)/shard_map/ppermute | solution.py:37
  99.5 98.8 %collective-permute-start.4 = (bf16[256,2048]{1,0:T(8,128)(2,1)S(1)}, bf16[256,2048]{1,0:T(8,128)(2,1)}, u32[]{:S(2)}, u32[]{:S(2)}) collective-permute-start(bf16[256,2048]{1,0:T(8,128)(2,1)S(1)} %copy-done.16), channel_id=1, source_target_pairs={{0,16},{4,20},{8,24},{12,28},{16,0},{20,4},{24,8},{28,12},{1,17},{... | collective-permute-start | bytes 3145736 | tf_op jit(solution)/shard_map/ppermute | solution.py:37
  100.6 102.9 %collective-permute-start.2 = (bf16[256,2048]{1,0:T(8,128)(2,1)}, bf16[256,2048]{1,0:T(8,128)(2,1)}, u32[]{:S(2)}, u32[]{:S(2)}) collective-permute-start(bf16[256,2048]{1,0:T(8,128)(2,1)} %copy-done.18), channel_id=1, source_target_pairs={{0,8},{4,12},{8,0},{12,4},{16,24},{20,28},{24,16},{28,20},{1,9},{5... | collective-permute-start | bytes 3145736 | tf_op jit(solution)/shard_map/ppermute | solution.py:37
  122.2 81.3 %collective-permute-start.5 = (bf16[256,2048]{1,0:T(8,128)(2,1)}, bf16[256,2048]{1,0:T(8,128)(2,1)}, u32[]{:S(2)}, u32[]{:S(2)}) collective-permute-start(bf16[256,2048]{1,0:T(8,128)(2,1)} %collective-permute-done.3.refs_5_), channel_id=1, source_target_pairs={{0,16},{4,20},{8,24},{12,28},{16,0},{20,4},{24,8},{28,12},{1,17},{... | collective-permute-start | bytes 3145736 | tf_op jit(solution)/shard_map/ppermute | solution.py:37
  192.7 9.6 %collective-permute-start.8 = (bf16[2048,128]{1,0:T(8,128)(2,1)}, bf16[2048,128]{1,0:T(8,128)(2,1)}, u32[]{:S(2)}, u32[]{:S(2)}) collective-permute-start(bf16[2048,128]{1,0:T(8,128)(2,1)} %collective-permute-done.7.refs_10_), channel_id=1, source_target_pairs={{0,8},{4,12},{8,0},{12,4},{16,24},{20,28},{24,16},{28,20},{1,9},{5... | collective-permute-start | bytes 1572872 | tf_op jit(solution)/shard_map/ppermute | solution.py:37
  194.0 9.5 %collective-permute-start.11 = (bf16[2048,128]{1,0:T(8,128)(2,1)}, bf16[2048,128]{1,0:T(8,128)(2,1)}, u32[]{:S(2)}, u32[]{:S(2)}) collective-permute-start(bf16[2048,128]{1,0:T(8,128)(2,1)} %collective-permute-done.9.refs_13_), channel_id=1, source_target_pairs={{0,16},{4,20},{8,24},{12,28},{16,0},{20,4},{24,8},{28,12},{1,17},{... | collective-permute-start | bytes 1572872 | tf_op jit(solution)/shard_map/ppermute | solution.py:37
  334.3 5.2 copy-start.11
  334.3 5.2 copy-start.12
  340.6 58.1 %collective-permute-start.25 = (bf16[256,1024]{1,0:T(8,128)(2,1)}, bf16[256,1024]{1,0:T(8,128)(2,1)}, u32[]{:S(2)}, u32[]{:S(2)}) collective-permute-start(bf16[256,1024]{1,0:T(8,128)(2,1)} %add_convert_fusion.3), channel_id=1, source_target_pairs={{0,8},{4,12},{8,0},{12,4},{16,24},{20,28},{24,16},{28,20},{1,9},{5... | collective-permute-start | bytes 1572872 | tf_op jit(solution)/shard_map/ppermute | solution.py:37
  341.3 62.2 %collective-permute-start.12 = (bf16[128,2048]{1,0:T(8,128)(2,1)}, bf16[128,2048]{1,0:T(8,128)(2,1)}, u32[]{:S(2)}, u32[]{:S(2)}) collective-permute-start(bf16[128,2048]{1,0:T(8,128)(2,1)} %get-tuple-element.96), channel_id=1, source_target_pairs={{0,1},{1,2},{2,3},{3,0},{4,5},{5,6},{6,7},{7,4},{8,9},{9,10},{10,1... | collective-permute-start | bytes 1572872 | tf_op jit(solution)/shard_map/ppermute | solution.py:134
  352.8 46.9 %collective-permute-start.26 = (bf16[256,1024]{1,0:T(8,128)(2,1)}, bf16[256,1024]{1,0:T(8,128)(2,1)}, u32[]{:S(2)}, u32[]{:S(2)}) collective-permute-start(bf16[256,1024]{1,0:T(8,128)(2,1)} %get-tuple-element.131), channel_id=1, source_target_pairs={{0,16},{4,20},{8,24},{12,28},{16,0},{20,4},{24,8},{28,12},{1,17},{... | collective-permute-start | bytes 1572872 | tf_op jit(solution)/shard_map/ppermute | solution.py:37
  354.0 36.2 %copy-start.6 = (bf16[256,2048]{1,0:T(8,128)(2,1)S(1)}, bf16[256,2048]{1,0:T(8,128)(2,1)}, u32[]{:S(2)}) copy-start(bf16[256,2048]{1,0:T(8,128)(2,1)} %get-tuple-element.105) | copy-start | bytes 3145732
  389.6 2.3 copy-start.4
  389.6 2.3 copy-start.5
  389.6 4.7 collective-permute-start.18
  389.7 6.0 %collective-permute-start.21 = (bf16[512,256]{1,0:T(8,128)(2,1)}, bf16[512,256]{1,0:T(8,128)(2,1)S(1)}, u32[]{:S(2)}, u32[]{:S(2)}) collective-permute-start(bf16[512,256]{1,0:T(8,128)(2,1)} %get-tuple-element.111), channel_id=1, source_target_pairs={{0,4},{4,0},{8,12},{12,8},{1,5},{5,1},{9,13},{13,9},{2,6},{6,2},{1... | collective-permute-start | bytes 786440 | tf_op jit(solution)/shard_map/ppermute | solution.py:37
  391.8 1.4 copy-start.9
  391.9 1.4 copy-start.10
  391.9 2.4 copy-start.21
  391.9 3.7 copy-start.14
  391.9 3.8 copy-start.20
  393.3 6.5 %copy-start.17 = (bf16[256,2048]{1,0:T(8,128)(2,1)S(1)}, bf16[256,2048]{1,0:T(8,128)(2,1)}, u32[]{:S(2)}) copy-start(bf16[256,2048]{1,0:T(8,128)(2,1)} %get-tuple-element.108) | copy-start | bytes 3145732
  393.3 7.6 %copy-start.13 = (f32[512,256]{1,0:T(8,128)S(1)}, f32[512,256]{1,0:T(8,128)}, u32[]{:S(2)}) copy-start(f32[512,256]{1,0:T(8,128)} %get-tuple-element.110) | copy-start | bytes 1572868
  393.3 7.7 %copy-start.3 = (f32[256,1024]{1,0:T(8,128)S(1)}, f32[256,1024]{1,0:T(8,128)}, u32[]{:S(2)}) copy-start(f32[256,1024]{1,0:T(8,128)} %get-tuple-element.127) | copy-start | bytes 3145732
  394.3 26.9 %collective-permute-start.13 = (bf16[128,2048]{1,0:T(8,128)(2,1)S(1)}, bf16[128,2048]{1,0:T(8,128)(2,1)S(1)}, u32[]{:S(2)}, u32[]{:S(2)}) collective-permute-start(bf16[128,2048]{1,0:T(8,128)(2,1)S(1)} %copy-done.21), channel_id=1, source_target_pairs={{0,2},{1,3},{2,0},{3,1},{4,6},{5,7},{6,4},{7,5},{8,10},{9,11},{10,... | collective-permute-start | bytes 1572872 | tf_op jit(solution)/shard_map/ppermute | solution.py:134
  395.7 26.4 %collective-permute-start.14 = (bf16[128,2048]{1,0:T(8,128)(2,1)S(1)}, bf16[128,2048]{1,0:T(8,128)(2,1)S(1)}, u32[]{:S(2)}, u32[]{:S(2)}) collective-permute-start(bf16[128,2048]{1,0:T(8,128)(2,1)S(1)} %copy-done.20), channel_id=1, source_target_pairs={{0,3},{1,0},{2,1},{3,2},{4,7},{5,4},{6,5},{7,6},{8,11},{9,8},{10,9... | collective-permute-start | bytes 1572872 | tf_op jit(solution)/shard_map/ppermute | solution.py:134
  398.7 26.1 %collective-permute-start.19 = (bf16[256,2048]{1,0:T(8,128)(2,1)S(1)}, bf16[256,2048]{1,0:T(8,128)(2,1)S(1)}, u32[]{:S(2)}, u32[]{:S(2)}) collective-permute-start(bf16[256,2048]{1,0:T(8,128)(2,1)S(1)} %add_convert_fusion.1), channel_id=1, source_target_pairs={{0,8},{4,12},{8,0},{12,4},{16,24},{20,28},{24,16},{28,20},{1,9},{5... | collective-permute-start | bytes 3145736 | tf_op jit(solution)/shard_map/ppermute | solution.py:37
  399.7 37.1 %collective-permute-start.20 = (bf16[256,2048]{1,0:T(8,128)(2,1)S(1)}, bf16[256,2048]{1,0:T(8,128)(2,1)S(1)}, u32[]{:S(2)}, u32[]{:S(2)}) collective-permute-start(bf16[256,2048]{1,0:T(8,128)(2,1)S(1)} %copy-done.17), channel_id=1, source_target_pairs={{0,16},{4,20},{8,24},{12,28},{16,0},{20,4},{24,8},{28,12},{1,17},{... | collective-permute-start | bytes 3145736 | tf_op jit(solution)/shard_map/ppermute | solution.py:37
  400.9 22.5 %copy-start.8 = (bf16[128,2048]{1,0:T(8,128)(2,1)S(1)}, bf16[128,2048]{1,0:T(8,128)(2,1)}, u32[]{:S(2)}) copy-start(bf16[128,2048]{1,0:T(8,128)(2,1)} %get-tuple-element.95) | copy-start | bytes 1572868
  403.5 33.3 %copy-start.1 = (f32[256,2048]{1,0:T(8,128)S(1)}, f32[256,2048]{1,0:T(8,128)}, u32[]{:S(2)}) copy-start(f32[256,2048]{1,0:T(8,128)} %get-tuple-element.104) | copy-start | bytes 6291460
  403.5 157.2 %collective-permute-start.28 = (bf16[256,1024]{1,0:T(8,128)(2,1)}, bf16[256,1024]{1,0:T(8,128)(2,1)}, u32[]{:S(2)}, u32[]{:S(2)}) collective-permute-start(bf16[256,1024]{1,0:T(8,128)(2,1)} %add_convert_fusion.2), channel_id=1, source_target_pairs={{0,16},{4,20},{8,24},{12,28},{16,0},{20,4},{24,8},{28,12},{1,17},{... | collective-permute-start | bytes 1572872 | tf_op jit(solution)/shard_map/ppermute | solution.py:37
  421.2 148.6 %collective-permute-start.24 = (bf16[256,2048]{1,0:T(8,128)(2,1)}, bf16[256,2048]{1,0:T(8,128)(2,1)}, u32[]{:S(2)}, u32[]{:S(2)}) collective-permute-start(bf16[256,2048]{1,0:T(8,128)(2,1)} %add_convert_fusion), channel_id=1, source_target_pairs={{0,16},{4,20},{8,24},{12,28},{16,0},{20,4},{24,8},{28,12},{1,17},{... | collective-permute-start | bytes 3145736 | tf_op jit(solution)/shard_map/ppermute | solution.py:37
  422.1 16.4 %collective-permute-start.22 = (bf16[512,256]{1,0:T(8,128)(2,1)S(1)}, bf16[512,256]{1,0:T(8,128)(2,1)S(1)}, u32[]{:S(2)}, u32[]{:S(2)}) collective-permute-start(bf16[512,256]{1,0:T(8,128)(2,1)S(1)} %add_convert_fusion.5), channel_id=1, source_target_pairs={{0,8},{4,12},{8,0},{12,4},{1,9},{5,13},{9,1},{13,5},{2,10},{6,14},... | collective-permute-start | bytes 786440 | tf_op jit(solution)/shard_map/ppermute | solution.py:37
  424.8 127.0 %collective-permute-start.17 = (bf16[128,2048]{1,0:T(8,128)(2,1)S(1)}, bf16[128,2048]{1,0:T(8,128)(2,1)S(1)}, u32[]{:S(2)}, u32[]{:S(2)}) collective-permute-start(bf16[128,2048]{1,0:T(8,128)(2,1)S(1)} %add_convert_fusion.4.refs_0_), channel_id=1, source_target_pairs={{0,3},{1,0},{2,1},{3,2},{4,7},{5,4},{6,5},{7,6},{8,11},{9,8},{10,9... | collective-permute-start | bytes 1572872 | tf_op jit(solution)/shard_map/ppermute | solution.py:144
  436.8 116.1 %collective-permute-start.16 = (bf16[128,2048]{1,0:T(8,128)(2,1)S(1)}, bf16[128,2048]{1,0:T(8,128)(2,1)}, u32[]{:S(2)}, u32[]{:S(2)}) collective-permute-start(bf16[128,2048]{1,0:T(8,128)(2,1)S(1)} %add_convert_fusion.4.refs_0_), channel_id=1, source_target_pairs={{0,2},{1,3},{2,0},{3,1},{4,6},{5,7},{6,4},{7,5},{8,10},{9,11},{10,... | collective-permute-start | bytes 1572872 | tf_op jit(solution)/shard_map/ppermute | solution.py:144
  438.6 119.4 %collective-permute-start.15 = (bf16[128,2048]{1,0:T(8,128)(2,1)S(1)}, bf16[128,2048]{1,0:T(8,128)(2,1)}, u32[]{:S(2)}, u32[]{:S(2)}) collective-permute-start(bf16[128,2048]{1,0:T(8,128)(2,1)S(1)} %add_convert_fusion.4.refs_0_), channel_id=1, source_target_pairs={{0,1},{1,2},{2,3},{3,0},{4,5},{5,6},{6,7},{7,4},{8,9},{9,10},{10,1... | collective-permute-start | bytes 1572872 | tf_op jit(solution)/shard_map/ppermute | solution.py:144
  545.5 4.0 copy-start.15
  545.5 6.3 %copy-start.19 = (bf16[256,1024]{1,0:T(8,128)(2,1)S(1)}, bf16[256,1024]{1,0:T(8,128)(2,1)}, u32[]{:S(2)}) copy-start(bf16[256,1024]{1,0:T(8,128)(2,1)} %get-tuple-element.134) | copy-start | bytes 1572868
  551.8 14.8 %collective-permute-start.27 = (bf16[256,1024]{1,0:T(8,128)(2,1)S(1)}, bf16[256,1024]{1,0:T(8,128)(2,1)S(1)}, u32[]{:S(2)}, u32[]{:S(2)}) collective-permute-start(bf16[256,1024]{1,0:T(8,128)(2,1)S(1)} %copy-done.19), channel_id=1, source_target_pairs={{0,8},{4,12},{8,0},{12,4},{16,24},{20,28},{24,16},{28,20},{1,9},{5... | collective-permute-start | bytes 1572872 | tf_op jit(solution)/shard_map/ppermute | solution.py:37
  552.9 35.5 %collective-permute-start.23 = (bf16[256,2048]{1,0:T(8,128)(2,1)}, bf16[256,2048]{1,0:T(8,128)(2,1)}, u32[]{:S(2)}, u32[]{:S(2)}) collective-permute-start(bf16[256,2048]{1,0:T(8,128)(2,1)} %get-tuple-element.123), channel_id=1, source_target_pairs={{0,8},{4,12},{8,0},{12,4},{16,24},{20,28},{24,16},{28,20},{1,9},{5... | collective-permute-start | bytes 3145736 | tf_op jit(solution)/shard_map/ppermute | solution.py:37
  558.0 8.6 %copy-start.2 = (f32[256,1024]{1,0:T(8,128)S(1)}, f32[256,1024]{1,0:T(8,128)}, u32[]{:S(2)}) copy-start(f32[256,1024]{1,0:T(8,128)} %get-tuple-element.132) | copy-start | bytes 3145732
  560.7 7.3 %copy-start = (f32[1024,256]{0,1:T(8,128)S(1)}, f32[1024,256]{0,1:T(8,128)}, u32[]{:S(2)}) copy-start(f32[1024,256]{0,1:T(8,128)} %add_bitcast_fusion.1) | copy-start | bytes 3145732
